TPU v7x, 32 devices: a whole 2x2x4 slice. The times are simulated.
32 devices in a mesh: dp: 4 (over y, core), seq: 8 (over z, x).
Axes of the slice: x: 2, y: 2, z: 4, core: 2. Of those that a mesh axis runs over, the one named last changes fastest.
Arguments:
- inputs: bfloat16 [8, 1024, 512], P('dp', 'seq'), may hold values from -6 to 6
- encoder: bfloat16 [8, 1024, 512], P('dp', 'seq'), may hold values from -6 to 6
- teacher: bfloat16 [8, 1024, 512], P('dp', 'seq')
- dec_seg: int32 [8, 1024], P('dp'), may hold values from 0 to 7, as said below
- enc_seg: int32 [8, 1024], P('dp'), may hold values from 0 to 7, as said below
- dec_valid: int32 [8, 1024], P('dp', 'seq'), may hold values from 0 to 1, as said below
- self_in: bfloat16 [512, 1536], P(('dp', 'seq')), may hold values from -0.25 to 0.25
- self_out: bfloat16 [512, 512], P(('dp', 'seq')), may hold values from -2 to 2
- cross_query: bfloat16 [512, 512], P(('dp', 'seq')), may hold values from -0.25 to 0.25
- cross_in: bfloat16 [512, 1024], P(('dp', 'seq')), may hold values from -0.25 to 0.25
- cross_out: bfloat16 [512, 512], P(('dp', 'seq')), may hold values from -2 to 2
- ffn_up: bfloat16 [512, 2048], P(('dp', 'seq')), may hold values from -0.25 to 0.25
- ffn_down: bfloat16 [2048, 512], P(('dp', 'seq')), may hold values from -0.125 to 0.125
- norm_gain: bfloat16 [3, 512], P(None, ('dp', 'seq')), may hold values from 0.5 to 1.5
- norm_bias: bfloat16 [3, 512], P(None, ('dp', 'seq')), may hold values from -1 to 1
Outputs:
- outputs: bfloat16 [8, 1024, 512], P('dp', 'seq')
- loss: float32 [], replicated
- grad_inputs: float32 [8, 1024, 512], P('dp', 'seq')
- grad_encoder: float32 [8, 1024, 512], P('dp', 'seq')
- grad_self_in: float32 [512, 1536], P(('dp', 'seq'))
- grad_self_out: float32 [512, 512], P(('dp', 'seq'))
- grad_cross_query: float32 [512, 512], P(('dp', 'seq'))
- grad_cross_in: float32 [512, 1024], P(('dp', 'seq'))
- grad_cross_out: float32 [512, 512], P(('dp', 'seq'))
- grad_ffn_up: float32 [512, 2048], P(('dp', 'seq'))
- grad_ffn_down: float32 [2048, 512], P(('dp', 'seq'))
- grad_norm_gain: float32 [3, 512], P(None, ('dp', 'seq'))
- grad_norm_bias: float32 [3, 512], P(None, ('dp', 'seq'))
Inputs may be any that keep to these rules, and one draw needn't show every extreme that they name: `dec_seg`: along each sequence the numbers start at 0 and never fall; every number but the largest marks one document of 60 to 640 tokens; the largest marks the padding at the sequence's end, at least one position. The first sequence holds one document of exactly 640 tokens followed by as many documents of exactly 60 tokens as fit before its last position; no sequence holds more documents than it. `enc_seg`: numbered as dec_seg: encoder document k belongs to decoder document k of the same sequence, every decoder document has one, and the largest number marks padding of at least one position, matched by the decoder's padding. The first sequence is laid out as in dec_seg. `dec_valid`: 1 exactly where dec_seg is below its sequence's largest number.
All inputs are finite; a program needn't handle non-finite values.
Results may differ from a plain program's by a relative error of at most 0.02.
Values may be sent and summed in bfloat16 or wider, within the bound.
No kernel may reach another device: no remote copies, remote signals or barrier semaphores. Data moves between devices by JAX's collectives and lax.ppermute only.
A program may use at most 192 MiB of HBM per device.

v0:
```python
import jax
import jax.numpy as jnp
from jax import lax
from jax.sharding import PartitionSpec as P

HEADS = 8
HEAD_DIM = 64


NORM_EPSILON = 1e-05
MASK_FLOOR = -1e30


def layer_norm(residual, gain_row, bias_row):
    centre = residual - jnp.mean(residual, axis=-1, keepdims=True)
    spread = jnp.mean(centre * centre, axis=-1, keepdims=True)
    return centre * lax.rsqrt(spread + NORM_EPSILON) * gain_row + bias_row


def to_heads(tensor):
    seq_count, positions, widths = tensor.shape
    return tensor.reshape(seq_count, positions, HEADS, HEAD_DIM).transpose(2, 0, 1, 3)


def from_heads(tensor):
    head_count, seq_count, positions, head_width = tensor.shape
    return tensor.transpose(1, 2, 0, 3).reshape(seq_count, positions, head_count * head_width)


def attend_forward(queries, keys_full, values_full, allowed):
    score_scale = HEAD_DIM ** (-0.5)

    def attend_one_head(pieces):
        query_heads, key_heads, value_heads = pieces
        scores = (
            jnp.einsum("sqd,skd->sqk", query_heads, key_heads, preferred_element_type=jnp.float32)
            * score_scale
        )
        masked = jnp.where(allowed, scores, MASK_FLOOR)
        row_peak = jnp.max(masked, axis=2, keepdims=True)
        numerators = jnp.where(allowed, jnp.exp(masked - row_peak), 0.0)
        row_total = jnp.sum(numerators, axis=2, keepdims=True)
        attn_probs = (numerators / row_total).astype(jnp.bfloat16)
        mixed_out = jnp.einsum(
            "sqk,skd->sqd", attn_probs, value_heads, preferred_element_type=jnp.float32
        )
        return (mixed_out.astype(jnp.bfloat16), (row_peak + jnp.log(row_total))[..., 0])

    mixed_heads, logsum = lax.map(
        attend_one_head, (to_heads(queries), to_heads(keys_full), to_heads(values_full))
    )
    return (from_heads(mixed_heads), logsum)


def query_grads(queries, keys_full, values_full, grad_out, logsum, allowed):
    score_scale = HEAD_DIM ** (-0.5)

    def query_one_head(pieces):
        query_heads, key_heads, value_heads, grad_heads, logsum_heads = pieces
        scores = (
            jnp.einsum("sqd,skd->sqk", query_heads, key_heads, preferred_element_type=jnp.float32)
            * score_scale
        )
        attn_probs = jnp.where(
            allowed, jnp.exp(jnp.where(allowed, scores, MASK_FLOOR) - logsum_heads[..., None]), 0.0
        )
        d_probs = jnp.einsum(
            "sqd,skd->sqk", grad_heads, value_heads, preferred_element_type=jnp.float32
        )
        row_delta = jnp.sum(attn_probs * d_probs, axis=2)
        d_scores = (attn_probs * (d_probs - row_delta[..., None])).astype(jnp.bfloat16)
        d_query = (
            jnp.einsum("sqk,skd->sqd", d_scores, key_heads, preferred_element_type=jnp.float32)
            * score_scale
        )
        d_keys = (
            jnp.einsum("sqk,sqd->skd", d_scores, query_heads, preferred_element_type=jnp.float32)
            * score_scale
        )
        d_values = jnp.einsum(
            "sqk,sqd->skd",
            attn_probs.astype(jnp.bfloat16),
            grad_heads,
            preferred_element_type=jnp.float32,
        )
        return (d_query, row_delta, d_keys, d_values)

    results = lax.map(
        query_one_head,
        (to_heads(queries), to_heads(keys_full), to_heads(values_full), to_heads(grad_out), logsum),
    )
    return (from_heads(results[0]), results[1], from_heads(results[2]), from_heads(results[3]))


def attention_back(branch_kind, queries, keys_full, values_full, grad_out, logsum, allowed):
    d_query, row_delta, keys_part, values_part = query_grads(
        queries, keys_full, values_full, grad_out, logsum, allowed
    )
    if branch_kind == "self":
        d_keys, d_values = (
            lax.psum_scatter(
                keys_part.astype(jnp.bfloat16), "seq", scatter_dimension=1, tiled=True
            ).astype(jnp.float32),
            lax.psum_scatter(
                values_part.astype(jnp.bfloat16), "seq", scatter_dimension=1, tiled=True
            ).astype(jnp.float32),
        )
    else:
        d_keys, d_values = (
            lax.psum_scatter(
                keys_part.astype(jnp.bfloat16), "seq", scatter_dimension=1, tiled=True
            ).astype(jnp.float32),
            lax.psum_scatter(
                values_part.astype(jnp.bfloat16), "seq", scatter_dimension=1, tiled=True
            ).astype(jnp.float32),
        )
    return (d_query, d_keys, d_values)


def shards(
    inputs,
    encoder,
    teacher,
    dec_seg,
    enc_seg,
    dec_valid,
    self_in,
    self_out,
    cross_query,
    cross_in,
    cross_out,
    ffn_up,
    ffn_down,
    norm_gain,
    norm_bias,
):
    seq_count, tok_rows, widths = inputs.shape
    flat_rows = seq_count * tok_rows
    seq_length = dec_seg.shape[1]
    row_start = lax.axis_index("seq") * tok_rows
    own_positions = row_start + jnp.arange(tok_rows, dtype=jnp.int32)
    all_positions = jnp.arange(seq_length, dtype=jnp.int32)
    dec_own = lax.dynamic_slice_in_dim(dec_seg, row_start, tok_rows, 1)
    allowed_self = (dec_own[:, :, None] == dec_seg[:, None, :]) & (
        all_positions[None, None, :] <= own_positions[None, :, None]
    )
    allowed_cross = dec_own[:, :, None] == enc_seg[:, None, :]
    fwd_weights = (
        lax.all_gather(self_in, ("dp", "seq"), axis=0, tiled=True),
        lax.all_gather(self_out, ("dp", "seq"), axis=0, tiled=True),
        lax.all_gather(cross_query, ("dp", "seq"), axis=0, tiled=True),
        lax.all_gather(cross_in, ("dp", "seq"), axis=0, tiled=True),
        lax.all_gather(cross_out, ("dp", "seq"), axis=0, tiled=True),
        lax.all_gather(ffn_up, ("dp", "seq"), axis=0, tiled=True),
        lax.all_gather(ffn_down, ("dp", "seq"), axis=0, tiled=True),
        lax.all_gather(norm_gain, ("dp", "seq"), axis=1, tiled=True),
        lax.all_gather(norm_bias, ("dp", "seq"), axis=1, tiled=True),
    )
    w_in, w_out, c_query, c_in, c_out, w_up, w_down, gains, biases = fwd_weights
    gain_rows = gains.astype(jnp.float32)
    bias_rows = biases.astype(jnp.float32)
    flat_in = inputs.reshape(flat_rows, widths)
    projected = jnp.dot(flat_in, w_in, preferred_element_type=jnp.float32).astype(jnp.bfloat16)
    queries = projected[:, :widths].reshape(seq_count, tok_rows, widths)
    keys_own = projected[:, widths : 2 * widths].reshape(seq_count, tok_rows, widths)
    values_own = projected[:, 2 * widths :].reshape(seq_count, tok_rows, widths)
    keys_full, values_full = (
        lax.all_gather(keys_own, "seq", axis=1, tiled=True),
        lax.all_gather(values_own, "seq", axis=1, tiled=True),
    )
    attended, self_logsum = attend_forward(queries, keys_full, values_full, allowed_self)
    flat_att = attended.reshape(flat_rows, widths)
    resid_one = flat_in.astype(jnp.float32) + jnp.dot(
        flat_att, w_out, preferred_element_type=jnp.float32
    )
    normed_one = layer_norm(resid_one, gain_rows[0], bias_rows[0])
    low_one = normed_one.astype(jnp.bfloat16)
    cross_q = (
        jnp.dot(low_one, c_query, preferred_element_type=jnp.float32)
        .astype(jnp.bfloat16)
        .reshape(seq_count, tok_rows, widths)
    )
    flat_enc = encoder.reshape(flat_rows, widths)
    enc_proj = jnp.dot(flat_enc, c_in, preferred_element_type=jnp.float32).astype(jnp.bfloat16)
    enc_keys = enc_proj[:, :widths].reshape(seq_count, tok_rows, widths)
    enc_values = enc_proj[:, widths:].reshape(seq_count, tok_rows, widths)
    enc_keys_full, enc_values_full = (
        lax.all_gather(enc_keys, "seq", axis=1, tiled=True),
        lax.all_gather(enc_values, "seq", axis=1, tiled=True),
    )
    cross_mix, cross_logsum = attend_forward(cross_q, enc_keys_full, enc_values_full, allowed_cross)
    flat_cross = cross_mix.reshape(flat_rows, widths)
    resid_two = normed_one + jnp.dot(flat_cross, c_out, preferred_element_type=jnp.float32)
    normed_two = layer_norm(resid_two, gain_rows[1], bias_rows[1])
    low_two = normed_two.astype(jnp.bfloat16)
    hidden_pre = jnp.dot(low_two, w_up, preferred_element_type=jnp.float32)
    hidden_act = jax.nn.silu(hidden_pre).astype(jnp.bfloat16)
    resid_three = normed_two + jnp.dot(hidden_act, w_down, preferred_element_type=jnp.float32)
    result = layer_norm(resid_three, gain_rows[2], bias_rows[2])
    valid_rows = dec_valid.reshape(flat_rows).astype(jnp.float32)
    error = (result - teacher.reshape(flat_rows, widths).astype(jnp.float32)) * valid_rows[:, None]
    total_sq, total_count = lax.psum((jnp.sum(error * error), jnp.sum(valid_rows)), ("dp", "seq"))
    loss_value = total_sq / (total_count * widths)
    back_weights = (
        lax.all_gather(self_in, ("dp", "seq"), axis=0, tiled=True),
        lax.all_gather(self_out, ("dp", "seq"), axis=0, tiled=True),
        lax.all_gather(cross_query, ("dp", "seq"), axis=0, tiled=True),
        lax.all_gather(cross_in, ("dp", "seq"), axis=0, tiled=True),
        lax.all_gather(cross_out, ("dp", "seq"), axis=0, tiled=True),
        lax.all_gather(ffn_up, ("dp", "seq"), axis=0, tiled=True),
        lax.all_gather(ffn_down, ("dp", "seq"), axis=0, tiled=True),
        lax.all_gather(norm_gain, ("dp", "seq"), axis=1, tiled=True),
        lax.all_gather(norm_bias, ("dp", "seq"), axis=1, tiled=True),
    )
    w_in, w_out, c_query, c_in, c_out, w_up, w_down, gains, biases = back_weights
    gain_rows = gains.astype(jnp.float32)
    bias_rows = biases.astype(jnp.float32)
    d_resid_three, d_gain_three, d_bias_three = jax.vjp(
        layer_norm, resid_three, gain_rows[2], bias_rows[2]
    )[1](error)
    d_ffn = d_resid_three.astype(jnp.bfloat16)
    g_ffn_down = jnp.dot(hidden_act.T, d_ffn, preferred_element_type=jnp.float32)
    d_act = jnp.dot(d_ffn, w_down.T, preferred_element_type=jnp.float32)
    d_hidden = jax.vjp(jax.nn.silu, hidden_pre)[1](d_act)[0].astype(jnp.bfloat16)
    g_ffn_up = jnp.dot(low_two.T, d_hidden, preferred_element_type=jnp.float32)
    d_normed_two = d_resid_three + jnp.dot(d_hidden, w_up.T, preferred_element_type=jnp.float32)
    d_resid_two, d_gain_two, d_bias_two = jax.vjp(
        layer_norm, resid_two, gain_rows[1], bias_rows[1]
    )[1](d_normed_two)
    d_cross = d_resid_two.astype(jnp.bfloat16)
    g_cross_out = jnp.dot(flat_cross.T, d_cross, preferred_element_type=jnp.float32)
    d_cross_mix = (
        jnp.dot(d_cross, c_out.T, preferred_element_type=jnp.float32)
        .astype(jnp.bfloat16)
        .reshape(seq_count, tok_rows, widths)
    )
    d_cross_q, d_enc_keys, d_enc_values = attention_back(
        "cross", cross_q, enc_keys_full, enc_values_full, d_cross_mix, cross_logsum, allowed_cross
    )
    d_enc_kv = (
        jnp.concatenate([d_enc_keys, d_enc_values], axis=2)
        .reshape(flat_rows, 2 * widths)
        .astype(jnp.bfloat16)
    )
    g_cross_in = jnp.dot(flat_enc.T, d_enc_kv, preferred_element_type=jnp.float32)
    grad_encoder = jnp.dot(d_enc_kv, c_in.T, preferred_element_type=jnp.float32).reshape(
        seq_count, tok_rows, widths
    )
    d_query_cross = d_cross_q.reshape(flat_rows, widths).astype(jnp.bfloat16)
    g_cross_query = jnp.dot(low_one.T, d_query_cross, preferred_element_type=jnp.float32)
    d_normed_one = d_resid_two + jnp.dot(
        d_query_cross, c_query.T, preferred_element_type=jnp.float32
    )
    d_resid_one, d_gain_one, d_bias_one = jax.vjp(
        layer_norm, resid_one, gain_rows[0], bias_rows[0]
    )[1](d_normed_one)
    d_self = d_resid_one.astype(jnp.bfloat16)
    g_self_out = jnp.dot(flat_att.T, d_self, preferred_element_type=jnp.float32)
    d_self_mix = (
        jnp.dot(d_self, w_out.T, preferred_element_type=jnp.float32)
        .astype(jnp.bfloat16)
        .reshape(seq_count, tok_rows, widths)
    )
    d_query, d_keys, d_values = attention_back(
        "self", queries, keys_full, values_full, d_self_mix, self_logsum, allowed_self
    )
    d_qkv = (
        jnp.concatenate([d_query, d_keys, d_values], axis=2)
        .reshape(flat_rows, 3 * widths)
        .astype(jnp.bfloat16)
    )
    g_self_in = jnp.dot(flat_in.T, d_qkv, preferred_element_type=jnp.float32)
    grad_inputs = (
        d_resid_one + jnp.dot(d_qkv, w_in.T, preferred_element_type=jnp.float32)
    ).reshape(seq_count, tok_rows, widths)
    g_gain = jnp.stack([d_gain_one, d_gain_two, d_gain_three])
    g_bias = jnp.stack([d_bias_one, d_bias_two, d_bias_three])
    summed = (
        lax.psum_scatter(g_self_in, ("dp", "seq"), scatter_dimension=0, tiled=True),
        lax.psum_scatter(g_self_out, ("dp", "seq"), scatter_dimension=0, tiled=True),
        lax.psum_scatter(g_cross_query, ("dp", "seq"), scatter_dimension=0, tiled=True),
        lax.psum_scatter(g_cross_in, ("dp", "seq"), scatter_dimension=0, tiled=True),
        lax.psum_scatter(g_cross_out, ("dp", "seq"), scatter_dimension=0, tiled=True),
        lax.psum_scatter(g_ffn_up, ("dp", "seq"), scatter_dimension=0, tiled=True),
        lax.psum_scatter(g_ffn_down, ("dp", "seq"), scatter_dimension=0, tiled=True),
        lax.psum_scatter(g_gain, ("dp", "seq"), scatter_dimension=1, tiled=True),
        lax.psum_scatter(g_bias, ("dp", "seq"), scatter_dimension=1, tiled=True),
    )
    outputs = result.astype(jnp.bfloat16).reshape(seq_count, tok_rows, widths)
    return (
        outputs,
        loss_value,
        grad_inputs,
        grad_encoder,
        summed[0],
        summed[1],
        summed[2],
        summed[3],
        summed[4],
        summed[5],
        summed[6],
        summed[7],
        summed[8],
    )


def solution(mesh):
    placed = (
        P("dp", "seq", None),
        P("dp", "seq", None),
        P("dp", "seq", None),
        P("dp", None),
        P("dp", None),
        P("dp", "seq"),
        P(("dp", "seq"), None),
        P(("dp", "seq"), None),
        P(("dp", "seq"), None),
        P(("dp", "seq"), None),
        P(("dp", "seq"), None),
        P(("dp", "seq"), None),
        P(("dp", "seq"), None),
        P(None, ("dp", "seq")),
        P(None, ("dp", "seq")),
    )
    return jax.shard_map(
        shards,
        mesh=mesh,
        in_specs=placed,
        out_specs=(
            P("dp", "seq", None),
            P(),
            P("dp", "seq", None),
            P("dp", "seq", None),
            P(("dp", "seq"), None),
            P(("dp", "seq"), None),
            P(("dp", "seq"), None),
            P(("dp", "seq"), None),
            P(("dp", "seq"), None),
            P(("dp", "seq"), None),
            P(("dp", "seq"), None),
            P(None, ("dp", "seq")),
            P(None, ("dp", "seq")),
        ),
        check_vma=False,
    )
```

profile of v0, /device:TPU:0, one launch (start us, length us, event | category | flops | bytes accessed | tf_op | source)
XLA Modules:
  0.0 2125.2 jit_solution(10514565736972931520)
XLA Ops:
  8.7 58.8 %all-gather.17.cloned.1.call-done = bf16[512,1024]{1,0:T(8,128)(2,1)} async-done(((bf16[16,1024]{1,0:T(8,128)(2,1)}), bf16[512,1024]{1,0:T(8,128)(2,1)}) %all-gather.17.cloned.1.call-update) | async-done | bytes 1048592 | tf_op jit(solution)/shard_map/all_gather | solution.py:152
  71.1 53.4 %all-gather.11.cloned.1.call-done = bf16[512,1536]{1,0:T(8,128)(2,1)} async-done(((bf16[16,1536]{1,0:T(8,128)(2,1)}), bf16[512,1536]{1,0:T(8,128)(2,1)}) %all-gather.11.cloned.1.call-update) | async-done | bytes 1572880 | tf_op jit(solution)/shard_map/all_gather | solution.py:149
  130.6 66.6 %all-gather = bf16[32,16,3]{1,2,0:T(4,128)(2,1)S(1)} all-gather(bf16[1,16,3]{1,2,0:T(4,128)(2,1)S(1)} %bitcast.454), channel_id=1, replica_groups=mesh['dp'=4,'seq'=8] {'dp','seq'}, dimensions={0}, use_global_device_ids=true | all-gather | bytes 3168 | tf_op jit(solution)/shard_map/all_gather | solution.py:156
  197.3 63.8 %all-gather.1 = bf16[32,16,3]{1,2,0:T(4,128)(2,1)S(1)} all-gather(bf16[1,16,3]{1,2,0:T(4,128)(2,1)S(1)} %bitcast.455), channel_id=1, replica_groups=mesh['dp'=4,'seq'=8] {'dp','seq'}, dimensions={0}, use_global_device_ids=true | all-gather | bytes 3168 | tf_op jit(solution)/shard_map/all_gather | solution.py:157
  263.0 70.9 %all_gather.50 = bf16[512,512]{1,0:T(8,128)(2,1)S(1)} all-gather(bf16[16,512]{1,0:T(8,128)(2,1)S(1)} %copy-done.56), channel_id=1, replica_groups=mesh['dp'=4,'seq'=8] {'dp','seq'}, dimensions={0}, use_global_device_ids=true | all-gather | bytes 540672 | tf_op jit(solution)/shard_map/all_gather | solution.py:150
  333.8 67.6 %all_gather.53 = bf16[512,512]{1,0:T(8,128)(2,1)S(1)} all-gather(bf16[16,512]{1,0:T(8,128)(2,1)S(1)} %copy-done.57), channel_id=1, replica_groups=mesh['dp'=4,'seq'=8] {'dp','seq'}, dimensions={0}, use_global_device_ids=true | all-gather | bytes 540672 | tf_op jit(solution)/shard_map/all_gather | solution.py:151
  401.4 73.9 %all_gather.57 = bf16[512,512]{1,0:T(8,128)(2,1)} all-gather(bf16[16,512]{1,0:T(8,128)(2,1)S(1)} %copy-done.58), channel_id=1, replica_groups=mesh['dp'=4,'seq'=8] {'dp','seq'}, dimensions={0}, use_global_device_ids=true | all-gather | bytes 540672 | tf_op jit(solution)/shard_map/all_gather | solution.py:153
  489.1 30.1 %while.56 = (s32[]{:T(128)}, bf16[8,2,128,64]{2,3,1,0:T(8,128)(2,1)}, f32[8,2,128]{2,1,0:T(2,128)}, bf16[8,2,128,64]{2,3,1,0:T(8,128)(2,1)}, bf16[8,2,1024,64]{2...) while((s32[]{:T(128)}, ...), condition=%wide.region_3.4_spmd.clone, body=%wide.region_0.3_spmd.clone.sunk | while | flops 71319296 | bytes 4166769 | solution.py:49
  523.3 25.9 %while.57 = (s32[]{:T(128)}, bf16[8,2,128,64]{2,3,1,0:T(8,128)(2,1)S(1)}, f32[8,2,128]{2,1,0:T(2,128)S(1)}, bf16[8,2,128,64]{2,3,1,0:T(8,128)(2,1)S(1)}, bf16[8,...) while((s32[]{:T(128)}, ...), condition=%wide.region_9.10_spmd.clone, body=%wide.region_6.9_spmd.clone.sunk | while | flops 70532864 | bytes 3773545 | solution.py:49
  569.1 66.6 %while.58 = (s32[]{:T(128)}, bf16[8,2,128,64]{2,3,1,0:T(8,128)(2,1)}, bf16[8,2,1024,64]{2,3,0,1:T(8,128)(2,1)}, bf16[8,2,1024,64]{2,3,0,1:T(8,128)(2,1)S(1)}, bf...) while((s32[]{:T(128)}, ...), condition=%wide.region_24.25_spmd.clone, body=%wide.region_22.24_spmd.clone.sunk | while | flops 170802944 | bytes 9979021 | solution.py:88
  651.0 62.5 %while.59 = (s32[]{:T(128)}, bf16[8,2,128,64]{2,3,1,0:T(8,128)(2,1)S(1)}, bf16[8,2,1024,64]{2,3,0,1:T(8,128)(2,1)}, bf16[8,2,1024,64]{2,3,0,1:T(8,128)(2,1)}, bf...) while((s32[]{:T(128)}, ...), condition=%wide.region_29.30_spmd.clone, body=%wide.region_27.29_spmd.clone.sunk | while | flops 171065088 | bytes 10110101 | solution.py:88
  745.6 29.7 %reduce-scatter.28.cloned.1.call-done = bf16[2,128,512]{2,1,0:T(8,128)(2,1)} async-done(((bf16[2,1024,512]{2,1,0:T(8,128)(2,1)}), bf16[2,128,512]{2,1,0:T(8,128)(2,1)}) %reduce-scatter.28.cloned.1.call-update) | async-done | bytes 262160 | tf_op jit(solution)/shard_map/reduce_scatter | solution.py:113
  781.4 64.0 %reduce-scatter.42.cloned.1.call-done = bf16[128,1024]{1,0:T(8,128)(2,1)} async-done(((bf16[1024,1024]{1,0:T(8,128)(2,1)}), bf16[128,1024]{1,0:T(8,128)(2,1)}) %reduce-scatter.42.cloned.1.call-update) | async-done | bytes 262160
  846.9 68.6 %reduce-scatter.40.cloned.1.call-done = bf16[128,1024]{1,0:T(8,128)(2,1)} async-done(((bf16[1024,1024]{1,0:T(8,128)(2,1)}), bf16[128,1024]{1,0:T(8,128)(2,1)}) %reduce-scatter.40.cloned.1.call-update) | async-done | bytes 262160
  929.8 39.8 %all-reduce = (f32[]{:T(128)}, f32[]{:T(128)}) all-reduce(f32[]{:T(128)} %get-tuple-element.484, f32[]{:T(128)} %convert_reduce_fusion), channel_id=1, replica_groups=mesh['dp'=4,'seq'=8] {'dp','seq'}, use_global_device_ids=true, to_apply=%region_15.16 | all-reduce | flops 2 | bytes 16 | tf_op jit(solution)/shard_map/psum | solution.py:202
  971.0 79.2 %reduce-scatter.50.cloned.1.call-done = f32[16,3]{1,0:T(8,128)} async-done(((f32[512,3]{1,0:T(8,128)}), f32[16,3]{1,0:T(8,128)}) %reduce-scatter.50.cloned.1.call-update) | async-done | bytes 208
  1051.5 131.6 %reduce-scatter.48.cloned.1.call-done = f32[16,3]{1,0:T(8,128)} async-done(((f32[512,3]{1,0:T(8,128)}), f32[16,3]{1,0:T(8,128)}) %reduce-scatter.48.cloned.1.call-update) | async-done | bytes 208
  1189.5 128.0 %reduce-scatter.34.cloned.1.call-done = f32[16,512]{1,0:T(8,128)} async-done(((f32[512,512]{1,0:T(8,128)}), f32[16,512]{1,0:T(8,128)}) %reduce-scatter.34.cloned.1.call-update) | async-done | bytes 32784 | tf_op jit(solution)/shard_map/reduce_scatter | solution.py:283
  1317.5 134.3 %reduce-scatter.32.cloned.1.call-done = f32[16,512]{1,0:T(8,128)} async-done(((f32[512,512]{1,0:T(8,128)}), f32[16,512]{1,0:T(8,128)}) %reduce-scatter.32.cloned.1.call-update) | async-done | bytes 32784 | tf_op jit(solution)/shard_map/reduce_scatter | solution.py:281
  1451.8 134.3 %reduce-scatter.30.cloned.1.call-done = f32[16,512]{1,0:T(8,128)} async-done(((f32[512,512]{1,0:T(8,128)}), f32[16,512]{1,0:T(8,128)}) %reduce-scatter.30.cloned.1.call-update) | async-done | bytes 32784 | tf_op jit(solution)/shard_map/reduce_scatter | solution.py:280
  1586.1 143.1 %reduce-scatter.38.cloned.1.call-done = f32[64,512]{1,0:T(8,128)} async-done(((f32[2048,512]{1,0:T(8,128)}), f32[64,512]{1,0:T(8,128)}) %reduce-scatter.38.cloned.1.call-update) | async-done | bytes 131088 | tf_op jit(solution)/shard_map/reduce_scatter | solution.py:285
  1729.2 138.2 %reduce-scatter.46.cloned.1.call-done = f32[16,1024]{1,0:T(8,128)} async-done(((f32[512,1024]{1,0:T(8,128)}), f32[16,1024]{1,0:T(8,128)}) %reduce-scatter.46.cloned.1.call-update) | async-done | bytes 65552
  1867.4 104.1 %reduce-scatter.44.cloned.1.call-done = f32[16,1536]{1,0:T(8,128)} async-done(((f32[512,1536]{1,0:T(8,128)}), f32[16,1536]{1,0:T(8,128)}) %reduce-scatter.44.cloned.1.call-update) | async-done | bytes 98320
  1971.5 145.7 %reduce-scatter.36.cloned.1.call-done = f32[16,2048]{1,0:T(8,128)} async-done(((f32[512,2048]{1,0:T(8,128)}), f32[16,2048]{1,0:T(8,128)}) %reduce-scatter.36.cloned.1.call-update) | async-done | bytes 131088 | tf_op jit(solution)/shard_map/reduce_scatter | solution.py:284
  (509 shorter events, 311.0 us)
Async XLA Ops:
  7.2 60.3 %all-gather.17.cloned.1.call-start = ((), (), s32[]{:S(2)}) async-start(), calls=%async_computation.16 | async-start | bytes 1081344 | tf_op jit(solution)/shard_map/all_gather | solution.py:152
  7.9 116.6 %all-gather.11.cloned.1.call-start = ((), (), s32[]{:S(2)}) async-start(), calls=%async_computation.13 | async-start | bytes 1622016 | tf_op jit(solution)/shard_map/all_gather | solution.py:149
  8.7 467.7 %all-gather.19.cloned.1.call-start = ((), (), s32[]{:S(2)}) async-start(), calls=%async_computation.17 | async-start | bytes 2359296 | tf_op jit(solution)/shard_map/all_gather | solution.py:188
  70.2 409.4 %all-gather.21.cloned.1.call-start = ((), (), s32[]{:S(2)}) async-start(), calls=%async_computation.18 | async-start | bytes 2359296 | tf_op jit(solution)/shard_map/all_gather | solution.py:189
  71.1 411.7 %all-gather.13.cloned.1.call-start = ((), (), s32[]{:S(2)}) async-start(), calls=%async_computation.14 | async-start | bytes 2359296 | tf_op jit(solution)/shard_map/all_gather | solution.py:168
  126.6 274.8 %copy-start.58 = (bf16[16,512]{1,0:T(8,128)(2,1)S(1)}, bf16[16,512]{1,0:T(8,128)(2,1)}, u32[]{:S(2)}) copy-start(bf16[16,512]{1,0:T(8,128)(2,1)} %param.33) | copy-start | bytes 49156
  126.7 348.7 %copy-start.24 = (s32[2,1024]{1,0:T(2,128)S(1)}, s32[2,1024]{1,0:T(2,128)}, u32[]{:S(2)}) copy-start(s32[2,1024]{1,0:T(2,128)} %param.26) | copy-start | bytes 24580
  127.6 358.3 %all-gather.15.cloned.1.call-start = ((), (), s32[]{:S(2)}) async-start(), calls=%async_computation.15 | async-start | bytes 2359296 | tf_op jit(solution)/shard_map/all_gather | solution.py:169
  128.5 422.4 %all-gather.23.cloned.1.call-start = ((), (), s32[]{:S(2)}) async-start(), calls=%async_computation.19 | async-start | bytes 2162688 | tf_op jit(solution)/shard_map/all_gather | solution.py:154
  129.3 425.9 %all-gather.25.cloned.1.call-start = ((), (), s32[]{:S(2)}) async-start(), calls=%async_computation.20 | async-start | bytes 2162688 | tf_op jit(solution)/shard_map/all_gather | solution.py:155
  130.0 614.6 %reduce-scatter.26.cloned.1.call-start = ((), (), s32[]{:S(2)}) async-start(), calls=%async_computation.21 | async-start | bytes 2359296 | tf_op jit(solution)/shard_map/reduce_scatter | solution.py:110
  639.7 135.6 %reduce-scatter.28.cloned.1.call-start = ((), (), s32[]{:S(2)}) async-start(), calls=%async_computation.22 | async-start | bytes 2359296 | tf_op jit(solution)/shard_map/reduce_scatter | solution.py:113
  647.7 197.6 %reduce-scatter.42.cloned.1.call-start = ((), (), s32[]{:S(2)}) async-start(), calls=%async_computation.29 | async-start | bytes 2359296
  723.2 192.2 %reduce-scatter.40.cloned.1.call-start = ((), (), s32[]{:S(2)}) async-start(), calls=%async_computation.28 | async-start | bytes 2359296
  733.1 317.1 %reduce-scatter.50.cloned.1.call-start = ((), (), s32[]{:S(2)}) async-start(), calls=%async_computation.33 | async-start | bytes 270336
  734.6 448.5 %reduce-scatter.48.cloned.1.call-start = ((), (), s32[]{:S(2)}) async-start(), calls=%async_computation.32 | async-start | bytes 270336
  735.5 581.9 %reduce-scatter.34.cloned.1.call-start = ((), (), s32[]{:S(2)}) async-start(), calls=%async_computation.25 | async-start | bytes 1081344 | tf_op jit(solution)/shard_map/reduce_scatter | solution.py:283
  737.0 714.8 %reduce-scatter.32.cloned.1.call-start = ((), (), s32[]{:S(2)}) async-start(), calls=%async_computation.24 | async-start | bytes 1081344 | tf_op jit(solution)/shard_map/reduce_scatter | solution.py:281
  738.5 847.5 %reduce-scatter.30.cloned.1.call-start = ((), (), s32[]{:S(2)}) async-start(), calls=%async_computation.23 | async-start | bytes 1081344 | tf_op jit(solution)/shard_map/reduce_scatter | solution.py:280
  740.0 989.2 %reduce-scatter.38.cloned.1.call-start = ((), (), s32[]{:S(2)}) async-start(), calls=%async_computation.27 | async-start | bytes 4325376 | tf_op jit(solution)/shard_map/reduce_scatter | solution.py:285
  744.5 1122.8 %reduce-scatter.46.cloned.1.call-start = ((), (), s32[]{:S(2)}) async-start(), calls=%async_computation.31 | async-start | bytes 2162688
  781.0 1190.5 %reduce-scatter.44.cloned.1.call-start = ((), (), s32[]{:S(2)}) async-start(), calls=%async_computation.30 | async-start | bytes 3244032
  924.5 1192.7 %reduce-scatter.36.cloned.1.call-start = ((), (), s32[]{:S(2)}) async-start(), calls=%async_computation.26 | async-start | bytes 4325376 | tf_op jit(solution)/shard_map/reduce_scatter | solution.py:284
  929.2 257.7 %copy-start.3 = (bf16[512,1536]{1,0:T(8,128)(2,1)S(1)}, bf16[512,1536]{1,0:T(8,128)(2,1)}, u32[]{:S(2)}) copy-start(bf16[512,1536]{1,0:T(8,128)(2,1)} %all-gather.11.cloned.1.call-done) | copy-start | bytes 4718596
  (76 other events, 1254.0 us)
Sparse Core Ops, SparseCore 0:
  11.0 56.4 all-gather.16
  70.5 54.0 all-gather.10
  126.6 50.1 all-gather.18
  178.7 50.3 all-gather.20
  231.6 50.2 all-gather.12
  283.8 52.1 all-gather.14
  338.9 55.4 all-gather.22
  397.4 56.7 all-gather.24
  639.8 65.4 reduce-scatter.25
  708.7 66.5 reduce-scatter.27
  778.8 66.5 reduce-scatter.41
  848.7 66.6 reduce-scatter.39
  917.7 132.3 reduce-scatter.49
  1052.9 130.1 reduce-scatter.47
  1185.8 131.6 reduce-scatter.33
  1320.2 131.5 reduce-scatter.31
  1454.5 131.5 reduce-scatter.29
  1588.9 140.2 reduce-scatter.37
  1732.1 135.1 reduce-scatter.45
  1873.2 98.2 reduce-scatter.43
  1974.3 142.7 reduce-scatter.35
where the time goes:
time: 2130 us
  waiting for transfers between devices  1420 us (67%)
  blocking collectives  383 us (18%)
  matrix products  192 us (9%)
  local copies, waits for them, and re-layouts  96.2 us (5%)
    unnamed x27, waiting for transfers between devices  589 us
    reduce_scatter x1, waiting for transfers between devices, shards(): lax.psum_scatter(g_ffn_up, ('dp', 'seq'), scatter_dimension=0, tiled=True)  146 us
    reduce_scatter x1, waiting for transfers between devices, shards(): lax.psum_scatter(g_ffn_down, ('dp', 'seq'), scatter_dimension=0, tiled=True)  143 us
    reduce_scatter x1, waiting for transfers between devices, shards(): lax.psum_scatter(g_cross_query, ('dp', 'seq'), scatter_dimension=0, tiled...  134 us
    reduce_scatter x1, waiting for transfers between devices, shards(): lax.psum_scatter(g_self_out, ('dp', 'seq'), scatter_dimension=0, tiled=True)  134 us
    reduce_scatter x1, waiting for transfers between devices, shards(): lax.psum_scatter(g_cross_out, ('dp', 'seq'), scatter_dimension=0, tiled=T...  128 us
    all_gather x1, blocking collectives, shards(): lax.all_gather(cross_out, ('dp', 'seq'), axis=0, tiled=True)  73.9 us
    all_gather x1, blocking collectives, shards(): lax.all_gather(self_out, ('dp', 'seq'), axis=0, tiled=True)  70.9 us
  transfers between devices with their start and end apart: 21, of which 14 were waited for; matrix products, arithmetic and copies ran while one was open for 10% of the time, Pallas kernels for 0%

commit v1 on v0

v1 whole, which is shorter than its diff:
```python
import functools

import jax
import jax.numpy as jnp
from jax import lax
from jax.experimental import pallas as pl
from jax.experimental.pallas import tpu as pltpu
from jax.sharding import PartitionSpec as P

HEADS = 8
HEAD_DIM = 64
EPS = 1e-5
NEG = -1e30
SCALE = 0.125
D = 512
FF = 2048
G = 32
BF = jnp.bfloat16
F32 = jnp.float32
MIB = 1 << 20

N_PACK = 17

NN = (((1,), (0,)), ((), ()))
NT = (((1,), (1,)), ((), ()))
TN = (((0,), (0,)), ((), ()))


def dot(a, b, dims=NN):
    return lax.dot_general(a, b, dims, preferred_element_type=F32)


def whole(shape):
    return pl.BlockSpec(shape, lambda i: (0,) * len(shape))


def chunks(first, count):
    return pl.BlockSpec((G, count, 16, D), lambda i: (0, first // count, 0, 0))


NORMS = pl.BlockSpec((G, 1, 16, D), lambda i: (0, 16, 0, 0))


def call(body, ins, outs, scratch=(), name=None, cost=None):
    return pl.pallas_call(
        body,
        grid=(1,),
        in_specs=[whole(a.shape) if s is None else s for a, s in ins],
        out_specs=[whole(s) for s, _ in outs],
        out_shape=[jax.ShapeDtypeStruct(s, t) for s, t in outs],
        scratch_shapes=list(scratch),
        compiler_params=pltpu.CompilerParams(vmem_limit_bytes=56 * MIB),
        name=name,
        cost_estimate=cost,
    )(*[a for a, _ in ins])


def cost(flops, nbytes):
    return pl.CostEstimate(flops=int(flops), bytes_accessed=int(nbytes), transcendentals=0)


def weight(ref, j):
    return ref[:, j].reshape(D, D)


def put(ref, j, value):
    ref[:, j] = value.astype(BF).reshape(G, 16, D)


def norm_rows(ref):
    return jnp.sum(ref[:, 0].astype(F32), axis=0)


def norm_forward(resid, gain, bias):
    centre = resid - jnp.mean(resid, axis=-1, keepdims=True)
    rstd = lax.rsqrt(jnp.mean(centre * centre, axis=-1, keepdims=True) + EPS)
    xhat = centre * rstd
    return xhat, rstd, xhat * gain + bias


def norm_back(g, xhat, rstd, gain):
    e = g * gain
    m1 = jnp.mean(e, axis=-1, keepdims=True)
    m2 = jnp.mean(e * xhat, axis=-1, keepdims=True)
    dr = (e - m1 - xhat * m2) * rstd
    return dr, jnp.sum(g * xhat, axis=0, keepdims=True), jnp.sum(g, axis=0, keepdims=True)


def head_half(x, e):
    lane = lax.broadcasted_iota(jnp.int32, x.shape, 1)
    return jnp.where((lane < HEAD_DIM) == (e == 0), x, jnp.zeros_like(x))


def attend(q_ref, kv_ref, mask_ref, p_ref, rl_ref, at_ref):
    def pair(hp, carry):
        c0 = pl.multiple_of(hp * 128, 128)
        k2 = kv_ref[:, pl.ds(c0, 128)]
        v2 = kv_ref[:, pl.ds(pl.multiple_of(D + c0, 128), 128)]
        q2 = q_ref[:, pl.ds(c0, 128)]
        for e in range(2):
            s = dot(k2, head_half(q2, e), NT) + mask_ref[...]
            p = jnp.exp(s - jnp.max(s, axis=0, keepdims=True))
            rl = 1.0 / jnp.sum(p, axis=0, keepdims=True)
            pb = p.astype(BF)
            p_ref[2 * hp + e] = pb
            rl_ref[2 * hp + e] = rl
            o = dot(v2, pb, TN) * rl
            at_ref[pl.ds(pl.multiple_of((2 * hp + e) * HEAD_DIM, HEAD_DIM), HEAD_DIM), :] = o[
                e * HEAD_DIM : (e + 1) * HEAD_DIM
            ].astype(BF)
        return carry

    lax.fori_loop(0, HEADS // 2, pair, 0)


def attend_back(q_ref, kv_ref, p_ref, rl_ref, do_ref, dkv_ref, dqt_ref):
    def pair(hp, carry):
        c0 = pl.multiple_of(hp * 128, 128)
        c1 = pl.multiple_of(D + c0, 128)
        k2 = kv_ref[:, pl.ds(c0, 128)]
        v2 = kv_ref[:, pl.ds(c1, 128)]
        q2 = q_ref[:, pl.ds(c0, 128)]
        do2 = do_ref[:, pl.ds(c0, 128)]
        dk = dv = None
        for e in range(2):
            dom = head_half(do2, e)
            dp = dot(v2, dom, NT)
            p = p_ref[2 * hp + e].astype(F32) * rl_ref[2 * hp + e]
            t = p * dp
            ds = (t - p * jnp.sum(t, axis=0, keepdims=True)).astype(BF)
            dk_e = dot(ds, head_half(q2, e))
            dv_e = dot(p.astype(BF), dom)
            dk = dk_e if dk is None else dk + dk_e
            dv = dv_e if dv is None else dv + dv_e
            dqt = dot(k2, ds, TN) * SCALE
            dqt_ref[pl.ds(pl.multiple_of((2 * hp + e) * HEAD_DIM, HEAD_DIM), HEAD_DIM), :] = dqt[
                e * HEAD_DIM : (e + 1) * HEAD_DIM
            ]
        dkv_ref[:, pl.ds(c0, 128)] = dk.astype(BF)
        dkv_ref[:, pl.ds(c1, 128)] = dv.astype(BF)
        return carry

    lax.fori_loop(0, HEADS // 2, pair, 0)


def self_forward(rows, xf, w, mask, q, kv, p, rl, at):
    q[...] = (dot(xf[:rows], weight(w, 0)).astype(BF).astype(F32) * SCALE).astype(BF)
    kv[:, :D] = dot(xf[...], weight(w, 1)).astype(BF)
    kv[:, D:] = dot(xf[...], weight(w, 2)).astype(BF)
    attend(q, kv, mask, p, rl, at)


def cross_forward(rows, xf, ef, at1, w_out, w_cin, w_cq, norms, mask, xh1, rs1, low1, q, kv, p, rl, at):
    gb = norm_rows(norms)
    resid = xf[:rows].astype(F32) + dot(at1[...], weight(w_out, 0), TN)
    xhat, rstd, n1 = norm_forward(resid, gb[0:1], gb[3:4])
    xh1[...] = xhat
    rs1[...] = rstd
    low1[...] = n1.astype(BF)
    q[...] = (dot(low1[...], weight(w_cq, 0)).astype(BF).astype(F32) * SCALE).astype(BF)
    kv[:, :D] = dot(ef[...], weight(w_cin, 0)).astype(BF)
    kv[:, D:] = dot(ef[...], weight(w_cin, 1)).astype(BF)
    attend(q, kv, mask, p, rl, at)


def ffn_both(xh1, at2, teach, valid, w_co, w_up, w_dn, norms,
             out, small, d_r2, d_mix, g_up, g_dn, g_co, act, hid):
    gb = norm_rows(norms)
    n1 = xh1[...] * gb[0:1] + gb[3:4]
    wco = weight(w_co, 0)
    xh2, rs2, n2 = norm_forward(n1 + dot(at2[...], wco, TN), gb[1:2], gb[4:5])
    low2 = n2.astype(BF)
    r3 = n2
    for j in range(4):
        h = dot(low2, weight(w_up, j))
        hid[j] = h
        a = (h / (1.0 + jnp.exp(-h))).astype(BF)
        act[:, j * D : (j + 1) * D] = a
    wdn = w_dn[...].reshape(FF, D)
    r3 = n2 + dot(act[...], wdn)
    xh3, rs3, final = norm_forward(r3, gb[2:3], gb[5:6])
    out[...] = final.astype(BF)
    err = (final - teach[...].astype(F32)) * valid[...]
    small[...] = jnp.zeros_like(small)
    small[6:7] = jnp.sum(err * err, axis=0, keepdims=True)
    d_r3, dg, db = norm_back(err, xh3, rs3, gb[2:3])
    small[2:3] = dg
    small[5:6] = db
    dffn = d_r3.astype(BF)
    g_dn[...] = dot(act[...], dffn, TN).astype(BF).reshape(G, 4, 16, D)
    dn2 = d_r3
    for j in range(4):
        da = dot(dffn, wdn[j * D : (j + 1) * D], NT)
        h = hid[j]
        sig = 1.0 / (1.0 + jnp.exp(-h))
        dh = (da * (sig * (1.0 + h * (1.0 - sig)))).astype(BF)
        put(g_up, j, dot(low2, dh, TN))
        dn2 = dn2 + dot(dh, weight(w_up, j), NT)
    dr2, dg, db = norm_back(dn2, xh2, rs2, gb[1:2])
    small[1:2] = dg
    small[4:5] = db
    d_r2[...] = dr2
    dcross = dr2.astype(BF)
    put(g_co, 0, dot(at2[...], dcross))
    d_mix[...] = dot(dcross, wco, NT).astype(BF)


def cross_back(ef, q, kv, p, rl, d_mix, w_cin, w_cq, w_out, norms, d_r2, low1, xh1, rs1, at1, small_in,
               d_enc, g_cin, g_cq, g_so, d_mix1, d_r1, small, dkv, dqt):
    attend_back(q, kv, p, rl, d_mix, dkv, dqt)
    d_enc[...] = (
        dot(dkv[:, :D], weight(w_cin, 0), NT) + dot(dkv[:, D:], weight(w_cin, 1), NT)
    ).astype(BF)
    put(g_cin, 0, dot(ef[...], dkv[:, :D], TN))
    put(g_cin, 1, dot(ef[...], dkv[:, D:], TN))
    dq = jnp.transpose(dqt[...]).astype(BF)
    put(g_cq, 0, dot(low1[...], dq, TN))
    gb = norm_rows(norms)
    dn1 = d_r2[...] + dot(dq, weight(w_cq, 0), NT)
    dr1, dg, db = norm_back(dn1, xh1[...], rs1[...], gb[0:1])
    small[...] = small_in[...]
    small[0:1] = dg
    small[3:4] = db
    d_r1[...] = dr1
    dself = dr1.astype(BF)
    put(g_so, 0, dot(at1[...], dself))
    d_mix1[...] = dot(dself, weight(w_out, 0), NT).astype(BF)


def self_back(rows, xf, q, kv, p, rl, d_mix, w, d_r1, d_x, d_own, g_in, dkv, dqt):
    attend_back(q, kv, p, rl, d_mix, dkv, dqt)
    d_x[...] = (dot(dkv[:, :D], weight(w, 1), NT) + dot(dkv[:, D:], weight(w, 2), NT)).astype(BF)
    dq = jnp.transpose(dqt[...]).astype(BF)
    d_own[...] = d_r1[...] + dot(dq, weight(w, 0), NT)
    put(g_in, 0, dot(xf[:rows], dq, TN))
    put(g_in, 1, dot(xf[...], dkv[:, :D], TN))
    put(g_in, 2, dot(xf[...], dkv[:, D:], TN))


def flip(axis, size, bit):
    return functools.partial(
        lax.ppermute, axis_name=axis, perm=[(i, i ^ bit) for i in range(size)]
    )


def make_shards(nd, ns):
    n_dev = nd * ns
    half = ns // 2
    per = G * 16 // n_dev

    def shards(inputs, encoder, teacher, dec_seg, enc_seg, dec_valid, self_in, self_out,
               cross_query, cross_in, cross_out, ffn_up, ffn_down, norm_gain, norm_bias):
        tok = inputs.shape[1]
        rows = 2 * tok
        length = dec_seg.shape[1]
        dp_at, seq_at = lax.axis_index("dp"), lax.axis_index("seq")
        dev = dp_at * ns + seq_at
        mine = seq_at // half

        def cut(w):
            return w.reshape(per, w.shape[1] // D, D).transpose(1, 0, 2)

        norms = lax.dynamic_update_slice(
            jnp.zeros((16, D), BF), jnp.concatenate([norm_gain, norm_bias], 0), (0, dev * per)
        )
        packed = [cut(self_in), cut(self_out), cut(cross_in), cut(cross_query), cut(cross_out), cut(ffn_up)]
        packed = jnp.concatenate(packed, 0)
        if per == 16:
            packed = jnp.concatenate([packed, ffn_down.reshape(4, 16, D), norms[None]], 0)
            wall = lax.all_gather(packed, ("dp", "seq"), axis=0)
        else:
            packed = jnp.concatenate([packed, ffn_down.reshape(4, per, D)], 0)
            wall = lax.all_gather(packed, ("dp", "seq"), axis=0)
            down = wall[:, 12:].reshape(G, 4, 16, D)
            rest = wall[:, :12].reshape(G, 16 // per, 12, per, D)
            rest = rest.transpose(0, 2, 1, 3, 4).reshape(G, 12, 16, D)
            all_norms = lax.all_gather(norms, ("dp", "seq"), axis=0)
            all_norms = all_norms.astype(F32).reshape(G, n_dev // G, 16, D).sum(1).astype(BF)
            wall = jnp.concatenate([rest, down, all_norms[:, None]], 1)

        def of(x, i):
            return lax.dynamic_index_in_dim(x, i, 0, keepdims=False)

        def top(x):
            return flip("seq", ns, half)(x)

        valid_rows = jnp.pad(of(dec_valid, 1 - mine).astype(BF)[None], ((0, 15), (0, D - tok)))
        got = top(
            jnp.concatenate(
                [of(inputs, 1 - mine), of(encoder, 1 - mine), of(teacher, 1 - mine), valid_rows], 0
            )
        )
        both = jnp.stack(
            [
                jnp.concatenate([of(inputs, mine), got[:tok]], 0),
                jnp.concatenate([of(encoder, mine), got[tok : 2 * tok]], 0),
            ]
        )
        teach = jnp.concatenate([of(teacher, mine), got[2 * tok : 3 * tok]], 0)
        valid = jnp.concatenate([of(dec_valid, mine).astype(F32), got[3 * tok, :tok].astype(F32)])[:, None]
        bit = 1
        while bit < half:
            both = jnp.concatenate([both, flip("seq", ns, bit)(both)], 1)
            bit *= 2
        xf, ef = both[0], both[1]

        slots = jnp.arange(half, dtype=jnp.int32)[:, None]
        pieces = (seq_at ^ slots ^ jnp.array([[0, half]], jnp.int32)).reshape(-1)
        pos = (pieces[:, None] * tok + jnp.arange(tok, dtype=jnp.int32)[None]).reshape(-1)
        dec_k = of(dec_seg, mine).reshape(ns, tok)[pieces].reshape(-1)
        enc_k = of(enc_seg, mine).reshape(ns, tok)[pieces].reshape(-1)
        dec_q = dec_k[:rows]
        ok_self = (dec_k[:, None] == dec_q[None]) & (pos[:, None] <= pos[None, :rows])
        ok_cross = enc_k[:, None] == dec_q[None]
        mask_self = jnp.where(ok_self, 0.0, NEG).astype(F32)
        mask_cross = jnp.where(ok_cross, 0.0, NEG).astype(F32)

        p_shape = (HEADS, length, rows)
        attn_flops = 4 * HEADS * length * rows * 128
        kv_flops = 4 * length * D * D
        q1, kv1, p1, rl1, at1 = call(
            functools.partial(self_forward, rows),
            [(xf, None), (wall, chunks(0, 3)), (mask_self, None)],
            [((rows, D), BF), ((length, 2 * D), BF), (p_shape, BF), ((HEADS, 1, rows), F32), ((D, rows), BF)],
            name="self_forward",
            cost=cost(attn_flops + kv_flops, 9 * MIB),
        )
        xh1, rs1, low1, q2, kv2, p2, rl2, at2 = call(
            functools.partial(cross_forward, rows),
            [(xf, None), (ef, None), (at1, None), (wall, chunks(3, 1)), (wall, chunks(4, 2)),
             (wall, chunks(6, 1)), (wall, NORMS), (mask_cross, None)],
            [((rows, D), F32), ((rows, 1), F32), ((rows, D), BF), ((rows, D), BF), ((length, 2 * D), BF),
             (p_shape, BF), ((HEADS, 1, rows), F32), ((D, rows), BF)],
            name="cross_forward",
            cost=cost(attn_flops + kv_flops, 12 * MIB),
        )
        out, small, d_r2, d_mix2, g_up, g_dn, g_co = call(
            ffn_both,
            [(xh1, None), (at2, None), (teach, None), (valid, None), (wall, chunks(7, 1)),
             (wall, chunks(8, 4)), (wall, chunks(12, 4)), (wall, NORMS)],
            [((rows, D), BF), ((16, D), F32), ((rows, D), F32), ((rows, D), BF), ((G, 4, 16, D), BF),
             ((G, 4, 16, D), BF), ((G, 1, 16, D), BF)],
            scratch=[pltpu.VMEM((rows, FF), BF), pltpu.VMEM((4, rows, D), F32)],
            name="ffn_both",
            cost=cost(12 * rows * D * FF, 12 * MIB),
        )

        back_scratch = [pltpu.VMEM((length, 2 * D), BF), pltpu.VMEM((D, rows), F32)]
        d_enc, g_cin, g_cq, g_so, d_mix1, d_r1, small = call(
            cross_back,
            [(ef, None), (q2, None), (kv2, None), (p2, None), (rl2, None), (d_mix2, None),
             (wall, chunks(4, 2)), (wall, chunks(6, 1)), (wall, chunks(3, 1)), (wall, NORMS),
             (d_r2, None), (low1, None), (xh1, None), (rs1, None), (at1, None), (small, None)],
            [((length, D), BF), ((G, 2, 16, D), BF), ((G, 1, 16, D), BF), ((G, 1, 16, D), BF),
             ((rows, D), BF), ((rows, D), F32), ((16, D), F32)],
            scratch=back_scratch,
            name="cross_back",
            cost=cost(3 * attn_flops + 2 * kv_flops, 14 * MIB),
        )
        d_x, d_own, g_in = call(
            functools.partial(self_back, rows),
            [(xf, None), (q1, None), (kv1, None), (p1, None), (rl1, None), (d_mix1, None),
             (wall, chunks(0, 3)), (d_r1, None)],
            [((length, D), BF), ((rows, D), F32), ((G, 3, 16, D), BF)],
            scratch=back_scratch,
            name="self_back",
            cost=cost(3 * attn_flops + 2 * kv_flops, 14 * MIB),
        )

        def by_device(g):
            if per == 16:
                return g
            n = g.shape[1]
            return g.reshape(G, n, 16 // per, per, D).transpose(0, 2, 1, 3, 4).reshape(n_dev, n, per, D)

        def reduce_to_owner(g, small=None):
            tail = g.shape[1:]
            dp_bits, seq_bits = nd.bit_length() - 1, ns.bit_length() - 1
            acc = g.reshape((2,) * (dp_bits + seq_bits) + tail)
            order = [("dp", 0)] + [("dp", b) for b in range(dp_bits - 1, 0, -1)]
            order += [("seq", b) for b in range(seq_bits)]
            names = [("dp", b) for b in range(dp_bits - 1, -1, -1)]
            names += [("seq", b) for b in range(seq_bits - 1, -1, -1)]
            for axis, b in order:
                at = names.index((axis, b))
                size = nd if axis == "dp" else ns
                here = ((dp_at if axis == "dp" else seq_at) >> b) & 1
                keep = lax.dynamic_index_in_dim(acc, here, at, keepdims=False)
                send = lax.dynamic_index_in_dim(acc, 1 - here, at, keepdims=False).astype(BF)
                shape = send.shape
                send = send.reshape(-1, D)
                if small is not None:
                    low_small = small.astype(BF)
                    send = jnp.concatenate([send, low_small], 0)
                recv = flip(axis, size, 1 << b)(send)
                if small is not None:
                    small = low_small.astype(F32) + recv[-16:].astype(F32)
                    recv = recv[:-16]
                acc = keep.astype(F32) + recv.reshape(shape).astype(F32)
                names.pop(at)
            return acc, small

        def wide(g):
            return g.transpose(1, 0, 2).reshape(per, -1)

        g_dn = g_dn if per == 16 else g_dn.reshape(n_dev, 4, per, D)
        s_ffn, _ = reduce_to_owner(jnp.concatenate([by_device(g_up), g_dn], 1))
        s_mid, _ = reduce_to_owner(
            jnp.concatenate([by_device(g_co), by_device(g_cin), by_device(g_cq), by_device(g_so)], 1)
        )
        lane = lax.broadcasted_iota(jnp.int32, (16, D), 1)
        row = lax.broadcasted_iota(jnp.int32, (16, D), 0)
        count = jnp.sum(dec_valid).astype(F32)
        small = jnp.where((row == 7) & (lane == dev), count, small)
        s_in, small = reduce_to_owner(by_device(g_in), small)
        loss = jnp.sum(small[6]) / (jnp.sum(small[7]) * D)
        g_norm = lax.dynamic_slice(small, (0, dev * per), (6, per))

        def rows_to_owner(part):
            bit = half // 2
            acc = part
            while bit:
                cut_at = bit * rows
                acc = acc[:cut_at].astype(F32) + flip("seq", ns, bit)(acc[cut_at:].astype(BF)).astype(F32)
                bit //= 2
            return acc

        e_own = rows_to_owner(d_enc)
        x_own = rows_to_owner(d_x) + d_own

        def back_home(kept, recv):
            return jnp.where(mine == 0, jnp.stack([kept, recv]), jnp.stack([recv, kept]))

        home = top(jnp.concatenate([out[tok:], x_own[tok:].astype(BF), e_own[tok:].astype(BF)], 0))
        outputs = back_home(out[:tok], home[:tok])
        grad_inputs = back_home(x_own[:tok], home[tok : 2 * tok].astype(F32))
        grad_encoder = back_home(e_own[:tok], home[2 * tok :].astype(F32))
        return (
            outputs,
            loss,
            grad_inputs,
            grad_encoder,
            wide(s_in),
            wide(s_mid[4:5]),
            wide(s_mid[3:4]),
            wide(s_mid[1:3]),
            wide(s_mid[0:1]),
            wide(s_ffn[:4]),
            s_ffn[4:].reshape(4 * per, D),
            g_norm[:3],
            g_norm[3:],
        )

    return shards


def solution(mesh):
    rows, both = P("dp", "seq", None), P(("dp", "seq"), None)
    norm = P(None, ("dp", "seq"))
    return jax.shard_map(
        make_shards(mesh.shape["dp"], mesh.shape["seq"]),
        mesh=mesh,
        in_specs=(rows, rows, rows, P("dp", None), P("dp", None), P("dp", "seq")) + (both,) * 7 + (norm, norm),
        out_specs=(rows, P(), rows, rows) + (both,) * 7 + (norm, norm),
        check_vma=False,
    )
```

time: 2130 us -> 319 us (0.15)
  waiting for transfers between devices: 1420 us -> 158 us
  blocking collectives: 383 us -> 0 us
  matrix products: 192 us -> 0 us
  local copies, waits for them, and re-layouts: 96.2 us -> 22.5 us
  Pallas kernels: 0 us -> 68.1 us
  starting transfers between devices: 0.86 us -> 36 us
    reduce_scatter x7 -> x0, waiting for transfers between devices: 715 us -> none  [the longest x1 146 us: shards(): lax.psum_scatter(g_ffn_up, ('dp', 'seq'), scatter_dimension=0, tiled=True)]
    unnamed x27 -> x1, waiting for transfers between devices: 589 us -> 0.02 us
    all_gather x5 -> x0, blocking collectives: 343 us -> none  [the longest x1 73.9 us: shards(): lax.all_gather(cross_out, ('dp', 'seq'), axis=0, tiled=True)]
    dot_general x133 -> x0, matrix products: 192 us -> none  [the longest x16 27.2 us: query_one_head(): jnp.einsum('sqk,sqd->skd', d_scores, query_heads, preferred_element_type=...]
    ppermute x0 -> x23, waiting for transfers between devices: none -> 150 us  [the longest x2 57.4 us: shards(): both = jnp.concatenate([both, flip('seq', ns, bit)(both)], 1)]
    all_gather x8 -> x1, waiting for transfers between devices: 112 us -> 7.78 us  [shards(): wall = lax.all_gather(packed, ('dp', 'seq'), axis=0)]
    pallas_call x0 -> x5, Pallas kernels: none -> 68.1 us  [call(): pl.pallas_call(body, grid=(1,), in_specs=[whole(a.shape) if s is None els...]
    unnamed x179 -> x42, local copies, waits for them, and re-layouts: 52.2 us -> 2.93 us
  transfers between devices with their start and end apart: 21 -> 24, of which waited for: 14 -> 16; matrix products, arithmetic and copies ran while one was open for 10% -> 8% of each run, Pallas kernels for 0% -> 5%
where the time goes in v1:
time: 319 us; the launch traced here: 318 us
  waiting for transfers between devices  158 us (50%)
  Pallas kernels  68.1 us (21%)
  starting transfers between devices  36 us (11%)
  local copies, waits for them, and re-layouts  22.5 us (7%)
  between operations  18 us (6%)
  other arithmetic  15.3 us (5%)
    pallas_call x5, Pallas kernels, call(): pl.pallas_call(body, grid=(1,), in_specs=[whole(a.shape) if s is None els...  68.1 us
    ppermute x2, waiting for transfers between devices, shards(): both = jnp.concatenate([both, flip('seq', ns, bit)(both)], 1)  57.4 us
    ppermute x15, waiting for transfers between devices, reduce_to_owner(): recv = flip(axis, size, 1 << b)(send)  44.5 us
    ppermute x2, waiting for transfers between devices, top(): return flip('seq', ns, half)(x)  36.1 us
    ppermute x15, starting transfers between devices, reduce_to_owner(): recv = flip(axis, size, 1 << b)(send)  20.4 us
    ppermute x4, waiting for transfers between devices, rows_to_owner(): flip('seq', ns, bit)(acc[cut_at:].astype(BF)).astype(F32)  12.2 us
    all_gather x1, waiting for transfers between devices, shards(): wall = lax.all_gather(packed, ('dp', 'seq'), axis=0)  7.78 us
    ppermute x4, starting transfers between devices, rows_to_owner(): flip('seq', ns, bit)(acc[cut_at:].astype(BF)).astype(F32)  6.73 us
  transfers between devices with their start and end apart: 24, of which 16 were waited for; matrix products, arithmetic and copies ran while one was open for 8% of the time, Pallas kernels for 5%

profile of v1, /device:TPU:0, one launch (start us, length us, event | category | flops | bytes accessed | tf_op | source)
XLA Modules:
  0.0 318.1 jit_solution(7889360926547584660)
XLA Ops:
  15.4 4.9 %collective-permute-start = (bf16[400,512]{1,0:T(8,128)(2,1)S(1)}, bf16[400,512]{1,0:T(8,128)(2,1)S(1)}, u32[]{:S(2)}, u32[]{:S(2)}) collective-permute-start(bf16[400,512]{1,0:T(8,128)(2,1)S(1)} %fusion.2), channel_id=1, source_target_pairs={{0,4},{1,5},{2,6},{3,7},{4,0},{5,1},{6,2},{7,3},{8,12},{9,13},{10,... | collective-permute-start | bytes 1228808 | tf_op jit(solution)/shard_map/ppermute | solution.py:285
  23.0 21.5 %collective-permute-done = bf16[400,512]{1,0:T(8,128)(2,1)S(1)} collective-permute-done((bf16[400,512]{1,0:T(8,128)(2,1)S(1)}, bf16[400,512]{1,0:T(8,128)(2,1)S(1)}, u32[]{:S(2)}, u32[]{:S(2)}) %collective-permute-start) | collective-permute-done | bytes 409632 | tf_op jit(solution)/shard_map/ppermute | solution.py:285
  46.3 18.9 %collective-permute-done.1 = bf16[2,256,512]{2,1,0:T(8,128)(2,1)S(1)} collective-permute-done((bf16[2,256,512]{2,1,0:T(8,128)(2,1)S(1)}, bf16[2,256,512]{2,1,0:T(8,128)(2,1)S(1)}, u32[]{:S(2)}, u32[]{:S(2)}) %collective-permute-start.1) | collective-permute-done | bytes 524320 | tf_op jit(solution)/shard_map/ppermute | solution.py:303
  70.0 38.5 %collective-permute-done.2 = bf16[2,512,512]{2,1,0:T(8,128)(2,1)S(1)} collective-permute-done((bf16[2,512,512]{2,1,0:T(8,128)(2,1)S(1)}, bf16[2,512,512]{2,1,0:T(8,128)(2,1)S(1)}, u32[]{:S(2)}, u32[]{:S(2)}) %collective-permute-start.2) | collective-permute-done | bytes 1048608 | tf_op jit(solution)/shard_map/ppermute | solution.py:303
  110.1 7.8 %all-gather.3.cloned.1.call-done = bf16[544,16,512]{2,1,0:T(8,128)(2,1)} async-done(((bf16[17,16,512]{2,1,0:T(8,128)(2,1)}), bf16[544,16,512]{2,1,0:T(8,128)(2,1)}) %all-gather.3.cloned.1.call-update) | async-done | bytes 8912912 | tf_op jit(solution)/shard_map/all_gather | solution.py:270
  117.8 12.0 %self_forward.1 = (bf16[256,512]{1,0:T(8,128)(2,1)}, bf16[1024,1024]{1,0:T(8,128)(2,1)}, bf16[8,1024,256]{2,1,0:T(8,128)(2,1)}, f32[8,1,256]{2,1,0:T(1,128)}, bf16[512,256]{1,0:T(8,128)(2,1)}) custom-call(bf16[1024,512]{1,0:T(8,128)(2,1)} %get-tuple-element.75.xf, bf16[32,17,16,512]{3,2,1,0:T(8,128)(2,1)} %bitcast.169, f32[1024,256]{1,0:T(8,128)} %get-tuple-element.101.mask), custom_call_target="tpu_custom_call" | custom-call | flops 2147483648 | bytes 9437184 | tf_op jit(solution)/shard_map/self_forward/pallas_call | solution.py:45
  129.8 14.0 %cross_forward.1 = (f32[256,512]{1,0:T(8,128)}, f32[256,1]{1,0:T(8,128)}, bf16[256,512]{1,0:T(8,128)(2,1)}, bf16[256,512]{1,0:T(8,128)(2,1)}, bf16[1024,1024]{1,...) custom-call(bf16[1024,512]{1,0:T(8,128)(2,1)} %get-tuple-element.75.xf, ...), custom_call_target="tpu_custom_call" | custom-call | flops 2147483648 | bytes 12582912 | tf_op jit(solution)/shard_map/cross_forward/pallas_call | solution.py:45
  143.9 10.1 %ffn_both.1 = (bf16[256,512]{1,0:T(8,128)(2,1)}, f32[16,512]{1,0:T(8,128)}, f32[256,512]{1,0:T(8,128)}, bf16[256,512]{1,0:T(8,128)(2,1)}, bf16[32,4,16,512]{3,2,...) custom-call(f32[256,512]{1,0:T(8,128)} %get-tuple-element.44.xh1, ...), custom_call_target="tpu_custom_call" | custom-call | flops 3221225472 | bytes 12582912 | tf_op jit(solution)/shard_map/ffn_both/pallas_call | solution.py:45
  154.0 16.5 %cross_back.1 = (bf16[1024,512]{1,0:T(8,128)(2,1)}, bf16[32,2,16,512]{3,2,1,0:T(8,128)(2,1)}, bf16[32,1,16,512]{3,2,1,0:T(8,128)(2,1)}, bf16[32,1,16,512]{3,2,1,...) custom-call(bf16[1024,512]{1,0:T(8,128)(2,1)} %get-tuple-element.76.ef, ...), custom_call_target="tpu_custom_call" | custom-call | flops 5368709120 | bytes 14680064 | tf_op jit(solution)/shard_map/cross_back/pallas_call | solution.py:45
  171.5 3.4 %collective-permute-start.5 = (bf16[512,512]{1,0:T(8,128)(2,1)S(1)}, bf16[512,512]{1,0:T(8,128)(2,1)S(1)}, u32[]{:S(2)}, u32[]{:S(2)}) collective-permute-start(bf16[512,512]{1,0:T(8,128)(2,1)S(1)} %slice.157), channel_id=1, source_target_pairs={{0,2},{1,3},{2,0},{3,1},{4,6},{5,7},{6,4},{7,5},{8,10},{9,11},{10,... | collective-permute-start | bytes 1572872 | tf_op jit(solution)/shard_map/ppermute | solution.py:424
  174.9 15.5 %self_back.1 = (bf16[1024,512]{1,0:T(8,128)(2,1)}, f32[256,512]{1,0:T(8,128)}, bf16[32,3,16,512]{3,2,1,0:T(8,128)(2,1)}) custom-call(bf16[1024,512]{1,0:T(8,128)(2,1)} %get-tuple-element.75.xf, bf16[256,512]{1,0:T(8,128)(2,1)} %get-tuple-element.47.q, bf16[1024,1024]{1,0:T(8,128)(2,1)} %get-tuple-element.48.kv, bf16[8,1024,256]{2,1,0:T(8,128)(2,1)} %get-tuple-element.49.p, ...), custom_call_target="tpu_custom_call" | custom-call | flops 5368709120 | bytes 14680064 | tf_op jit(solution)/shard_map/self_back/pallas_call | solution.py:45
  198.7 6.9 %collective-permute-done.3 = bf16[512,512]{1,0:T(8,128)(2,1)S(1)} collective-permute-done((bf16[512,512]{1,0:T(8,128)(2,1)S(1)}, bf16[512,512]{1,0:T(8,128)(2,1)S(1)}, u32[]{:S(2)}, u32[]{:S(2)}) %collective-permute-start.3) | collective-permute-done | bytes 524320 | tf_op jit(solution)/shard_map/ppermute | solution.py:424
  207.9 5.3 %collective-permute-done.4 = bf16[256,512]{1,0:T(8,128)(2,1)S(1)} collective-permute-done((bf16[256,512]{1,0:T(8,128)(2,1)S(1)}, bf16[256,512]{1,0:T(8,128)(2,1)S(1)}, u32[]{:S(2)}, u32[]{:S(2)}) %collective-permute-start.4) | collective-permute-done | bytes 262176 | tf_op jit(solution)/shard_map/ppermute | solution.py:424
  217.4 14.7 %collective-permute-done.7 = bf16[384,512]{1,0:T(8,128)(2,1)S(1)} collective-permute-done((bf16[384,512]{1,0:T(8,128)(2,1)S(1)}, bf16[384,512]{1,0:T(8,128)(2,1)S(1)}, u32[]{:S(2)}, u32[]{:S(2)}) %collective-permute-start.7) | collective-permute-done | bytes 393248 | tf_op jit(solution)/shard_map/ppermute | solution.py:285
  236.9 4.6 %collective-permute-done.10 = bf16[208,512]{1,0:T(8,128)(2,1)S(1)} collective-permute-done((bf16[208,512]{1,0:T(8,128)(2,1)S(1)}, bf16[208,512]{1,0:T(8,128)(2,1)S(1)}, u32[]{:S(2)}, u32[]{:S(2)}) %collective-permute-start.10) | collective-permute-done | bytes 213024 | tf_op jit(solution)/shard_map/ppermute | solution.py:395
  243.5 3.0 collective-permute-done.11
  247.6 4.4 %collective-permute-done.12 = bf16[64,512]{1,0:T(8,128)(2,1)S(1)} collective-permute-done((bf16[64,512]{1,0:T(8,128)(2,1)S(1)}, bf16[64,512]{1,0:T(8,128)(2,1)S(1)}, u32[]{:S(2)}, u32[]{:S(2)}) %collective-permute-start.12) | collective-permute-done | bytes 65568 | tf_op jit(solution)/shard_map/ppermute | solution.py:395
  255.0 4.6 %collective-permute-done.14 = bf16[640,512]{1,0:T(8,128)(2,1)S(1)} collective-permute-done((bf16[640,512]{1,0:T(8,128)(2,1)S(1)}, bf16[640,512]{1,0:T(8,128)(2,1)S(1)}, u32[]{:S(2)}, u32[]{:S(2)}) %collective-permute-start.14) | collective-permute-done | bytes 655392 | tf_op jit(solution)/shard_map/ppermute | solution.py:395
  264.8 3.2 %collective-permute-done.15 = bf16[320,512]{1,0:T(8,128)(2,1)} collective-permute-done((bf16[320,512]{1,0:T(8,128)(2,1)}, bf16[320,512]{1,0:T(8,128)(2,1)}, u32[]{:S(2)}, u32[]{:S(2)}) %collective-permute-start.15) | collective-permute-done | bytes 327712 | tf_op jit(solution)/shard_map/ppermute | solution.py:395
  271.3 8.4 %collective-permute-done.19 = bf16[1024,512]{1,0:T(8,128)(2,1)S(1)} collective-permute-done((bf16[1024,512]{1,0:T(8,128)(2,1)S(1)}, bf16[1024,512]{1,0:T(8,128)(2,1)S(1)}, u32[]{:S(2)}, u32[]{:S(2)}) %collective-permute-start.19) | collective-permute-done | bytes 1048608 | tf_op jit(solution)/shard_map/ppermute | solution.py:395
  283.9 2.9 collective-permute-start.17
  286.8 6.6 %collective-permute-done.20 = bf16[512,512]{1,0:T(8,128)(2,1)S(1)} collective-permute-done((bf16[512,512]{1,0:T(8,128)(2,1)S(1)}, bf16[512,512]{1,0:T(8,128)(2,1)S(1)}, u32[]{:S(2)}, u32[]{:S(2)}) %collective-permute-start.20) | collective-permute-done | bytes 524320 | tf_op jit(solution)/shard_map/ppermute | solution.py:395
  295.7 5.5 %collective-permute-done.21 = bf16[256,512]{1,0:T(8,128)(2,1)S(1)} collective-permute-done((bf16[256,512]{1,0:T(8,128)(2,1)S(1)}, bf16[256,512]{1,0:T(8,128)(2,1)S(1)}, u32[]{:S(2)}, u32[]{:S(2)}) %collective-permute-start.21) | collective-permute-done | bytes 262176 | tf_op jit(solution)/shard_map/ppermute | solution.py:395
  304.6 4.1 %collective-permute-done.22 = bf16[128,512]{1,0:T(8,128)(2,1)S(1)} collective-permute-done((bf16[128,512]{1,0:T(8,128)(2,1)S(1)}, bf16[128,512]{1,0:T(8,128)(2,1)S(1)}, u32[]{:S(2)}, u32[]{:S(2)}) %collective-permute-start.22) | collective-permute-done | bytes 131104 | tf_op jit(solution)/shard_map/ppermute | solution.py:395
  (192 shorter events, 62.7 us)
Async XLA Ops:
  7.2 110.6 %all-gather.3.cloned.1.call-start = ((), (), s32[]{:S(2)}) async-start(), calls=%async_computation | async-start | bytes 9191424 | tf_op jit(solution)/shard_map/all_gather | solution.py:270
  15.4 29.1 %collective-permute-start = (bf16[400,512]{1,0:T(8,128)(2,1)S(1)}, bf16[400,512]{1,0:T(8,128)(2,1)S(1)}, u32[]{:S(2)}, u32[]{:S(2)}) collective-permute-start(bf16[400,512]{1,0:T(8,128)(2,1)S(1)} %fusion.2), channel_id=1, source_target_pairs={{0,4},{1,5},{2,6},{3,7},{4,0},{5,1},{6,2},{7,3},{8,12},{9,13},{10,... | collective-permute-start | bytes 1228808 | tf_op jit(solution)/shard_map/ppermute | solution.py:285
  44.6 20.7 %collective-permute-start.1 = (bf16[2,256,512]{2,1,0:T(8,128)(2,1)S(1)}, bf16[2,256,512]{2,1,0:T(8,128)(2,1)S(1)}, u32[]{:S(2)}, u32[]{:S(2)}) collective-permute-start(bf16[2,256,512]{2,1,0:T(8,128)(2,1)S(1)} %pad_maximum_fusion.5), channel_id=1, source_target_pairs={{0,1},{1,0},{2,3},{3,2},{4,5},{5,4},{6,7},{7,6},{8,9},{9,8},{10,11... | collective-permute-start | bytes 1572872 | tf_op jit(solution)/shard_map/ppermute | solution.py:303
  65.4 43.1 %collective-permute-start.2 = (bf16[2,512,512]{2,1,0:T(8,128)(2,1)S(1)}, bf16[2,512,512]{2,1,0:T(8,128)(2,1)S(1)}, u32[]{:S(2)}, u32[]{:S(2)}) collective-permute-start(bf16[2,512,512]{2,1,0:T(8,128)(2,1)S(1)} %pad_maximum_fusion.3), channel_id=1, source_target_pairs={{0,2},{1,3},{2,0},{3,1},{4,6},{5,7},{6,4},{7,5},{8,10},{9,11},{10,... | collective-permute-start | bytes 3145736 | tf_op jit(solution)/shard_map/ppermute | solution.py:303
  171.5 25.0 %collective-permute-start.5 = (bf16[512,512]{1,0:T(8,128)(2,1)S(1)}, bf16[512,512]{1,0:T(8,128)(2,1)S(1)}, u32[]{:S(2)}, u32[]{:S(2)}) collective-permute-start(bf16[512,512]{1,0:T(8,128)(2,1)S(1)} %slice.157), channel_id=1, source_target_pairs={{0,2},{1,3},{2,0},{3,1},{4,6},{5,7},{6,4},{7,5},{8,10},{9,11},{10,... | collective-permute-start | bytes 1572872 | tf_op jit(solution)/shard_map/ppermute | solution.py:424
  191.7 13.9 %collective-permute-start.3 = (bf16[512,512]{1,0:T(8,128)(2,1)S(1)}, bf16[512,512]{1,0:T(8,128)(2,1)S(1)}, u32[]{:S(2)}, u32[]{:S(2)}) collective-permute-start(bf16[512,512]{1,0:T(8,128)(2,1)S(1)} %slice.152), channel_id=1, source_target_pairs={{0,2},{1,3},{2,0},{3,1},{4,6},{5,7},{6,4},{7,5},{8,10},{9,11},{10,... | collective-permute-start | bytes 1572872 | tf_op jit(solution)/shard_map/ppermute | solution.py:424
  193.2 21.9 %collective-permute-start.8 = (bf16[784,512]{1,0:T(8,128)(2,1)S(1)}, bf16[784,512]{1,0:T(8,128)(2,1)S(1)}, u32[]{:S(2)}, u32[]{:S(2)}) collective-permute-start(bf16[784,512]{1,0:T(8,128)(2,1)S(1)} %pad_maximum_fusion.4), channel_id=1, source_target_pairs={{0,8},{8,0},{16,24},{24,16},{1,9},{9,1},{17,25},{25,17},{2,10},{10... | collective-permute-start | bytes 2408456 | tf_op jit(solution)/shard_map/ppermute | solution.py:395
  193.8 42.6 %collective-permute-start.13 = (bf16[1280,512]{1,0:T(8,128)(2,1)S(1)}, bf16[1280,512]{1,0:T(8,128)(2,1)S(1)}, u32[]{:S(2)}, u32[]{:S(2)}) collective-permute-start(bf16[1280,512]{1,0:T(8,128)(2,1)S(1)} %bitcast.195), channel_id=1, source_target_pairs={{0,8},{8,0},{16,24},{24,16},{1,9},{9,1},{17,25},{25,17},{2,10},{10... | collective-permute-start | bytes 3932168 | tf_op jit(solution)/shard_map/ppermute | solution.py:395
  197.1 10.7 %collective-permute-start.6 = (bf16[256,512]{1,0:T(8,128)(2,1)S(1)}, bf16[256,512]{1,0:T(8,128)(2,1)S(1)}, u32[]{:S(2)}, u32[]{:S(2)}) collective-permute-start(bf16[256,512]{1,0:T(8,128)(2,1)S(1)} %slice.264), channel_id=1, source_target_pairs={{0,1},{1,0},{2,3},{3,2},{4,5},{5,4},{6,7},{7,6},{8,9},{9,8},{10,11... | collective-permute-start | bytes 786440 | tf_op jit(solution)/shard_map/ppermute | solution.py:424
  205.8 7.4 %collective-permute-start.4 = (bf16[256,512]{1,0:T(8,128)(2,1)S(1)}, bf16[256,512]{1,0:T(8,128)(2,1)S(1)}, u32[]{:S(2)}, u32[]{:S(2)}) collective-permute-start(bf16[256,512]{1,0:T(8,128)(2,1)S(1)} %slice.265), channel_id=1, source_target_pairs={{0,1},{1,0},{2,3},{3,2},{4,5},{5,4},{6,7},{7,6},{8,9},{9,8},{10,11... | collective-permute-start | bytes 786440 | tf_op jit(solution)/shard_map/ppermute | solution.py:424
  207.7 44.5 %collective-permute-start.18 = (bf16[2048,512]{1,0:T(8,128)(2,1)S(1)}, bf16[2048,512]{1,0:T(8,128)(2,1)S(1)}, u32[]{:S(2)}, u32[]{:S(2)}) collective-permute-start(bf16[2048,512]{1,0:T(8,128)(2,1)S(1)} %bitcast.189), channel_id=1, source_target_pairs={{0,8},{8,0},{16,24},{24,16},{1,9},{9,1},{17,25},{25,17},{2,10},{10... | collective-permute-start | bytes 6291464 | tf_op jit(solution)/shard_map/ppermute | solution.py:395
  213.4 18.6 %collective-permute-start.7 = (bf16[384,512]{1,0:T(8,128)(2,1)S(1)}, bf16[384,512]{1,0:T(8,128)(2,1)S(1)}, u32[]{:S(2)}, u32[]{:S(2)}) collective-permute-start(bf16[384,512]{1,0:T(8,128)(2,1)S(1)} %pad_maximum_fusion.7), channel_id=1, source_target_pairs={{0,4},{1,5},{2,6},{3,7},{4,0},{5,1},{6,2},{7,3},{8,12},{9,13},{10,... | collective-permute-start | bytes 1179656 | tf_op jit(solution)/shard_map/ppermute | solution.py:285
  215.6 18.9 %collective-permute-start.9 = (bf16[400,512]{1,0:T(8,128)(2,1)S(1)}, bf16[400,512]{1,0:T(8,128)(2,1)S(1)}, u32[]{:S(2)}, u32[]{:S(2)}) collective-permute-start(bf16[400,512]{1,0:T(8,128)(2,1)S(1)} %pad_maximum_fusion.6), channel_id=1, source_target_pairs={{0,16},{8,24},{16,0},{24,8},{1,17},{9,25},{17,1},{25,9},{2,18},{10... | collective-permute-start | bytes 1228808 | tf_op jit(solution)/shard_map/ppermute | solution.py:395
  234.8 6.8 %collective-permute-start.10 = (bf16[208,512]{1,0:T(8,128)(2,1)S(1)}, bf16[208,512]{1,0:T(8,128)(2,1)S(1)}, u32[]{:S(2)}, u32[]{:S(2)}) collective-permute-start(bf16[208,512]{1,0:T(8,128)(2,1)S(1)} %pad_maximum_fusion.9), channel_id=1, source_target_pairs={{0,1},{1,0},{2,3},{3,2},{4,5},{5,4},{6,7},{7,6},{8,9},{9,8},{10,11... | collective-permute-start | bytes 638984 | tf_op jit(solution)/shard_map/ppermute | solution.py:395
  241.7 4.9 %collective-permute-start.11 = (bf16[112,512]{1,0:T(8,128)(2,1)S(1)}, bf16[112,512]{1,0:T(8,128)(2,1)S(1)}, u32[]{:S(2)}, u32[]{:S(2)}) collective-permute-start(bf16[112,512]{1,0:T(8,128)(2,1)S(1)} %pad_maximum_fusion.10), channel_id=1, source_target_pairs={{0,2},{1,3},{2,0},{3,1},{4,6},{5,7},{6,4},{7,5},{8,10},{9,11},{10,... | collective-permute-start | bytes 344072 | tf_op jit(solution)/shard_map/ppermute | solution.py:395
  241.9 17.7 %collective-permute-start.14 = (bf16[640,512]{1,0:T(8,128)(2,1)S(1)}, bf16[640,512]{1,0:T(8,128)(2,1)S(1)}, u32[]{:S(2)}, u32[]{:S(2)}) collective-permute-start(bf16[640,512]{1,0:T(8,128)(2,1)S(1)} %bitcast.201), channel_id=1, source_target_pairs={{0,16},{8,24},{16,0},{24,8},{1,17},{9,25},{17,1},{25,9},{2,18},{10... | collective-permute-start | bytes 1966088 | tf_op jit(solution)/shard_map/ppermute | solution.py:395
  246.6 5.4 %collective-permute-start.12 = (bf16[64,512]{1,0:T(8,128)(2,1)S(1)}, bf16[64,512]{1,0:T(8,128)(2,1)S(1)}, u32[]{:S(2)}, u32[]{:S(2)}) collective-permute-start(bf16[64,512]{1,0:T(8,128)(2,1)S(1)} %pad_maximum_fusion.11), channel_id=1, source_target_pairs={{0,4},{1,5},{2,6},{3,7},{4,0},{5,1},{6,2},{7,3},{8,12},{9,13},{10,... | collective-permute-start | bytes 196616 | tf_op jit(solution)/shard_map/ppermute | solution.py:395
  253.3 26.4 %collective-permute-start.19 = (bf16[1024,512]{1,0:T(8,128)(2,1)S(1)}, bf16[1024,512]{1,0:T(8,128)(2,1)S(1)}, u32[]{:S(2)}, u32[]{:S(2)}) collective-permute-start(bf16[1024,512]{1,0:T(8,128)(2,1)S(1)} %bitcast.197), channel_id=1, source_target_pairs={{0,16},{8,24},{16,0},{24,8},{1,17},{9,25},{17,1},{25,9},{2,18},{10... | collective-permute-start | bytes 3145736 | tf_op jit(solution)/shard_map/ppermute | solution.py:395
  260.7 7.4 %collective-permute-start.15 = (bf16[320,512]{1,0:T(8,128)(2,1)}, bf16[320,512]{1,0:T(8,128)(2,1)}, u32[]{:S(2)}, u32[]{:S(2)}) collective-permute-start(bf16[320,512]{1,0:T(8,128)(2,1)} %bitcast.63), channel_id=1, source_target_pairs={{0,1},{1,0},{2,3},{3,2},{4,5},{5,4},{6,7},{7,6},{8,9},{9,8},{10,11... | collective-permute-start | bytes 983048 | tf_op jit(solution)/shard_map/ppermute | solution.py:395
  269.2 14.6 %collective-permute-start.16 = (bf16[160,512]{1,0:T(8,128)(2,1)S(1)}, bf16[160,512]{1,0:T(8,128)(2,1)S(1)}, u32[]{:S(2)}, u32[]{:S(2)}) collective-permute-start(bf16[160,512]{1,0:T(8,128)(2,1)S(1)} %bitcast.216), channel_id=1, source_target_pairs={{0,2},{1,3},{2,0},{3,1},{4,6},{5,7},{6,4},{7,5},{8,10},{9,11},{10,... | collective-permute-start | bytes 491528 | tf_op jit(solution)/shard_map/ppermute | solution.py:395
  281.7 11.6 %collective-permute-start.20 = (bf16[512,512]{1,0:T(8,128)(2,1)S(1)}, bf16[512,512]{1,0:T(8,128)(2,1)S(1)}, u32[]{:S(2)}, u32[]{:S(2)}) collective-permute-start(bf16[512,512]{1,0:T(8,128)(2,1)S(1)} %bitcast.204), channel_id=1, source_target_pairs={{0,1},{1,0},{2,3},{3,2},{4,5},{5,4},{6,7},{7,6},{8,9},{9,8},{10,11... | collective-permute-start | bytes 1572872 | tf_op jit(solution)/shard_map/ppermute | solution.py:395
  283.9 11.2 %collective-permute-start.17 = (bf16[80,512]{1,0:T(8,128)(2,1)S(1)}, bf16[80,512]{1,0:T(8,128)(2,1)S(1)}, u32[]{:S(2)}, u32[]{:S(2)}) collective-permute-start(bf16[80,512]{1,0:T(8,128)(2,1)S(1)} %bitcast.224), channel_id=1, source_target_pairs={{0,4},{1,5},{2,6},{3,7},{4,0},{5,1},{6,2},{7,3},{8,12},{9,13},{10,... | collective-permute-start | bytes 245768 | tf_op jit(solution)/shard_map/ppermute | solution.py:395
  293.6 7.7 %collective-permute-start.21 = (bf16[256,512]{1,0:T(8,128)(2,1)S(1)}, bf16[256,512]{1,0:T(8,128)(2,1)S(1)}, u32[]{:S(2)}, u32[]{:S(2)}) collective-permute-start(bf16[256,512]{1,0:T(8,128)(2,1)S(1)} %bitcast.212), channel_id=1, source_target_pairs={{0,2},{1,3},{2,0},{3,1},{4,6},{5,7},{6,4},{7,5},{8,10},{9,11},{10,... | collective-permute-start | bytes 786440 | tf_op jit(solution)/shard_map/ppermute | solution.py:395
  301.4 7.3 %collective-permute-start.22 = (bf16[128,512]{1,0:T(8,128)(2,1)S(1)}, bf16[128,512]{1,0:T(8,128)(2,1)S(1)}, u32[]{:S(2)}, u32[]{:S(2)}) collective-permute-start(bf16[128,512]{1,0:T(8,128)(2,1)S(1)} %bitcast.220), channel_id=1, source_target_pairs={{0,4},{1,5},{2,6},{3,7},{4,0},{5,1},{6,2},{7,3},{8,12},{9,13},{10,... | collective-permute-start | bytes 393224 | tf_op jit(solution)/shard_map/ppermute | solution.py:395
  (20 other events, 91.8 us)
Sparse Core Ops, SparseCore 0:
  15.3 102.5 all-gather.2

commit v2 on v1

v2 whole, which is shorter than its diff:
```python
import functools

import jax
import jax.numpy as jnp
from jax import lax
from jax.experimental import pallas as pl
from jax.experimental.pallas import tpu as pltpu
from jax.sharding import PartitionSpec as P

HEADS = 8
HEAD_DIM = 64
EPS = 1e-5
NEG = -1e30
SCALE = 0.125
D = 512
FF = 2048
HALF = 256
G = 32
BF = jnp.bfloat16
F32 = jnp.float32
MIB = 1 << 20

N_PACK = 17

NN = (((1,), (0,)), ((), ()))
NT = (((1,), (1,)), ((), ()))
TN = (((0,), (0,)), ((), ()))


def dot(a, b, dims=NN):
    return lax.dot_general(a, b, dims, preferred_element_type=F32)


def whole(shape):
    return pl.BlockSpec(shape, lambda i: (0,) * len(shape))


def chunks(first, count):
    return pl.BlockSpec((G, count, 16, D), lambda i: (0, first // count, 0, 0))


SMEM = pl.BlockSpec(memory_space=pltpu.SMEM)
NORMS = pl.BlockSpec((G, 1, 16, D), lambda i: (0, 16, 0, 0))


def call(body, ins, outs, scratch=(), name=None):
    return pl.pallas_call(
        body,
        grid=(1,),
        in_specs=[whole(a.shape) if s is None else s for a, s in ins],
        out_specs=[whole(s) for s, _ in outs],
        out_shape=[jax.ShapeDtypeStruct(s, t) for s, t in outs],
        scratch_shapes=list(scratch),
        compiler_params=pltpu.CompilerParams(vmem_limit_bytes=56 * MIB),
        name=name,
    )(*[a for a, _ in ins])


def weight(ref, j):
    return ref[:, j].reshape(D, D)


def norm_rows(ref):
    return jnp.sum(ref[:, 0].astype(F32), axis=0)


def norm_forward(resid, gain, bias):
    centre = resid - jnp.mean(resid, axis=-1, keepdims=True)
    rstd = lax.rsqrt(jnp.mean(centre * centre, axis=-1, keepdims=True) + EPS)
    xhat = centre * rstd
    return xhat, rstd, xhat * gain + bias


def norm_back(g, xhat, rstd, gain):
    e = g * gain
    m1 = jnp.mean(e, axis=-1, keepdims=True)
    m2 = jnp.mean(e * xhat, axis=-1, keepdims=True)
    dr = (e - m1 - xhat * m2) * rstd
    return dr, jnp.sum(g * xhat, axis=0, keepdims=True), jnp.sum(g, axis=0, keepdims=True)


def head_half(x, e):
    lane = lax.broadcasted_iota(jnp.int32, x.shape, 1)
    return jnp.where((lane < HEAD_DIM) == (e == 0), x, jnp.zeros_like(x))


def attend(q_ref, kv_ref, mask_ref, p_ref, rl_ref, at_ref):
    def pair(hp, carry):
        c0 = pl.multiple_of(hp * 128, 128)
        k2 = kv_ref[:, pl.ds(c0, 128)]
        v2 = kv_ref[:, pl.ds(pl.multiple_of(D + c0, 128), 128)]
        q2 = q_ref[:, pl.ds(c0, 128)]
        for e in range(2):
            s = dot(k2, head_half(q2, e), NT) + mask_ref[...]
            p = jnp.exp(s - jnp.max(s, axis=0, keepdims=True))
            rl = 1.0 / jnp.sum(p, axis=0, keepdims=True)
            pb = p.astype(BF)
            p_ref[2 * hp + e] = pb
            rl_ref[2 * hp + e] = rl
            o = dot(v2, pb, TN) * rl
            at_ref[pl.ds(pl.multiple_of((2 * hp + e) * HEAD_DIM, HEAD_DIM), HEAD_DIM), :] = o[
                e * HEAD_DIM : (e + 1) * HEAD_DIM
            ].astype(BF)
        return carry

    lax.fori_loop(0, HEADS // 2, pair, 0)


def attend_back(first, q_ref, kv_ref, p_ref, rl_ref, do_ref, dkv_ref, dqt_ref):
    def pair(i, carry):
        hp = first // 2 + i
        c0 = pl.multiple_of(hp * 128, 128)
        o0 = pl.multiple_of(i * 128, 128)
        k2 = kv_ref[:, pl.ds(c0, 128)]
        v2 = kv_ref[:, pl.ds(pl.multiple_of(D + c0, 128), 128)]
        q2 = q_ref[:, pl.ds(c0, 128)]
        do2 = do_ref[:, pl.ds(c0, 128)]
        dk = dv = None
        for e in range(2):
            dom = head_half(do2, e)
            dp = dot(v2, dom, NT)
            p = p_ref[2 * hp + e].astype(F32) * rl_ref[2 * hp + e]
            t = p * dp
            ds = (t - p * jnp.sum(t, axis=0, keepdims=True)).astype(BF)
            dk_e = dot(ds, head_half(q2, e))
            dv_e = dot(p.astype(BF), dom)
            dk = dk_e if dk is None else dk + dk_e
            dv = dv_e if dv is None else dv + dv_e
            dqt = dot(k2, ds, TN) * SCALE
            dqt_ref[pl.ds(pl.multiple_of((2 * i + e) * HEAD_DIM, HEAD_DIM), HEAD_DIM), :] = dqt[
                e * HEAD_DIM : (e + 1) * HEAD_DIM
            ]
        dkv_ref[:, pl.ds(o0, 128)] = dk.astype(BF)
        dkv_ref[:, pl.ds(pl.multiple_of(HALF + o0, 128), 128)] = dv.astype(BF)
        return carry

    lax.fori_loop(0, HEADS // 4, pair, 0)


def cols(ref, c, width):
    picks = [ref[:, pl.ds(pl.multiple_of((2 * y + c) * width, width), width)] for y in range(2)]
    return jnp.concatenate(picks, 1)


def rows_of(ref, c, width):
    picks = [ref[pl.ds(pl.multiple_of((2 * y + c) * width, width), width), :] for y in range(2)]
    return jnp.concatenate(picks, 0)


def put_half(ref, lhs, dq, dk, dv, lhs_q):
    a = jnp.concatenate([dot(lhs_q, dq, TN), dot(lhs, dk, TN)], 1)
    ref[:, :, 0:16] = a.astype(BF).reshape(2, 8, 16, D)
    v = dot(lhs, dv, TN).reshape(2, 8, 2, 8, HALF)
    ref[:, :, 16:24] = jnp.concatenate([v[:, :, 0], v[:, :, 1]], -1).astype(BF)


def self_forward(rows, xf, w, mask, q, kv, p, rl, at):
    q[...] = (dot(xf[:rows], weight(w, 0)).astype(BF).astype(F32) * SCALE).astype(BF)
    kv[:, :D] = dot(xf[...], weight(w, 1)).astype(BF)
    kv[:, D:] = dot(xf[...], weight(w, 2)).astype(BF)
    attend(q, kv, mask, p, rl, at)


def cross_forward(rows, xf, ef, at1, w_out, w_cin, w_cq, norms, mask, xh1, rs1, low1, q, kv, p, rl, at):
    gb = norm_rows(norms)
    resid = xf[:rows].astype(F32) + dot(at1[...], weight(w_out, 0), TN)
    xhat, rstd, n1 = norm_forward(resid, gb[0:1], gb[3:4])
    xh1[...] = xhat
    rs1[...] = rstd
    low1[...] = n1.astype(BF)
    q[...] = (dot(low1[...], weight(w_cq, 0)).astype(BF).astype(F32) * SCALE).astype(BF)
    kv[:, :D] = dot(ef[...], weight(w_cin, 0)).astype(BF)
    kv[:, D:] = dot(ef[...], weight(w_cin, 1)).astype(BF)
    attend(q, kv, mask, p, rl, at)


def ffn_both(core, xh1, at2, teach, valid, w_co, w_up, w_dn, norms,
             out, small, d_r2, d_mix, keep, send, act, hid, low2):
    gb = norm_rows(norms)
    n1 = xh1[...] * gb[0:1] + gb[3:4]
    wco = weight(w_co, 0)
    xh2, rs2, n2 = norm_forward(n1 + dot(at2[...], wco, TN), gb[1:2], gb[4:5])
    low2[...] = n2.astype(BF)
    for j in range(4):
        h = dot(low2[...], weight(w_up, j))
        hid[j] = h
        act[:, j * D : (j + 1) * D] = (h / (1.0 + jnp.exp(-h))).astype(BF)
    wdn = w_dn[...].reshape(FF, D)
    r3 = n2 + dot(act[...], wdn)
    xh3, rs3, final = norm_forward(r3, gb[2:3], gb[5:6])
    out[...] = final.astype(BF)
    err = (final - teach[...].astype(F32)) * valid[...]
    small[...] = jnp.zeros_like(small)
    small[6:7] = jnp.sum(err * err, axis=0, keepdims=True)
    d_r3, dg, db = norm_back(err, xh3, rs3, gb[2:3])
    small[2:3] = dg
    small[5:6] = db
    dffn = d_r3.astype(BF)
    c = core[0]
    sides = ((send, 1 - c), (keep, c))
    for ref, at in sides:
        ref[:, :, 4:8] = dot(cols(act, at, FF // 4), dffn, TN).astype(BF).reshape(2, 8, 4, 16, D)
    dn2 = d_r3
    for j in range(4):
        da = dot(dffn, wdn[j * D : (j + 1) * D], NT)
        h = hid[j]
        sig = 1.0 / (1.0 + jnp.exp(-h))
        dh = (da * (sig * (1.0 + h * (1.0 - sig)))).astype(BF)
        for ref, at in sides:
            ref[:, :, j] = dot(cols(low2, at, 128), dh, TN).astype(BF).reshape(2, 8, 16, D)
        dn2 = dn2 + dot(dh, weight(w_up, j), NT)
    dr2, dg, db = norm_back(dn2, xh2, rs2, gb[1:2])
    small[1:2] = dg
    small[4:5] = db
    d_r2[...] = dr2
    dcross = dr2.astype(BF)
    for ref, at in sides:
        ref[:, :, 8] = dot(rows_of(at2, at, 128), dcross).astype(BF).reshape(2, 8, 16, D)
    d_mix[...] = dot(dcross, wco, NT).astype(BF)


def cross_back_a(q, kv, p, rl, d_mix, dkv, dq, dqt):
    attend_back(0, q, kv, p, rl, d_mix, dkv, dqt)
    dq[...] = jnp.transpose(dqt[...]).astype(BF)


def project(dkv_a, dkv_b, wk, wv):
    out = dot(dkv_a[:, :HALF], wk[:, :HALF], NT) + dot(dkv_b[:, :HALF], wk[:, HALF:], NT)
    return out + dot(dkv_a[:, HALF:], wv[:, :HALF], NT) + dot(dkv_b[:, HALF:], wv[:, HALF:], NT)


def cross_back_b(core, ef, q, kv, p, rl, d_mix, dkv_a, dq_a, w_cin, w_cq, w_out, norms, d_r2, low1, xh1,
                 rs1, at1, small_in, d_enc, d_mix1, d_r1, small, keep, send, dkv, dqt):
    attend_back(4, q, kv, p, rl, d_mix, dkv, dqt)
    d_enc[...] = project(dkv_a, dkv, weight(w_cin, 0), weight(w_cin, 1)).astype(BF)
    dq = jnp.concatenate([dq_a[...], jnp.transpose(dqt[...]).astype(BF)], 1)
    gb = norm_rows(norms)
    dn1 = d_r2[...] + dot(dq, weight(w_cq, 0), NT)
    dr1, dg, db = norm_back(dn1, xh1[...], rs1[...], gb[0:1])
    small[...] = small_in[...]
    small[0:1] = dg
    small[3:4] = db
    d_r1[...] = dr1
    dself = dr1.astype(BF)
    c = core[0]
    for ref, at in ((send, 1 - c), (keep, c)):
        lhs = cols(ef, at, 128)
        for j in range(2):
            span = slice(j * HALF, (j + 1) * HALF)
            g = jnp.concatenate([dot(lhs, dkv_a[:, span], TN), dot(lhs, dkv[:, span], TN)], 1)
            ref[:, :, j] = g.astype(BF).reshape(2, 8, 16, D)
        ref[:, :, 2] = dot(cols(low1, at, 128), dq, TN).astype(BF).reshape(2, 8, 16, D)
        ref[:, :, 3] = dot(rows_of(at1, at, 128), dself).astype(BF).reshape(2, 8, 16, D)
    d_mix1[...] = dot(dself, weight(w_out, 0), NT).astype(BF)


def self_back_a(rows, core, xf, q, kv, p, rl, d_mix, dkv, dq, keep, send, dqt):
    attend_back(0, q, kv, p, rl, d_mix, dkv, dqt)
    dq[...] = jnp.transpose(dqt[...]).astype(BF)
    c = core[0]
    for ref, at in ((send, 1 - c), (keep, c)):
        lhs = cols(xf, at, 128)
        put_half(ref, lhs, dq[...], dkv[:, :HALF], dkv[:, HALF:], lhs[:rows])


def self_back_b(rows, core, xf, q, kv, p, rl, d_mix, dkv_a, dq_a, w, d_r1, d_x, d_own, keep, send, dkv, dqt):
    attend_back(4, q, kv, p, rl, d_mix, dkv, dqt)
    d_x[...] = project(dkv_a, dkv, weight(w, 1), weight(w, 2)).astype(BF)
    dq = jnp.transpose(dqt[...]).astype(BF)
    d_own[...] = d_r1[...] + dot(jnp.concatenate([dq_a[...], dq], 1), weight(w, 0), NT)
    c = core[0]
    for ref, at in ((send, 1 - c), (keep, c)):
        lhs = cols(xf, at, 128)
        put_half(ref, lhs, dq, dkv[:, :HALF], dkv[:, HALF:], lhs[:rows])


def flip(axis, size, bit):
    return functools.partial(
        lax.ppermute, axis_name=axis, perm=[(i, i ^ bit) for i in range(size)]
    )


def tie(x, *deps):
    return lax.optimization_barrier((x, *deps))[0]


def pick(x, i, at):
    if isinstance(i, int):
        return lax.index_in_dim(x, i, at, keepdims=False)
    return lax.dynamic_index_in_dim(x, i, at, keepdims=False)


class Halved:
    def __init__(self, terms, axes):
        self.terms, self.axes = list(terms), list(axes)

    def total(self, terms=None):
        terms = self.terms if terms is None else terms
        return sum(t.astype(F32) for t in terms[1:]) + terms[0].astype(F32) if len(terms) > 1 else terms[0].astype(F32)

    def give(self, bit, here):
        at = self.axes.index(bit)
        away = [pick(t, 1 - here, at) for t in self.terms]
        self.terms = [pick(t, here, at) for t in self.terms]
        self.axes.pop(at)
        return self.total(away).astype(BF)

    def take(self, got):
        self.terms.append(got)


class Everywhere(Halved):
    def give(self, bit, here):
        self.terms = [self.total().astype(BF)]
        return self.terms[0]


class Near(Halved):
    def give(self, bit, here):
        return super().give(bit, 0)


def make_shards(nd, ns):
    n_dev = nd * ns
    half = ns // 2
    per = G * 16 // n_dev

    def shards(inputs, encoder, teacher, dec_seg, enc_seg, dec_valid, self_in, self_out,
               cross_query, cross_in, cross_out, ffn_up, ffn_down, norm_gain, norm_bias):
        tok = inputs.shape[1]
        rows = 2 * tok
        length = dec_seg.shape[1]
        dp_at, seq_at = lax.axis_index("dp"), lax.axis_index("seq")
        dev = dp_at * ns + seq_at
        mine = seq_at // half

        def cut(w):
            return w.reshape(per, w.shape[1] // D, D).transpose(1, 0, 2)

        norms = lax.dynamic_update_slice(
            jnp.zeros((16, D), BF), jnp.concatenate([norm_gain, norm_bias], 0), (0, dev * per)
        )
        packed = [cut(self_in), cut(self_out), cut(cross_in), cut(cross_query), cut(cross_out), cut(ffn_up)]
        packed = jnp.concatenate(packed, 0)
        if per == 16:
            packed = jnp.concatenate([packed, ffn_down.reshape(4, 16, D), norms[None]], 0)
            wall = lax.all_gather(packed, ("dp", "seq"), axis=0)
        else:
            packed = jnp.concatenate([packed, ffn_down.reshape(4, per, D)], 0)
            wall = lax.all_gather(packed, ("dp", "seq"), axis=0)
            down = wall[:, 12:].reshape(G, 4, 16, D)
            rest = wall[:, :12].reshape(G, 16 // per, 12, per, D)
            rest = rest.transpose(0, 2, 1, 3, 4).reshape(G, 12, 16, D)
            all_norms = lax.all_gather(norms, ("dp", "seq"), axis=0)
            all_norms = all_norms.astype(F32).reshape(G, n_dev // G, 16, D).sum(1).astype(BF)
            wall = jnp.concatenate([rest, down, all_norms[:, None]], 1)

        def of(x, i):
            return lax.dynamic_index_in_dim(x, i, 0, keepdims=False)

        def top(x):
            return flip("seq", ns, half)(x)

        valid_rows = jnp.pad(of(dec_valid, 1 - mine).astype(BF)[None], ((0, 15), (0, D - tok)))
        got = top(
            jnp.concatenate(
                [of(inputs, 1 - mine), of(encoder, 1 - mine), of(teacher, 1 - mine), valid_rows], 0
            )
        )
        both = jnp.stack(
            [
                jnp.concatenate([of(inputs, mine), got[:tok]], 0),
                jnp.concatenate([of(encoder, mine), got[tok : 2 * tok]], 0),
            ]
        )
        teach = jnp.concatenate([of(teacher, mine), got[2 * tok : 3 * tok]], 0)
        valid = jnp.concatenate([of(dec_valid, mine).astype(F32), got[3 * tok, :tok].astype(F32)])[:, None]
        bit = 1
        while bit < half:
            both = jnp.concatenate([both, flip("seq", ns, bit)(both)], 1)
            bit *= 2
        xf, ef = both[0], both[1]

        slots = jnp.arange(half, dtype=jnp.int32)[:, None]
        pieces = (seq_at ^ slots ^ jnp.array([[0, half]], jnp.int32)).reshape(-1)
        pos = (pieces[:, None] * tok + jnp.arange(tok, dtype=jnp.int32)[None]).reshape(-1)
        dec_k = of(dec_seg, mine).reshape(ns, tok)[pieces].reshape(-1)
        enc_k = of(enc_seg, mine).reshape(ns, tok)[pieces].reshape(-1)
        dec_q = dec_k[:rows]
        ok_self = (dec_k[:, None] == dec_q[None]) & (pos[:, None] <= pos[None, :rows])
        ok_cross = enc_k[:, None] == dec_q[None]
        mask_self = jnp.where(ok_self, 0.0, NEG).astype(F32)
        mask_cross = jnp.where(ok_cross, 0.0, NEG).astype(F32)

        p_shape = (HEADS, length, rows)
        q1, kv1, p1, rl1, at1 = call(
            functools.partial(self_forward, rows),
            [(xf, None), (wall, chunks(0, 3)), (mask_self, None)],
            [((rows, D), BF), ((length, 2 * D), BF), (p_shape, BF), ((HEADS, 1, rows), F32), ((D, rows), BF)],
            name="self_forward",
        )
        xh1, rs1, low1, q2, kv2, p2, rl2, at2 = call(
            functools.partial(cross_forward, rows),
            [(xf, None), (ef, None), (at1, None), (wall, chunks(3, 1)), (wall, chunks(4, 2)),
             (wall, chunks(6, 1)), (wall, NORMS), (mask_cross, None)],
            [((rows, D), F32), ((rows, 1), F32), ((rows, D), BF), ((rows, D), BF), ((length, 2 * D), BF),
             (p_shape, BF), ((HEADS, 1, rows), F32), ((D, rows), BF)],
            name="cross_forward",
        )
        core = ((dp_at & 1) if nd == 4 and ns == 8 else jnp.zeros_like(dp_at)).astype(jnp.int32)[None]
        out, small, d_r2, d_mix2, keep1, send1 = call(
            ffn_both,
            [(core, SMEM), (xh1, None), (at2, None), (teach, None), (valid, None), (wall, chunks(7, 1)),
             (wall, chunks(8, 4)), (wall, chunks(12, 4)), (wall, NORMS)],
            [((rows, D), BF), ((16, D), F32), ((rows, D), F32), ((rows, D), BF)] + [((2, 8, 9, 16, D), BF)] * 2,
            scratch=[pltpu.VMEM((rows, FF), BF), pltpu.VMEM((4, rows, D), F32), pltpu.VMEM((rows, D), BF)],
            name="ffn_both",
        )

        kv_half = [((length, D), BF), ((rows, HALF), BF)]
        d_rows = [pltpu.VMEM((HALF, rows), F32)]
        both_scratch = [pltpu.VMEM((length, D), BF)] + d_rows
        halves = lambda n: [((2, 8, n, 16, D), BF)] * 2
        packed = [((2, 8, 24, D), BF)] * 2

        def trade(bit, *groups):
            axis, b = bit
            size, at = (nd, dp_at) if axis == "dp" else (ns, seq_at)
            sends = [g.give(bit, (at >> b) & 1) for g in groups]
            flat = [x.reshape(-1, D) for x in sends]
            got = flip(axis, size, 1 << b)(flat[0] if len(flat) == 1 else jnp.concatenate(flat, 0))
            start = 0
            for g, x, f in zip(groups, sends, flat):
                g.take(lax.slice_in_dim(got, start, start + f.shape[0]).reshape(x.shape))
                start += f.shape[0]
            return got

        def other_core(x):
            return flip("dp", nd, 1)(x)

        core_bit, y_bit = ("dp", 0), ("dp", 1)
        x_bit, zl_bit, zh_bit = ("seq", 0), ("seq", 1), ("seq", 2)
        fast = nd == 4 and ns == 8

        def weight_sum(keep, got):
            split = (2, 2, 2, 2) + keep.shape[2:]
            return Halved([keep.reshape(split), got.reshape(split)], [y_bit, zh_bit, zl_bit, x_bit])

        got1 = other_core(send1)
        dkv2, dq2 = call(
            cross_back_a,
            [(q2, None), (kv2, None), (p2, None), (rl2, None), (d_mix2, None)],
            kv_half,
            scratch=d_rows,
            name="cross_back_a",
        )
        d_enc, d_mix1, d_r1, small, keep2, send2 = call(
            cross_back_b,
            [(core, SMEM), (ef, None), (q2, None), (kv2, None), (p2, None), (rl2, None),
             (tie(d_mix2, got1), None), (dkv2, None), (dq2, None), (wall, chunks(4, 2)), (wall, chunks(6, 1)),
             (wall, chunks(3, 1)), (wall, NORMS), (d_r2, None), (low1, None), (xh1, None), (rs1, None),
             (at1, None), (small, None)],
            [((length, D), BF), ((rows, D), BF), ((rows, D), F32), ((16, D), F32)] + halves(4),
            scratch=both_scratch,
            name="cross_back_b",
        )
        lane = lax.broadcasted_iota(jnp.int32, (16, D), 1)
        row = lax.broadcasted_iota(jnp.int32, (16, D), 0)
        small = jnp.where((row == 7) & (lane == dev), jnp.sum(dec_valid).astype(F32), small)
        small = Everywhere([small], [])

        def own_first(part):
            return Near([part.reshape((2,) * (half.bit_length() - 1) + (rows, D))],
                        [("seq", b) for b in range(half.bit_length() - 2, -1, -1)])

        self_a = [(core, SMEM), (xf, None), (q1, None), (kv1, None), (p1, None), (rl1, None), (d_mix1, None)]
        self_b_outs = [((length, D), BF), ((rows, D), F32)] + packed
        enc = own_first(d_enc)
        if fast:
            group1 = weight_sum(keep1, got1)
            trade(y_bit, group1)
            got2 = other_core(send2)
            got_e = trade(x_bit, enc)
            dkv1, dq1, keep3, send3 = call(
                functools.partial(self_back_a, rows), self_a, kv_half + packed, scratch=d_rows, name="self_back_a"
            )
            got3 = other_core(send3)
            trade(zl_bit, enc)
            self_b = self_a[:-1] + [(tie(d_mix1, got2, got_e), None)]
        else:
            dkv1, dq1, keep3, send3 = call(
                functools.partial(self_back_a, rows), self_a, kv_half + packed, scratch=d_rows, name="self_back_a"
            )
            self_b = self_a
        d_x, d_own, keep4, send4 = call(
            functools.partial(self_back_b, rows),
            self_b + [(dkv1, None), (dq1, None), (wall, chunks(0, 3)), (d_r1, None)],
            self_b_outs,
            scratch=both_scratch,
            name="self_back_b",
        )
        dx = own_first(d_x)

        def back_home(kept, recv):
            return jnp.where(mine == 0, jnp.stack([kept, recv]), jnp.stack([recv, kept]))

        def wide(g):
            return g.transpose(1, 0, 2).reshape(per, -1)

        def unpack(a, b):
            def three(g):
                v = g[..., 16:, :]
                v = jnp.concatenate([v[..., :HALF], v[..., HALF:]], -2)
                return g[..., :16, :HALF], g[..., :16, HALF:], v

            parts = [x for pair in zip(three(a), three(b)) for x in pair]
            return jnp.concatenate(parts, -1)

        if fast:
            e_own = enc.total()
            home = top(jnp.concatenate([out[tok:], e_own[tok:].astype(BF)], 0))
            group2, group3 = weight_sum(keep2, got2), weight_sum(keep3, got3)
            trade(y_bit, group2, group3)
            trade(zl_bit, group1)
            trade(x_bit, dx)
            low_small = small.give(core_bit, 0)
            got4 = other_core(jnp.concatenate([send4.reshape(-1, D), low_small], 0))
            small.take(got4[-16:])
            group4 = weight_sum(keep4, got4[:-16])
            trade(zl_bit, dx)
            trade(x_bit, group1, group2, group3)
            trade(y_bit, group4, small)
            x_own = dx.total() + d_own
            away_x = x_own[tok:].astype(BF)
            away_1 = group1.give(zh_bit, (seq_at >> 2) & 1)
            got = top(jnp.concatenate([away_x, away_1.reshape(-1, D)], 0))
            home_x = got[:tok]
            group1.take(got[tok:].reshape(away_1.shape))
            trade(x_bit, group4, small)
            trade(zl_bit, group2, group3, group4, small)
            trade(zh_bit, group2, group3, group4, small)
            s1, s2, small = group1.total(), group2.total(), small.total()
            g_up, g_down, g_co = wide(s1[:4]), s1[4:8].reshape(4 * per, D), s1[8]
            g_cin, g_cq, g_so = wide(s2[:2]), s2[2], s2[3]
            g_in = unpack(group3.total(), group4.total())
        else:
            for b in range(half.bit_length() - 1):
                trade(("seq", b), enc, dx)
            e_own = enc.total()
            x_own = dx.total() + d_own
            home = top(jnp.concatenate([out[tok:], e_own[tok:].astype(BF), x_own[tok:].astype(BF)], 0))
            home_x = home[2 * tok :]
            small = lax.psum(small.terms[0], ("dp", "seq"))

            def summed(g):
                return lax.psum_scatter(g, ("dp", "seq"), scatter_dimension=0, tiled=True).astype(F32)

            def rejoin(keep, send):
                g = jnp.stack([keep, send], 1)
                return g.reshape((G,) + g.shape[3:])

            def full(g):
                return g.transpose(0, 2, 1, 3).reshape(G * 16, -1)

            all1, all2 = rejoin(keep1, send1), rejoin(keep2, send2)
            g_up = summed(full(all1[:, :4]))
            g_down = summed(all1[:, 4:8].reshape(FF, D))
            g_co = summed(full(all1[:, 8:]))
            g_cin, g_cq, g_so = summed(full(all2[:, :2])), summed(full(all2[:, 2:3])), summed(full(all2[:, 3:]))
            g_in = summed(unpack(rejoin(keep3, send3), rejoin(keep4, send4)).reshape(G * 16, -1))

        loss = jnp.sum(small[6]) / (jnp.sum(small[7]) * D)
        g_norm = lax.dynamic_slice(small, (0, dev * per), (6, per))
        outputs = back_home(out[:tok], home[:tok])
        grad_encoder = back_home(e_own[:tok], home[tok : 2 * tok].astype(F32))
        grad_inputs = back_home(x_own[:tok], home_x.astype(F32))
        return (outputs, loss, grad_inputs, grad_encoder, g_in, g_so, g_cq, g_cin, g_co, g_up, g_down,
                g_norm[:3], g_norm[3:])

    return shards


def solution(mesh):
    rows, both = P("dp", "seq", None), P(("dp", "seq"), None)
    norm = P(None, ("dp", "seq"))
    return jax.shard_map(
        make_shards(mesh.shape["dp"], mesh.shape["seq"]),
        mesh=mesh,
        in_specs=(rows, rows, rows, P("dp", None), P("dp", None), P("dp", "seq")) + (both,) * 7 + (norm, norm),
        out_specs=(rows, P(), rows, rows) + (both,) * 7 + (norm, norm),
        check_vma=False,
    )
```

time: 319 us -> 310 us (0.972)
  waiting for transfers between devices: 158 us -> 134 us
  starting transfers between devices: 36 us -> 25.8 us
  local copies, waits for them, and re-layouts: 22.5 us -> 32.4 us
  Pallas kernels: 68.1 us -> 77.1 us
  other arithmetic: 15.3 us -> 20.9 us
    ppermute x19 -> x16, waiting for transfers between devices: 56.7 us -> 39.5 us  [the longest x12 39.5 us: trade(): flip(axis, size, 1 << b)]
    ppermute x19 -> x16, starting transfers between devices: 27.2 us -> 14.5 us  [the longest x12 13.9 us: trade(): flip(axis, size, 1 << b)]
    dynamic_slice x4 -> x38, local copies, waits for them, and re-layouts: 1.58 us -> 12.2 us  [pick(): return lax.dynamic_index_in_dim(x, i, at, keepdims=False)]
    pallas_call x5 -> x7, Pallas kernels: 68.1 us -> 77.1 us  [call(): pl.pallas_call(body, grid=(1,), in_specs=[whole(a.shape) if s is None els...]
    convert_element_type x6 -> x23, other arithmetic: 0.19 us -> 7.73 us  [the longest x18 6.95 us: give(): return self.total(away).astype(BF)]
    ppermute x2 -> x3, waiting for transfers between devices: 36.1 us -> 31 us  [top(): return flip('seq', ns, half)(x)]
    ppermute x2 -> x3, starting transfers between devices: 6.5 us -> 9.08 us  [top(): return flip('seq', ns, half)(x)]
  transfers between devices with their start and end apart: 24 -> 22, of which waited for: 16 -> 12; matrix products, arithmetic and copies ran while one was open for 8% -> 11% of each run, Pallas kernels for 5% -> 9%
where the time goes in v2:
time: 310 us; the launch traced here: 309 us
  waiting for transfers between devices  134 us (43%)
  Pallas kernels  77.1 us (25%)
  local copies, waits for them, and re-layouts  32.4 us (10%)
  starting transfers between devices  25.8 us (8%)
  other arithmetic  20.9 us (7%)
  between operations  18.3 us (6%)
    pallas_call x7, Pallas kernels, call(): pl.pallas_call(body, grid=(1,), in_specs=[whole(a.shape) if s is None els...  77.1 us
    ppermute x2, waiting for transfers between devices, shards(): both = jnp.concatenate([both, flip('seq', ns, bit)(both)], 1)  56.2 us
    ppermute x12, waiting for transfers between devices, trade(): flip(axis, size, 1 << b)  39.5 us
    ppermute x3, waiting for transfers between devices, top(): return flip('seq', ns, half)(x)  31 us
    ppermute x12, starting transfers between devices, trade(): flip(axis, size, 1 << b)  13.9 us
    dynamic_slice x38, local copies, waits for them, and re-layouts, pick(): return lax.dynamic_index_in_dim(x, i, at, keepdims=False)  12.2 us
    ppermute x3, starting transfers between devices, top(): return flip('seq', ns, half)(x)  9.08 us
    all_gather x1, waiting for transfers between devices, shards(): wall = lax.all_gather(packed, ('dp', 'seq'), axis=0)  7.78 us
  transfers between devices with their start and end apart: 22, of which 12 were waited for; matrix products, arithmetic and copies ran while one was open for 11% of the time, Pallas kernels for 9%

profile of v2, /device:TPU:0, one launch (start us, length us, event | category | flops | bytes accessed | tf_op | source)
XLA Modules:
  0.0 308.9 jit_solution(6545843679203351118)
XLA Ops:
  15.4 4.9 %collective-permute-start = (bf16[400,512]{1,0:T(8,128)(2,1)S(1)}, bf16[400,512]{1,0:T(8,128)(2,1)S(1)}, u32[]{:S(2)}, u32[]{:S(2)}) collective-permute-start(bf16[400,512]{1,0:T(8,128)(2,1)S(1)} %fusion.7), channel_id=1, source_target_pairs={{0,4},{1,5},{2,6},{3,7},{4,0},{5,1},{6,2},{7,3},{8,12},{9,13},{10,... | collective-permute-start | bytes 1228808 | tf_op jit(solution)/shard_map/ppermute | solution.py:362
  20.5 24.0 %collective-permute-done = bf16[400,512]{1,0:T(8,128)(2,1)S(1)} collective-permute-done((bf16[400,512]{1,0:T(8,128)(2,1)S(1)}, bf16[400,512]{1,0:T(8,128)(2,1)S(1)}, u32[]{:S(2)}, u32[]{:S(2)}) %collective-permute-start) | collective-permute-done | bytes 409632 | tf_op jit(solution)/shard_map/ppermute | solution.py:362
  46.9 18.4 %collective-permute-done.1 = bf16[2,256,512]{2,1,0:T(8,128)(2,1)S(1)} collective-permute-done((bf16[2,256,512]{2,1,0:T(8,128)(2,1)S(1)}, bf16[2,256,512]{2,1,0:T(8,128)(2,1)S(1)}, u32[]{:S(2)}, u32[]{:S(2)}) %collective-permute-start.1) | collective-permute-done | bytes 524320 | tf_op jit(solution)/shard_map/ppermute | solution.py:380
  66.7 1.8 compare_select_fusion
  70.7 37.8 %collective-permute-done.2 = bf16[2,512,512]{2,1,0:T(8,128)(2,1)S(1)} collective-permute-done((bf16[2,512,512]{2,1,0:T(8,128)(2,1)S(1)}, bf16[2,512,512]{2,1,0:T(8,128)(2,1)S(1)}, u32[]{:S(2)}, u32[]{:S(2)}) %collective-permute-start.2) | collective-permute-done | bytes 1048608 | tf_op jit(solution)/shard_map/ppermute | solution.py:380
  110.1 7.8 %all-gather.3.cloned.1.call-done = bf16[544,16,512]{2,1,0:T(8,128)(2,1)} async-done(((bf16[17,16,512]{2,1,0:T(8,128)(2,1)}), bf16[544,16,512]{2,1,0:T(8,128)(2,1)}) %all-gather.3.cloned.1.call-update) | async-done | bytes 8912912 | tf_op jit(solution)/shard_map/all_gather | solution.py:347
  117.9 12.0 %self_forward.1 = (bf16[256,512]{1,0:T(8,128)(2,1)}, bf16[1024,1024]{1,0:T(8,128)(2,1)}, bf16[8,1024,256]{2,1,0:T(8,128)(2,1)}, f32[8,1,256]{2,1,0:T(1,128)}, bf16[512,256]{1,0:T(8,128)(2,1)}) custom-call(bf16[1024,512]{1,0:T(8,128)(2,1)} %get-tuple-element.89.xf, bf16[32,17,16,512]{3,2,1,0:T(8,128)(2,1)} %bitcast.341, f32[1024,256]{1,0:T(8,128)} %get-tuple-element.121.mask), custom_call_target="tpu_custom_call" | custom-call | tf_op jit(solution)/shard_map/self_forward/pallas_call | solution.py:47
  129.8 14.0 %cross_forward.1 = (f32[256,512]{1,0:T(8,128)}, f32[256,1]{1,0:T(8,128)}, bf16[256,512]{1,0:T(8,128)(2,1)}, bf16[256,512]{1,0:T(8,128)(2,1)}, bf16[1024,1024]{1,...) custom-call(bf16[1024,512]{1,0:T(8,128)(2,1)} %get-tuple-element.89.xf, ...), custom_call_target="tpu_custom_call" | custom-call | tf_op jit(solution)/shard_map/cross_forward/pallas_call | solution.py:47
  143.8 10.8 %ffn_both.1 = (bf16[256,512]{1,0:T(8,128)(2,1)}, f32[16,512]{1,0:T(8,128)}, f32[256,512]{1,0:T(8,128)}, bf16[256,512]{1,0:T(8,128)(2,1)}, bf16[2,8,9,16,512]{4,3...) custom-call(s32[1]{0:T(128)} %bitcast.core, f32[256,512]{1,0:T(8,128)} %get-tuple-element.51.xh1, ...), custom_call_target="tpu_custom_call" | custom-call | tf_op jit(solution)/shard_map/ffn_both/pallas_call | solution.py:47
  156.2 7.8 %cross_back_a.1 = (bf16[1024,512]{1,0:T(8,128)(2,1)}, bf16[256,256]{1,0:T(8,128)(2,1)}) custom-call(bf16[256,512]{1,0:T(8,128)(2,1)} %get-tuple-element.54.q, bf16[1024,1024]{1,0:T(8,128)(2,1)} %get-tuple-element.55.kv, bf16[8,1024,256]{2,1,0:T(8,128)(2,1)} %get-tuple-element.56.p, f32[8,1,256]{2,1,0:T(1,128)} %get-tuple-element.57.rl, ...), custom_call_target="tpu_custom_call" | custom-call | tf_op jit(solution)/shard_map/cross_back_a/pallas_call | solution.py:47
  166.3 12.9 %cross_back_b.1 = (bf16[1024,512]{1,0:T(8,128)(2,1)}, bf16[256,512]{1,0:T(8,128)(2,1)}, f32[256,512]{1,0:T(8,128)}, f32[16,512]{1,0:T(8,128)}, bf16[2,8,4,16,512...) custom-call(s32[1]{0:T(128)} %bitcast.core, bf16[1024,512]{1,0:T(8,128)(2,1)} %get-tuple-element.90.ef, ...), custom_call_target="tpu_custom_call" | custom-call | tf_op jit(solution)/shard_map/cross_back_b/pallas_call | solution.py:47
  181.2 1.9 slice.294
  183.0 2.0 collective-permute-start.4
  188.1 8.7 %self_back_a.1 = (bf16[1024,512]{1,0:T(8,128)(2,1)}, bf16[256,256]{1,0:T(8,128)(2,1)}, bf16[2,8,24,512]{3,2,1,0:T(8,128)(2,1)}, bf16[2,8,24,512]{3,2,1,0:T(8,128)(2,1)}) custom-call(s32[1]{0:T(128)} %bitcast.core, bf16[1024,512]{1,0:T(8,128)(2,1)} %get-tuple-element.89.xf, bf16[256,512]{1,0:T(8,128)(2,1)} %get-tuple-element.70.q, ...), custom_call_target="tpu_custom_call" | custom-call | tf_op jit(solution)/shard_map/self_back_a/pallas_call | solution.py:47
  203.3 3.0 collective-permute-start.5
  208.3 4.7 %collective-permute-done.5 = bf16[256,512]{1,0:T(8,128)(2,1)S(1)} collective-permute-done((bf16[256,512]{1,0:T(8,128)(2,1)S(1)}, bf16[256,512]{1,0:T(8,128)(2,1)S(1)}, u32[]{:S(2)}, u32[]{:S(2)}) %collective-permute-start.5) | collective-permute-done | bytes 262176 | tf_op jit(solution)/shard_map/ppermute | solution.py:431
  214.9 2.7 collective-permute-start.6
  217.6 11.0 %self_back_b.1 = (bf16[1024,512]{1,0:T(8,128)(2,1)}, f32[256,512]{1,0:T(8,128)}, bf16[2,8,24,512]{3,2,1,0:T(8,128)(2,1)}, bf16[2,8,24,512]{3,2,1,0:T(8,128)(2,1)}) custom-call(s32[1]{0:T(128)} %bitcast.core, bf16[1024,512]{1,0:T(8,128)(2,1)} %get-tuple-element.89.xf, bf16[256,512]{1,0:T(8,128)(2,1)} %get-tuple-element.70.q, ...), custom_call_target="tpu_custom_call" | custom-call | tf_op jit(solution)/shard_map/self_back_b/pallas_call | solution.py:47
  240.7 2.3 collective-permute-done.18
  243.6 9.8 %collective-permute-done.14 = bf16[208,512]{1,0:T(8,128)(2,1)S(1)} collective-permute-done((bf16[208,512]{1,0:T(8,128)(2,1)S(1)}, bf16[208,512]{1,0:T(8,128)(2,1)S(1)}, u32[]{:S(2)}, u32[]{:S(2)}) %collective-permute-start.14) | collective-permute-done | bytes 213024 | tf_op jit(solution)/shard_map/ppermute | solution.py:431
  257.4 1.9 collective-permute-done.15
  259.9 12.6 %collective-permute-done.12 = bf16[640,512]{1,0:T(8,128)(2,1)S(1)} collective-permute-done((bf16[640,512]{1,0:T(8,128)(2,1)S(1)}, bf16[640,512]{1,0:T(8,128)(2,1)S(1)}, u32[]{:S(2)}, u32[]{:S(2)}) %collective-permute-start.12) | collective-permute-done | bytes 655392 | tf_op jit(solution)/shard_map/ppermute | solution.py:431
  275.2 7.9 %collective-permute-done.16 = bf16[240,512]{1,0:T(8,128)(2,1)S(1)} collective-permute-done((bf16[240,512]{1,0:T(8,128)(2,1)S(1)}, bf16[240,512]{1,0:T(8,128)(2,1)S(1)}, u32[]{:S(2)}, u32[]{:S(2)}) %collective-permute-start.16) | collective-permute-done | bytes 245792 | tf_op jit(solution)/shard_map/ppermute | solution.py:431
  284.6 7.0 %collective-permute-done.20 = bf16[272,512]{1,0:T(8,128)(2,1)S(1)} collective-permute-done((bf16[272,512]{1,0:T(8,128)(2,1)S(1)}, bf16[272,512]{1,0:T(8,128)(2,1)S(1)}, u32[]{:S(2)}, u32[]{:S(2)}) %collective-permute-start.20) | collective-permute-done | bytes 278560 | tf_op jit(solution)/shard_map/ppermute | solution.py:362
  (254 shorter events, 63.1 us)
Async XLA Ops:
  7.2 110.6 %all-gather.3.cloned.1.call-start = ((), (), s32[]{:S(2)}) async-start(), calls=%async_computation | async-start | bytes 9191424 | tf_op jit(solution)/shard_map/all_gather | solution.py:347
  15.4 29.1 %collective-permute-start = (bf16[400,512]{1,0:T(8,128)(2,1)S(1)}, bf16[400,512]{1,0:T(8,128)(2,1)S(1)}, u32[]{:S(2)}, u32[]{:S(2)}) collective-permute-start(bf16[400,512]{1,0:T(8,128)(2,1)S(1)} %fusion.7), channel_id=1, source_target_pairs={{0,4},{1,5},{2,6},{3,7},{4,0},{5,1},{6,2},{7,3},{8,12},{9,13},{10,... | collective-permute-start | bytes 1228808 | tf_op jit(solution)/shard_map/ppermute | solution.py:362
  44.6 20.7 %collective-permute-start.1 = (bf16[2,256,512]{2,1,0:T(8,128)(2,1)S(1)}, bf16[2,256,512]{2,1,0:T(8,128)(2,1)S(1)}, u32[]{:S(2)}, u32[]{:S(2)}) collective-permute-start(bf16[2,256,512]{2,1,0:T(8,128)(2,1)S(1)} %pad_maximum_fusion.4), channel_id=1, source_target_pairs={{0,1},{1,0},{2,3},{3,2},{4,5},{5,4},{6,7},{7,6},{8,9},{9,8},{10,11... | collective-permute-start | bytes 1572872 | tf_op jit(solution)/shard_map/ppermute | solution.py:380
  65.4 43.0 %collective-permute-start.2 = (bf16[2,512,512]{2,1,0:T(8,128)(2,1)S(1)}, bf16[2,512,512]{2,1,0:T(8,128)(2,1)S(1)}, u32[]{:S(2)}, u32[]{:S(2)}) collective-permute-start(bf16[2,512,512]{2,1,0:T(8,128)(2,1)S(1)} %pad_maximum_fusion.1), channel_id=1, source_target_pairs={{0,2},{1,3},{2,0},{3,1},{4,6},{5,7},{6,4},{7,5},{8,10},{9,11},{10,... | collective-permute-start | bytes 3145736 | tf_op jit(solution)/shard_map/ppermute | solution.py:380
  154.5 11.1 %collective-permute-start.3 = (bf16[2,8,9,16,512]{4,3,2,1,0:T(8,128)(2,1)}, bf16[2,8,9,16,512]{4,3,2,1,0:T(8,128)(2,1)S(1)}, u32[]{:S(2)}, u32[]{:S(2)}) collective-permute-start(bf16[2,8,9,16,512]{4,3,2,1,0:T(8,128)(2,1)} %get-tuple-element.59), channel_id=1, source_target_pairs={{0,8},{8,0},{16,24},{24,16},{1,9},{9,1},{17,25},{25,17},{2,10},{10... | collective-permute-start | bytes 7077896 | tf_op jit(solution)/shard_map/ppermute | solution.py:439
  156.1 43.9 %copy-start.26 = (pred[512]{0:T(512)(128)(4,1)}, pred[512]{0:T(512)(128)(4,1)S(1)}, u32[]{:S(2)}) copy-start(pred[512]{0:T(512)(128)(4,1)S(1)} %iota_compare_fusion.1) | copy-start | bytes 1540
  156.2 43.8 %copy-start.28 = (pred[16]{0:T(512)(128)(4,1)}, pred[16]{0:T(512)(128)(4,1)S(1)}, u32[]{:S(2)}) copy-start(pred[16]{0:T(512)(128)(4,1)S(1)} %iota_compare_fusion.2) | copy-start | bytes 52
  183.0 19.1 %collective-permute-start.4 = (bf16[512,512]{1,0:T(8,128)(2,1)}, bf16[512,512]{1,0:T(8,128)(2,1)}, u32[]{:S(2)}, u32[]{:S(2)}) collective-permute-start(bf16[512,512]{1,0:T(8,128)(2,1)} %bitcast.33), channel_id=1, source_target_pairs={{0,1},{1,0},{2,3},{3,2},{4,5},{5,4},{6,7},{7,6},{8,9},{9,8},{10,11... | collective-permute-start | bytes 1572872 | tf_op jit(solution)/shard_map/ppermute | solution.py:431
  185.0 32.6 %collective-permute-start.7 = (bf16[2,8,4,16,512]{4,3,2,1,0:T(8,128)(2,1)}, bf16[2,8,4,16,512]{4,3,2,1,0:T(8,128)(2,1)}, u32[]{:S(2)}, u32[]{:S(2)}) collective-permute-start(bf16[2,8,4,16,512]{4,3,2,1,0:T(8,128)(2,1)} %get-tuple-element.68), channel_id=1, source_target_pairs={{0,8},{8,0},{16,24},{24,16},{1,9},{9,1},{17,25},{25,17},{2,10},{10... | collective-permute-start | bytes 3145736 | tf_op jit(solution)/shard_map/ppermute | solution.py:439
  186.6 51.3 %collective-permute-start.10 = (bf16[1152,512]{1,0:T(8,128)(2,1)}, bf16[1152,512]{1,0:T(8,128)(2,1)S(1)}, u32[]{:S(2)}, u32[]{:S(2)}) collective-permute-start(bf16[1152,512]{1,0:T(8,128)(2,1)} %bitcast.49), channel_id=1, source_target_pairs={{0,16},{8,24},{16,0},{24,8},{1,17},{9,25},{17,1},{25,9},{2,18},{10... | collective-permute-start | bytes 3538952 | tf_op jit(solution)/shard_map/ppermute | solution.py:431
  196.8 9.5 %collective-permute-start.8 = (bf16[2,8,24,512]{3,2,1,0:T(8,128)(2,1)}, bf16[2,8,24,512]{3,2,1,0:T(8,128)(2,1)S(1)}, u32[]{:S(2)}, u32[]{:S(2)}) collective-permute-start(bf16[2,8,24,512]{3,2,1,0:T(8,128)(2,1)} %get-tuple-element.75), channel_id=1, source_target_pairs={{0,8},{8,0},{16,24},{24,16},{1,9},{9,1},{17,25},{25,17},{2,10},{10... | collective-permute-start | bytes 1179656 | tf_op jit(solution)/shard_map/ppermute | solution.py:439
  203.3 9.8 %collective-permute-start.5 = (bf16[256,512]{1,0:T(8,128)(2,1)S(1)}, bf16[256,512]{1,0:T(8,128)(2,1)S(1)}, u32[]{:S(2)}, u32[]{:S(2)}) collective-permute-start(bf16[256,512]{1,0:T(8,128)(2,1)S(1)} %fusion.6), channel_id=1, source_target_pairs={{0,2},{1,3},{2,0},{3,1},{4,6},{5,7},{6,4},{7,5},{8,10},{9,11},{10,... | collective-permute-start | bytes 786440 | tf_op jit(solution)/shard_map/ppermute | solution.py:431
  214.9 20.4 %collective-permute-start.6 = (bf16[256,512]{1,0:T(8,128)(2,1)}, bf16[256,512]{1,0:T(8,128)(2,1)}, u32[]{:S(2)}, u32[]{:S(2)}) collective-permute-start(bf16[256,512]{1,0:T(8,128)(2,1)} %pad_maximum_fusion.8), channel_id=1, source_target_pairs={{0,4},{1,5},{2,6},{3,7},{4,0},{5,1},{6,2},{7,3},{8,12},{9,13},{10,... | collective-permute-start | bytes 786440 | tf_op jit(solution)/shard_map/ppermute | solution.py:362
  229.8 13.1 %collective-permute-start.18 = (bf16[512,512]{1,0:T(8,128)(2,1)S(1)}, bf16[512,512]{1,0:T(8,128)(2,1)S(1)}, u32[]{:S(2)}, u32[]{:S(2)}) collective-permute-start(bf16[512,512]{1,0:T(8,128)(2,1)S(1)} %bitcast.411), channel_id=1, source_target_pairs={{0,1},{1,0},{2,3},{3,2},{4,5},{5,4},{6,7},{7,6},{8,9},{9,8},{10,11... | collective-permute-start | bytes 1572872 | tf_op jit(solution)/shard_map/ppermute | solution.py:431
  231.9 23.4 %collective-permute-start.9 = (bf16[704,512]{1,0:T(8,128)(2,1)S(1)}, bf16[704,512]{1,0:T(8,128)(2,1)S(1)}, u32[]{:S(2)}, u32[]{:S(2)}) collective-permute-start(bf16[704,512]{1,0:T(8,128)(2,1)S(1)} %pad_maximum_fusion.2), channel_id=1, source_target_pairs={{0,16},{8,24},{16,0},{24,8},{1,17},{9,25},{17,1},{25,9},{2,18},{10... | collective-permute-start | bytes 2162696 | tf_op jit(solution)/shard_map/ppermute | solution.py:431
  233.2 5.4 %collective-permute-start.13 = (bf16[400,512]{1,0:T(8,128)(2,1)S(1)}, bf16[400,512]{1,0:T(8,128)(2,1)S(1)}, u32[]{:S(2)}, u32[]{:S(2)}) collective-permute-start(bf16[400,512]{1,0:T(8,128)(2,1)S(1)} %pad_maximum_fusion.5), channel_id=1, source_target_pairs={{0,8},{8,0},{16,24},{24,16},{1,9},{9,1},{17,25},{25,17},{2,10},{10... | collective-permute-start | bytes 1228808 | tf_op jit(solution)/shard_map/ppermute | solution.py:439
  238.3 16.9 %collective-permute-start.11 = (bf16[576,512]{1,0:T(8,128)(2,1)S(1)}, bf16[576,512]{1,0:T(8,128)(2,1)S(1)}, u32[]{:S(2)}, u32[]{:S(2)}) collective-permute-start(bf16[576,512]{1,0:T(8,128)(2,1)S(1)} %fusion), channel_id=1, source_target_pairs={{0,2},{1,3},{2,0},{3,1},{4,6},{5,7},{6,4},{7,5},{8,10},{9,11},{10,... | collective-permute-start | bytes 1769480 | tf_op jit(solution)/shard_map/ppermute | solution.py:431
  238.9 14.5 %collective-permute-start.14 = (bf16[208,512]{1,0:T(8,128)(2,1)S(1)}, bf16[208,512]{1,0:T(8,128)(2,1)S(1)}, u32[]{:S(2)}, u32[]{:S(2)}) collective-permute-start(bf16[208,512]{1,0:T(8,128)(2,1)S(1)} %pad_maximum_fusion.10), channel_id=1, source_target_pairs={{0,16},{8,24},{16,0},{24,8},{1,17},{9,25},{17,1},{25,9},{2,18},{10... | collective-permute-start | bytes 638984 | tf_op jit(solution)/shard_map/ppermute | solution.py:431
  243.0 16.7 %collective-permute-start.19 = (bf16[256,512]{1,0:T(8,128)(2,1)S(1)}, bf16[256,512]{1,0:T(8,128)(2,1)S(1)}, u32[]{:S(2)}, u32[]{:S(2)}) collective-permute-start(bf16[256,512]{1,0:T(8,128)(2,1)S(1)} %fusion.4), channel_id=1, source_target_pairs={{0,2},{1,3},{2,0},{3,1},{4,6},{5,7},{6,4},{7,5},{8,10},{9,11},{10,... | collective-permute-start | bytes 786440 | tf_op jit(solution)/shard_map/ppermute | solution.py:431
  253.6 5.7 %collective-permute-start.15 = (bf16[112,512]{1,0:T(8,128)(2,1)S(1)}, bf16[112,512]{1,0:T(8,128)(2,1)S(1)}, u32[]{:S(2)}, u32[]{:S(2)}) collective-permute-start(bf16[112,512]{1,0:T(8,128)(2,1)S(1)} %pad_maximum_fusion.12), channel_id=1, source_target_pairs={{0,1},{1,0},{2,3},{3,2},{4,5},{5,4},{6,7},{7,6},{8,9},{9,8},{10,11... | collective-permute-start | bytes 344072 | tf_op jit(solution)/shard_map/ppermute | solution.py:431
  256.5 16.0 %collective-permute-start.12 = (bf16[640,512]{1,0:T(8,128)(2,1)S(1)}, bf16[640,512]{1,0:T(8,128)(2,1)S(1)}, u32[]{:S(2)}, u32[]{:S(2)}) collective-permute-start(bf16[640,512]{1,0:T(8,128)(2,1)S(1)} %pad_maximum_fusion.3), channel_id=1, source_target_pairs={{0,1},{1,0},{2,3},{3,2},{4,5},{5,4},{6,7},{7,6},{8,9},{9,8},{10,11... | collective-permute-start | bytes 1966088 | tf_op jit(solution)/shard_map/ppermute | solution.py:431
  272.9 10.3 %collective-permute-start.16 = (bf16[240,512]{1,0:T(8,128)(2,1)S(1)}, bf16[240,512]{1,0:T(8,128)(2,1)S(1)}, u32[]{:S(2)}, u32[]{:S(2)}) collective-permute-start(bf16[240,512]{1,0:T(8,128)(2,1)S(1)} %pad_maximum_fusion.9), channel_id=1, source_target_pairs={{0,2},{1,3},{2,0},{3,1},{4,6},{5,7},{6,4},{7,5},{8,10},{9,11},{10,... | collective-permute-start | bytes 737288 | tf_op jit(solution)/shard_map/ppermute | solution.py:431
  273.7 17.9 %collective-permute-start.20 = (bf16[272,512]{1,0:T(8,128)(2,1)S(1)}, bf16[272,512]{1,0:T(8,128)(2,1)S(1)}, u32[]{:S(2)}, u32[]{:S(2)}) collective-permute-start(bf16[272,512]{1,0:T(8,128)(2,1)S(1)} %pad_maximum_fusion.6), channel_id=1, source_target_pairs={{0,4},{1,5},{2,6},{3,7},{4,0},{5,1},{6,2},{7,3},{8,12},{9,13},{10,... | collective-permute-start | bytes 835592 | tf_op jit(solution)/shard_map/ppermute | solution.py:362
  284.1 10.4 %collective-permute-start.17 = (bf16[128,512]{1,0:T(8,128)(2,1)S(1)}, bf16[128,512]{1,0:T(8,128)(2,1)S(1)}, u32[]{:S(2)}, u32[]{:S(2)}) collective-permute-start(bf16[128,512]{1,0:T(8,128)(2,1)S(1)} %pad_maximum_fusion.11), channel_id=1, source_target_pairs={{0,4},{1,5},{2,6},{3,7},{4,0},{5,1},{6,2},{7,3},{8,12},{9,13},{10,... | collective-permute-start | bytes 393224 | tf_op jit(solution)/shard_map/ppermute | solution.py:431
  (30 other events, 255.7 us)
Sparse Core Ops, SparseCore 0:
  15.3 102.5 all-gather.2

commit v3 on v2

v3 whole, which is shorter than its diff:
```python
import functools

import jax
import jax.numpy as jnp
from jax import lax
from jax.experimental import pallas as pl
from jax.experimental.pallas import tpu as pltpu
from jax.sharding import PartitionSpec as P

HEADS = 8
HEAD_DIM = 64
EPS = 1e-5
NEG = -1e30
SCALE = 0.125
D = 512
FF = 2048
HALF = 256
G = 32
BF = jnp.bfloat16
F32 = jnp.float32
MIB = 1 << 20

PLACE_1, PLACE_2, SLOT = 1, 17, 33

NN = (((1,), (0,)), ((), ()))
NT = (((1,), (1,)), ((), ()))
TN = (((0,), (0,)), ((), ()))


def dot(a, b, dims=NN):
    return lax.dot_general(a, b, dims, preferred_element_type=F32)


def whole(shape):
    return pl.BlockSpec(shape, lambda i: (0,) * len(shape))


SMEM = pl.BlockSpec(memory_space=pltpu.SMEM)


def chunks(first, count):
    return pl.BlockSpec((G, count, 16, D), lambda i: (0, first // count, 0, 0))


def whole_weight(ref, j):
    return ref[:, j].reshape(D, D)


def call(body, ins, outs, scratch=(), name=None):
    return pl.pallas_call(
        body,
        grid=(1,),
        in_specs=[whole(a.shape) if s is None else s for a, s in ins],
        out_specs=[whole(s) for s, _ in outs],
        out_shape=[jax.ShapeDtypeStruct(s, t) for s, t in outs],
        scratch_shapes=list(scratch),
        compiler_params=pltpu.CompilerParams(vmem_limit_bytes=56 * MIB),
        name=name,
        cost_estimate=pl.CostEstimate(flops=1000, bytes_accessed=1000, transcendentals=0),
    )(*[a for a, _ in ins])


def weight(ids, near, far, j):
    picks = []
    for g in range(G):
        at = ids[SLOT + g]
        low = at & (G // 2 - 1)
        picks.append(jnp.where(at < G // 2, near[low, j], far[low, j]))
    return jnp.concatenate(picks, 0)


def norm_rows(ref):
    return jnp.sum(ref[:, 0].astype(F32), axis=0)


def put(ids, first, ref, j, value):
    value = value.astype(BF)
    for i in range(16):
        ref[ids[first + i], j] = value[16 * i : 16 * i + 16]


def norm_forward(resid, gain, bias):
    centre = resid - jnp.mean(resid, axis=-1, keepdims=True)
    rstd = lax.rsqrt(jnp.mean(centre * centre, axis=-1, keepdims=True) + EPS)
    xhat = centre * rstd
    return xhat, rstd, xhat * gain + bias


def norm_back(g, xhat, rstd, gain):
    e = g * gain
    m1 = jnp.mean(e, axis=-1, keepdims=True)
    m2 = jnp.mean(e * xhat, axis=-1, keepdims=True)
    dr = (e - m1 - xhat * m2) * rstd
    return dr, jnp.sum(g * xhat, axis=0, keepdims=True), jnp.sum(g, axis=0, keepdims=True)


def head_half(x, e):
    lane = lax.broadcasted_iota(jnp.int32, x.shape, 1)
    return jnp.where((lane < HEAD_DIM) == (e == 0), x, jnp.zeros_like(x))


def attend(q_ref, kv_ref, mask_ref, p_ref, rl_ref, at_ref):
    def pair(hp, carry):
        c0 = pl.multiple_of(hp * 128, 128)
        k2 = kv_ref[:, pl.ds(c0, 128)]
        v2 = kv_ref[:, pl.ds(pl.multiple_of(D + c0, 128), 128)]
        q2 = q_ref[:, pl.ds(c0, 128)]
        for e in range(2):
            s = dot(k2, head_half(q2, e), NT) + mask_ref[...]
            p = jnp.exp(s - jnp.max(s, axis=0, keepdims=True))
            rl = 1.0 / jnp.sum(p, axis=0, keepdims=True)
            pb = p.astype(BF)
            p_ref[2 * hp + e] = pb
            rl_ref[2 * hp + e] = rl
            o = dot(v2, pb, TN) * rl
            at_ref[pl.ds(pl.multiple_of((2 * hp + e) * HEAD_DIM, HEAD_DIM), HEAD_DIM), :] = o[
                e * HEAD_DIM : (e + 1) * HEAD_DIM
            ].astype(BF)
        return carry

    lax.fori_loop(0, HEADS // 2, pair, 0)


def attend_back(first, q_ref, kv_ref, p_ref, rl_ref, do_ref, dkv_ref, dqt_ref):
    def pair(i, carry):
        hp = first // 2 + i
        c0 = pl.multiple_of(hp * 128, 128)
        o0 = pl.multiple_of(i * 128, 128)
        k2 = kv_ref[:, pl.ds(c0, 128)]
        v2 = kv_ref[:, pl.ds(pl.multiple_of(D + c0, 128), 128)]
        q2 = q_ref[:, pl.ds(c0, 128)]
        do2 = do_ref[:, pl.ds(c0, 128)]
        dk = dv = None
        for e in range(2):
            dom = head_half(do2, e)
            dp = dot(v2, dom, NT)
            p = p_ref[2 * hp + e].astype(F32) * rl_ref[2 * hp + e]
            t = p * dp
            ds = (t - p * jnp.sum(t, axis=0, keepdims=True)).astype(BF)
            dk_e = dot(ds, head_half(q2, e))
            dv_e = dot(p.astype(BF), dom)
            dk = dk_e if dk is None else dk + dk_e
            dv = dv_e if dv is None else dv + dv_e
            dqt = dot(k2, ds, TN) * SCALE
            dqt_ref[pl.ds(pl.multiple_of((2 * i + e) * HEAD_DIM, HEAD_DIM), HEAD_DIM), :] = dqt[
                e * HEAD_DIM : (e + 1) * HEAD_DIM
            ]
        dkv_ref[:, pl.ds(o0, 128)] = dk.astype(BF)
        dkv_ref[:, pl.ds(pl.multiple_of(HALF + o0, 128), 128)] = dv.astype(BF)
        return carry

    lax.fori_loop(0, HEADS // 4, pair, 0)


def cols(ref, c, width):
    picks = [ref[:, pl.ds(pl.multiple_of((2 * y + c) * width, width), width)] for y in range(2)]
    return jnp.concatenate(picks, 1)


def rows_of(ref, c, width):
    picks = [ref[pl.ds(pl.multiple_of((2 * y + c) * width, width), width), :] for y in range(2)]
    return jnp.concatenate(picks, 0)


def put_half(ids, ref, lhs, dq, dk, dv, lhs_q):
    qk = jnp.concatenate([dot(lhs_q, dq, TN), dot(lhs, dk, TN)], 1).astype(BF)
    v = dot(lhs, dv, TN)
    for i in range(16):
        at = ids[PLACE_2 + i]
        ref[at, 0:16] = qk[16 * i : 16 * i + 16]
        ref[at, 16:24] = jnp.concatenate([v[16 * i : 16 * i + 8], v[16 * i + 8 : 16 * i + 16]], 1).astype(BF)


def sides(ids, keep, send):
    return ((send, 1 - ids[0]), (keep, ids[0]))


def pack(s_in, s_out, c_in, c_q, c_out, up, down, gain, bias, at, pa, pb):
    for j in range(3):
        pa[j] = s_in[:, j * D : (j + 1) * D]
    pb[8] = s_out[...]
    for j in range(2):
        pb[9 + j] = c_in[:, j * D : (j + 1) * D]
    pb[11] = c_q[...]
    pb[12] = c_out[...]
    for j in range(4):
        pb[j] = up[:, j * D : (j + 1) * D]
        pb[4 + j] = down[16 * j : 16 * j + 16, :]
    rows = jnp.concatenate([gain[...], bias[...], jnp.zeros((10, 16), BF)], 0)
    column = lax.broadcasted_iota(jnp.int32, (16, D), 1)
    row = lax.broadcasted_iota(jnp.int32, (16, D), 0)
    pick = (column == at[0] * 16 + row).astype(BF)
    pb[13] = dot(rows, pick).astype(BF)


def join(full, near, far):
    half = near.shape[0]
    full[:half] = near[...]
    full[half:] = far[...]


def self_forward(rows, ids, near, far, wa, wa_far, mask, xf, q, kv, p, rl, at):
    join(xf, near, far)
    q[...] = (dot(xf[:rows], weight(ids, wa, wa_far, 0)).astype(BF).astype(F32) * SCALE).astype(BF)
    kv[:, :D] = dot(xf[...], weight(ids, wa, wa_far, 1)).astype(BF)
    kv[:, D:] = dot(xf[...], weight(ids, wa, wa_far, 2)).astype(BF)
    attend(q, kv, mask, p, rl, at)


def cross_forward(rows, ids, xf, near, far, at1, wb, norms, mask, ef, xh1, rs1, low1, q, kv, p, rl, at):
    join(ef, near, far)
    gb = norm_rows(norms)
    resid = xf[:rows].astype(F32) + dot(at1[...], whole_weight(wb, 0), TN)
    xhat, rstd, n1 = norm_forward(resid, gb[0:1], gb[3:4])
    xh1[...] = xhat
    rs1[...] = rstd
    low1[...] = n1.astype(BF)
    q[...] = (dot(low1[...], whole_weight(wb, 3)).astype(BF).astype(F32) * SCALE).astype(BF)
    kv[:, :D] = dot(ef[...], whole_weight(wb, 1)).astype(BF)
    kv[:, D:] = dot(ef[...], whole_weight(wb, 2)).astype(BF)
    attend(q, kv, mask, p, rl, at)


def ffn_both(ids, xh1, at2, teach, valid, w_up, w_dn, w_co, norms,
             out, small, d_r2, d_mix, keep, send, act, hid, low2, wup):
    gb = norm_rows(norms)
    n1 = xh1[...] * gb[0:1] + gb[3:4]
    wco = whole_weight(w_co, 0)
    for j in range(4):
        wup[j] = whole_weight(w_up, j)
    wdn = w_dn[...].reshape(FF, D)
    xh2, rs2, n2 = norm_forward(n1 + dot(at2[...], wco, TN), gb[1:2], gb[4:5])
    low2[...] = n2.astype(BF)
    for j in range(4):
        h = dot(low2[...], wup[j])
        hid[j] = h
        act[:, j * D : (j + 1) * D] = (h / (1.0 + jnp.exp(-h))).astype(BF)
    r3 = n2 + dot(act[...], wdn)
    xh3, rs3, final = norm_forward(r3, gb[2:3], gb[5:6])
    out[...] = final.astype(BF)
    err = (final - teach[...].astype(F32)) * valid[...]
    small[...] = jnp.zeros_like(small)
    small[6:7] = jnp.sum(err * err, axis=0, keepdims=True)
    d_r3, dg, db = norm_back(err, xh3, rs3, gb[2:3])
    small[2:3] = dg
    small[5:6] = db
    dffn = d_r3.astype(BF)
    for ref, at in sides(ids, keep, send):
        g = dot(cols(act, at, FF // 4), dffn, TN).astype(BF)
        for i in range(16):
            ref[ids[PLACE_1 + i], 4:8] = g[64 * i : 64 * i + 64].reshape(4, 16, D)
    dn2 = d_r3
    for j in range(4):
        da = dot(dffn, wdn[j * D : (j + 1) * D], NT)
        h = hid[j]
        sig = 1.0 / (1.0 + jnp.exp(-h))
        dh = (da * (sig * (1.0 + h * (1.0 - sig)))).astype(BF)
        for ref, at in sides(ids, keep, send):
            put(ids, PLACE_1, ref, j, dot(cols(low2, at, 128), dh, TN))
        dn2 = dn2 + dot(dh, wup[j], NT)
    dr2, dg, db = norm_back(dn2, xh2, rs2, gb[1:2])
    small[1:2] = dg
    small[4:5] = db
    d_r2[...] = dr2
    dcross = dr2.astype(BF)
    for ref, at in sides(ids, keep, send):
        put(ids, PLACE_1, ref, 8, dot(rows_of(at2, at, 128), dcross))
    d_mix[...] = dot(dcross, wco, NT).astype(BF)


def cross_back_a(q, kv, p, rl, d_mix, dkv, dq, dqt):
    attend_back(0, q, kv, p, rl, d_mix, dkv, dqt)
    dq[...] = jnp.transpose(dqt[...]).astype(BF)


def project(near, far, dkv_a, dkv_b, wk, wv):
    out = dot(dkv_a[:, :HALF], wk[:, :HALF], NT) + dot(dkv_b[:, :HALF], wk[:, HALF:], NT)
    out = out + dot(dkv_a[:, HALF:], wv[:, :HALF], NT) + dot(dkv_b[:, HALF:], wv[:, HALF:], NT)
    half = out.shape[0] // 2
    near[...] = out[:half].astype(BF)
    far[...] = out[half:].astype(BF)


def cross_back_b(ids, ef, q, kv, p, rl, d_mix, dkv_a, dq_a, wb, norms, d_r2, low1, xh1,
                 rs1, at1, small_in, near, far, d_mix1, d_r1, small, keep, send, dkv, dqt):
    attend_back(4, q, kv, p, rl, d_mix, dkv, dqt)
    project(near, far, dkv_a, dkv, whole_weight(wb, 1), whole_weight(wb, 2))
    dq = jnp.concatenate([dq_a[...], jnp.transpose(dqt[...]).astype(BF)], 1)
    gb = norm_rows(norms)
    dn1 = d_r2[...] + dot(dq, whole_weight(wb, 3), NT)
    dr1, dg, db = norm_back(dn1, xh1[...], rs1[...], gb[0:1])
    small[...] = small_in[...]
    small[0:1] = dg
    small[3:4] = db
    d_r1[...] = dr1
    dself = dr1.astype(BF)
    for ref, at in sides(ids, keep, send):
        lhs = cols(ef, at, 128)
        for j in range(2):
            span = slice(j * HALF, (j + 1) * HALF)
            g = jnp.concatenate([dot(lhs, dkv_a[:, span], TN), dot(lhs, dkv[:, span], TN)], 1)
            put(ids, PLACE_2, ref, j, g)
        put(ids, PLACE_2, ref, 2, dot(cols(low1, at, 128), dq, TN))
        put(ids, PLACE_2, ref, 3, dot(rows_of(at1, at, 128), dself))
    d_mix1[...] = dot(dself, whole_weight(wb, 0), NT).astype(BF)


def self_back_a(rows, ids, xf, q, kv, p, rl, d_mix, dkv, dq, keep, send, dqt):
    attend_back(0, q, kv, p, rl, d_mix, dkv, dqt)
    dq[...] = jnp.transpose(dqt[...]).astype(BF)
    for ref, at in sides(ids, keep, send):
        lhs = cols(xf, at, 128)
        put_half(ids, ref, lhs, dq[...], dkv[:, :HALF], dkv[:, HALF:], lhs[:rows])


def self_back_b(rows, ids, xf, q, kv, p, rl, d_mix, dkv_a, dq_a, wa, wa_far, d_r1, near, far, d_own, keep, send, dkv, dqt):
    attend_back(4, q, kv, p, rl, d_mix, dkv, dqt)
    project(near, far, dkv_a, dkv, weight(ids, wa, wa_far, 1), weight(ids, wa, wa_far, 2))
    dq = jnp.transpose(dqt[...]).astype(BF)
    d_own[...] = d_r1[...] + dot(jnp.concatenate([dq_a[...], dq], 1), weight(ids, wa, wa_far, 0), NT)
    for ref, at in sides(ids, keep, send):
        lhs = cols(xf, at, 128)
        put_half(ids, ref, lhs, dq, dkv[:, :HALF], dkv[:, HALF:], lhs[:rows])


def tie(*values):
    return lax.optimization_barrier(values)


class Halved:
    def __init__(self, *terms):
        self.terms = list(terms)

    def total(self, terms=None):
        first, *rest = [t.astype(F32) for t in (self.terms if terms is None else terms)]
        return sum(rest, first)

    def give(self):
        half = self.terms[0].shape[0] // 2
        away = [t[half:] for t in self.terms]
        self.terms = [t[:half] for t in self.terms]
        return self.total(away).astype(BF)

    def take(self, got):
        self.terms.append(got)


class Everywhere(Halved):
    def give(self):
        self.terms = [self.total().astype(BF)]
        return self.terms[0]


def make_shards(nd, ns):
    n_dev = nd * ns
    half = ns // 2
    per = G * 16 // n_dev
    fast = nd == 4 and ns == 8

    core, y, x, zl, zh = ("dp", 1), ("dp", 2), ("seq", 1), ("seq", 2), ("seq", 4)

    def shards(inputs, encoder, teacher, dec_seg, enc_seg, dec_valid, self_in, self_out,
               cross_query, cross_in, cross_out, ffn_up, ffn_down, norm_gain, norm_bias):
        tok = inputs.shape[1]
        rows = 2 * tok
        length = dec_seg.shape[1]
        dp_at, seq_at = lax.axis_index("dp"), lax.axis_index("seq")
        dev = dp_at * ns + seq_at
        mine = seq_at // half

        def flip(bit, arrays):
            axis, b = bit
            size = nd if axis == "dp" else ns
            flat = [v.reshape(-1, D) for v in arrays]
            got = lax.ppermute(
                flat[0] if len(flat) == 1 else jnp.concatenate(flat, 0),
                axis, [(i, i ^ b) for i in range(size)],
            )
            out, start = [], 0
            for v, f in zip(arrays, flat):
                out.append(lax.slice_in_dim(got, start, start + f.shape[0]).reshape(v.shape))
                start += f.shape[0]
            return out

        def trade(bit, *groups):
            for g, got in zip(groups, flip(bit, [g.give() for g in groups])):
                g.take(got)

        def of(v, i):
            return lax.dynamic_index_in_dim(v, i, 0, keepdims=False)

        def other(v):
            return of(v, 1 - mine)

        def append(v, got):
            return jnp.concatenate([v, got], 0)

        valid_away = jnp.pad(other(dec_valid).astype(BF)[None], ((0, 15), (0, D - tok)))

        if fast:
            mats = [self_in, self_out, cross_in, cross_query, cross_out, ffn_up, ffn_down, norm_gain, norm_bias]
            wa, pack_b = call(
                pack,
                [(w, None) for w in mats] + [(dev.astype(jnp.int32)[None], SMEM)],
                [((3, 16, D), BF), ((14, 16, D), BF)],
                name="pack",
            )
            wb = lax.all_gather(pack_b, ("dp", "seq"))
            wa = wa[None]
            got_x, got_a = flip(zh, [other(inputs), wa])
            got_x, got_a, away_e = tie(got_x, got_a, other(encoder))
            xf, wa = jnp.stack([of(inputs, mine), got_x])[None], append(wa, got_a)
            got_e, got_t, got_v = flip(zh, [away_e, other(teacher), valid_away])
            got_x, got_a = flip(zl, [xf, wa])
            xf, wa = append(xf, got_x), append(wa, got_a)
            (got_a,) = flip(x, [wa])
            (got_x,) = flip(x, [xf])
            wa = append(wa, got_a)
            wa = append(wa, flip(y, [wa])[0])
            (wa_far,) = flip(core, [wa])
            ef = jnp.stack([of(encoder, mine), got_e])[None]
            got_a, ef = tie(got_a, ef)
            ef = append(ef, flip(zl, [ef])[0])
            got_x, ef = tie(got_x, ef)
            (got_e,) = flip(x, [ef])
            x_bits = e_bits = (2, 1)
        else:
            got_x, got_e, got_t, got_v = flip(
                ("seq", half), [other(inputs), other(encoder), other(teacher), valid_away]
            )
            xf, ef = jnp.stack([of(inputs, mine), got_x])[None], jnp.stack([of(encoder, mine), got_e])[None]
            x_bits = e_bits = tuple(1 << b for b in range(half.bit_length() - 1))
            for bit in x_bits:
                got_x, got_e = flip(("seq", bit), [xf, ef])
                if bit != x_bits[-1]:
                    xf, ef = append(xf, got_x), append(ef, got_e)

            def gathered(w):
                return lax.all_gather(w, ("dp", "seq"), axis=0, tiled=True)

            def grouped(w):
                return w.reshape(G, 16, w.shape[1] // D, D).transpose(0, 2, 1, 3)

            wa = grouped(gathered(self_in))
            norms = lax.dynamic_update_slice(
                jnp.zeros((16, D), BF), jnp.concatenate([norm_gain, norm_bias], 0), (0, dev * per)
            )
            all_norms = lax.psum(norms.astype(F32), ("dp", "seq")).astype(BF)
            all_norms = jnp.pad(all_norms[None], ((0, G - 1), (0, 0), (0, 0)))[:, None]
            rest = [grouped(gathered(w)) for w in (self_out, cross_in, cross_query, cross_out)]
            down = gathered(ffn_down).reshape(G, 4, 16, D)
            wb = jnp.concatenate([grouped(gathered(ffn_up)), down] + rest + [all_norms], 1)
            wa, wa_far = wa[: G // 2], wa[G // 2 :]
        x_near, x_far = xf.reshape(-1, D), got_x.reshape(-1, D)
        teach = jnp.concatenate([of(teacher, mine), got_t], 0)
        valid = jnp.concatenate([of(dec_valid, mine).astype(F32), got_v[0, :tok].astype(F32)])[:, None]

        def spread(v, bits):
            return sum((((v & b) != 0).astype(jnp.int32) << i) for i, b in enumerate(bits))

        if fast:
            i16 = jnp.arange(16, dtype=jnp.int32)
            g32 = jnp.arange(32, dtype=jnp.int32)
            dev16 = (dp_at >> 1) * 8 + seq_at
            ids = jnp.concatenate(
                [
                    (dp_at & 1).astype(jnp.int32)[None],
                    spread(i16 ^ dev16, (4, 2, 1, 8)),
                    spread(i16 ^ dev16, (4, 1, 2, 8)),
                    spread(g32 ^ dev, (4, 2, 1, 16, 8)),
                ]
            )
        else:
            i16, g32 = jnp.arange(16, dtype=jnp.int32), jnp.arange(32, dtype=jnp.int32)
            ids = jnp.concatenate([jnp.zeros((1,), jnp.int32), i16, i16, g32])

        slots = jnp.arange(half, dtype=jnp.int32)

        def pieces(bits):
            masks = sum((((slots >> i) & 1) * b) for i, b in enumerate(bits))[:, None]
            return (seq_at ^ masks ^ jnp.array([[0, half]], jnp.int32)).reshape(-1)

        pos = (pieces(x_bits)[:, None] * tok + jnp.arange(tok, dtype=jnp.int32)[None]).reshape(-1)
        dec_k = of(dec_seg, mine).reshape(ns, tok)[pieces(x_bits)].reshape(-1)
        enc_k = of(enc_seg, mine).reshape(ns, tok)[pieces(e_bits)].reshape(-1)
        dec_q = dec_k[:rows]
        ok_self = (dec_k[:, None] == dec_q[None]) & (pos[:, None] <= pos[None, :rows])
        ok_cross = enc_k[:, None] == dec_q[None]
        mask_self = jnp.where(ok_self, 0.0, NEG).astype(F32)
        mask_cross = jnp.where(ok_cross, 0.0, NEG).astype(F32)

        sm = (ids, SMEM)
        p_shape = (HEADS, length, rows)
        xf, q1, kv1, p1, rl1, at1 = call(
            functools.partial(self_forward, rows),
            [sm, (x_near, None), (x_far, None), (wa, None), (wa_far, None), (mask_self, None)],
            [((length, D), BF), ((rows, D), BF), ((length, 2 * D), BF), (p_shape, BF), ((HEADS, 1, rows), F32), ((D, rows), BF)],
            name="self_forward",
        )
        got_e, at1 = tie(got_e, at1)
        e_near, e_far = ef.reshape(-1, D), got_e.reshape(-1, D)
        ef, xh1, rs1, low1, q2, kv2, p2, rl2, at2 = call(
            functools.partial(cross_forward, rows),
            [sm, (xf, None), (e_near, None), (e_far, None), (at1, None), (wb, chunks(8, 4)), (wb, chunks(13, 1)),
             (mask_cross, None)],
            [((length, D), BF), ((rows, D), F32), ((rows, 1), F32), ((rows, D), BF), ((rows, D), BF), ((length, 2 * D), BF),
             (p_shape, BF), ((HEADS, 1, rows), F32), ((D, rows), BF)],
            name="cross_forward",
        )
        out, small, d_r2, d_mix2, keep1, send1 = call(
            ffn_both,
            [sm, (xh1, None), (at2, None), (teach, None), (valid, None), (wb, chunks(0, 4)), (wb, chunks(4, 4)),
             (wb, chunks(12, 1)), (wb, chunks(13, 1))],
            [((rows, D), BF), ((16, D), F32), ((rows, D), F32), ((rows, D), BF)] + [((16, 9, 16, D), BF)] * 2,
            scratch=[pltpu.VMEM((rows, FF), BF), pltpu.VMEM((4, rows, D), F32), pltpu.VMEM((rows, D), BF),
                     pltpu.VMEM((4, D, D), BF)],
            name="ffn_both",
        )

        kv_half = [((length, D), BF), ((rows, HALF), BF)]
        d_rows = [pltpu.VMEM((HALF, rows), F32)]
        both_scratch = [pltpu.VMEM((length, D), BF)] + d_rows
        packed = [((16, 24, D), BF)] * 2

        if fast:
            (got1,) = flip(core, [send1])
        dkv2, dq2 = call(
            cross_back_a,
            [(q2, None), (kv2, None), (p2, None), (rl2, None), (d_mix2, None)],
            kv_half,
            scratch=d_rows,
            name="cross_back_a",
        )
        if fast:
            got1, d_mix2, dkv2 = tie(got1, d_mix2, dkv2)
            group1 = Halved(keep1, got1)
            trade(y, group1)
        two_halves = [((length // 2, D), BF)] * 2
        enc_near, enc_far, d_mix1, d_r1, small, keep2, send2 = call(
            cross_back_b,
            [sm, (ef, None), (q2, None), (kv2, None), (p2, None), (rl2, None), (d_mix2, None),
             (dkv2, None), (dq2, None), (wb, chunks(8, 4)), (wb, chunks(13, 1)), (d_r2, None), (low1, None), (xh1, None), (rs1, None),
             (at1, None), (small, None)],
            two_halves + [((rows, D), BF), ((rows, D), F32), ((16, D), F32)] + [((16, 4, 16, D), BF)] * 2,
            scratch=both_scratch,
            name="cross_back_b",
        )
        lane = lax.broadcasted_iota(jnp.int32, (16, D), 1)
        row = lax.broadcasted_iota(jnp.int32, (16, D), 0)
        small = jnp.where((row == 7) & (lane == dev), jnp.sum(dec_valid).astype(F32), small)
        small = Everywhere(small)
        if fast:
            (got2,) = flip(core, [send2])
            (got_e,) = flip(x, [enc_far])
        dkv1, dq1, keep3, send3 = call(
            functools.partial(self_back_a, rows),
            [sm, (xf, None), (q1, None), (kv1, None), (p1, None), (rl1, None), (d_mix1, None)],
            kv_half + packed,
            scratch=d_rows,
            name="self_back_a",
        )
        if fast:
            (got3,) = flip(core, [send3])
            got2, got3, d_mix1, got_e, group1.terms[-1] = tie(got2, got3, d_mix1, got_e, group1.terms[-1])
            group2, group3, enc = Halved(keep2, got2), Halved(keep3, got3), Halved(enc_near, got_e)
            trade(y, group2, group3)
            trade(x, group1)
            trade(zl, enc)
        x_near, x_far, d_own, keep4, send4 = call(
            functools.partial(self_back_b, rows),
            [sm, (xf, None), (q1, None), (kv1, None), (p1, None), (rl1, None), (d_mix1, None),
             (dkv1, None), (dq1, None), (wa, None), (wa_far, None), (d_r1, None)],
            two_halves + [((rows, D), F32)] + packed,
            scratch=both_scratch,
            name="self_back_b",
        )

        def back_home(kept, recv):
            return jnp.where(mine == 0, jnp.stack([kept, recv]), jnp.stack([recv, kept]))

        def wide(g):
            return g.transpose(1, 0, 2).reshape(per, -1)

        def unpack(a, b):
            def three(g):
                v = g[..., 16:, :]
                v = jnp.concatenate([v[..., :HALF], v[..., HALF:]], -2)
                return g[..., :16, :HALF], g[..., :16, HALF:], v

            return jnp.concatenate([v for pair in zip(three(a), three(b)) for v in pair], -1)

        if fast:
            x_far, send4, group1.terms[-1] = tie(x_far, send4, group1.terms[-1])
            low_small = small.give()
            (got_x,) = flip(x, [x_far])
            got4, got_small = flip(core, [send4, low_small])
            small.take(got_small)
            group4, dx = Halved(keep4, got4), Halved(x_near, got_x)
            trade(zl, group1, group2, group3)
            trade(y, group4, small)
            dx.terms[-1], group4.terms[-1] = tie(dx.terms[-1], group4.terms[-1])
            trade(zl, dx, group4, small)
            group1.terms[-1], e_own = tie(group1.terms[-1], enc.total())
            away_1 = group1.give()
            got_1, home, home_e = flip(zh, [away_1, out[tok:], e_own[tok:].astype(BF)])
            group1.take(got_1)
            trade(x, group2, group3)
            x_own = dx.total() + d_own
            away_x = x_own[tok:].astype(BF)
            away_2, away_3 = group2.give(), group3.give()
            home_x, got_2, got_3 = flip(zh, [away_x, away_2, away_3])
            group2.take(got_2)
            group3.take(got_3)
            trade(x, group4, small)
            trade(zh, group4, small)
            s1, s2, small = group1.total()[0], group2.total()[0], small.total()
            g_up, g_down, g_co = wide(s1[:4]), s1[4:8].reshape(4 * per, D), s1[8]
            g_cin, g_cq, g_so = wide(s2[:2]), s2[2], s2[3]
            g_in = unpack(group3.total()[0], group4.total()[0])
        else:
            enc = Halved(jnp.concatenate([enc_near, enc_far], 0))
            dx = Halved(jnp.concatenate([x_near, x_far], 0))
            for bit in reversed(x_bits):
                trade(("seq", bit), enc, dx)
            e_own = enc.total()
            x_own = dx.total() + d_own
            home, home_e, home_x = flip(
                ("seq", half), [out[tok:], e_own[tok:].astype(BF), x_own[tok:].astype(BF)]
            )
            small = lax.psum(small.terms[0], ("dp", "seq"))

            def summed(g):
                return lax.psum_scatter(g, ("dp", "seq"), scatter_dimension=0, tiled=True).astype(F32)

            def rejoin(keep, send):
                g = jnp.stack([keep.reshape((2, 8) + keep.shape[1:]), send.reshape((2, 8) + keep.shape[1:])], 1)
                return g.reshape((G,) + keep.shape[1:])

            def full(g):
                return g.transpose(0, 2, 1, 3).reshape(G * 16, -1)

            all1, all2 = rejoin(keep1, send1), rejoin(keep2, send2)
            g_up = summed(full(all1[:, :4]))
            g_down = summed(all1[:, 4:8].reshape(FF, D))
            g_co = summed(full(all1[:, 8:]))
            g_cin, g_cq, g_so = summed(full(all2[:, :2])), summed(full(all2[:, 2:3])), summed(full(all2[:, 3:]))
            g_in = summed(unpack(rejoin(keep3, send3), rejoin(keep4, send4)).reshape(G * 16, -1))

        loss = jnp.sum(small[6]) / (jnp.sum(small[7]) * D)
        g_norm = lax.dynamic_slice(small, (0, dev * per), (6, per))
        outputs = back_home(out[:tok], home)
        grad_encoder = back_home(e_own[:tok], home_e.astype(F32))
        grad_inputs = back_home(x_own[:tok], home_x.astype(F32))
        return (outputs, loss, grad_inputs, grad_encoder, g_in, g_so, g_cq, g_cin, g_co, g_up, g_down,
                g_norm[:3], g_norm[3:])

    return shards


def solution(mesh):
    rows, both = P("dp", "seq", None), P(("dp", "seq"), None)
    norm = P(None, ("dp", "seq"))
    return jax.shard_map(
        make_shards(mesh.shape["dp"], mesh.shape["seq"]),
        mesh=mesh,
        in_specs=(rows, rows, rows, P("dp", None), P("dp", None), P("dp", "seq")) + (both,) * 7 + (norm, norm),
        out_specs=(rows, P(), rows, rows) + (both,) * 7 + (norm, norm),
        check_vma=False,
    )
```

time: 310 us -> 265 us (0.85)
  waiting for transfers between devices: 134 us -> 88.4 us
  local copies, waits for them, and re-layouts: 32.4 us -> 15.1 us
  other arithmetic: 20.9 us -> 30.6 us
  starting transfers between devices: 25.8 us -> 29.7 us
    ppermute x21 -> x27, waiting for transfers between devices: 127 us -> 73.9 us  [flip(): lax.ppermute(flat[0] if len(flat) == 1 else jnp.concatenate(flat, 0), axi...]
    dynamic_slice x39 -> x3, local copies, waits for them, and re-layouts: 12.2 us -> 1.02 us  [of(): return lax.dynamic_index_in_dim(v, i, 0, keepdims=False)]
    all_gather x1, waiting for transfers between devices: 7.78 us -> 14.5 us  [shards(): wb = lax.all_gather(pack_b, ('dp', 'seq'))]
    convert_element_type x18 -> x16, other arithmetic: 6.95 us -> 13 us  [give(): return self.total(away).astype(BF)]
    ppermute x21 -> x27, starting transfers between devices: 25.8 us -> 29.7 us  [flip(): lax.ppermute(flat[0] if len(flat) == 1 else jnp.concatenate(flat, 0), axi...]
    reshape x4 -> x0, local copies, waits for them, and re-layouts: 3.38 us -> none  [the longest x3 2.49 us: cut(): return w.reshape(per, w.shape[1] // D, D).transpose(1, 0, 2)]
    pallas_call x7 -> x8, Pallas kernels: 77.1 us -> 80 us  [call(): pl.pallas_call(body, grid=(1,), in_specs=[whole(a.shape) if s is None els...]
  transfers between devices with their start and end apart: 22 -> 28, of which waited for: 12 -> 16; matrix products, arithmetic and copies ran while one was open for 11% -> 13% of each run, Pallas kernels for 9% -> 20%
where the time goes in v3:
time: 265 us; the launch traced here: 262 us
  waiting for transfers between devices  88.4 us (33%)
  Pallas kernels  80 us (30%)
  other arithmetic  30.6 us (12%)
  starting transfers between devices  29.7 us (11%)
  between operations  18.1 us (7%)
  local copies, waits for them, and re-layouts  15.1 us (6%)
    pallas_call x8, Pallas kernels, call(): pl.pallas_call(body, grid=(1,), in_specs=[whole(a.shape) if s is None els...  80 us
    ppermute x27, waiting for transfers between devices, flip(): lax.ppermute(flat[0] if len(flat) == 1 else jnp.concatenate(flat, 0), axi...  73.9 us
    ppermute x27, starting transfers between devices, flip(): lax.ppermute(flat[0] if len(flat) == 1 else jnp.concatenate(flat, 0), axi...  29.7 us
    all_gather x1, waiting for transfers between devices, shards(): wb = lax.all_gather(pack_b, ('dp', 'seq'))  14.5 us
    convert_element_type x16, other arithmetic, give(): return self.total(away).astype(BF)  13 us
  transfers between devices with their start and end apart: 28, of which 16 were waited for; matrix products, arithmetic and copies ran while one was open for 13% of the time, Pallas kernels for 20%

profile of v3, /device:TPU:0, one launch (start us, length us, event | category | flops | bytes accessed | tf_op | source)
XLA Modules:
  0.0 262.0 jit_solution(11055075600055097809)
XLA Ops:
  11.0 4.1 %collective-permute-start = (bf16[176,512]{1,0:T(8,128)(2,1)S(1)}, bf16[176,512]{1,0:T(8,128)(2,1)S(1)}, u32[]{:S(2)}, u32[]{:S(2)}) collective-permute-start(bf16[176,512]{1,0:T(8,128)(2,1)S(1)} %pad_maximum_fusion.14), channel_id=1, source_target_pairs={{0,4},{1,5},{2,6},{3,7},{4,0},{5,1},{6,2},{7,3},{8,12},{9,13},{10,... | collective-permute-start | bytes 540680 | tf_op jit(solution)/shard_map/ppermute | solution.py:375
  18.5 5.0 %collective-permute-done = bf16[176,512]{1,0:T(8,128)(2,1)S(1)} collective-permute-done((bf16[176,512]{1,0:T(8,128)(2,1)S(1)}, bf16[176,512]{1,0:T(8,128)(2,1)S(1)}, u32[]{:S(2)}, u32[]{:S(2)}) %collective-permute-start) | collective-permute-done | bytes 180256 | tf_op jit(solution)/shard_map/ppermute | solution.py:375
  24.5 3.4 %collective-permute-start.4 = (bf16[272,512]{1,0:T(8,128)(2,1)S(1)}, bf16[272,512]{1,0:T(8,128)(2,1)}, u32[]{:S(2)}, u32[]{:S(2)}) collective-permute-start(bf16[272,512]{1,0:T(8,128)(2,1)S(1)} %fusion.3), channel_id=1, source_target_pairs={{0,4},{1,5},{2,6},{3,7},{4,0},{5,1},{6,2},{7,3},{8,12},{9,13},{10,... | collective-permute-start | bytes 835592 | tf_op jit(solution)/shard_map/ppermute | solution.py:375
  27.9 16.0 %collective-permute-done.1 = bf16[352,512]{1,0:T(8,128)(2,1)S(1)} collective-permute-done((bf16[352,512]{1,0:T(8,128)(2,1)S(1)}, bf16[352,512]{1,0:T(8,128)(2,1)S(1)}, u32[]{:S(2)}, u32[]{:S(2)}) %collective-permute-start.1) | collective-permute-done | bytes 360480 | tf_op jit(solution)/shard_map/ppermute | solution.py:375
  47.0 6.9 %collective-permute-done.3 = bf16[192,512]{1,0:T(8,128)(2,1)S(1)} collective-permute-done((bf16[192,512]{1,0:T(8,128)(2,1)S(1)}, bf16[192,512]{1,0:T(8,128)(2,1)S(1)}, u32[]{:S(2)}, u32[]{:S(2)}) %collective-permute-start.3) | collective-permute-done | bytes 196640 | tf_op jit(solution)/shard_map/ppermute | solution.py:375
  55.4 2.5 collective-permute-start.2
  58.1 3.7 %collective-permute-done.6 = bf16[384,512]{1,0:T(8,128)(2,1)S(1)} collective-permute-done((bf16[384,512]{1,0:T(8,128)(2,1)S(1)}, bf16[384,512]{1,0:T(8,128)(2,1)S(1)}, u32[]{:S(2)}, u32[]{:S(2)}) %collective-permute-start.6) | collective-permute-done | bytes 393248 | tf_op jit(solution)/shard_map/ppermute | solution.py:375
  61.9 4.8 %collective-permute-done.5 = bf16[256,512]{1,0:T(8,128)(2,1)S(1)} collective-permute-done((bf16[256,512]{1,0:T(8,128)(2,1)S(1)}, bf16[256,512]{1,0:T(8,128)(2,1)S(1)}, u32[]{:S(2)}, u32[]{:S(2)}) %collective-permute-start.5) | collective-permute-done | bytes 262176 | tf_op jit(solution)/shard_map/ppermute | solution.py:375
  73.8 12.0 %self_forward.1 = (bf16[1024,512]{1,0:T(8,128)(2,1)}, bf16[256,512]{1,0:T(8,128)(2,1)}, bf16[1024,1024]{1,0:T(8,128)(2,1)}, bf16[8,1024,256]{2,1,0:T(8,128)(2,1)...) custom-call(s32[65]{0:T(128)} %pad_add_fusion.ids, bf16[512,512]{1,0:T(8,128)(2,1)} %bitcast.256, ...), custom_call_target="tpu_custom_call" | custom-call | flops 1000 | bytes 1000 | tf_op jit(solution)/shard_map/self_forward/pallas_call | solution.py:50
  85.8 3.6 %collective-permute-done.8 = bf16[512,512]{1,0:T(8,128)(2,1)} collective-permute-done((bf16[512,512]{1,0:T(8,128)(2,1)S(1)}, bf16[512,512]{1,0:T(8,128)(2,1)}, u32[]{:S(2)}, u32[]{:S(2)}) %collective-permute-start.8) | collective-permute-done | bytes 524320 | tf_op jit(solution)/shard_map/ppermute | solution.py:375
  89.4 14.5 %all-gather.3.cloned.1.call-done = bf16[448,16,512]{2,1,0:T(8,128)(2,1)} async-done(((bf16[14,16,512]{2,1,0:T(8,128)(2,1)}), bf16[448,16,512]{2,1,0:T(8,128)(2,1)}) %all-gather.3.cloned.1.call-update) | async-done | bytes 7340048 | tf_op jit(solution)/shard_map/all_gather | solution.py:408
  103.9 13.6 %cross_forward.1 = (bf16[1024,512]{1,0:T(8,128)(2,1)}, f32[256,512]{1,0:T(8,128)}, f32[256,1]{1,0:T(8,128)}, bf16[256,512]{1,0:T(8,128)(2,1)}, bf16[256,512]{1,0...) custom-call(s32[65]{0:T(128)} %pad_add_fusion.ids, ...), custom_call_target="tpu_custom_call" | custom-call | flops 1000 | bytes 1000 | tf_op jit(solution)/shard_map/cross_forward/pallas_call | solution.py:50
  117.5 11.2 %ffn_both.1 = (bf16[256,512]{1,0:T(8,128)(2,1)}, f32[16,512]{1,0:T(8,128)}, f32[256,512]{1,0:T(8,128)}, bf16[256,512]{1,0:T(8,128)(2,1)}, bf16[16,9,16,512]{3,2,...) custom-call(s32[65]{0:T(128)} %pad_add_fusion.ids, f32[256,512]{1,0:T(8,128)} %get-tuple-element.89.xh1, ...), custom_call_target="tpu_custom_call" | custom-call | flops 1000 | bytes 1000 | tf_op jit(solution)/shard_map/ffn_both/pallas_call | solution.py:50
  128.9 7.8 %cross_back_a.1 = (bf16[1024,512]{1,0:T(8,128)(2,1)}, bf16[256,256]{1,0:T(8,128)(2,1)}) custom-call(bf16[256,512]{1,0:T(8,128)(2,1)} %get-tuple-element.95.q, bf16[1024,1024]{1,0:T(8,128)(2,1)} %get-tuple-element.96.kv, bf16[8,1024,256]{2,1,0:T(8,128)(2,1)} %get-tuple-element.97.p, f32[8,1,256]{2,1,0:T(1,128)} %get-tuple-element.98.rl, ...), custom_call_target="tpu_custom_call" | custom-call | flops 1000 | bytes 1000 | tf_op jit(solution)/shard_map/cross_back_a/pallas_call | solution.py:50
  139.6 13.4 %cross_back_b.1 = (bf16[512,512]{1,0:T(8,128)(2,1)}, bf16[512,512]{1,0:T(8,128)(2,1)}, bf16[256,512]{1,0:T(8,128)(2,1)}, f32[256,512]{1,0:T(8,128)}, f32[16,512]...) custom-call(s32[65]{0:T(128)} %pad_add_fusion.ids, ...), custom_call_target="tpu_custom_call" | custom-call | flops 1000 | bytes 1000 | tf_op jit(solution)/shard_map/cross_back_b/pallas_call | solution.py:50
  154.3 9.1 %self_back_a.1 = (bf16[1024,512]{1,0:T(8,128)(2,1)}, bf16[256,256]{1,0:T(8,128)(2,1)}, bf16[16,24,512]{2,1,0:T(8,128)(2,1)}, bf16[16,24,512]{2,1,0:T(8,128)(2,1)}) custom-call(s32[65]{0:T(128)} %pad_add_fusion.ids, bf16[1024,512]{1,0:T(8,128)(2,1)} %get-tuple-element.83.xf, bf16[256,512]{1,0:T(8,128)(2,1)} %get-tuple-element.110.q, ...), custom_call_target="tpu_custom_call" | custom-call | flops 1000 | bytes 1000 | tf_op jit(solution)/shard_map/self_back_a/pallas_call | solution.py:50
  171.6 2.5 collective-permute-start.17
  176.7 11.1 %self_back_b.1 = (bf16[512,512]{1,0:T(8,128)(2,1)}, bf16[512,512]{1,0:T(8,128)(2,1)}, f32[256,512]{1,0:T(8,128)}, bf16[16,24,512]{2,1,0:T(8,128)(2,1)}, bf16[16,24,512]{2,1,0:T(8,128)(2,1)}) custom-call(s32[65]{0:T(128)} %pad_add_fusion.ids, bf16[1024,512]{1,0:T(8,128)(2,1)} %get-tuple-element.83.xf, bf16[256,512]{1,0:T(8,128)(2,1)} %get-tuple-element.110.q, ...), custom_call_target="tpu_custom_call" | custom-call | flops 1000 | bytes 1000 | tf_op jit(solution)/shard_map/self_back_b/pallas_call | solution.py:50
  191.1 2.6 collective-permute-done.15
  196.9 5.5 %collective-permute-done.20 = bf16[208,512]{1,0:T(8,128)(2,1)S(1)} collective-permute-done((bf16[208,512]{1,0:T(8,128)(2,1)S(1)}, bf16[208,512]{1,0:T(8,128)(2,1)S(1)}, u32[]{:S(2)}, u32[]{:S(2)}) %collective-permute-start.20) | collective-permute-done | bytes 213024 | tf_op jit(solution)/shard_map/ppermute | solution.py:375
  204.4 9.3 %collective-permute-done.16 = bf16[640,512]{1,0:T(8,128)(2,1)S(1)} collective-permute-done((bf16[640,512]{1,0:T(8,128)(2,1)S(1)}, bf16[640,512]{1,0:T(8,128)(2,1)S(1)}, u32[]{:S(2)}, u32[]{:S(2)}) %collective-permute-start.16) | collective-permute-done | bytes 655392 | tf_op jit(solution)/shard_map/ppermute | solution.py:375
  219.2 5.6 %collective-permute-done.25 = bf16[176,512]{1,0:T(8,128)(2,1)S(1)} collective-permute-done((bf16[176,512]{1,0:T(8,128)(2,1)S(1)}, bf16[176,512]{1,0:T(8,128)(2,1)S(1)}, u32[]{:S(2)}, u32[]{:S(2)}) %collective-permute-start.25) | collective-permute-done | bytes 180256 | tf_op jit(solution)/shard_map/ppermute | solution.py:375
  227.3 3.7 %collective-permute-done.23 = bf16[64,512]{1,0:T(8,128)(2,1)S(1)} collective-permute-done((bf16[64,512]{1,0:T(8,128)(2,1)S(1)}, bf16[64,512]{1,0:T(8,128)(2,1)S(1)}, u32[]{:S(2)}, u32[]{:S(2)}) %collective-permute-start.23) | collective-permute-done | bytes 65568 | tf_op jit(solution)/shard_map/ppermute | solution.py:375
  234.8 3.6 %collective-permute-done.24 = bf16[40,512]{1,0:T(8,128)(2,1)S(1)} collective-permute-done((bf16[40,512]{1,0:T(8,128)(2,1)S(1)}, bf16[40,512]{1,0:T(8,128)(2,1)S(1)}, u32[]{:S(2)}, u32[]{:S(2)}) %collective-permute-start.24) | collective-permute-done | bytes 40992 | tf_op jit(solution)/shard_map/ppermute | solution.py:375
  (244 shorter events, 68.4 us)
Async XLA Ops:
  7.2 96.7 %all-gather.3.cloned.1.call-start = ((), (), s32[]{:S(2)}) async-start(), calls=%async_computation | async-start | bytes 7569408 | tf_op jit(solution)/shard_map/all_gather | solution.py:408
  11.0 12.5 %collective-permute-start = (bf16[176,512]{1,0:T(8,128)(2,1)S(1)}, bf16[176,512]{1,0:T(8,128)(2,1)S(1)}, u32[]{:S(2)}, u32[]{:S(2)}) collective-permute-start(bf16[176,512]{1,0:T(8,128)(2,1)S(1)} %pad_maximum_fusion.14), channel_id=1, source_target_pairs={{0,4},{1,5},{2,6},{3,7},{4,0},{5,1},{6,2},{7,3},{8,12},{9,13},{10,... | collective-permute-start | bytes 540680 | tf_op jit(solution)/shard_map/ppermute | solution.py:375
  23.6 20.3 %collective-permute-start.1 = (bf16[352,512]{1,0:T(8,128)(2,1)S(1)}, bf16[352,512]{1,0:T(8,128)(2,1)S(1)}, u32[]{:S(2)}, u32[]{:S(2)}) collective-permute-start(bf16[352,512]{1,0:T(8,128)(2,1)S(1)} %pad_maximum_fusion.8), channel_id=1, source_target_pairs={{0,2},{1,3},{2,0},{3,1},{4,6},{5,7},{6,4},{7,5},{8,10},{9,11},{10,... | collective-permute-start | bytes 1081352 | tf_op jit(solution)/shard_map/ppermute | solution.py:375
  24.5 20.9 %collective-permute-start.4 = (bf16[272,512]{1,0:T(8,128)(2,1)S(1)}, bf16[272,512]{1,0:T(8,128)(2,1)}, u32[]{:S(2)}, u32[]{:S(2)}) collective-permute-start(bf16[272,512]{1,0:T(8,128)(2,1)S(1)} %fusion.3), channel_id=1, source_target_pairs={{0,4},{1,5},{2,6},{3,7},{4,0},{5,1},{6,2},{7,3},{8,12},{9,13},{10,... | collective-permute-start | bytes 835592 | tf_op jit(solution)/shard_map/ppermute | solution.py:375
  43.9 10.0 %collective-permute-start.3 = (bf16[192,512]{1,0:T(8,128)(2,1)S(1)}, bf16[192,512]{1,0:T(8,128)(2,1)S(1)}, u32[]{:S(2)}, u32[]{:S(2)}) collective-permute-start(bf16[192,512]{1,0:T(8,128)(2,1)S(1)} %bitcast.319), channel_id=1, source_target_pairs={{0,1},{1,0},{2,3},{3,2},{4,5},{5,4},{6,7},{7,6},{8,9},{9,8},{10,11... | collective-permute-start | bytes 589832 | tf_op jit(solution)/shard_map/ppermute | solution.py:375
  54.0 7.8 %collective-permute-start.6 = (bf16[384,512]{1,0:T(8,128)(2,1)S(1)}, bf16[384,512]{1,0:T(8,128)(2,1)S(1)}, u32[]{:S(2)}, u32[]{:S(2)}) collective-permute-start(bf16[384,512]{1,0:T(8,128)(2,1)S(1)} %bitcast.301), channel_id=1, source_target_pairs={{0,16},{8,24},{16,0},{24,8},{1,17},{9,25},{17,1},{25,9},{2,18},{10... | collective-permute-start | bytes 1179656 | tf_op jit(solution)/shard_map/ppermute | solution.py:375
  55.4 12.8 %collective-permute-start.2 = (bf16[512,512]{1,0:T(8,128)(2,1)S(1)}, bf16[512,512]{1,0:T(8,128)(2,1)S(1)}, u32[]{:S(2)}, u32[]{:S(2)}) collective-permute-start(bf16[512,512]{1,0:T(8,128)(2,1)S(1)} %bitcast.255), channel_id=1, source_target_pairs={{0,1},{1,0},{2,3},{3,2},{4,5},{5,4},{6,7},{7,6},{8,9},{9,8},{10,11... | collective-permute-start | bytes 1572872 | tf_op jit(solution)/shard_map/ppermute | solution.py:375
  58.0 8.7 %collective-permute-start.5 = (bf16[256,512]{1,0:T(8,128)(2,1)S(1)}, bf16[256,512]{1,0:T(8,128)(2,1)S(1)}, u32[]{:S(2)}, u32[]{:S(2)}) collective-permute-start(bf16[256,512]{1,0:T(8,128)(2,1)S(1)} %bitcast.276), channel_id=1, source_target_pairs={{0,2},{1,3},{2,0},{3,1},{4,6},{5,7},{6,4},{7,5},{8,10},{9,11},{10,... | collective-permute-start | bytes 786440 | tf_op jit(solution)/shard_map/ppermute | solution.py:375
  61.8 11.0 %collective-permute-start.7 = (bf16[768,512]{1,0:T(8,128)(2,1)S(1)}, bf16[768,512]{1,0:T(8,128)(2,1)S(1)}, u32[]{:S(2)}, u32[]{:S(2)}) collective-permute-start(bf16[768,512]{1,0:T(8,128)(2,1)S(1)} %bitcast.246), channel_id=1, source_target_pairs={{0,8},{8,0},{16,24},{24,16},{1,9},{9,1},{17,25},{25,17},{2,10},{10... | collective-permute-start | bytes 2359304 | tf_op jit(solution)/shard_map/ppermute | solution.py:375
  68.3 21.2 %collective-permute-start.8 = (bf16[512,512]{1,0:T(8,128)(2,1)S(1)}, bf16[512,512]{1,0:T(8,128)(2,1)}, u32[]{:S(2)}, u32[]{:S(2)}) collective-permute-start(bf16[512,512]{1,0:T(8,128)(2,1)S(1)} %bitcast.257), channel_id=1, source_target_pairs={{0,1},{1,0},{2,3},{3,2},{4,5},{5,4},{6,7},{7,6},{8,9},{9,8},{10,11... | collective-permute-start | bytes 1572872 | tf_op jit(solution)/shard_map/ppermute | solution.py:375
  128.7 8.0 %collective-permute-start.9 = (bf16[2304,512]{1,0:T(8,128)(2,1)}, bf16[2304,512]{1,0:T(8,128)(2,1)S(1)}, u32[]{:S(2)}, u32[]{:S(2)}) collective-permute-start(bf16[2304,512]{1,0:T(8,128)(2,1)} %bitcast.334), channel_id=1, source_target_pairs={{0,8},{8,0},{16,24},{24,16},{1,9},{9,1},{17,25},{25,17},{2,10},{10... | collective-permute-start | bytes 7077896 | tf_op jit(solution)/shard_map/ppermute | solution.py:375
  138.1 29.6 %collective-permute-start.13 = (bf16[1152,512]{1,0:T(8,128)(2,1)S(1)}, bf16[1152,512]{1,0:T(8,128)(2,1)}, u32[]{:S(2)}, u32[]{:S(2)}) collective-permute-start(bf16[1152,512]{1,0:T(8,128)(2,1)S(1)} %bitcast.270), channel_id=1, source_target_pairs={{0,16},{8,24},{16,0},{24,8},{1,17},{9,25},{17,1},{25,9},{2,18},{10... | collective-permute-start | bytes 3538952 | tf_op jit(solution)/shard_map/ppermute | solution.py:375
  153.0 14.7 %collective-permute-start.10 = (bf16[1024,512]{1,0:T(8,128)(2,1)}, bf16[1024,512]{1,0:T(8,128)(2,1)}, u32[]{:S(2)}, u32[]{:S(2)}) collective-permute-start(bf16[1024,512]{1,0:T(8,128)(2,1)} %bitcast.335), channel_id=1, source_target_pairs={{0,8},{8,0},{16,24},{24,16},{1,9},{9,1},{17,25},{25,17},{2,10},{10... | collective-permute-start | bytes 3145736 | tf_op jit(solution)/shard_map/ppermute | solution.py:375
  153.1 14.7 %collective-permute-start.12 = (bf16[512,512]{1,0:T(8,128)(2,1)}, bf16[512,512]{1,0:T(8,128)(2,1)}, u32[]{:S(2)}, u32[]{:S(2)}) collective-permute-start(bf16[512,512]{1,0:T(8,128)(2,1)} %get-tuple-element.116), channel_id=1, source_target_pairs={{0,1},{1,0},{2,3},{3,2},{4,5},{5,4},{6,7},{7,6},{8,9},{9,8},{10,11... | collective-permute-start | bytes 1572872 | tf_op jit(solution)/shard_map/ppermute | solution.py:375
  169.4 19.5 %collective-permute-start.14 = (bf16[576,512]{1,0:T(8,128)(2,1)S(1)}, bf16[576,512]{1,0:T(8,128)(2,1)S(1)}, u32[]{:S(2)}, u32[]{:S(2)}) collective-permute-start(bf16[576,512]{1,0:T(8,128)(2,1)S(1)} %bitcast.295), channel_id=1, source_target_pairs={{0,1},{1,0},{2,3},{3,2},{4,5},{5,4},{6,7},{7,6},{8,9},{9,8},{10,11... | collective-permute-start | bytes 1769480 | tf_op jit(solution)/shard_map/ppermute | solution.py:375
  171.6 16.2 %collective-permute-start.17 = (bf16[256,512]{1,0:T(8,128)(2,1)S(1)}, bf16[256,512]{1,0:T(8,128)(2,1)S(1)}, u32[]{:S(2)}, u32[]{:S(2)}) collective-permute-start(bf16[256,512]{1,0:T(8,128)(2,1)S(1)} %add_convert_fusion.5), channel_id=1, source_target_pairs={{0,2},{1,3},{2,0},{3,1},{4,6},{5,7},{6,4},{7,5},{8,10},{9,11},{10,... | collective-permute-start | bytes 786440 | tf_op jit(solution)/shard_map/ppermute | solution.py:375
  176.5 17.2 %collective-permute-start.15 = (bf16[704,512]{1,0:T(8,128)(2,1)S(1)}, bf16[704,512]{1,0:T(8,128)(2,1)S(1)}, u32[]{:S(2)}, u32[]{:S(2)}) collective-permute-start(bf16[704,512]{1,0:T(8,128)(2,1)S(1)} %pad_maximum_fusion), channel_id=1, source_target_pairs={{0,16},{8,24},{16,0},{24,8},{1,17},{9,25},{17,1},{25,9},{2,18},{10... | collective-permute-start | bytes 2162696 | tf_op jit(solution)/shard_map/ppermute | solution.py:375
  189.0 7.3 %collective-permute-start.19 = (bf16[400,512]{1,0:T(8,128)(2,1)S(1)}, bf16[400,512]{1,0:T(8,128)(2,1)S(1)}, u32[]{:S(2)}, u32[]{:S(2)}) collective-permute-start(bf16[400,512]{1,0:T(8,128)(2,1)S(1)} %pad_maximum_fusion.5), channel_id=1, source_target_pairs={{0,8},{8,0},{16,24},{24,16},{1,9},{9,1},{17,25},{25,17},{2,10},{10... | collective-permute-start | bytes 1228808 | tf_op jit(solution)/shard_map/ppermute | solution.py:375
  189.1 14.3 %collective-permute-start.21 = (bf16[512,512]{1,0:T(8,128)(2,1)S(1)}, bf16[512,512]{1,0:T(8,128)(2,1)S(1)}, u32[]{:S(2)}, u32[]{:S(2)}) collective-permute-start(bf16[512,512]{1,0:T(8,128)(2,1)S(1)} %copy-done.32), channel_id=1, source_target_pairs={{0,1},{1,0},{2,3},{3,2},{4,5},{5,4},{6,7},{7,6},{8,9},{9,8},{10,11... | collective-permute-start | bytes 1572872 | tf_op jit(solution)/shard_map/ppermute | solution.py:375
  196.0 17.7 %collective-permute-start.16 = (bf16[640,512]{1,0:T(8,128)(2,1)S(1)}, bf16[640,512]{1,0:T(8,128)(2,1)S(1)}, u32[]{:S(2)}, u32[]{:S(2)}) collective-permute-start(bf16[640,512]{1,0:T(8,128)(2,1)S(1)} %pad_maximum_fusion.1), channel_id=1, source_target_pairs={{0,2},{1,3},{2,0},{3,1},{4,6},{5,7},{6,4},{7,5},{8,10},{9,11},{10,... | collective-permute-start | bytes 1966088 | tf_op jit(solution)/shard_map/ppermute | solution.py:375
  203.6 22.9 %collective-permute-start.22 = (bf16[368,512]{1,0:T(8,128)(2,1)S(1)}, bf16[368,512]{1,0:T(8,128)(2,1)S(1)}, u32[]{:S(2)}, u32[]{:S(2)}) collective-permute-start(bf16[368,512]{1,0:T(8,128)(2,1)S(1)} %pad_maximum_fusion.7), channel_id=1, source_target_pairs={{0,2},{1,3},{2,0},{3,1},{4,6},{5,7},{6,4},{7,5},{8,10},{9,11},{10,... | collective-permute-start | bytes 1130504 | tf_op jit(solution)/shard_map/ppermute | solution.py:375
  215.9 25.0 %collective-permute-start.18 = (bf16[400,512]{1,0:T(8,128)(2,1)}, bf16[400,512]{1,0:T(8,128)(2,1)}, u32[]{:S(2)}, u32[]{:S(2)}) collective-permute-start(bf16[400,512]{1,0:T(8,128)(2,1)} %pad_maximum_fusion.4), channel_id=1, source_target_pairs={{0,4},{1,5},{2,6},{3,7},{4,0},{5,1},{6,2},{7,3},{8,12},{9,13},{10,... | collective-permute-start | bytes 1228808 | tf_op jit(solution)/shard_map/ppermute | solution.py:375
  231.1 7.3 %collective-permute-start.24 = (bf16[40,512]{1,0:T(8,128)(2,1)S(1)}, bf16[40,512]{1,0:T(8,128)(2,1)S(1)}, u32[]{:S(2)}, u32[]{:S(2)}) collective-permute-start(bf16[40,512]{1,0:T(8,128)(2,1)S(1)} %pad_maximum_fusion.18), channel_id=1, source_target_pairs={{0,4},{1,5},{2,6},{3,7},{4,0},{5,1},{6,2},{7,3},{8,12},{9,13},{10,... | collective-permute-start | bytes 122888 | tf_op jit(solution)/shard_map/ppermute | solution.py:375
  233.8 13.8 %collective-permute-start.26 = (bf16[216,512]{1,0:T(8,128)(2,1)}, bf16[216,512]{1,0:T(8,128)(2,1)}, u32[]{:S(2)}, u32[]{:S(2)}) collective-permute-start(bf16[216,512]{1,0:T(8,128)(2,1)} %pad_maximum_fusion.11), channel_id=1, source_target_pairs={{0,4},{1,5},{2,6},{3,7},{4,0},{5,1},{6,2},{7,3},{8,12},{9,13},{10,... | collective-permute-start | bytes 663560 | tf_op jit(solution)/shard_map/ppermute | solution.py:375
  (40 other events, 273.3 us)
Sparse Core Ops, SparseCore 0:
  11.0 92.9 all-gather.2

commit v4 on v3

--- a/solution.py
+++ b/solution.py
@@ -20,7 +20,7 @@
 F32 = jnp.float32
 MIB = 1 << 20
 
-PLACE_1, PLACE_2, SLOT = 1, 17, 33
+DEVICE, PLACE_1, PLACE_2, SLOT = 1, 2, 18, 34
 
 NN = (((1,), (0,)), ((), ()))
 NT = (((1,), (1,)), ((), ()))
@@ -46,7 +46,7 @@
     return ref[:, j].reshape(D, D)
 
 
-def call(body, ins, outs, scratch=(), name=None):
+def call(body, ins, outs, scratch=(), name=None, vmem=16):
     return pl.pallas_call(
         body,
         grid=(1,),
@@ -54,7 +54,7 @@
         out_specs=[whole(s) for s, _ in outs],
         out_shape=[jax.ShapeDtypeStruct(s, t) for s, t in outs],
         scratch_shapes=list(scratch),
-        compiler_params=pltpu.CompilerParams(vmem_limit_bytes=56 * MIB),
+        compiler_params=pltpu.CompilerParams(vmem_limit_bytes=vmem * MIB),
         name=name,
         cost_estimate=pl.CostEstimate(flops=1000, bytes_accessed=1000, transcendentals=0),
     )(*[a for a, _ in ins])
@@ -73,10 +73,12 @@
     return jnp.sum(ref[:, 0].astype(F32), axis=0)
 
 
-def put(ids, first, ref, j, value):
+def put(ids, first, ref, chunks_each, j, value):
     value = value.astype(BF)
+    each = value.shape[0] // 16
     for i in range(16):
-        ref[ids[first + i], j] = value[16 * i : 16 * i + 16]
+        at = ids[first + i] * (16 * chunks_each) + 16 * j
+        ref[pl.ds(pl.multiple_of(at, 16), each), :] = value[each * i : each * i + each]
 
 
 def norm_forward(resid, gain, bias):
@@ -162,15 +164,6 @@
     return jnp.concatenate(picks, 0)
 
 
-def put_half(ids, ref, lhs, dq, dk, dv, lhs_q):
-    qk = jnp.concatenate([dot(lhs_q, dq, TN), dot(lhs, dk, TN)], 1).astype(BF)
-    v = dot(lhs, dv, TN)
-    for i in range(16):
-        at = ids[PLACE_2 + i]
-        ref[at, 0:16] = qk[16 * i : 16 * i + 16]
-        ref[at, 16:24] = jnp.concatenate([v[16 * i : 16 * i + 8], v[16 * i + 8 : 16 * i + 16]], 1).astype(BF)
-
-
 def sides(ids, keep, send):
     return ((send, 1 - ids[0]), (keep, ids[0]))
 
@@ -241,14 +234,14 @@
     err = (final - teach[...].astype(F32)) * valid[...]
     small[...] = jnp.zeros_like(small)
     small[6:7] = jnp.sum(err * err, axis=0, keepdims=True)
+    lane = lax.broadcasted_iota(jnp.int32, (1, D), 1)
+    small[7:8] = jnp.where(lane == ids[DEVICE], jnp.sum(valid[...]), 0.0)
     d_r3, dg, db = norm_back(err, xh3, rs3, gb[2:3])
     small[2:3] = dg
     small[5:6] = db
     dffn = d_r3.astype(BF)
     for ref, at in sides(ids, keep, send):
-        g = dot(cols(act, at, FF // 4), dffn, TN).astype(BF)
-        for i in range(16):
-            ref[ids[PLACE_1 + i], 4:8] = g[64 * i : 64 * i + 64].reshape(4, 16, D)
+        put(ids, PLACE_1, ref, 9, 4, dot(cols(act, at, FF // 4), dffn, TN))
     dn2 = d_r3
     for j in range(4):
         da = dot(dffn, wdn[j * D : (j + 1) * D], NT)
@@ -256,7 +249,7 @@
         sig = 1.0 / (1.0 + jnp.exp(-h))
         dh = (da * (sig * (1.0 + h * (1.0 - sig)))).astype(BF)
         for ref, at in sides(ids, keep, send):
-            put(ids, PLACE_1, ref, j, dot(cols(low2, at, 128), dh, TN))
+            put(ids, PLACE_1, ref, 9, j, dot(cols(low2, at, 128), dh, TN))
         dn2 = dn2 + dot(dh, wup[j], NT)
     dr2, dg, db = norm_back(dn2, xh2, rs2, gb[1:2])
     small[1:2] = dg
@@ -264,7 +257,7 @@
     d_r2[...] = dr2
     dcross = dr2.astype(BF)
     for ref, at in sides(ids, keep, send):
-        put(ids, PLACE_1, ref, 8, dot(rows_of(at2, at, 128), dcross))
+        put(ids, PLACE_1, ref, 9, 8, dot(rows_of(at2, at, 128), dcross))
     d_mix[...] = dot(dcross, wco, NT).astype(BF)
 
 
@@ -273,25 +266,27 @@
     dq[...] = jnp.transpose(dqt[...]).astype(BF)
 
 
-def project(near, far, dkv_a, dkv_b, wk, wv):
+def project(own, parts, dkv_a, dkv_b, wk, wv, extra=0.0):
     out = dot(dkv_a[:, :HALF], wk[:, :HALF], NT) + dot(dkv_b[:, :HALF], wk[:, HALF:], NT)
     out = out + dot(dkv_a[:, HALF:], wv[:, :HALF], NT) + dot(dkv_b[:, HALF:], wv[:, HALF:], NT)
-    half = out.shape[0] // 2
-    near[...] = out[:half].astype(BF)
-    far[...] = out[half:].astype(BF)
-
-
-def cross_back_b(ids, ef, q, kv, p, rl, d_mix, dkv_a, dq_a, wb, norms, d_r2, low1, xh1,
-                 rs1, at1, small_in, near, far, d_mix1, d_r1, small, keep, send, dkv, dqt):
+    each = own.shape[0]
+    own[...] = out[:each] + extra
+    for i, part in enumerate(parts):
+        part[...] = out[each * (i + 1) : each * (i + 2)].astype(BF)
+
+
+def cross_back_b(n_parts, ids, ef, q, kv, p, rl, d_mix, dkv_a, dq_a, wb, norms, d_r2, low1, xh1,
+                 rs1, at1, small, own, *rest):
+    parts, (d_mix1, d_r1, keep, send, dkv, dqt) = rest[:n_parts], rest[n_parts:]
     attend_back(4, q, kv, p, rl, d_mix, dkv, dqt)
-    project(near, far, dkv_a, dkv, whole_weight(wb, 1), whole_weight(wb, 2))
+    project(own, parts, dkv_a, dkv, whole_weight(wb, 1), whole_weight(wb, 2))
     dq = jnp.concatenate([dq_a[...], jnp.transpose(dqt[...]).astype(BF)], 1)
     gb = norm_rows(norms)
     dn1 = d_r2[...] + dot(dq, whole_weight(wb, 3), NT)
     dr1, dg, db = norm_back(dn1, xh1[...], rs1[...], gb[0:1])
-    small[...] = small_in[...]
-    small[0:1] = dg
-    small[3:4] = db
+    row = lax.broadcasted_iota(jnp.int32, (16, D), 0)
+    sums = jnp.where(row == 0, dg, jnp.where(row == 3, db, small[...]))
+    send[1024:1040] = sums.astype(BF)
     d_r1[...] = dr1
     dself = dr1.astype(BF)
     for ref, at in sides(ids, keep, send):
@@ -299,56 +294,110 @@
         for j in range(2):
             span = slice(j * HALF, (j + 1) * HALF)
             g = jnp.concatenate([dot(lhs, dkv_a[:, span], TN), dot(lhs, dkv[:, span], TN)], 1)
-            put(ids, PLACE_2, ref, j, g)
-        put(ids, PLACE_2, ref, 2, dot(cols(low1, at, 128), dq, TN))
-        put(ids, PLACE_2, ref, 3, dot(rows_of(at1, at, 128), dself))
+            put(ids, PLACE_2, ref, 4, j, g)
+        put(ids, PLACE_2, ref, 4, 2, dot(cols(low1, at, 128), dq, TN))
+        put(ids, PLACE_2, ref, 4, 3, dot(rows_of(at1, at, 128), dself))
     d_mix1[...] = dot(dself, whole_weight(wb, 0), NT).astype(BF)
 
 
-def self_back_a(rows, ids, xf, q, kv, p, rl, d_mix, dkv, dq, keep, send, dqt):
-    attend_back(0, q, kv, p, rl, d_mix, dkv, dqt)
-    dq[...] = jnp.transpose(dqt[...]).astype(BF)
+def self_back_b(n_parts, rows, ids, xf, q, kv, p, rl, d_mix, dkv_a, dq_a, wa, wa_far, d_r1, own, *rest):
+    parts, (keep, send, dkv, dqt) = rest[:n_parts], rest[n_parts:]
+    attend_back(4, q, kv, p, rl, d_mix, dkv, dqt)
+    dq = jnp.concatenate([dq_a[...], jnp.transpose(dqt[...]).astype(BF)], 1)
+    through_q = d_r1[...] + dot(dq, weight(ids, wa, wa_far, 0), NT)
+    project(own, parts, dkv_a, dkv, weight(ids, wa, wa_far, 1), weight(ids, wa, wa_far, 2), through_q)
     for ref, at in sides(ids, keep, send):
         lhs = cols(xf, at, 128)
-        put_half(ids, ref, lhs, dq[...], dkv[:, :HALF], dkv[:, HALF:], lhs[:rows])
-
-
-def self_back_b(rows, ids, xf, q, kv, p, rl, d_mix, dkv_a, dq_a, wa, wa_far, d_r1, near, far, d_own, keep, send, dkv, dqt):
-    attend_back(4, q, kv, p, rl, d_mix, dkv, dqt)
-    project(near, far, dkv_a, dkv, weight(ids, wa, wa_far, 1), weight(ids, wa, wa_far, 2))
-    dq = jnp.transpose(dqt[...]).astype(BF)
-    d_own[...] = d_r1[...] + dot(jnp.concatenate([dq_a[...], dq], 1), weight(ids, wa, wa_far, 0), NT)
-    for ref, at in sides(ids, keep, send):
-        lhs = cols(xf, at, 128)
-        put_half(ids, ref, lhs, dq, dkv[:, :HALF], dkv[:, HALF:], lhs[:rows])
+        put(ids, PLACE_2, ref, 3, 0, dot(lhs[:rows], dq, TN))
+        for j in range(2):
+            span = slice(j * HALF, (j + 1) * HALF)
+            g = jnp.concatenate([dot(lhs, dkv_a[:, span], TN), dot(lhs, dkv[:, span], TN)], 1)
+            put(ids, PLACE_2, ref, 3, 1 + j, g)
+
+
+def tree_sum(terms):
+    while len(terms) > 1:
+        terms = [a + b for a, b in zip(terms[::2], terms[1::2])] + terms[len(terms) & ~1 :]
+    return terms[0]
+
+
+ANY = pl.BlockSpec(memory_space=pl.ANY)
+
+
+def fetch(ref, start, count, to, sem):
+    copy = pltpu.make_async_copy(ref.at[pl.ds(start, count)], to, sem)
+    copy.start()
+    return copy
+
+
+def mix(name, *outs):
+    arrays, terms, plan = [], [], []
+    for dtype, segments in outs:
+        plan.append([])
+        for segment in segments:
+            used = []
+            for array, start, count in segment:
+                at = [i for i, v in enumerate(arrays) if v is array]
+                if not at:
+                    arrays.append(array)
+                used.append(len(terms))
+                terms.append((at[0] if at else len(arrays) - 1, start, count, array.dtype))
+            plan[-1].append(used)
+
+    def body(*refs):
+        for out, segments in zip(refs[len(arrays) :], plan):
+            first = 0
+            for used in segments:
+                count = terms[used[0]][2]
+                parts = [refs[k][start : start + count].astype(F32) for k, start, _, _ in (terms[i] for i in used)]
+                out[first : first + count] = tree_sum(parts).astype(out.dtype)
+                first += count
+
+    shapes = [((sum(t[0][2] for t in segments), D), dtype) for dtype, segments in outs]
+    return call(body, [(v, None) for v in arrays], shapes, name=name)
+
+
+def finish(counts, *refs):
+    where, refs = refs[0], refs[1:]
+    sources, results = refs[: len(counts)], refs[len(counts) :]
+    refs = [ref.at[:count] for ref, count in zip(sources, counts)]
+    one, (out, home, e_keep, x_keep, home_x, z_own, z_got, *refs) = refs[:6], refs[6:]
+    two, three = refs[:6], refs[6:]
+    outputs, loss, g_x, g_e, g_in, g_so, g_cq, g_cin, g_co, g_up, g_down, g_gain, g_bias = results
+    mine = where[0]
+    tok = e_keep.shape[0]
+    outputs[mine] = out[...]
+    outputs[1 - mine] = home[:tok]
+    g_e[mine] = e_keep[...]
+    g_e[1 - mine] = home[tok : 2 * tok].astype(F32)
+    g_x[mine] = x_keep[...]
+    g_x[1 - mine] = home_x[...].astype(F32)
+    t1 = tree_sum([r[...].astype(F32) for r in one] + [home[2 * tok :].astype(F32)])
+    for j in range(4):
+        g_up[:, j * D : (j + 1) * D] = t1[16 * j : 16 * j + 16]
+    g_down[...] = t1[64:128]
+    g_co[...] = t1[128:144]
+    t2 = tree_sum([r[...].astype(F32) for r in two[:3]] + [r[:64].astype(F32) for r in two[3:]] + [z_got[:64].astype(F32)])
+    for j in range(2):
+        g_cin[:, j * D : (j + 1) * D] = t2[16 * j : 16 * j + 16]
+    g_cq[...] = t2[32:48]
+    g_so[...] = t2[48:64]
+    t3 = tree_sum([r[...].astype(F32) for r in three] + [r[128:176].astype(F32) for r in two[3:]] + [z_got[64:112].astype(F32)])
+    for j in range(3):
+        g_in[:, j * D : (j + 1) * D] = t3[16 * j : 16 * j + 16]
+    small = z_own[112:128].astype(F32) + z_got[112:128].astype(F32)
+    total = jnp.sum(small[6:7], axis=1, keepdims=True)
+    loss[...] = total / (jnp.sum(small[7:8], axis=1, keepdims=True) * D)
+    column = lax.broadcasted_iota(jnp.int32, (16, D), 1)
+    row = lax.broadcasted_iota(jnp.int32, (16, D), 0)
+    pick = (column == where[1] * 16 + row).astype(F32)
+    own = lax.dot_general(small[:8], pick, NT, precision=lax.Precision.HIGHEST, preferred_element_type=F32)
+    g_gain[...] = own[0:3]
+    g_bias[...] = own[3:6]
 
 
 def tie(*values):
     return lax.optimization_barrier(values)
-
-
-class Halved:
-    def __init__(self, *terms):
-        self.terms = list(terms)
-
-    def total(self, terms=None):
-        first, *rest = [t.astype(F32) for t in (self.terms if terms is None else terms)]
-        return sum(rest, first)
-
-    def give(self):
-        half = self.terms[0].shape[0] // 2
-        away = [t[half:] for t in self.terms]
-        self.terms = [t[:half] for t in self.terms]
-        return self.total(away).astype(BF)
-
-    def take(self, got):
-        self.terms.append(got)
-
-
-class Everywhere(Halved):
-    def give(self):
-        self.terms = [self.total().astype(BF)]
-        return self.terms[0]
 
 
 def make_shards(nd, ns):
@@ -356,6 +405,7 @@
     half = ns // 2
     per = G * 16 // n_dev
     fast = nd == 4 and ns == 8
+    run = functools.partial(call, vmem=16 if fast else 44)
 
     core, y, x, zl, zh = ("dp", 1), ("dp", 2), ("seq", 1), ("seq", 2), ("seq", 4)
 
@@ -382,9 +432,8 @@
                 start += f.shape[0]
             return out
 
-        def trade(bit, *groups):
-            for g, got in zip(groups, flip(bit, [g.give() for g in groups])):
-                g.take(got)
+        def swap(bit, array):
+            return flip(bit, [array])[0]
 
         def of(v, i):
             return lax.dynamic_index_in_dim(v, i, 0, keepdims=False)
@@ -399,11 +448,12 @@
 
         if fast:
             mats = [self_in, self_out, cross_in, cross_query, cross_out, ffn_up, ffn_down, norm_gain, norm_bias]
-            wa, pack_b = call(
+            wa, pack_b = run(
                 pack,
                 [(w, None) for w in mats] + [(dev.astype(jnp.int32)[None], SMEM)],
                 [((3, 16, D), BF), ((14, 16, D), BF)],
                 name="pack",
+                vmem=56,
             )
             wb = lax.all_gather(pack_b, ("dp", "seq"))
             wa = wa[None]
@@ -464,15 +514,15 @@
             dev16 = (dp_at >> 1) * 8 + seq_at
             ids = jnp.concatenate(
                 [
-                    (dp_at & 1).astype(jnp.int32)[None],
+                    jnp.stack([dp_at & 1, dev]).astype(jnp.int32),
                     spread(i16 ^ dev16, (4, 2, 1, 8)),
-                    spread(i16 ^ dev16, (4, 1, 2, 8)),
+                    spread(i16 ^ dev16, (4, 2, 1, 8)),
                     spread(g32 ^ dev, (4, 2, 1, 16, 8)),
                 ]
             )
         else:
             i16, g32 = jnp.arange(16, dtype=jnp.int32), jnp.arange(32, dtype=jnp.int32)
-            ids = jnp.concatenate([jnp.zeros((1,), jnp.int32), i16, i16, g32])
+            ids = jnp.concatenate([jnp.stack([0 * dev, dev]).astype(jnp.int32), i16, i16, g32])
 
         slots = jnp.arange(half, dtype=jnp.int32)
 
@@ -491,7 +541,7 @@
 
         sm = (ids, SMEM)
         p_shape = (HEADS, length, rows)
-        xf, q1, kv1, p1, rl1, at1 = call(
+        xf, q1, kv1, p1, rl1, at1 = run(
             functools.partial(self_forward, rows),
             [sm, (x_near, None), (x_far, None), (wa, None), (wa_far, None), (mask_self, None)],
             [((length, D), BF), ((rows, D), BF), ((length, 2 * D), BF), (p_shape, BF), ((HEADS, 1, rows), F32), ((D, rows), BF)],
@@ -499,7 +549,7 @@
         )
         got_e, at1 = tie(got_e, at1)
         e_near, e_far = ef.reshape(-1, D), got_e.reshape(-1, D)
-        ef, xh1, rs1, low1, q2, kv2, p2, rl2, at2 = call(
+        ef, xh1, rs1, low1, q2, kv2, p2, rl2, at2 = run(
             functools.partial(cross_forward, rows),
             [sm, (xf, None), (e_near, None), (e_far, None), (at1, None), (wb, chunks(8, 4)), (wb, chunks(13, 1)),
              (mask_cross, None)],
@@ -507,11 +557,11 @@
              (p_shape, BF), ((HEADS, 1, rows), F32), ((D, rows), BF)],
             name="cross_forward",
         )
-        out, small, d_r2, d_mix2, keep1, send1 = call(
+        out, small, d_r2, d_mix2, keep1, send1 = run(
             ffn_both,
             [sm, (xh1, None), (at2, None), (teach, None), (valid, None), (wb, chunks(0, 4)), (wb, chunks(4, 4)),
              (wb, chunks(12, 1)), (wb, chunks(13, 1))],
-            [((rows, D), BF), ((16, D), F32), ((rows, D), F32), ((rows, D), BF)] + [((16, 9, 16, D), BF)] * 2,
+            [((rows, D), BF), ((16, D), F32), ((rows, D), F32), ((rows, D), BF)] + [((2304, D), BF)] * 2,
             scratch=[pltpu.VMEM((rows, FF), BF), pltpu.VMEM((4, rows, D), F32), pltpu.VMEM((rows, D), BF),
                      pltpu.VMEM((4, D, D), BF)],
             name="ffn_both",
@@ -520,11 +570,12 @@
         kv_half = [((length, D), BF), ((rows, HALF), BF)]
         d_rows = [pltpu.VMEM((HALF, rows), F32)]
         both_scratch = [pltpu.VMEM((length, D), BF)] + d_rows
-        packed = [((16, 24, D), BF)] * 2
-
-        if fast:
-            (got1,) = flip(core, [send1])
-        dkv2, dq2 = call(
+        row_parts = [((rows, D), F32)] + [((rows, D), BF)] * (half - 1)
+        partners = [sum(((i >> k) & 1) * b for k, b in enumerate(x_bits)) for i in range(1, half)]
+
+        if fast:
+            got1 = swap(core, send1)
+        dkv2, dq2 = run(
             cross_back_a,
             [(q2, None), (kv2, None), (p2, None), (rl2, None), (d_mix2, None)],
             kv_half,
@@ -533,126 +584,132 @@
         )
         if fast:
             got1, d_mix2, dkv2 = tie(got1, d_mix2, dkv2)
-            group1 = Halved(keep1, got1)
-            trade(y, group1)
-        two_halves = [((length // 2, D), BF)] * 2
-        enc_near, enc_far, d_mix1, d_r1, small, keep2, send2 = call(
-            cross_back_b,
+            got_y1 = swap(y, (keep1[1152:].astype(F32) + got1[1152:].astype(F32)).astype(BF))
+        e_own, *rest = run(
+            functools.partial(cross_back_b, half - 1),
             [sm, (ef, None), (q2, None), (kv2, None), (p2, None), (rl2, None), (d_mix2, None),
-             (dkv2, None), (dq2, None), (wb, chunks(8, 4)), (wb, chunks(13, 1)), (d_r2, None), (low1, None), (xh1, None), (rs1, None),
-             (at1, None), (small, None)],
-            two_halves + [((rows, D), BF), ((rows, D), F32), ((16, D), F32)] + [((16, 4, 16, D), BF)] * 2,
+             (dkv2, None), (dq2, None), (wb, chunks(8, 4)), (wb, chunks(13, 1)), (d_r2, None), (low1, None),
+             (xh1, None), (rs1, None), (at1, None), (small, None)],
+            row_parts + [((rows, D), BF), ((rows, D), F32), ((1024, D), BF), ((1040, D), BF)],
             scratch=both_scratch,
             name="cross_back_b",
         )
-        lane = lax.broadcasted_iota(jnp.int32, (16, D), 1)
-        row = lax.broadcasted_iota(jnp.int32, (16, D), 0)
-        small = jnp.where((row == 7) & (lane == dev), jnp.sum(dec_valid).astype(F32), small)
-        small = Everywhere(small)
-        if fast:
-            (got2,) = flip(core, [send2])
-            (got_e,) = flip(x, [enc_far])
-        dkv1, dq1, keep3, send3 = call(
-            functools.partial(self_back_a, rows),
-            [sm, (xf, None), (q1, None), (kv1, None), (p1, None), (rl1, None), (d_mix1, None)],
-            kv_half + packed,
+        e_parts, (d_mix1, d_r1, keep2, send2) = rest[: half - 1], rest[half - 1 :]
+        if fast:
+            got2 = swap(core, send2)
+        e_got = [swap(("seq", m), part) for m, part in zip(partners, e_parts)]
+        dkv1, dq1 = run(
+            cross_back_a,
+            [(q1, None), (kv1, None), (p1, None), (rl1, None), (d_mix1, None)],
+            kv_half,
             scratch=d_rows,
             name="self_back_a",
         )
         if fast:
-            (got3,) = flip(core, [send3])
-            got2, got3, d_mix1, got_e, group1.terms[-1] = tie(got2, got3, d_mix1, got_e, group1.terms[-1])
-            group2, group3, enc = Halved(keep2, got2), Halved(keep3, got3), Halved(enc_near, got_e)
-            trade(y, group2, group3)
-            trade(x, group1)
-            trade(zl, enc)
-        x_near, x_far, d_own, keep4, send4 = call(
-            functools.partial(self_back_b, rows),
+            got2, got_y1, d_mix1, dkv1, *e_got = tie(got2, got_y1, d_mix1, dkv1, *e_got)
+            one = lambda start, count: [(v, start, count) for v in (keep1, got1, got_y1)]
+            away, *quads1 = mix(
+                "sum_y2",
+                (BF, [[(keep2, 512, 512), (got2, 512, 512)], [(send2, 1024, 16), (got2, 1024, 16)]]),
+                *[(BF, [one(288 * i, 288)]) for i in (1, 2, 3)],
+            )
+            got_y2 = swap(y, away)
+            small_y2 = (away, 512, 16)
+            q1_got = [swap(("seq", m), part) for m, part in zip(partners, quads1)]
+        x_own, *rest = run(
+            functools.partial(self_back_b, half - 1, rows),
             [sm, (xf, None), (q1, None), (kv1, None), (p1, None), (rl1, None), (d_mix1, None),
              (dkv1, None), (dq1, None), (wa, None), (wa_far, None), (d_r1, None)],
-            two_halves + [((rows, D), F32)] + packed,
+            row_parts + [((768, D), BF)] * 2,
             scratch=both_scratch,
             name="self_back_b",
         )
+        x_parts, (keep3, send3) = rest[: half - 1], rest[half - 1 :]
+
+        def summed_rows(name, own, got, *more):
+            terms = [own] + got
+            return mix(name, (F32, [[(t, 0, tok) for t in terms]]),
+                       (BF, [*more[:1], [(t, tok, tok) for t in terms], *more[1:]]))
+
+        if fast:
+            q1_got[0], q1_got[1], q1_got[2], got_y2, send3, *x_parts = tie(*q1_got, got_y2, send3, *x_parts)
+        x_got = [swap(("seq", m), part) for m, part in zip(partners, x_parts)]
+        if fast:
+            got3 = swap(core, send3)
+        more = [one(144, 144) + [(v, 144, 144) for v in q1_got]] if fast else []
+        e_keep, away = summed_rows("sum_e", e_own, e_got, [(out, tok, tok)], *more)
+        home = swap(("seq", half), away)
+        if fast:
+            (away,) = mix("sum_y3", (BF, [[(keep3, 384, 384), (got3, 384, 384)]]))
+            got_y3 = swap(y, away)
+        x_keep, away = summed_rows("sum_x", x_own, x_got)
+        home_x = swap(("seq", half), away)
+
+        if fast:
+            def two(start, count):
+                return [(v, start, count) for v in (keep2, got2, got_y2)]
+
+            def three(start, count):
+                return [(v, start, count) for v in (keep3, got3, got_y3)]
+
+            quads = mix(
+                "sum_quads",
+                *[(BF, [two(128 * i, 128), three(96 * i, 96), [small_y2, (got_y2, 512, 16)]]) for i in (1, 2, 3)],
+            )
+            q_got = [swap(("seq", m), part) for m, part in zip(partners, quads)]
+            (away,) = mix(
+                "sum_zh",
+                (BF, [two(64, 64) + [(v, 64, 64) for v in q_got], three(48, 48) + [(v, 176, 48) for v in q_got],
+                      [(quads[0], 224, 16)] + [(v, 224, 16) for v in q_got]]),
+            )
+            got_z = swap(zh, away)
+            where = jnp.stack([mine, dev]).astype(jnp.int32)
+
+            last = [(v, 144) for v in (keep1, got1, got_y1, *q1_got)] + [(out, tok)]
+            last += [(v, v.shape[0]) for v in (home, e_keep, x_keep, home_x, away, got_z)]
+            last += [(v, 64) for v in (keep2, got2, got_y2)] + [(v, v.shape[0]) for v in q_got]
+            last += [(v, 48) for v in (keep3, got3, got_y3)]
+            counts = [c for _, c in last]
+            flat = [((per, w), F32) for w in (3 * D, D, D, 2 * D, D, FF)] + [((4 * per, D), F32)]
+            done = run(
+                functools.partial(finish, counts),
+                [(where, SMEM)] + [(v, None) for v, _ in last],
+                [((2, tok, D), BF), ((1, 1), F32), ((2, tok, D), F32), ((2, tok, D), F32)] + flat + [((3, per), F32)] * 2,
+                name="finish",
+            )
+            return (done[0], done[1].reshape(()), *done[2:])
 
         def back_home(kept, recv):
             return jnp.where(mine == 0, jnp.stack([kept, recv]), jnp.stack([recv, kept]))
 
-        def wide(g):
-            return g.transpose(1, 0, 2).reshape(per, -1)
-
-        def unpack(a, b):
-            def three(g):
-                v = g[..., 16:, :]
-                v = jnp.concatenate([v[..., :HALF], v[..., HALF:]], -2)
-                return g[..., :16, :HALF], g[..., :16, HALF:], v
-
-            return jnp.concatenate([v for pair in zip(three(a), three(b)) for v in pair], -1)
-
-        if fast:
-            x_far, send4, group1.terms[-1] = tie(x_far, send4, group1.terms[-1])
-            low_small = small.give()
-            (got_x,) = flip(x, [x_far])
-            got4, got_small = flip(core, [send4, low_small])
-            small.take(got_small)
-            group4, dx = Halved(keep4, got4), Halved(x_near, got_x)
-            trade(zl, group1, group2, group3)
-            trade(y, group4, small)
-            dx.terms[-1], group4.terms[-1] = tie(dx.terms[-1], group4.terms[-1])
-            trade(zl, dx, group4, small)
-            group1.terms[-1], e_own = tie(group1.terms[-1], enc.total())
-            away_1 = group1.give()
-            got_1, home, home_e = flip(zh, [away_1, out[tok:], e_own[tok:].astype(BF)])
-            group1.take(got_1)
-            trade(x, group2, group3)
-            x_own = dx.total() + d_own
-            away_x = x_own[tok:].astype(BF)
-            away_2, away_3 = group2.give(), group3.give()
-            home_x, got_2, got_3 = flip(zh, [away_x, away_2, away_3])
-            group2.take(got_2)
-            group3.take(got_3)
-            trade(x, group4, small)
-            trade(zh, group4, small)
-            s1, s2, small = group1.total()[0], group2.total()[0], small.total()
-            g_up, g_down, g_co = wide(s1[:4]), s1[4:8].reshape(4 * per, D), s1[8]
-            g_cin, g_cq, g_so = wide(s2[:2]), s2[2], s2[3]
-            g_in = unpack(group3.total()[0], group4.total()[0])
-        else:
-            enc = Halved(jnp.concatenate([enc_near, enc_far], 0))
-            dx = Halved(jnp.concatenate([x_near, x_far], 0))
-            for bit in reversed(x_bits):
-                trade(("seq", bit), enc, dx)
-            e_own = enc.total()
-            x_own = dx.total() + d_own
-            home, home_e, home_x = flip(
-                ("seq", half), [out[tok:], e_own[tok:].astype(BF), x_own[tok:].astype(BF)]
-            )
-            small = lax.psum(small.terms[0], ("dp", "seq"))
-
-            def summed(g):
-                return lax.psum_scatter(g, ("dp", "seq"), scatter_dimension=0, tiled=True).astype(F32)
-
-            def rejoin(keep, send):
-                g = jnp.stack([keep.reshape((2, 8) + keep.shape[1:]), send.reshape((2, 8) + keep.shape[1:])], 1)
-                return g.reshape((G,) + keep.shape[1:])
-
-            def full(g):
-                return g.transpose(0, 2, 1, 3).reshape(G * 16, -1)
-
-            all1, all2 = rejoin(keep1, send1), rejoin(keep2, send2)
-            g_up = summed(full(all1[:, :4]))
-            g_down = summed(all1[:, 4:8].reshape(FF, D))
-            g_co = summed(full(all1[:, 8:]))
-            g_cin, g_cq, g_so = summed(full(all2[:, :2])), summed(full(all2[:, 2:3])), summed(full(all2[:, 3:]))
-            g_in = summed(unpack(rejoin(keep3, send3), rejoin(keep4, send4)).reshape(G * 16, -1))
-
-        loss = jnp.sum(small[6]) / (jnp.sum(small[7]) * D)
+        def summed(g):
+            return lax.psum_scatter(g, ("dp", "seq"), scatter_dimension=0, tiled=True).astype(F32)
+
+        def rejoin(keep, send, n):
+            g = jnp.stack([v[: 256 * n].reshape(2, 8, n, 16, D) for v in (keep, send)], 1)
+            return g.reshape(G, n, 16, D)
+
+        def full(g):
+            return g.transpose(0, 2, 1, 3).reshape(G * 16, -1)
+
+        small = lax.psum(send2[1024:].astype(F32), ("dp", "seq"))
+        all1, all2, all3 = rejoin(keep1, send1, 9), rejoin(keep2, send2, 4), rejoin(keep3, send3, 3)
         g_norm = lax.dynamic_slice(small, (0, dev * per), (6, per))
-        outputs = back_home(out[:tok], home)
-        grad_encoder = back_home(e_own[:tok], home_e.astype(F32))
-        grad_inputs = back_home(x_own[:tok], home_x.astype(F32))
-        return (outputs, loss, grad_inputs, grad_encoder, g_in, g_so, g_cq, g_cin, g_co, g_up, g_down,
-                g_norm[:3], g_norm[3:])
+        return (
+            back_home(out[:tok], home[:tok]),
+            jnp.sum(small[6]) / (jnp.sum(small[7]) * D),
+            back_home(x_keep, home_x.astype(F32)),
+            back_home(e_keep, home[tok:].astype(F32)),
+            summed(full(all3)),
+            summed(full(all2[:, 3:])),
+            summed(full(all2[:, 2:3])),
+            summed(full(all2[:, :2])),
+            summed(full(all1[:, 8:])),
+            summed(full(all1[:, :4])),
+            summed(all1[:, 4:8].reshape(FF, D)),
+            g_norm[:3],
+            g_norm[3:],
+        )
 
     return shards
 

time: 265 us -> 237 us (0.89)
  Pallas kernels: 80 us -> 52.8 us
  other arithmetic: 30.6 us -> 7.19 us
  waiting for transfers between devices: 88.4 us -> 102 us
  local copies, waits for them, and re-layouts: 15.1 us -> 22.8 us
  starting transfers between devices: 29.7 us -> 36.9 us
  between operations: 18.1 us -> 14.5 us
    pallas_call x8 -> x15, Pallas kernels: 80 us -> 52.8 us  [call(): pl.pallas_call(body, grid=(1,), in_specs=[whole(a.shape) if s is None els...]
    unnamed x75 -> x58, local copies, waits for them, and re-layouts: 2.66 us -> 17.1 us
    convert_element_type x21 -> x1, other arithmetic: 13.2 us -> 0.37 us  [shards(): (keep1[1152:].astype(F32) + got1[1152:].astype(F32)).astype(BF)]
    ppermute x27 -> x30, waiting for transfers between devices: 73.9 us -> 86.2 us  [flip(): lax.ppermute(flat[0] if len(flat) == 1 else jnp.concatenate(flat, 0), axi...]
    ppermute x27 -> x30, starting transfers between devices: 29.7 us -> 36.8 us  [flip(): lax.ppermute(flat[0] if len(flat) == 1 else jnp.concatenate(flat, 0), axi...]
    add x7 -> x0, other arithmetic: 4.22 us -> none  [the longest x6 4.09 us: total(): return sum(rest, first)]
    slice x9 -> x5, local copies, waits for them, and re-layouts: 3.52 us -> 0.77 us  [flip(): lax.slice_in_dim(got, start, start + f.shape[0]).reshape(v.shape)]
  transfers between devices with their start and end apart: 28 -> 31, of which waited for: 16 -> 19; matrix products, arithmetic and copies ran while one was open for 13% -> 5% of each run, Pallas kernels for 20% -> 13%
where the time goes in v4:
time: 237 us; the launch traced here: 236 us
  waiting for transfers between devices  102 us (43%)
  Pallas kernels  52.8 us (22%)
  starting transfers between devices  36.9 us (16%)
  local copies, waits for them, and re-layouts  22.8 us (10%)
  between operations  14.5 us (6%)
  other arithmetic  7.19 us (3%)
    ppermute x30, waiting for transfers between devices, flip(): lax.ppermute(flat[0] if len(flat) == 1 else jnp.concatenate(flat, 0), axi...  86.2 us
    pallas_call x15, Pallas kernels, call(): pl.pallas_call(body, grid=(1,), in_specs=[whole(a.shape) if s is None els...  52.8 us
    ppermute x30, starting transfers between devices, flip(): lax.ppermute(flat[0] if len(flat) == 1 else jnp.concatenate(flat, 0), axi...  36.8 us
    unnamed x58, local copies, waits for them, and re-layouts  17.1 us
    all_gather x1, waiting for transfers between devices, shards(): wb = lax.all_gather(pack_b, ('dp', 'seq'))  15.9 us
  transfers between devices with their start and end apart: 31, of which 19 were waited for; matrix products, arithmetic and copies ran while one was open for 5% of the time, Pallas kernels for 13%

profile of v4, /device:TPU:0, one launch (start us, length us, event | category | flops | bytes accessed | tf_op | source)
XLA Modules:
  0.0 236.3 jit_solution(15350965014828719106)
XLA Ops:
  11.0 4.1 %collective-permute-start = (bf16[176,512]{1,0:T(8,128)(2,1)S(1)}, bf16[176,512]{1,0:T(8,128)(2,1)S(1)}, u32[]{:S(2)}, u32[]{:S(2)}) collective-permute-start(bf16[176,512]{1,0:T(8,128)(2,1)S(1)} %pad_maximum_fusion.7), channel_id=1, source_target_pairs={{0,4},{1,5},{2,6},{3,7},{4,0},{5,1},{6,2},{7,3},{8,12},{9,13},{10,... | collective-permute-start | bytes 540680 | tf_op jit(solution)/shard_map/ppermute | solution.py:425
  20.5 3.0 %collective-permute-done = bf16[176,512]{1,0:T(8,128)(2,1)S(1)} collective-permute-done((bf16[176,512]{1,0:T(8,128)(2,1)S(1)}, bf16[176,512]{1,0:T(8,128)(2,1)S(1)}, u32[]{:S(2)}, u32[]{:S(2)}) %collective-permute-start) | collective-permute-done | bytes 180256 | tf_op jit(solution)/shard_map/ppermute | solution.py:425
  25.8 3.4 %collective-permute-start.4 = (bf16[272,512]{1,0:T(8,128)(2,1)}, bf16[272,512]{1,0:T(8,128)(2,1)S(1)}, u32[]{:S(2)}, u32[]{:S(2)}) collective-permute-start(bf16[272,512]{1,0:T(8,128)(2,1)} %fusion.1), channel_id=1, source_target_pairs={{0,4},{1,5},{2,6},{3,7},{4,0},{5,1},{6,2},{7,3},{8,12},{9,13},{10,... | collective-permute-start | bytes 835592 | tf_op jit(solution)/shard_map/ppermute | solution.py:425
  29.2 14.8 %collective-permute-done.1 = bf16[352,512]{1,0:T(8,128)(2,1)S(1)} collective-permute-done((bf16[352,512]{1,0:T(8,128)(2,1)}, bf16[352,512]{1,0:T(8,128)(2,1)S(1)}, u32[]{:S(2)}, u32[]{:S(2)}) %collective-permute-start.1) | collective-permute-done | bytes 360480 | tf_op jit(solution)/shard_map/ppermute | solution.py:425
  46.3 5.5 %collective-permute-done.3 = bf16[192,512]{1,0:T(8,128)(2,1)S(1)} collective-permute-done((bf16[192,512]{1,0:T(8,128)(2,1)S(1)}, bf16[192,512]{1,0:T(8,128)(2,1)S(1)}, u32[]{:S(2)}, u32[]{:S(2)}) %collective-permute-start.3) | collective-permute-done | bytes 196640 | tf_op jit(solution)/shard_map/ppermute | solution.py:425
  55.7 5.6 %collective-permute-done.6 = bf16[384,512]{1,0:T(8,128)(2,1)S(1)} collective-permute-done((bf16[384,512]{1,0:T(8,128)(2,1)S(1)}, bf16[384,512]{1,0:T(8,128)(2,1)S(1)}, u32[]{:S(2)}, u32[]{:S(2)}) %collective-permute-start.6) | collective-permute-done | bytes 393248 | tf_op jit(solution)/shard_map/ppermute | solution.py:425
  77.1 8.7 %self_forward.1 = (bf16[1024,512]{1,0:T(8,128)(2,1)S(1)}, bf16[256,512]{1,0:T(8,128)(2,1)S(1)}, bf16[1024,1024]{1,0:T(8,128)(2,1)S(1)}, bf16[8,1024,256]{2,1,0:T...) custom-call(s32[66]{0:T(128)S(1)} %concatenate.39.ids, bf16[512,512]{1,0:T(8,128)(2,1)S(1)} %bitcast.74, ...), custom_call_target="tpu_custom_call" | custom-call | flops 1000 | bytes 1000 | tf_op jit(solution)/shard_map/self_forward/pallas_call | solution.py:50
  90.1 15.9 %all-gather.3.cloned.1.call-done = bf16[448,16,512]{2,1,0:T(8,128)(2,1)} async-done(((bf16[14,16,512]{2,1,0:T(8,128)(2,1)}), bf16[448,16,512]{2,1,0:T(8,128)(2,1)}) %all-gather.3.cloned.1.call-update) | async-done | bytes 7340048 | tf_op jit(solution)/shard_map/all_gather | solution.py:458
  106.0 3.1 %copy-done = bf16[448,16,512]{2,1,0:T(8,128)(2,1)S(1)} copy-done((bf16[448,16,512]{2,1,0:T(8,128)(2,1)S(1)}, bf16[448,16,512]{2,1,0:T(8,128)(2,1)}, u32[]{:S(2)}) %copy-start) | copy-done | bytes 7340056
  112.5 10.3 %cross_forward.1 = (bf16[1024,512]{1,0:T(8,128)(2,1)S(1)}, f32[256,512]{1,0:T(8,128)S(1)}, f32[256,1]{1,0:T(8,128)S(1)}, bf16[256,512]{1,0:T(8,128)(2,1)S(1)}, b...) custom-call(s32[66]{0:T(128)S(1)} %concatenate.39.ids, ...), custom_call_target="tpu_custom_call" | custom-call | flops 1000 | bytes 1000 | tf_op jit(solution)/shard_map/cross_forward/pallas_call | solution.py:50
  122.8 6.5 %ffn_both.1 = (bf16[256,512]{1,0:T(8,128)(2,1)S(1)}, f32[16,512]{1,0:T(8,128)S(1)}, f32[256,512]{1,0:T(8,128)S(1)}, bf16[256,512]{1,0:T(8,128)(2,1)S(1)}, bf16[2...) custom-call(s32[66]{0:T(128)S(1)} %concatenate.39.ids, f32[256,512]{1,0:T(8,128)S(1)} %get-tuple-element.116.xh1, ...), custom_call_target="tpu_custom_call" | custom-call | flops 1000 | bytes 1000 | tf_op jit(solution)/shard_map/ffn_both/pallas_call | solution.py:50
  129.6 3.9 %cross_back_a.1 = (bf16[1024,512]{1,0:T(8,128)(2,1)S(1)}, bf16[256,256]{1,0:T(8,128)(2,1)S(1)}) custom-call(bf16[256,512]{1,0:T(8,128)(2,1)S(1)} %get-tuple-element.121.q, bf16[1024,1024]{1,0:T(8,128)(2,1)S(1)} %get-tuple-element.122.kv, bf16[8,1024,256]{2,1,0:T(8,128)(2,1)S(1)} %get-tuple-element.123.p, f32[8,1,256]{2,1,0:T(1,128)S(1)} %get-tuple-element.124.rl, ...), custom_call_target="tpu_custom_call" | custom-call | flops 1000 | bytes 1000 | tf_op jit(solution)/shard_map/cross_back_a/pallas_call | solution.py:50
  135.2 7.4 %cross_back_b.1 = (f32[256,512]{1,0:T(8,128)S(1)}, bf16[256,512]{1,0:T(8,128)(2,1)S(1)}, bf16[256,512]{1,0:T(8,128)(2,1)S(1)}, bf16[256,512]{1,0:T(8,128)(2,1)S(...) custom-call(s32[66]{0:T(128)S(1)} %concatenate.39.ids, ...), custom_call_target="tpu_custom_call" | custom-call | flops 1000 | bytes 1000 | tf_op jit(solution)/shard_map/cross_back_b/pallas_call | solution.py:50
  142.7 3.3 %collective-permute-start.12 = (bf16[256,512]{1,0:T(8,128)(2,1)S(1)}, bf16[256,512]{1,0:T(8,128)(2,1)S(1)}, u32[]{:S(2)}, u32[]{:S(2)}) collective-permute-start(bf16[256,512]{1,0:T(8,128)(2,1)S(1)} %get-tuple-element.142), channel_id=1, source_target_pairs={{0,2},{1,3},{2,0},{3,1},{4,6},{5,7},{6,4},{7,5},{8,10},{9,11},{10,... | collective-permute-start | bytes 786440 | tf_op jit(solution)/shard_map/ppermute | solution.py:425
  147.6 3.9 %self_back_a.1 = (bf16[1024,512]{1,0:T(8,128)(2,1)S(1)}, bf16[256,256]{1,0:T(8,128)(2,1)S(1)}) custom-call(bf16[256,512]{1,0:T(8,128)(2,1)S(1)} %copy-done.17, bf16[1024,1024]{1,0:T(8,128)(2,1)S(1)} %get-tuple-element.138.kv, bf16[8,1024,256]{2,1,0:T(8,128)(2,1)S(1)} %copy-done.3, f32[8,1,256]{2,1,0:T(1,128)S(1)} %get-tuple-element.140.rl, ...), custom_call_target="tpu_custom_call" | custom-call | flops 1000 | bytes 1000 | tf_op jit(solution)/shard_map/self_back_a/pallas_call | solution.py:50
  153.2 6.8 %collective-permute-done.13.refs_2_ = bf16[256,512]{1,0:T(8,128)(2,1)S(1)} collective-permute-done((bf16[256,512]{1,0:T(8,128)(2,1)S(1)}, bf16[256,512]{1,0:T(8,128)(2,1)S(1)}, u32[]{:S(2)}, u32[]{:S(2)}) %collective-permute-start.13) | collective-permute-done | bytes 262176 | tf_op jit(solution)/shard_map/ppermute | solution.py:425
  163.9 3.3 %collective-permute-start.15 = (bf16[288,512]{1,0:T(8,128)(2,1)S(1)}, bf16[288,512]{1,0:T(8,128)(2,1)S(1)}, u32[]{:S(2)}, u32[]{:S(2)}) collective-permute-start(bf16[288,512]{1,0:T(8,128)(2,1)S(1)} %get-tuple-element.148), channel_id=1, source_target_pairs={{0,2},{1,3},{2,0},{3,1},{4,6},{5,7},{6,4},{7,5},{8,10},{9,11},{10,... | collective-permute-start | bytes 884744 | tf_op jit(solution)/shard_map/ppermute | solution.py:425
  168.6 7.1 %self_back_b.1 = (f32[256,512]{1,0:T(8,128)S(1)}, bf16[256,512]{1,0:T(8,128)(2,1)S(1)}, bf16[256,512]{1,0:T(8,128)(2,1)S(1)}, bf16[256,512]{1,0:T(8,128)(2,1)S(1...) custom-call(s32[66]{0:T(128)S(1)} %concatenate.39.ids, bf16[1024,512]{1,0:T(8,128)(2,1)S(1)} %copy-done.6, ...), custom_call_target="tpu_custom_call" | custom-call | flops 1000 | bytes 1000 | tf_op jit(solution)/shard_map/self_back_b/pallas_call | solution.py:50
  175.7 5.6 %collective-permute-done.16.refs_9_.refs_5_ = bf16[288,512]{1,0:T(8,128)(2,1)S(1)} collective-permute-done((bf16[288,512]{1,0:T(8,128)(2,1)S(1)}, bf16[288,512]{1,0:T(8,128)(2,1)S(1)}, u32[]{:S(2)}, u32[]{:S(2)}) %collective-permute-start.16) | collective-permute-done | bytes 294944 | tf_op jit(solution)/shard_map/ppermute | solution.py:425
  189.6 5.3 %collective-permute-done.25.refs_5_.refs_8_.refs_22_ = bf16[384,512]{1,0:T(8,128)(2,1)S(1)} collective-permute-done((bf16[384,512]{1,0:T(8,128)(2,1)S(1)}, bf16[384,512]{1,0:T(8,128)(2,1)S(1)}, u32[]{:S(2)}, u32[]{:S(2)}) %collective-permute-start.25) | collective-permute-done | bytes 393248 | tf_op jit(solution)/shard_map/ppermute | solution.py:425
  199.7 9.0 %collective-permute-done.22.refs_3_ = bf16[256,512]{1,0:T(8,128)(2,1)S(1)} collective-permute-done((bf16[256,512]{1,0:T(8,128)(2,1)S(1)}, bf16[256,512]{1,0:T(8,128)(2,1)S(1)}, u32[]{:S(2)}, u32[]{:S(2)}) %collective-permute-start.22) | collective-permute-done | bytes 262176 | tf_op jit(solution)/shard_map/ppermute | solution.py:425
  209.7 7.1 %collective-permute-done.28.refs_5_.refs_19_ = bf16[240,512]{1,0:T(8,128)(2,1)S(1)} collective-permute-done((bf16[240,512]{1,0:T(8,128)(2,1)S(1)}, bf16[240,512]{1,0:T(8,128)(2,1)S(1)}, u32[]{:S(2)}, u32[]{:S(2)}) %collective-permute-start.28) | collective-permute-done | bytes 245792 | tf_op jit(solution)/shard_map/ppermute | solution.py:425
  216.8 3.3 %collective-permute-done.26.refs_3_.refs_17_ = bf16[240,512]{1,0:T(8,128)(2,1)S(1)} collective-permute-done((bf16[240,512]{1,0:T(8,128)(2,1)S(1)}, bf16[240,512]{1,0:T(8,128)(2,1)S(1)}, u32[]{:S(2)}, u32[]{:S(2)}) %collective-permute-start.26) | collective-permute-done | bytes 245792 | tf_op jit(solution)/shard_map/ppermute | solution.py:425
  220.3 7.2 %collective-permute-done.29.refs_13_ = bf16[128,512]{1,0:T(8,128)(2,1)S(1)} collective-permute-done((bf16[128,512]{1,0:T(8,128)(2,1)S(1)}, bf16[128,512]{1,0:T(8,128)(2,1)S(1)}, u32[]{:S(2)}, u32[]{:S(2)}) %collective-permute-start.29) | collective-permute-done | bytes 131104 | tf_op jit(solution)/shard_map/ppermute | solution.py:425
  (155 shorter events, 67.9 us)
Async XLA Ops:
  7.2 98.8 %all-gather.3.cloned.1.call-start = ((), (), s32[]{:S(2)}) async-start(), calls=%async_computation | async-start | bytes 7569408 | tf_op jit(solution)/shard_map/all_gather | solution.py:458
  11.0 12.5 %collective-permute-start = (bf16[176,512]{1,0:T(8,128)(2,1)S(1)}, bf16[176,512]{1,0:T(8,128)(2,1)S(1)}, u32[]{:S(2)}, u32[]{:S(2)}) collective-permute-start(bf16[176,512]{1,0:T(8,128)(2,1)S(1)} %pad_maximum_fusion.7), channel_id=1, source_target_pairs={{0,4},{1,5},{2,6},{3,7},{4,0},{5,1},{6,2},{7,3},{8,12},{9,13},{10,... | collective-permute-start | bytes 540680 | tf_op jit(solution)/shard_map/ppermute | solution.py:425
  24.3 19.6 %collective-permute-start.1 = (bf16[352,512]{1,0:T(8,128)(2,1)}, bf16[352,512]{1,0:T(8,128)(2,1)S(1)}, u32[]{:S(2)}, u32[]{:S(2)}) collective-permute-start(bf16[352,512]{1,0:T(8,128)(2,1)} %pad_maximum_fusion.3), channel_id=1, source_target_pairs={{0,2},{1,3},{2,0},{3,1},{4,6},{5,7},{6,4},{7,5},{8,10},{9,11},{10,... | collective-permute-start | bytes 1081352 | tf_op jit(solution)/shard_map/ppermute | solution.py:425
  25.8 19.7 %collective-permute-start.4 = (bf16[272,512]{1,0:T(8,128)(2,1)}, bf16[272,512]{1,0:T(8,128)(2,1)S(1)}, u32[]{:S(2)}, u32[]{:S(2)}) collective-permute-start(bf16[272,512]{1,0:T(8,128)(2,1)} %fusion.1), channel_id=1, source_target_pairs={{0,4},{1,5},{2,6},{3,7},{4,0},{5,1},{6,2},{7,3},{8,12},{9,13},{10,... | collective-permute-start | bytes 835592 | tf_op jit(solution)/shard_map/ppermute | solution.py:425
  53.0 14.5 %collective-permute-start.2 = (bf16[512,512]{1,0:T(8,128)(2,1)S(1)}, bf16[512,512]{1,0:T(8,128)(2,1)S(1)}, u32[]{:S(2)}, u32[]{:S(2)}) collective-permute-start(bf16[512,512]{1,0:T(8,128)(2,1)S(1)} %bitcast.73), channel_id=1, source_target_pairs={{0,1},{1,0},{2,3},{3,2},{4,5},{5,4},{6,7},{7,6},{8,9},{9,8},{10,11... | collective-permute-start | bytes 1572872 | tf_op jit(solution)/shard_map/ppermute | solution.py:425
  68.4 21.7 %collective-permute-start.8 = (bf16[512,512]{1,0:T(8,128)(2,1)}, bf16[512,512]{1,0:T(8,128)(2,1)}, u32[]{:S(2)}, u32[]{:S(2)}) collective-permute-start(bf16[512,512]{1,0:T(8,128)(2,1)} %bitcast.34.near), channel_id=1, source_target_pairs={{0,1},{1,0},{2,3},{3,2},{4,5},{5,4},{6,7},{7,6},{8,9},{9,8},{10,11... | collective-permute-start | bytes 1572872 | tf_op jit(solution)/shard_map/ppermute | solution.py:425
  134.3 28.2 %collective-permute-start.11 = (bf16[1152,512]{1,0:T(8,128)(2,1)S(1)}, bf16[1152,512]{1,0:T(8,128)(2,1)S(1)}, u32[]{:S(2)}, u32[]{:S(2)}) collective-permute-start(bf16[1152,512]{1,0:T(8,128)(2,1)S(1)} %add_convert_fusion), channel_id=1, source_target_pairs={{0,16},{8,24},{16,0},{24,8},{1,17},{9,25},{17,1},{25,9},{2,18},{10... | collective-permute-start | bytes 3538952 | tf_op jit(solution)/shard_map/ppermute | solution.py:425
  142.6 17.4 %collective-permute-start.10 = (bf16[1040,512]{1,0:T(8,128)(2,1)S(1)}, bf16[1040,512]{1,0:T(8,128)(2,1)S(1)}, u32[]{:S(2)}, u32[]{:S(2)}) collective-permute-start(bf16[1040,512]{1,0:T(8,128)(2,1)S(1)} %get-tuple-element.135.refs_2_), channel_id=1, source_target_pairs={{0,8},{8,0},{16,24},{24,16},{1,9},{9,1},{17,25},{25,17},{2,10},{10... | collective-permute-start | bytes 3194888 | tf_op jit(solution)/shard_map/ppermute | solution.py:425
  142.7 10.5 %collective-permute-start.12 = (bf16[256,512]{1,0:T(8,128)(2,1)S(1)}, bf16[256,512]{1,0:T(8,128)(2,1)S(1)}, u32[]{:S(2)}, u32[]{:S(2)}) collective-permute-start(bf16[256,512]{1,0:T(8,128)(2,1)S(1)} %get-tuple-element.142), channel_id=1, source_target_pairs={{0,2},{1,3},{2,0},{3,1},{4,6},{5,7},{6,4},{7,5},{8,10},{9,11},{10,... | collective-permute-start | bytes 786440 | tf_op jit(solution)/shard_map/ppermute | solution.py:425
  146.1 14.0 %collective-permute-start.13 = (bf16[256,512]{1,0:T(8,128)(2,1)S(1)}, bf16[256,512]{1,0:T(8,128)(2,1)S(1)}, u32[]{:S(2)}, u32[]{:S(2)}) collective-permute-start(bf16[256,512]{1,0:T(8,128)(2,1)S(1)} %get-tuple-element.143), channel_id=1, source_target_pairs={{0,1},{1,0},{2,3},{3,2},{4,5},{5,4},{6,7},{7,6},{8,9},{9,8},{10,11... | collective-permute-start | bytes 786440 | tf_op jit(solution)/shard_map/ppermute | solution.py:425
  147.4 12.7 %collective-permute-start.14 = (bf16[256,512]{1,0:T(8,128)(2,1)S(1)}, bf16[256,512]{1,0:T(8,128)(2,1)S(1)}, u32[]{:S(2)}, u32[]{:S(2)}) collective-permute-start(bf16[256,512]{1,0:T(8,128)(2,1)S(1)} %get-tuple-element.144), channel_id=1, source_target_pairs={{0,3},{1,2},{2,1},{3,0},{4,7},{5,6},{6,5},{7,4},{8,11},{9,10},{10,... | collective-permute-start | bytes 786440 | tf_op jit(solution)/shard_map/ppermute | solution.py:425
  162.9 18.4 %collective-permute-start.18 = (bf16[528,512]{1,0:T(8,128)(2,1)S(1)}, bf16[528,512]{1,0:T(8,128)(2,1)S(1)}, u32[]{:S(2)}, u32[]{:S(2)}) collective-permute-start(bf16[528,512]{1,0:T(8,128)(2,1)S(1)} %get-tuple-element.151.refs_6_), channel_id=1, source_target_pairs={{0,16},{8,24},{16,0},{24,8},{1,17},{9,25},{17,1},{25,9},{2,18},{10... | collective-permute-start | bytes 1622024 | tf_op jit(solution)/shard_map/ppermute | solution.py:425
  163.9 11.8 %collective-permute-start.15 = (bf16[288,512]{1,0:T(8,128)(2,1)S(1)}, bf16[288,512]{1,0:T(8,128)(2,1)S(1)}, u32[]{:S(2)}, u32[]{:S(2)}) collective-permute-start(bf16[288,512]{1,0:T(8,128)(2,1)S(1)} %get-tuple-element.148), channel_id=1, source_target_pairs={{0,2},{1,3},{2,0},{3,1},{4,6},{5,7},{6,4},{7,5},{8,10},{9,11},{10,... | collective-permute-start | bytes 884744 | tf_op jit(solution)/shard_map/ppermute | solution.py:425
  167.2 14.1 %collective-permute-start.16 = (bf16[288,512]{1,0:T(8,128)(2,1)S(1)}, bf16[288,512]{1,0:T(8,128)(2,1)S(1)}, u32[]{:S(2)}, u32[]{:S(2)}) collective-permute-start(bf16[288,512]{1,0:T(8,128)(2,1)S(1)} %get-tuple-element.149), channel_id=1, source_target_pairs={{0,1},{1,0},{2,3},{3,2},{4,5},{5,4},{6,7},{7,6},{8,9},{9,8},{10,11... | collective-permute-start | bytes 884744 | tf_op jit(solution)/shard_map/ppermute | solution.py:425
  168.5 12.8 %collective-permute-start.17 = (bf16[288,512]{1,0:T(8,128)(2,1)S(1)}, bf16[288,512]{1,0:T(8,128)(2,1)S(1)}, u32[]{:S(2)}, u32[]{:S(2)}) collective-permute-start(bf16[288,512]{1,0:T(8,128)(2,1)S(1)} %get-tuple-element.150), channel_id=1, source_target_pairs={{0,3},{1,2},{2,1},{3,0},{4,7},{5,6},{6,5},{7,4},{8,11},{9,10},{10,... | collective-permute-start | bytes 884744 | tf_op jit(solution)/shard_map/ppermute | solution.py:425
  183.7 11.2 %collective-permute-start.25 = (bf16[384,512]{1,0:T(8,128)(2,1)S(1)}, bf16[384,512]{1,0:T(8,128)(2,1)S(1)}, u32[]{:S(2)}, u32[]{:S(2)}) collective-permute-start(bf16[384,512]{1,0:T(8,128)(2,1)S(1)} %sum_y3.1), channel_id=1, source_target_pairs={{0,16},{8,24},{16,0},{24,8},{1,17},{9,25},{17,1},{25,9},{2,18},{10... | collective-permute-start | bytes 1179656 | tf_op jit(solution)/shard_map/ppermute | solution.py:425
  184.2 13.5 %collective-permute-start.20 = (bf16[256,512]{1,0:T(8,128)(2,1)S(1)}, bf16[256,512]{1,0:T(8,128)(2,1)S(1)}, u32[]{:S(2)}, u32[]{:S(2)}) collective-permute-start(bf16[256,512]{1,0:T(8,128)(2,1)S(1)} %get-tuple-element.171), channel_id=1, source_target_pairs={{0,2},{1,3},{2,0},{3,1},{4,6},{5,7},{6,4},{7,5},{8,10},{9,11},{10,... | collective-permute-start | bytes 786440 | tf_op jit(solution)/shard_map/ppermute | solution.py:425
  185.4 12.4 %collective-permute-start.21 = (bf16[256,512]{1,0:T(8,128)(2,1)S(1)}, bf16[256,512]{1,0:T(8,128)(2,1)S(1)}, u32[]{:S(2)}, u32[]{:S(2)}) collective-permute-start(bf16[256,512]{1,0:T(8,128)(2,1)S(1)} %get-tuple-element.172), channel_id=1, source_target_pairs={{0,1},{1,0},{2,3},{3,2},{4,5},{5,4},{6,7},{7,6},{8,9},{9,8},{10,11... | collective-permute-start | bytes 786440 | tf_op jit(solution)/shard_map/ppermute | solution.py:425
  186.2 34.1 %collective-permute-start.19 = (bf16[400,512]{1,0:T(8,128)(2,1)S(1)}, bf16[400,512]{1,0:T(8,128)(2,1)S(1)}, u32[]{:S(2)}, u32[]{:S(2)}) collective-permute-start(bf16[400,512]{1,0:T(8,128)(2,1)S(1)} %get-tuple-element.168), channel_id=1, source_target_pairs={{0,4},{1,5},{2,6},{3,7},{4,0},{5,1},{6,2},{7,3},{8,12},{9,13},{10,... | collective-permute-start | bytes 1228808 | tf_op jit(solution)/shard_map/ppermute | solution.py:425
  188.4 20.3 %collective-permute-start.22 = (bf16[256,512]{1,0:T(8,128)(2,1)S(1)}, bf16[256,512]{1,0:T(8,128)(2,1)S(1)}, u32[]{:S(2)}, u32[]{:S(2)}) collective-permute-start(bf16[256,512]{1,0:T(8,128)(2,1)S(1)} %get-tuple-element.173), channel_id=1, source_target_pairs={{0,3},{1,2},{2,1},{3,0},{4,7},{5,6},{6,5},{7,4},{8,11},{9,10},{10,... | collective-permute-start | bytes 786440 | tf_op jit(solution)/shard_map/ppermute | solution.py:425
  195.2 14.5 %collective-permute-start.27 = (bf16[240,512]{1,0:T(8,128)(2,1)S(1)}, bf16[240,512]{1,0:T(8,128)(2,1)S(1)}, u32[]{:S(2)}, u32[]{:S(2)}) collective-permute-start(bf16[240,512]{1,0:T(8,128)(2,1)S(1)} %get-tuple-element.180), channel_id=1, source_target_pairs={{0,1},{1,0},{2,3},{3,2},{4,5},{5,4},{6,7},{7,6},{8,9},{9,8},{10,11... | collective-permute-start | bytes 737288 | tf_op jit(solution)/shard_map/ppermute | solution.py:425
  197.6 19.2 %collective-permute-start.28 = (bf16[240,512]{1,0:T(8,128)(2,1)S(1)}, bf16[240,512]{1,0:T(8,128)(2,1)S(1)}, u32[]{:S(2)}, u32[]{:S(2)}) collective-permute-start(bf16[240,512]{1,0:T(8,128)(2,1)S(1)} %get-tuple-element.181), channel_id=1, source_target_pairs={{0,3},{1,2},{2,1},{3,0},{4,7},{5,6},{6,5},{7,4},{8,11},{9,10},{10,... | collective-permute-start | bytes 737288 | tf_op jit(solution)/shard_map/ppermute | solution.py:425
  197.7 22.3 %collective-permute-start.26 = (bf16[240,512]{1,0:T(8,128)(2,1)S(1)}, bf16[240,512]{1,0:T(8,128)(2,1)S(1)}, u32[]{:S(2)}, u32[]{:S(2)}) collective-permute-start(bf16[240,512]{1,0:T(8,128)(2,1)S(1)} %get-tuple-element.179.refs_9_), channel_id=1, source_target_pairs={{0,2},{1,3},{2,0},{3,1},{4,6},{5,7},{6,4},{7,5},{8,10},{9,11},{10,... | collective-permute-start | bytes 737288 | tf_op jit(solution)/shard_map/ppermute | solution.py:425
  208.9 11.5 %collective-permute-start.23 = (bf16[128,512]{1,0:T(8,128)(2,1)S(1)}, bf16[128,512]{1,0:T(8,128)(2,1)S(1)}, u32[]{:S(2)}, u32[]{:S(2)}) collective-permute-start(bf16[128,512]{1,0:T(8,128)(2,1)S(1)} %get-tuple-element.175), channel_id=1, source_target_pairs={{0,4},{1,5},{2,6},{3,7},{4,0},{5,1},{6,2},{7,3},{8,12},{9,13},{10,... | collective-permute-start | bytes 393224 | tf_op jit(solution)/shard_map/ppermute | solution.py:425
  (34 other events, 200.4 us)
Sparse Core Ops, SparseCore 0:
  10.9 94.9 all-gather.2

commit v5 on v4

--- a/solution.py
+++ b/solution.py
@@ -20,7 +20,7 @@
 F32 = jnp.float32
 MIB = 1 << 20
 
-DEVICE, PLACE_1, PLACE_2, SLOT = 1, 2, 18, 34
+DEVICE, PLACE_1, PLACE_2, SLOT_A, SLOT_B, SLOT_F = 1, 2, 18, 34, 66, 98
 
 NN = (((1,), (0,)), ((), ()))
 NT = (((1,), (1,)), ((), ()))
@@ -36,14 +36,6 @@
 
 
 SMEM = pl.BlockSpec(memory_space=pltpu.SMEM)
-
-
-def chunks(first, count):
-    return pl.BlockSpec((G, count, 16, D), lambda i: (0, first // count, 0, 0))
-
-
-def whole_weight(ref, j):
-    return ref[:, j].reshape(D, D)
 
 
 def call(body, ins, outs, scratch=(), name=None, vmem=16):
@@ -51,8 +43,8 @@
         body,
         grid=(1,),
         in_specs=[whole(a.shape) if s is None else s for a, s in ins],
-        out_specs=[whole(s) for s, _ in outs],
-        out_shape=[jax.ShapeDtypeStruct(s, t) for s, t in outs],
+        out_specs=[whole(o[0]) if len(o) == 2 else pl.BlockSpec(memory_space=pltpu.HBM) for o in outs],
+        out_shape=[jax.ShapeDtypeStruct(*o) if len(o) == 2 else pltpu.HBM(*o[:2]) for o in outs],
         scratch_shapes=list(scratch),
         compiler_params=pltpu.CompilerParams(vmem_limit_bytes=vmem * MIB),
         name=name,
@@ -60,17 +52,30 @@
     )(*[a for a, _ in ins])
 
 
-def weight(ids, near, far, j):
-    picks = []
-    for g in range(G):
-        at = ids[SLOT + g]
-        low = at & (G // 2 - 1)
-        picks.append(jnp.where(at < G // 2, near[low, j], far[low, j]))
-    return jnp.concatenate(picks, 0)
-
-
-def norm_rows(ref):
-    return jnp.sum(ref[:, 0].astype(F32), axis=0)
+def unpack(ids, table, parts, *targets):
+    each = parts[0].shape[0]
+    for p, part in enumerate(parts):
+        for i in range(each):
+            group = ids[table + each * p + i]
+            for ref, first, count, height in targets:
+                at = pl.multiple_of(group * height, 16)
+                block = part[i, first : first + count]
+                if height == 16:
+                    ref[:, pl.ds(at, 16), :] = block
+                else:
+                    ref[pl.ds(at, height), :] = block.reshape(height, D)
+
+
+def norm_rows(parts):
+    return sum(jnp.sum(part[:, 5].astype(F32), axis=0) for part in parts)
+
+
+def set_mask(mask, segs, key, query, position):
+    length, rows = mask.shape
+    columns = jnp.transpose(segs[...])
+    same = columns[:, key : key + 1] == segs[query : query + 1, :rows]
+    ahead = columns[:, position : position + 1] <= segs[position : position + 1, :rows]
+    mask[...] = jnp.where(same & ahead, 0.0, NEG)
 
 
 def put(ids, first, ref, chunks_each, j, value):
@@ -101,8 +106,17 @@
     return jnp.where((lane < HEAD_DIM) == (e == 0), x, jnp.zeros_like(x))
 
 
-def attend(q_ref, kv_ref, mask_ref, p_ref, rl_ref, at_ref):
+def attend(q_ref, kv_ref, mask_ref, p_ref, rl_ref, at_ref, p_out, sems):
+    def leave(hp, slot):
+        return pltpu.make_async_copy(p_ref.at[slot], p_out.at[pl.ds(2 * hp, 2)], sems.at[slot])
+
     def pair(hp, carry):
+        slot = hp % 2
+
+        @pl.when(hp >= 2)
+        def _():
+            leave(hp - 2, slot).wait()
+
         c0 = pl.multiple_of(hp * 128, 128)
         k2 = kv_ref[:, pl.ds(c0, 128)]
         v2 = kv_ref[:, pl.ds(pl.multiple_of(D + c0, 128), 128)]
@@ -112,15 +126,25 @@
             p = jnp.exp(s - jnp.max(s, axis=0, keepdims=True))
             rl = 1.0 / jnp.sum(p, axis=0, keepdims=True)
             pb = p.astype(BF)
-            p_ref[2 * hp + e] = pb
+            p_ref[slot, e] = pb
             rl_ref[2 * hp + e] = rl
             o = dot(v2, pb, TN) * rl
             at_ref[pl.ds(pl.multiple_of((2 * hp + e) * HEAD_DIM, HEAD_DIM), HEAD_DIM), :] = o[
                 e * HEAD_DIM : (e + 1) * HEAD_DIM
             ].astype(BF)
+        leave(hp, slot).start()
         return carry
 
-    lax.fori_loop(0, HEADS // 2, pair, 0)
+    pairs = HEADS // 2
+    lax.fori_loop(0, pairs, pair, 0)
+    for hp in (pairs - 2, pairs - 1):
+        leave(hp, hp % 2).wait()
+
+
+def keep_copy(held, out, sem):
+    copy = pltpu.make_async_copy(held, out, sem)
+    copy.start()
+    return copy
 
 
 def attend_back(first, q_ref, kv_ref, p_ref, rl_ref, do_ref, dkv_ref, dqt_ref):
@@ -168,22 +192,22 @@
     return ((send, 1 - ids[0]), (keep, ids[0]))
 
 
-def pack(s_in, s_out, c_in, c_q, c_out, up, down, gain, bias, at, pa, pb):
+def pack(s_in, s_out, c_in, c_q, c_out, up, down, gain, bias, at, pa, pb, pf):
     for j in range(3):
         pa[j] = s_in[:, j * D : (j + 1) * D]
-    pb[8] = s_out[...]
+    pb[0] = s_out[...]
     for j in range(2):
-        pb[9 + j] = c_in[:, j * D : (j + 1) * D]
-    pb[11] = c_q[...]
-    pb[12] = c_out[...]
+        pb[1 + j] = c_in[:, j * D : (j + 1) * D]
+    pb[3] = c_q[...]
+    pb[4] = c_out[...]
     for j in range(4):
-        pb[j] = up[:, j * D : (j + 1) * D]
-        pb[4 + j] = down[16 * j : 16 * j + 16, :]
+        pf[j] = up[:, j * D : (j + 1) * D]
+        pf[4 + j] = down[16 * j : 16 * j + 16, :]
     rows = jnp.concatenate([gain[...], bias[...], jnp.zeros((10, 16), BF)], 0)
     column = lax.broadcasted_iota(jnp.int32, (16, D), 1)
     row = lax.broadcasted_iota(jnp.int32, (16, D), 0)
     pick = (column == at[0] * 16 + row).astype(BF)
-    pb[13] = dot(rows, pick).astype(BF)
+    pb[5] = dot(rows, pick).astype(BF)
 
 
 def join(full, near, far):
@@ -192,43 +216,59 @@
     full[half:] = far[...]
 
 
-def self_forward(rows, ids, near, far, wa, wa_far, mask, xf, q, kv, p, rl, at):
+def self_forward(rows, ids, near, far, wa0, wa1, wa2, wa3, segs,
+                 xf_out, w_out, q_out, kv_out, p_out, rl, at, mask, xf, w, q, kv, p, p_sems, sems):
     join(xf, near, far)
-    q[...] = (dot(xf[:rows], weight(ids, wa, wa_far, 0)).astype(BF).astype(F32) * SCALE).astype(BF)
-    kv[:, :D] = dot(xf[...], weight(ids, wa, wa_far, 1)).astype(BF)
-    kv[:, D:] = dot(xf[...], weight(ids, wa, wa_far, 2)).astype(BF)
-    attend(q, kv, mask, p, rl, at)
-
-
-def cross_forward(rows, ids, xf, near, far, at1, wb, norms, mask, ef, xh1, rs1, low1, q, kv, p, rl, at):
+    copies = [keep_copy(xf, xf_out, sems.at[0])]
+    unpack(ids, SLOT_A, (wa0, wa1, wa2, wa3), (w, 0, 3, 16))
+    copies.append(keep_copy(w, w_out, sems.at[1]))
+    set_mask(mask, segs, 0, 0, 1)
+    q[...] = (dot(xf[:rows], w[0]).astype(BF).astype(F32) * SCALE).astype(BF)
+    kv[:, :D] = dot(xf[...], w[1]).astype(BF)
+    kv[:, D:] = dot(xf[...], w[2]).astype(BF)
+    copies += [keep_copy(q, q_out, sems.at[2]), keep_copy(kv, kv_out, sems.at[3])]
+    attend(q, kv, mask, p, rl, at, p_out, p_sems)
+    for copy in copies:
+        copy.wait()
+
+
+def cross_forward(rows, ids, xf, near, far, at1, wb0, wb1, wb2, wb3, segs,
+                  ef_out, w, norms, xh1, rs1, low1_out, q_out, kv_out, p_out, rl, at,
+                  mask, ef, low1, q, kv, p, p_sems, sems):
     join(ef, near, far)
-    gb = norm_rows(norms)
-    resid = xf[:rows].astype(F32) + dot(at1[...], whole_weight(wb, 0), TN)
+    copies = [keep_copy(ef, ef_out, sems.at[0])]
+    unpack(ids, SLOT_B, (wb0, wb1, wb2, wb3), (w, 0, 5, 16))
+    set_mask(mask, segs, 2, 0, 3)
+    gb = norm_rows((wb0, wb1, wb2, wb3))
+    norms[...] = gb
+    resid = xf[...].astype(F32) + dot(at1[...], w[0], TN)
     xhat, rstd, n1 = norm_forward(resid, gb[0:1], gb[3:4])
     xh1[...] = xhat
     rs1[...] = rstd
     low1[...] = n1.astype(BF)
-    q[...] = (dot(low1[...], whole_weight(wb, 3)).astype(BF).astype(F32) * SCALE).astype(BF)
-    kv[:, :D] = dot(ef[...], whole_weight(wb, 1)).astype(BF)
-    kv[:, D:] = dot(ef[...], whole_weight(wb, 2)).astype(BF)
-    attend(q, kv, mask, p, rl, at)
-
-
-def ffn_both(ids, xh1, at2, teach, valid, w_up, w_dn, w_co, norms,
-             out, small, d_r2, d_mix, keep, send, act, hid, low2, wup):
-    gb = norm_rows(norms)
+    copies.append(keep_copy(low1, low1_out, sems.at[1]))
+    q[...] = (dot(low1[...], w[3]).astype(BF).astype(F32) * SCALE).astype(BF)
+    kv[:, :D] = dot(ef[...], w[1]).astype(BF)
+    kv[:, D:] = dot(ef[...], w[2]).astype(BF)
+    copies += [keep_copy(q, q_out, sems.at[2]), keep_copy(kv, kv_out, sems.at[3])]
+    attend(q, kv, mask, p, rl, at, p_out, p_sems)
+    for copy in copies:
+        copy.wait()
+
+
+def ffn_both(ids, xh1, at2, teach, valid, wb, norms, wf0, wf1, wf2, wf3,
+             out, small, d_r2, d_mix, keep, send, act, hid, low2, wup, wdn):
+    gb = norms[...]
     n1 = xh1[...] * gb[0:1] + gb[3:4]
-    wco = whole_weight(w_co, 0)
-    for j in range(4):
-        wup[j] = whole_weight(w_up, j)
-    wdn = w_dn[...].reshape(FF, D)
+    wco = wb[4]
+    unpack(ids, SLOT_F, (wf0, wf1, wf2, wf3), (wup, 0, 4, 16), (wdn, 4, 4, 64))
     xh2, rs2, n2 = norm_forward(n1 + dot(at2[...], wco, TN), gb[1:2], gb[4:5])
     low2[...] = n2.astype(BF)
     for j in range(4):
         h = dot(low2[...], wup[j])
         hid[j] = h
         act[:, j * D : (j + 1) * D] = (h / (1.0 + jnp.exp(-h))).astype(BF)
-    r3 = n2 + dot(act[...], wdn)
+    r3 = n2 + dot(act[...], wdn[...])
     xh3, rs3, final = norm_forward(r3, gb[2:3], gb[5:6])
     out[...] = final.astype(BF)
     err = (final - teach[...].astype(F32)) * valid[...]
@@ -279,10 +319,10 @@
                  rs1, at1, small, own, *rest):
     parts, (d_mix1, d_r1, keep, send, dkv, dqt) = rest[:n_parts], rest[n_parts:]
     attend_back(4, q, kv, p, rl, d_mix, dkv, dqt)
-    project(own, parts, dkv_a, dkv, whole_weight(wb, 1), whole_weight(wb, 2))
+    project(own, parts, dkv_a, dkv, wb[1], wb[2])
     dq = jnp.concatenate([dq_a[...], jnp.transpose(dqt[...]).astype(BF)], 1)
-    gb = norm_rows(norms)
-    dn1 = d_r2[...] + dot(dq, whole_weight(wb, 3), NT)
+    gb = norms[...]
+    dn1 = d_r2[...] + dot(dq, wb[3], NT)
     dr1, dg, db = norm_back(dn1, xh1[...], rs1[...], gb[0:1])
     row = lax.broadcasted_iota(jnp.int32, (16, D), 0)
     sums = jnp.where(row == 0, dg, jnp.where(row == 3, db, small[...]))
@@ -297,15 +337,15 @@
             put(ids, PLACE_2, ref, 4, j, g)
         put(ids, PLACE_2, ref, 4, 2, dot(cols(low1, at, 128), dq, TN))
         put(ids, PLACE_2, ref, 4, 3, dot(rows_of(at1, at, 128), dself))
-    d_mix1[...] = dot(dself, whole_weight(wb, 0), NT).astype(BF)
-
-
-def self_back_b(n_parts, rows, ids, xf, q, kv, p, rl, d_mix, dkv_a, dq_a, wa, wa_far, d_r1, own, *rest):
+    d_mix1[...] = dot(dself, wb[0], NT).astype(BF)
+
+
+def self_back_b(n_parts, rows, ids, xf, q, kv, p, rl, d_mix, dkv_a, dq_a, wa, d_r1, own, *rest):
     parts, (keep, send, dkv, dqt) = rest[:n_parts], rest[n_parts:]
     attend_back(4, q, kv, p, rl, d_mix, dkv, dqt)
     dq = jnp.concatenate([dq_a[...], jnp.transpose(dqt[...]).astype(BF)], 1)
-    through_q = d_r1[...] + dot(dq, weight(ids, wa, wa_far, 0), NT)
-    project(own, parts, dkv_a, dkv, weight(ids, wa, wa_far, 1), weight(ids, wa, wa_far, 2), through_q)
+    through_q = d_r1[...] + dot(dq, wa[0], NT)
+    project(own, parts, dkv_a, dkv, wa[1], wa[2], through_q)
     for ref, at in sides(ids, keep, send):
         lhs = cols(xf, at, 128)
         put(ids, PLACE_2, ref, 3, 0, dot(lhs[:rows], dq, TN))
@@ -405,7 +445,7 @@
     half = ns // 2
     per = G * 16 // n_dev
     fast = nd == 4 and ns == 8
-    run = functools.partial(call, vmem=16 if fast else 44)
+    run = functools.partial(call, vmem=20 if fast else 48)
 
     core, y, x, zl, zh = ("dp", 1), ("dp", 2), ("seq", 1), ("seq", 2), ("seq", 4)
 
@@ -446,43 +486,60 @@
 
         valid_away = jnp.pad(other(dec_valid).astype(BF)[None], ((0, 15), (0, D - tok)))
 
+        row_bits = (2, 1) if fast else tuple(1 << b for b in range(half.bit_length() - 1))
+        slots = jnp.arange(half, dtype=jnp.int32)
+
+        def pieces(bits):
+            masks = sum((((slots >> i) & 1) * b) for i, b in enumerate(bits))[:, None]
+            return (seq_at ^ masks ^ jnp.array([[0, half]], jnp.int32)).reshape(-1)
+
+        pos = (pieces(row_bits)[:, None] * tok + jnp.arange(tok, dtype=jnp.int32)[None]).reshape(-1)
+        dec_k = of(dec_seg, mine).reshape(ns, tok)[pieces(row_bits)].reshape(-1)
+        enc_k = of(enc_seg, mine).reshape(ns, tok)[pieces(row_bits)].reshape(-1)
+        segs = jnp.stack([dec_k, pos, enc_k] + [jnp.zeros_like(pos)] * 5).astype(F32)
+
         if fast:
             mats = [self_in, self_out, cross_in, cross_query, cross_out, ffn_up, ffn_down, norm_gain, norm_bias]
-            wa, pack_b = run(
+            wa, wb, wf = run(
                 pack,
                 [(w, None) for w in mats] + [(dev.astype(jnp.int32)[None], SMEM)],
-                [((3, 16, D), BF), ((14, 16, D), BF)],
+                [((3, 16, D), BF), ((6, 16, D), BF), ((8, 16, D), BF)],
                 name="pack",
                 vmem=56,
             )
-            wb = lax.all_gather(pack_b, ("dp", "seq"))
-            wa = wa[None]
+            wa, wb, wf = wa[None], wb[None], wf[None]
             got_x, got_a = flip(zh, [other(inputs), wa])
-            got_x, got_a, away_e = tie(got_x, got_a, other(encoder))
+            got_x, got_a, wb, wf, segs = tie(got_x, got_a, wb, wf, segs)
+            got_b, got_f = flip(zh, [wb, wf])
             xf, wa = jnp.stack([of(inputs, mine), got_x])[None], append(wa, got_a)
+            got_x, got_a = flip(zl, [xf, wa])
+            got_x, got_a, got_b, got_f, away_e = tie(got_x, got_a, got_b, got_f, other(encoder))
+            xf, wa = append(xf, got_x), append(wa, got_a)
+            wb, wf = append(wb, got_b), append(wf, got_f)
+            got_x, got_a = flip(x, [xf, wa])
             got_e, got_t, got_v = flip(zh, [away_e, other(teacher), valid_away])
-            got_x, got_a = flip(zl, [xf, wa])
-            xf, wa = append(xf, got_x), append(wa, got_a)
-            (got_a,) = flip(x, [wa])
-            (got_x,) = flip(x, [xf])
-            wa = append(wa, got_a)
-            wa = append(wa, flip(y, [wa])[0])
-            (wa_far,) = flip(core, [wa])
+            got_b, got_f = swap(y, wb), swap(zl, wf)
             ef = jnp.stack([of(encoder, mine), got_e])[None]
-            got_a, ef = tie(got_a, ef)
-            ef = append(ef, flip(zl, [ef])[0])
-            got_x, ef = tie(got_x, ef)
-            (got_e,) = flip(x, [ef])
-            x_bits = e_bits = (2, 1)
+            got_x, got_a, got_b, got_f, ef = tie(got_x, got_a, got_b, got_f, ef)
+            wa, wb, wf = append(wa, got_a), append(wb, got_b), append(wf, got_f)
+            got_a, got_b, got_e, got_f = swap(y, wa), swap(x, wb), swap(zl, ef), swap(x, wf)
+            wa_far = swap(core, wa)
+            got_a, got_b, got_e, wa_far = tie(got_a, got_b, got_e, wa_far)
+            wa = [wa, got_a, wa_far, swap(core, got_a)]
+            wb, ef = append(wb, got_b), append(ef, got_e)
+            got_b, got_e = swap(zl, wb), swap(x, ef)
+            got_f, wa[3] = tie(got_f, wa[3])
+            wf = append(wf, got_f)
+            got_f = swap(y, wf)
+            wb_far, wf_far = swap(core, wb), swap(core, wf)
         else:
             got_x, got_e, got_t, got_v = flip(
                 ("seq", half), [other(inputs), other(encoder), other(teacher), valid_away]
             )
             xf, ef = jnp.stack([of(inputs, mine), got_x])[None], jnp.stack([of(encoder, mine), got_e])[None]
-            x_bits = e_bits = tuple(1 << b for b in range(half.bit_length() - 1))
-            for bit in x_bits:
+            for bit in row_bits:
                 got_x, got_e = flip(("seq", bit), [xf, ef])
-                if bit != x_bits[-1]:
+                if bit != row_bits[-1]:
                     xf, ef = append(xf, got_x), append(ef, got_e)
 
             def gathered(w):
@@ -492,15 +549,16 @@
                 return w.reshape(G, 16, w.shape[1] // D, D).transpose(0, 2, 1, 3)
 
             wa = grouped(gathered(self_in))
-            norms = lax.dynamic_update_slice(
+            mine_only = lax.dynamic_update_slice(
                 jnp.zeros((16, D), BF), jnp.concatenate([norm_gain, norm_bias], 0), (0, dev * per)
             )
-            all_norms = lax.psum(norms.astype(F32), ("dp", "seq")).astype(BF)
+            all_norms = lax.psum(mine_only.astype(F32), ("dp", "seq")).astype(BF)
             all_norms = jnp.pad(all_norms[None], ((0, G - 1), (0, 0), (0, 0)))[:, None]
             rest = [grouped(gathered(w)) for w in (self_out, cross_in, cross_query, cross_out)]
             down = gathered(ffn_down).reshape(G, 4, 16, D)
-            wb = jnp.concatenate([grouped(gathered(ffn_up)), down] + rest + [all_norms], 1)
-            wa, wa_far = wa[: G // 2], wa[G // 2 :]
+            wb = jnp.concatenate(rest + [all_norms], 1)
+            wf = jnp.concatenate([grouped(gathered(ffn_up)), down], 1)
+            wa, wb, wf = [[w[8 * i : 8 * i + 8] for i in range(4)] for w in (wa, wb, wf)]
         x_near, x_far = xf.reshape(-1, D), got_x.reshape(-1, D)
         teach = jnp.concatenate([of(teacher, mine), got_t], 0)
         valid = jnp.concatenate([of(dec_valid, mine).astype(F32), got_v[0, :tok].astype(F32)])[:, None]
@@ -512,58 +570,66 @@
             i16 = jnp.arange(16, dtype=jnp.int32)
             g32 = jnp.arange(32, dtype=jnp.int32)
             dev16 = (dp_at >> 1) * 8 + seq_at
+
+            def came_from(bits):
+                return dev ^ sum((((g32 >> i) & 1) * b for i, b in enumerate(bits)))
+
             ids = jnp.concatenate(
                 [
                     jnp.stack([dp_at & 1, dev]).astype(jnp.int32),
                     spread(i16 ^ dev16, (4, 2, 1, 8)),
                     spread(i16 ^ dev16, (4, 2, 1, 8)),
-                    spread(g32 ^ dev, (4, 2, 1, 16, 8)),
+                    came_from((4, 2, 1, 16, 8)),
+                    came_from((4, 16, 1, 2, 8)),
+                    came_from((4, 2, 1, 16, 8)),
                 ]
             )
         else:
             i16, g32 = jnp.arange(16, dtype=jnp.int32), jnp.arange(32, dtype=jnp.int32)
-            ids = jnp.concatenate([jnp.stack([0 * dev, dev]).astype(jnp.int32), i16, i16, g32])
-
-        slots = jnp.arange(half, dtype=jnp.int32)
-
-        def pieces(bits):
-            masks = sum((((slots >> i) & 1) * b) for i, b in enumerate(bits))[:, None]
-            return (seq_at ^ masks ^ jnp.array([[0, half]], jnp.int32)).reshape(-1)
-
-        pos = (pieces(x_bits)[:, None] * tok + jnp.arange(tok, dtype=jnp.int32)[None]).reshape(-1)
-        dec_k = of(dec_seg, mine).reshape(ns, tok)[pieces(x_bits)].reshape(-1)
-        enc_k = of(enc_seg, mine).reshape(ns, tok)[pieces(e_bits)].reshape(-1)
-        dec_q = dec_k[:rows]
-        ok_self = (dec_k[:, None] == dec_q[None]) & (pos[:, None] <= pos[None, :rows])
-        ok_cross = enc_k[:, None] == dec_q[None]
-        mask_self = jnp.where(ok_self, 0.0, NEG).astype(F32)
-        mask_cross = jnp.where(ok_cross, 0.0, NEG).astype(F32)
+            ids = jnp.concatenate([jnp.stack([0 * dev, dev]).astype(jnp.int32), i16, i16, g32, g32, g32])
 
         sm = (ids, SMEM)
         p_shape = (HEADS, length, rows)
-        xf, q1, kv1, p1, rl1, at1 = run(
+        def held(*shapes):
+            return (
+                [pltpu.VMEM((length, rows), F32)]
+                + [pltpu.VMEM(v, BF) for v in shapes]
+                + [pltpu.VMEM((2, 2, length, rows), BF), pltpu.SemaphoreType.DMA((2,)), pltpu.SemaphoreType.DMA((4,))]
+            )
+
+        all_rows, own_rows, both_kv = (length, D), (rows, D), (length, 2 * D)
+        own_x = x_near[:rows]
+        xf, wa, q1, kv1, p1, rl1, at1 = run(
             functools.partial(self_forward, rows),
-            [sm, (x_near, None), (x_far, None), (wa, None), (wa_far, None), (mask_self, None)],
-            [((length, D), BF), ((rows, D), BF), ((length, 2 * D), BF), (p_shape, BF), ((HEADS, 1, rows), F32), ((D, rows), BF)],
+            [sm, (x_near, None), (x_far, None)] + [(v, None) for v in wa] + [(segs, None)],
+            [(all_rows, BF, True), ((3, D, D), BF, True), (own_rows, BF, True), (both_kv, BF, True),
+             (p_shape, BF, True), ((HEADS, 1, rows), F32), ((D, rows), BF)],
+            scratch=held(all_rows, (3, D, D), own_rows, both_kv),
             name="self_forward",
         )
-        got_e, at1 = tie(got_e, at1)
+        if fast:
+            got_b, got_e, wb_far, at1 = tie(got_b, got_e, wb_far, at1)
+            wb = [wb, got_b, wb_far, swap(core, got_b)]
         e_near, e_far = ef.reshape(-1, D), got_e.reshape(-1, D)
-        ef, xh1, rs1, low1, q2, kv2, p2, rl2, at2 = run(
+        ef, wb, norms, xh1, rs1, low1, q2, kv2, p2, rl2, at2 = run(
             functools.partial(cross_forward, rows),
-            [sm, (xf, None), (e_near, None), (e_far, None), (at1, None), (wb, chunks(8, 4)), (wb, chunks(13, 1)),
-             (mask_cross, None)],
-            [((length, D), BF), ((rows, D), F32), ((rows, 1), F32), ((rows, D), BF), ((rows, D), BF), ((length, 2 * D), BF),
-             (p_shape, BF), ((HEADS, 1, rows), F32), ((D, rows), BF)],
+            [sm, (own_x, None), (e_near, None), (e_far, None), (at1, None)] + [(v, None) for v in wb] + [(segs, None)],
+            [(all_rows, BF, True), ((5, D, D), BF), ((16, D), F32), (own_rows, F32), ((rows, 1), F32),
+             (own_rows, BF, True), (own_rows, BF, True), (both_kv, BF, True), (p_shape, BF, True),
+             ((HEADS, 1, rows), F32), ((D, rows), BF)],
+            scratch=held(all_rows, own_rows, own_rows, both_kv),
             name="cross_forward",
         )
+        if fast:
+            got_f, wf_far, at2 = tie(got_f, wf_far, at2)
+            wf = [wf, got_f, wf_far, swap(core, got_f)]
         out, small, d_r2, d_mix2, keep1, send1 = run(
             ffn_both,
-            [sm, (xh1, None), (at2, None), (teach, None), (valid, None), (wb, chunks(0, 4)), (wb, chunks(4, 4)),
-             (wb, chunks(12, 1)), (wb, chunks(13, 1))],
+            [sm, (xh1, None), (at2, None), (teach, None), (valid, None), (wb, None), (norms, None)]
+            + [(v, None) for v in wf],
             [((rows, D), BF), ((16, D), F32), ((rows, D), F32), ((rows, D), BF)] + [((2304, D), BF)] * 2,
             scratch=[pltpu.VMEM((rows, FF), BF), pltpu.VMEM((4, rows, D), F32), pltpu.VMEM((rows, D), BF),
-                     pltpu.VMEM((4, D, D), BF)],
+                     pltpu.VMEM((4, D, D), BF), pltpu.VMEM((FF, D), BF)],
             name="ffn_both",
         )
 
@@ -571,7 +637,7 @@
         d_rows = [pltpu.VMEM((HALF, rows), F32)]
         both_scratch = [pltpu.VMEM((length, D), BF)] + d_rows
         row_parts = [((rows, D), F32)] + [((rows, D), BF)] * (half - 1)
-        partners = [sum(((i >> k) & 1) * b for k, b in enumerate(x_bits)) for i in range(1, half)]
+        partners = [sum(((i >> k) & 1) * b for k, b in enumerate(row_bits)) for i in range(1, half)]
 
         if fast:
             got1 = swap(core, send1)
@@ -588,7 +654,7 @@
         e_own, *rest = run(
             functools.partial(cross_back_b, half - 1),
             [sm, (ef, None), (q2, None), (kv2, None), (p2, None), (rl2, None), (d_mix2, None),
-             (dkv2, None), (dq2, None), (wb, chunks(8, 4)), (wb, chunks(13, 1)), (d_r2, None), (low1, None),
+             (dkv2, None), (dq2, None), (wb, None), (norms, None), (d_r2, None), (low1, None),
              (xh1, None), (rs1, None), (at1, None), (small, None)],
             row_parts + [((rows, D), BF), ((rows, D), F32), ((1024, D), BF), ((1040, D), BF)],
             scratch=both_scratch,
@@ -619,7 +685,7 @@
         x_own, *rest = run(
             functools.partial(self_back_b, half - 1, rows),
             [sm, (xf, None), (q1, None), (kv1, None), (p1, None), (rl1, None), (d_mix1, None),
-             (dkv1, None), (dq1, None), (wa, None), (wa_far, None), (d_r1, None)],
+             (dkv1, None), (dq1, None), (wa, None), (d_r1, None)],
             row_parts + [((768, D), BF)] * 2,
             scratch=both_scratch,
             name="self_back_b",

time: 237 us -> 221 us (0.932)
  starting transfers between devices: 36.9 us -> 57.6 us
  waiting for transfers between devices: 102 us -> 81.5 us
  between operations: 14.5 us -> 1.35 us
  Pallas kernels: 52.8 us -> 57.1 us
  local copies, waits for them, and re-layouts: 22.8 us -> 18.6 us
  other arithmetic: 7.19 us -> 4.48 us
    ppermute x30 -> x41, starting transfers between devices: 36.8 us -> 57.6 us  [flip(): lax.ppermute(flat[0] if len(flat) == 1 else jnp.concatenate(flat, 0), axi...]
    all_gather x1 -> x0, waiting for transfers between devices: 15.9 us -> none  [shards(): wb = lax.all_gather(pack_b, ('dp', 'seq'))]
    unnamed x58 -> x68, local copies, waits for them, and re-layouts: 17.1 us -> 12.1 us
    ppermute x30 -> x41, waiting for transfers between devices: 86.2 us -> 81.5 us  [flip(): lax.ppermute(flat[0] if len(flat) == 1 else jnp.concatenate(flat, 0), axi...]
    pallas_call x15, Pallas kernels: 52.8 us -> 57.1 us  [call(): pl.pallas_call(body, grid=(1,), in_specs=[whole(a.shape) if s is None els...]
  transfers between devices with their start and end apart: 31 -> 41, of which waited for: 19 -> 20; matrix products, arithmetic and copies ran while one was open for 5% -> 5% of each run, Pallas kernels for 13% -> 20%
where the time goes in v5:
time: 221 us
  waiting for transfers between devices  81.5 us (37%)
  starting transfers between devices  57.6 us (26%)
  Pallas kernels  57.1 us (26%)
  local copies, waits for them, and re-layouts  18.6 us (8%)
  other arithmetic  4.48 us (2%)
    ppermute x41, waiting for transfers between devices, flip(): lax.ppermute(flat[0] if len(flat) == 1 else jnp.concatenate(flat, 0), axi...  81.5 us
    ppermute x41, starting transfers between devices, flip(): lax.ppermute(flat[0] if len(flat) == 1 else jnp.concatenate(flat, 0), axi...  57.6 us
    pallas_call x15, Pallas kernels, call(): pl.pallas_call(body, grid=(1,), in_specs=[whole(a.shape) if s is None els...  57.1 us
    unnamed x68, local copies, waits for them, and re-layouts  12.1 us
  transfers between devices with their start and end apart: 41, of which 20 were waited for; matrix products, arithmetic and copies ran while one was open for 5% of the time, Pallas kernels for 20%

profile of v5, /device:TPU:0, one launch (start us, length us, event | category | flops | bytes accessed | tf_op | source)
XLA Modules:
  0.0 220.6 jit_solution(14261870758681346981)
XLA Ops:
  4.4 4.1 %collective-permute-start = (bf16[176,512]{1,0:T(8,128)(2,1)S(1)}, bf16[176,512]{1,0:T(8,128)(2,1)S(1)}, u32[]{:S(2)}, u32[]{:S(2)}) collective-permute-start(bf16[176,512]{1,0:T(8,128)(2,1)S(1)} %pad_maximum_fusion.13), channel_id=1, source_target_pairs={{0,4},{1,5},{2,6},{3,7},{4,0},{5,1},{6,2},{7,3},{8,12},{9,13},{10,... | collective-permute-start | bytes 540680 | tf_op jit(solution)/shard_map/ppermute | solution.py:465
  10.8 6.2 %collective-permute-done = bf16[176,512]{1,0:T(8,128)(2,1)S(1)} collective-permute-done((bf16[176,512]{1,0:T(8,128)(2,1)S(1)}, bf16[176,512]{1,0:T(8,128)(2,1)S(1)}, u32[]{:S(2)}, u32[]{:S(2)}) %collective-permute-start) | collective-permute-done | bytes 180256 | tf_op jit(solution)/shard_map/ppermute | solution.py:465
  18.7 3.4 %collective-permute-start.2 = (bf16[224,512]{1,0:T(8,128)(2,1)S(1)}, bf16[224,512]{1,0:T(8,128)(2,1)S(1)}, u32[]{:S(2)}, u32[]{:S(2)}) collective-permute-start(bf16[224,512]{1,0:T(8,128)(2,1)S(1)} %pad_maximum_fusion.10), channel_id=1, source_target_pairs={{0,4},{1,5},{2,6},{3,7},{4,0},{5,1},{6,2},{7,3},{8,12},{9,13},{10,... | collective-permute-start | bytes 688136 | tf_op jit(solution)/shard_map/ppermute | solution.py:465
  22.9 8.5 %collective-permute-done.2 = bf16[224,512]{1,0:T(8,128)(2,1)S(1)} collective-permute-done((bf16[224,512]{1,0:T(8,128)(2,1)S(1)}, bf16[224,512]{1,0:T(8,128)(2,1)S(1)}, u32[]{:S(2)}, u32[]{:S(2)}) %collective-permute-start.2) | collective-permute-done | bytes 229408 | tf_op jit(solution)/shard_map/ppermute | solution.py:465
  40.8 7.5 %collective-permute-done.6 = bf16[272,512]{1,0:T(8,128)(2,1)S(1)} collective-permute-done((bf16[272,512]{1,0:T(8,128)(2,1)S(1)}, bf16[272,512]{1,0:T(8,128)(2,1)S(1)}, u32[]{:S(2)}, u32[]{:S(2)}) %collective-permute-start.6) | collective-permute-done | bytes 278560 | tf_op jit(solution)/shard_map/ppermute | solution.py:465
  53.0 4.4 %collective-permute-start.9 = (bf16[256,512]{1,0:T(8,128)(2,1)S(1)}, bf16[256,512]{1,0:T(8,128)(2,1)S(1)}, u32[]{:S(2)}, u32[]{:S(2)}) collective-permute-start(bf16[256,512]{1,0:T(8,128)(2,1)S(1)} %bitcast.108), channel_id=1, source_target_pairs={{0,2},{1,3},{2,0},{3,1},{4,6},{5,7},{6,4},{7,5},{8,10},{9,11},{10,... | collective-permute-start | bytes 786440 | tf_op jit(solution)/shard_map/ppermute | solution.py:465
  59.4 4.4 %collective-permute-done.9 = bf16[256,512]{1,0:T(8,128)(2,1)S(1)} collective-permute-done((bf16[256,512]{1,0:T(8,128)(2,1)S(1)}, bf16[256,512]{1,0:T(8,128)(2,1)S(1)}, u32[]{:S(2)}, u32[]{:S(2)}) %collective-permute-start.9) | collective-permute-done | bytes 262176 | tf_op jit(solution)/shard_map/ppermute | solution.py:465
  64.6 3.5 %collective-permute-start.11 = (bf16[768,512]{1,0:T(8,128)(2,1)}, bf16[768,512]{1,0:T(8,128)(2,1)}, u32[]{:S(2)}, u32[]{:S(2)}) collective-permute-start(bf16[768,512]{1,0:T(8,128)(2,1)} %bitcast.45), channel_id=1, source_target_pairs={{0,2},{1,3},{2,0},{3,1},{4,6},{5,7},{6,4},{7,5},{8,10},{9,11},{10,... | collective-permute-start | bytes 2359304 | tf_op jit(solution)/shard_map/ppermute | solution.py:465
  78.4 9.8 %self_forward.1 = (bf16[1024,512]{1,0:T(8,128)(2,1)}, bf16[3,512,512]{2,1,0:T(8,128)(2,1)}, bf16[256,512]{1,0:T(8,128)(2,1)}, bf16[1024,1024]{1,0:T(8,128)(2,1)}...) custom-call(s32[130]{0:T(256)S(1)} %concatenate.63.ids, ...), custom_call_target="tpu_custom_call" | custom-call | flops 1000 | bytes 1000 | tf_op jit(solution)/shard_map/self_forward/pallas_call | solution.py:42
  93.7 11.2 %cross_forward.1 = (bf16[1024,512]{1,0:T(8,128)(2,1)}, bf16[5,512,512]{2,1,0:T(8,128)(2,1)S(1)}, f32[16,512]{1,0:T(8,128)S(1)}, f32[256,512]{1,0:T(8,128)S(1)}, ...) custom-call(s32[130]{0:T(256)S(1)} %concatenate.63.ids, ...), custom_call_target="tpu_custom_call" | custom-call | flops 1000 | bytes 1000 | tf_op jit(solution)/shard_map/cross_forward/pallas_call | solution.py:42
  110.2 8.4 %ffn_both.1 = (bf16[256,512]{1,0:T(8,128)(2,1)S(1)}, f32[16,512]{1,0:T(8,128)S(1)}, f32[256,512]{1,0:T(8,128)S(1)}, bf16[256,512]{1,0:T(8,128)(2,1)S(1)}, bf16[2...) custom-call(s32[130]{0:T(256)S(1)} %concatenate.63.ids, f32[256,512]{1,0:T(8,128)S(1)} %get-tuple-element.156.xh1, ...), custom_call_target="tpu_custom_call" | custom-call | flops 1000 | bytes 1000 | tf_op jit(solution)/shard_map/ffn_both/pallas_call | solution.py:42
  118.9 4.2 %cross_back_a.1 = (bf16[1024,512]{1,0:T(8,128)(2,1)S(1)}, bf16[256,256]{1,0:T(8,128)(2,1)S(1)}) custom-call(bf16[256,512]{1,0:T(8,128)(2,1)S(1)} %copy-done.12, bf16[1024,1024]{1,0:T(8,128)(2,1)S(1)} %copy-done.3, bf16[8,1024,256]{2,1,0:T(8,128)(2,1)S(1)} %copy-done, f32[8,1,256]{2,1,0:T(1,128)S(1)} %get-tuple-element.170.rl, ...), custom_call_target="tpu_custom_call" | custom-call | flops 1000 | bytes 1000 | tf_op jit(solution)/shard_map/cross_back_a/pallas_call | solution.py:42
  125.2 7.4 %cross_back_b.1 = (f32[256,512]{1,0:T(8,128)S(1)}, bf16[256,512]{1,0:T(8,128)(2,1)S(1)}, bf16[256,512]{1,0:T(8,128)(2,1)S(1)}, bf16[256,512]{1,0:T(8,128)(2,1)S(...) custom-call(s32[130]{0:T(256)S(1)} %concatenate.63.ids, ...), custom_call_target="tpu_custom_call" | custom-call | flops 1000 | bytes 1000 | tf_op jit(solution)/shard_map/cross_back_b/pallas_call | solution.py:42
  132.7 4.3 %collective-permute-start.23 = (bf16[256,512]{1,0:T(8,128)(2,1)S(1)}, bf16[256,512]{1,0:T(8,128)(2,1)S(1)}, u32[]{:S(2)}, u32[]{:S(2)}) collective-permute-start(bf16[256,512]{1,0:T(8,128)(2,1)S(1)} %get-tuple-element.188), channel_id=1, source_target_pairs={{0,2},{1,3},{2,0},{3,1},{4,6},{5,7},{6,4},{7,5},{8,10},{9,11},{10,... | collective-permute-start | bytes 786440 | tf_op jit(solution)/shard_map/ppermute | solution.py:465
  138.6 3.9 %self_back_a.1 = (bf16[1024,512]{1,0:T(8,128)(2,1)S(1)}, bf16[256,256]{1,0:T(8,128)(2,1)S(1)}) custom-call(bf16[256,512]{1,0:T(8,128)(2,1)S(1)} %copy-done.9, bf16[1024,1024]{1,0:T(8,128)(2,1)S(1)} %copy-done.2, bf16[8,1024,256]{2,1,0:T(8,128)(2,1)S(1)} %copy-done.1, f32[8,1,256]{2,1,0:T(1,128)S(1)} %get-tuple-element.186.rl, ...), custom_call_target="tpu_custom_call" | custom-call | flops 1000 | bytes 1000 | tf_op jit(solution)/shard_map/self_back_a/pallas_call | solution.py:42
  144.2 6.8 %collective-permute-done.24.refs_2_ = bf16[256,512]{1,0:T(8,128)(2,1)S(1)} collective-permute-done((bf16[256,512]{1,0:T(8,128)(2,1)S(1)}, bf16[256,512]{1,0:T(8,128)(2,1)S(1)}, u32[]{:S(2)}, u32[]{:S(2)}) %collective-permute-start.24) | collective-permute-done | bytes 262176 | tf_op jit(solution)/shard_map/ppermute | solution.py:465
  153.8 4.2 %collective-permute-start.26 = (bf16[288,512]{1,0:T(8,128)(2,1)S(1)}, bf16[288,512]{1,0:T(8,128)(2,1)S(1)}, u32[]{:S(2)}, u32[]{:S(2)}) collective-permute-start(bf16[288,512]{1,0:T(8,128)(2,1)S(1)} %get-tuple-element.194), channel_id=1, source_target_pairs={{0,2},{1,3},{2,0},{3,1},{4,6},{5,7},{6,4},{7,5},{8,10},{9,11},{10,... | collective-permute-start | bytes 884744 | tf_op jit(solution)/shard_map/ppermute | solution.py:465
  159.5 7.2 %self_back_b.1 = (f32[256,512]{1,0:T(8,128)S(1)}, bf16[256,512]{1,0:T(8,128)(2,1)S(1)}, bf16[256,512]{1,0:T(8,128)(2,1)S(1)}, bf16[256,512]{1,0:T(8,128)(2,1)S(1...) custom-call(s32[130]{0:T(256)S(1)} %concatenate.63.ids, bf16[1024,512]{1,0:T(8,128)(2,1)S(1)} %copy-done.7, ...), custom_call_target="tpu_custom_call" | custom-call | flops 1000 | bytes 1000 | tf_op jit(solution)/shard_map/self_back_b/pallas_call | solution.py:42
  166.8 5.3 %collective-permute-done.27.refs_9_.refs_5_ = bf16[288,512]{1,0:T(8,128)(2,1)S(1)} collective-permute-done((bf16[288,512]{1,0:T(8,128)(2,1)S(1)}, bf16[288,512]{1,0:T(8,128)(2,1)S(1)}, u32[]{:S(2)}, u32[]{:S(2)}) %collective-permute-start.27) | collective-permute-done | bytes 294944 | tf_op jit(solution)/shard_map/ppermute | solution.py:465
  180.3 5.5 %collective-permute-done.36.refs_5_.refs_8_.refs_22_ = bf16[384,512]{1,0:T(8,128)(2,1)S(1)} collective-permute-done((bf16[384,512]{1,0:T(8,128)(2,1)S(1)}, bf16[384,512]{1,0:T(8,128)(2,1)S(1)}, u32[]{:S(2)}, u32[]{:S(2)}) %collective-permute-start.36) | collective-permute-done | bytes 393248 | tf_op jit(solution)/shard_map/ppermute | solution.py:465
  191.3 8.3 %collective-permute-done.33.refs_3_ = bf16[256,512]{1,0:T(8,128)(2,1)S(1)} collective-permute-done((bf16[256,512]{1,0:T(8,128)(2,1)S(1)}, bf16[256,512]{1,0:T(8,128)(2,1)S(1)}, u32[]{:S(2)}, u32[]{:S(2)}) %collective-permute-start.33) | collective-permute-done | bytes 262176 | tf_op jit(solution)/shard_map/ppermute | solution.py:465
  201.3 6.4 %collective-permute-done.39.refs_5_.refs_19_ = bf16[240,512]{1,0:T(8,128)(2,1)S(1)} collective-permute-done((bf16[240,512]{1,0:T(8,128)(2,1)S(1)}, bf16[240,512]{1,0:T(8,128)(2,1)S(1)}, u32[]{:S(2)}, u32[]{:S(2)}) %collective-permute-start.39) | collective-permute-done | bytes 245792 | tf_op jit(solution)/shard_map/ppermute | solution.py:465
  207.7 3.2 %collective-permute-done.37.refs_3_.refs_17_ = bf16[240,512]{1,0:T(8,128)(2,1)S(1)} collective-permute-done((bf16[240,512]{1,0:T(8,128)(2,1)S(1)}, bf16[240,512]{1,0:T(8,128)(2,1)S(1)}, u32[]{:S(2)}, u32[]{:S(2)}) %collective-permute-start.37) | collective-permute-done | bytes 245792 | tf_op jit(solution)/shard_map/ppermute | solution.py:465
  211.3 7.3 %collective-permute-done.40.refs_13_ = bf16[128,512]{1,0:T(8,128)(2,1)S(1)} collective-permute-done((bf16[128,512]{1,0:T(8,128)(2,1)S(1)}, bf16[128,512]{1,0:T(8,128)(2,1)S(1)}, u32[]{:S(2)}, u32[]{:S(2)}) %collective-permute-start.40) | collective-permute-done | bytes 131104 | tf_op jit(solution)/shard_map/ppermute | solution.py:465
  (196 shorter events, 73.6 us)
Async XLA Ops:
  17.9 14.6 %collective-permute-start.1 = (bf16[352,512]{1,0:T(8,128)(2,1)S(1)}, bf16[352,512]{1,0:T(8,128)(2,1)S(1)}, u32[]{:S(2)}, u32[]{:S(2)}) collective-permute-start(bf16[352,512]{1,0:T(8,128)(2,1)S(1)} %pad_maximum_fusion.6), channel_id=1, source_target_pairs={{0,2},{1,3},{2,0},{3,1},{4,6},{5,7},{6,4},{7,5},{8,10},{9,11},{10,... | collective-permute-start | bytes 1081352 | tf_op jit(solution)/shard_map/ppermute | solution.py:465
  32.6 16.5 %collective-permute-start.3 = (bf16[704,512]{1,0:T(8,128)(2,1)S(1)}, bf16[704,512]{1,0:T(8,128)(2,1)S(1)}, u32[]{:S(2)}, u32[]{:S(2)}) collective-permute-start(bf16[704,512]{1,0:T(8,128)(2,1)S(1)} %pad_maximum_fusion), channel_id=1, source_target_pairs={{0,1},{1,0},{2,3},{3,2},{4,5},{5,4},{6,7},{7,6},{8,9},{9,8},{10,11... | collective-permute-start | bytes 2162696 | tf_op jit(solution)/shard_map/ppermute | solution.py:465
  34.0 14.4 %collective-permute-start.6 = (bf16[272,512]{1,0:T(8,128)(2,1)S(1)}, bf16[272,512]{1,0:T(8,128)(2,1)S(1)}, u32[]{:S(2)}, u32[]{:S(2)}) collective-permute-start(bf16[272,512]{1,0:T(8,128)(2,1)S(1)} %fusion.1), channel_id=1, source_target_pairs={{0,4},{1,5},{2,6},{3,7},{4,0},{5,1},{6,2},{7,3},{8,12},{9,13},{10,... | collective-permute-start | bytes 835592 | tf_op jit(solution)/shard_map/ppermute | solution.py:465
  49.3 14.5 %collective-permute-start.10 = (bf16[384,512]{1,0:T(8,128)(2,1)S(1)}, bf16[384,512]{1,0:T(8,128)(2,1)S(1)}, u32[]{:S(2)}, u32[]{:S(2)}) collective-permute-start(bf16[384,512]{1,0:T(8,128)(2,1)S(1)} %bitcast.86), channel_id=1, source_target_pairs={{0,8},{8,0},{16,24},{24,16},{1,9},{9,1},{17,25},{25,17},{2,10},{10... | collective-permute-start | bytes 1179656 | tf_op jit(solution)/shard_map/ppermute | solution.py:465
  49.4 14.4 %collective-permute-start.7 = (bf16[384,512]{1,0:T(8,128)(2,1)S(1)}, bf16[384,512]{1,0:T(8,128)(2,1)S(1)}, u32[]{:S(2)}, u32[]{:S(2)}) collective-permute-start(bf16[384,512]{1,0:T(8,128)(2,1)S(1)} %bitcast.87), channel_id=1, source_target_pairs={{0,16},{8,24},{16,0},{24,8},{1,17},{9,25},{17,1},{25,9},{2,18},{10... | collective-permute-start | bytes 1179656 | tf_op jit(solution)/shard_map/ppermute | solution.py:465
  51.0 12.8 %collective-permute-start.8 = (bf16[384,512]{1,0:T(8,128)(2,1)S(1)}, bf16[384,512]{1,0:T(8,128)(2,1)S(1)}, u32[]{:S(2)}, u32[]{:S(2)}) collective-permute-start(bf16[384,512]{1,0:T(8,128)(2,1)S(1)} %bitcast.127), channel_id=1, source_target_pairs={{0,1},{1,0},{2,3},{3,2},{4,5},{5,4},{6,7},{7,6},{8,9},{9,8},{10,11... | collective-permute-start | bytes 1179656 | tf_op jit(solution)/shard_map/ppermute | solution.py:465
  58.1 16.1 %collective-permute-start.14 = (bf16[512,512]{1,0:T(8,128)(2,1)S(1)}, bf16[512,512]{1,0:T(8,128)(2,1)S(1)}, u32[]{:S(2)}, u32[]{:S(2)}) collective-permute-start(bf16[512,512]{1,0:T(8,128)(2,1)S(1)} %bitcast.124), channel_id=1, source_target_pairs={{0,1},{1,0},{2,3},{3,2},{4,5},{5,4},{6,7},{7,6},{8,9},{9,8},{10,11... | collective-permute-start | bytes 1572872 | tf_op jit(solution)/shard_map/ppermute | solution.py:465
  64.6 24.5 %collective-permute-start.13 = (bf16[768,512]{1,0:T(8,128)(2,1)}, bf16[768,512]{1,0:T(8,128)(2,1)}, u32[]{:S(2)}, u32[]{:S(2)}) collective-permute-start(bf16[768,512]{1,0:T(8,128)(2,1)} %bitcast.45), channel_id=1, source_target_pairs={{0,8},{8,0},{16,24},{24,16},{1,9},{9,1},{17,25},{25,17},{2,10},{10... | collective-permute-start | bytes 2359304 | tf_op jit(solution)/shard_map/ppermute | solution.py:465
  64.6 24.5 %collective-permute-start.11 = (bf16[768,512]{1,0:T(8,128)(2,1)}, bf16[768,512]{1,0:T(8,128)(2,1)}, u32[]{:S(2)}, u32[]{:S(2)}) collective-permute-start(bf16[768,512]{1,0:T(8,128)(2,1)} %bitcast.45), channel_id=1, source_target_pairs={{0,2},{1,3},{2,0},{3,1},{4,6},{5,7},{6,4},{7,5},{8,10},{9,11},{10,... | collective-permute-start | bytes 2359304 | tf_op jit(solution)/shard_map/ppermute | solution.py:465
  69.1 19.2 %collective-permute-start.12 = (bf16[512,512]{1,0:T(8,128)(2,1)S(1)}, bf16[512,512]{1,0:T(8,128)(2,1)S(1)}, u32[]{:S(2)}, u32[]{:S(2)}) collective-permute-start(bf16[512,512]{1,0:T(8,128)(2,1)S(1)} %bitcast.84), channel_id=1, source_target_pairs={{0,1},{1,0},{2,3},{3,2},{4,5},{5,4},{6,7},{7,6},{8,9},{9,8},{10,11... | collective-permute-start | bytes 1572872 | tf_op jit(solution)/shard_map/ppermute | solution.py:465
  75.8 30.4 %collective-permute-start.18 = (bf16[1024,512]{1,0:T(8,128)(2,1)}, bf16[1024,512]{1,0:T(8,128)(2,1)}, u32[]{:S(2)}, u32[]{:S(2)}) collective-permute-start(bf16[1024,512]{1,0:T(8,128)(2,1)} %bitcast.57), channel_id=1, source_target_pairs={{0,8},{8,0},{16,24},{24,16},{1,9},{9,1},{17,25},{25,17},{2,10},{10... | collective-permute-start | bytes 3145736 | tf_op jit(solution)/shard_map/ppermute | solution.py:465
  75.8 30.4 %collective-permute-start.17 = (bf16[1024,512]{1,0:T(8,128)(2,1)}, bf16[1024,512]{1,0:T(8,128)(2,1)}, u32[]{:S(2)}, u32[]{:S(2)}) collective-permute-start(bf16[1024,512]{1,0:T(8,128)(2,1)} %bitcast.57), channel_id=1, source_target_pairs={{0,16},{8,24},{16,0},{24,8},{1,17},{9,25},{17,1},{25,9},{2,18},{10... | collective-permute-start | bytes 3145736 | tf_op jit(solution)/shard_map/ppermute | solution.py:465
  123.6 28.2 %collective-permute-start.22 = (bf16[1152,512]{1,0:T(8,128)(2,1)S(1)}, bf16[1152,512]{1,0:T(8,128)(2,1)S(1)}, u32[]{:S(2)}, u32[]{:S(2)}) collective-permute-start(bf16[1152,512]{1,0:T(8,128)(2,1)S(1)} %add_convert_fusion), channel_id=1, source_target_pairs={{0,16},{8,24},{16,0},{24,8},{1,17},{9,25},{17,1},{25,9},{2,18},{10... | collective-permute-start | bytes 3538952 | tf_op jit(solution)/shard_map/ppermute | solution.py:465
  132.6 18.4 %collective-permute-start.21 = (bf16[1040,512]{1,0:T(8,128)(2,1)S(1)}, bf16[1040,512]{1,0:T(8,128)(2,1)S(1)}, u32[]{:S(2)}, u32[]{:S(2)}) collective-permute-start(bf16[1040,512]{1,0:T(8,128)(2,1)S(1)} %get-tuple-element.181.refs_2_), channel_id=1, source_target_pairs={{0,8},{8,0},{16,24},{24,16},{1,9},{9,1},{17,25},{25,17},{2,10},{10... | collective-permute-start | bytes 3194888 | tf_op jit(solution)/shard_map/ppermute | solution.py:465
  137.0 14.0 %collective-permute-start.24 = (bf16[256,512]{1,0:T(8,128)(2,1)S(1)}, bf16[256,512]{1,0:T(8,128)(2,1)S(1)}, u32[]{:S(2)}, u32[]{:S(2)}) collective-permute-start(bf16[256,512]{1,0:T(8,128)(2,1)S(1)} %get-tuple-element.189), channel_id=1, source_target_pairs={{0,1},{1,0},{2,3},{3,2},{4,5},{5,4},{6,7},{7,6},{8,9},{9,8},{10,11... | collective-permute-start | bytes 786440 | tf_op jit(solution)/shard_map/ppermute | solution.py:465
  152.2 19.9 %collective-permute-start.29 = (bf16[528,512]{1,0:T(8,128)(2,1)S(1)}, bf16[528,512]{1,0:T(8,128)(2,1)S(1)}, u32[]{:S(2)}, u32[]{:S(2)}) collective-permute-start(bf16[528,512]{1,0:T(8,128)(2,1)S(1)} %get-tuple-element.197.refs_6_), channel_id=1, source_target_pairs={{0,16},{8,24},{16,0},{24,8},{1,17},{9,25},{17,1},{25,9},{2,18},{10... | collective-permute-start | bytes 1622024 | tf_op jit(solution)/shard_map/ppermute | solution.py:465
  153.8 13.0 %collective-permute-start.26 = (bf16[288,512]{1,0:T(8,128)(2,1)S(1)}, bf16[288,512]{1,0:T(8,128)(2,1)S(1)}, u32[]{:S(2)}, u32[]{:S(2)}) collective-permute-start(bf16[288,512]{1,0:T(8,128)(2,1)S(1)} %get-tuple-element.194), channel_id=1, source_target_pairs={{0,2},{1,3},{2,0},{3,1},{4,6},{5,7},{6,4},{7,5},{8,10},{9,11},{10,... | collective-permute-start | bytes 884744 | tf_op jit(solution)/shard_map/ppermute | solution.py:465
  158.0 14.1 %collective-permute-start.27 = (bf16[288,512]{1,0:T(8,128)(2,1)S(1)}, bf16[288,512]{1,0:T(8,128)(2,1)S(1)}, u32[]{:S(2)}, u32[]{:S(2)}) collective-permute-start(bf16[288,512]{1,0:T(8,128)(2,1)S(1)} %get-tuple-element.195), channel_id=1, source_target_pairs={{0,1},{1,0},{2,3},{3,2},{4,5},{5,4},{6,7},{7,6},{8,9},{9,8},{10,11... | collective-permute-start | bytes 884744 | tf_op jit(solution)/shard_map/ppermute | solution.py:465
  175.1 13.2 %collective-permute-start.31 = (bf16[256,512]{1,0:T(8,128)(2,1)S(1)}, bf16[256,512]{1,0:T(8,128)(2,1)S(1)}, u32[]{:S(2)}, u32[]{:S(2)}) collective-permute-start(bf16[256,512]{1,0:T(8,128)(2,1)S(1)} %get-tuple-element.219), channel_id=1, source_target_pairs={{0,2},{1,3},{2,0},{3,1},{4,6},{5,7},{6,4},{7,5},{8,10},{9,11},{10,... | collective-permute-start | bytes 786440 | tf_op jit(solution)/shard_map/ppermute | solution.py:465
  177.1 34.1 %collective-permute-start.30 = (bf16[400,512]{1,0:T(8,128)(2,1)S(1)}, bf16[400,512]{1,0:T(8,128)(2,1)S(1)}, u32[]{:S(2)}, u32[]{:S(2)}) collective-permute-start(bf16[400,512]{1,0:T(8,128)(2,1)S(1)} %get-tuple-element.216), channel_id=1, source_target_pairs={{0,4},{1,5},{2,6},{3,7},{4,0},{5,1},{6,2},{7,3},{8,12},{9,13},{10,... | collective-permute-start | bytes 1228808 | tf_op jit(solution)/shard_map/ppermute | solution.py:465
  178.5 21.1 %collective-permute-start.33 = (bf16[256,512]{1,0:T(8,128)(2,1)S(1)}, bf16[256,512]{1,0:T(8,128)(2,1)S(1)}, u32[]{:S(2)}, u32[]{:S(2)}) collective-permute-start(bf16[256,512]{1,0:T(8,128)(2,1)S(1)} %get-tuple-element.221), channel_id=1, source_target_pairs={{0,3},{1,2},{2,1},{3,0},{4,7},{5,6},{6,5},{7,4},{8,11},{9,10},{10,... | collective-permute-start | bytes 786440 | tf_op jit(solution)/shard_map/ppermute | solution.py:465
  186.0 15.3 %collective-permute-start.38 = (bf16[240,512]{1,0:T(8,128)(2,1)S(1)}, bf16[240,512]{1,0:T(8,128)(2,1)S(1)}, u32[]{:S(2)}, u32[]{:S(2)}) collective-permute-start(bf16[240,512]{1,0:T(8,128)(2,1)S(1)} %get-tuple-element.228), channel_id=1, source_target_pairs={{0,1},{1,0},{2,3},{3,2},{4,5},{5,4},{6,7},{7,6},{8,9},{9,8},{10,11... | collective-permute-start | bytes 737288 | tf_op jit(solution)/shard_map/ppermute | solution.py:465
  188.3 19.4 %collective-permute-start.39 = (bf16[240,512]{1,0:T(8,128)(2,1)S(1)}, bf16[240,512]{1,0:T(8,128)(2,1)S(1)}, u32[]{:S(2)}, u32[]{:S(2)}) collective-permute-start(bf16[240,512]{1,0:T(8,128)(2,1)S(1)} %get-tuple-element.229), channel_id=1, source_target_pairs={{0,3},{1,2},{2,1},{3,0},{4,7},{5,6},{6,5},{7,4},{8,11},{9,10},{10,... | collective-permute-start | bytes 737288 | tf_op jit(solution)/shard_map/ppermute | solution.py:465
  188.8 22.1 %collective-permute-start.37 = (bf16[240,512]{1,0:T(8,128)(2,1)S(1)}, bf16[240,512]{1,0:T(8,128)(2,1)S(1)}, u32[]{:S(2)}, u32[]{:S(2)}) collective-permute-start(bf16[240,512]{1,0:T(8,128)(2,1)S(1)} %get-tuple-element.227.refs_9_), channel_id=1, source_target_pairs={{0,2},{1,3},{2,0},{3,1},{4,6},{5,7},{6,4},{7,5},{8,10},{9,11},{10,... | collective-permute-start | bytes 737288 | tf_op jit(solution)/shard_map/ppermute | solution.py:465
  (48 other events, 401.0 us)

commit v6 on v5

--- a/solution.py
+++ b/solution.py
@@ -20,7 +20,7 @@
 F32 = jnp.float32
 MIB = 1 << 20
 
-DEVICE, PLACE_1, PLACE_2, SLOT_A, SLOT_B, SLOT_F = 1, 2, 18, 34, 66, 98
+DEVICE, MINE, PLACE_1, PLACE_2, SLOT_A, SLOT_B, SLOT_F = 1, 2, 3, 19, 35, 67, 99
 
 NN = (((1,), (0,)), ((), ()))
 NT = (((1,), (1,)), ((), ()))
@@ -36,6 +36,7 @@
 
 
 SMEM = pl.BlockSpec(memory_space=pltpu.SMEM)
+HBM = pl.BlockSpec(memory_space=pltpu.HBM)
 
 
 def call(body, ins, outs, scratch=(), name=None, vmem=16):
@@ -127,7 +128,7 @@
             rl = 1.0 / jnp.sum(p, axis=0, keepdims=True)
             pb = p.astype(BF)
             p_ref[slot, e] = pb
-            rl_ref[2 * hp + e] = rl
+            rl_ref[pl.ds(2 * hp + e, 1), :] = rl
             o = dot(v2, pb, TN) * rl
             at_ref[pl.ds(pl.multiple_of((2 * hp + e) * HEAD_DIM, HEAD_DIM), HEAD_DIM), :] = o[
                 e * HEAD_DIM : (e + 1) * HEAD_DIM
@@ -160,7 +161,7 @@
         for e in range(2):
             dom = head_half(do2, e)
             dp = dot(v2, dom, NT)
-            p = p_ref[2 * hp + e].astype(F32) * rl_ref[2 * hp + e]
+            p = p_ref[2 * hp + e].astype(F32) * rl_ref[pl.ds(2 * hp + e, 1), :]
             t = p * dp
             ds = (t - p * jnp.sum(t, axis=0, keepdims=True)).astype(BF)
             dk_e = dot(ds, head_half(q2, e))
@@ -217,7 +218,8 @@
 
 
 def self_forward(rows, ids, near, far, wa0, wa1, wa2, wa3, segs,
-                 xf_out, w_out, q_out, kv_out, p_out, rl, at, mask, xf, w, q, kv, p, p_sems, sems):
+                 xf_out, w_out, q_out, kv_out, p_out, rl_out, at,
+                 mask, xf, w, q, kv, p, p_sems, sems, rl):
     join(xf, near, far)
     copies = [keep_copy(xf, xf_out, sems.at[0])]
     unpack(ids, SLOT_A, (wa0, wa1, wa2, wa3), (w, 0, 3, 16))
@@ -228,23 +230,26 @@
     kv[:, D:] = dot(xf[...], w[2]).astype(BF)
     copies += [keep_copy(q, q_out, sems.at[2]), keep_copy(kv, kv_out, sems.at[3])]
     attend(q, kv, mask, p, rl, at, p_out, p_sems)
+    copies.append(keep_copy(rl, rl_out, sems.at[8]))
     for copy in copies:
         copy.wait()
 
 
 def cross_forward(rows, ids, xf, near, far, at1, wb0, wb1, wb2, wb3, segs,
-                  ef_out, w, norms, xh1, rs1, low1_out, q_out, kv_out, p_out, rl, at,
-                  mask, ef, low1, q, kv, p, p_sems, sems):
+                  ef_out, w, norms_out, xh1, rs1_out, low1_out, q_out, kv_out, p_out, rl_out, at_out,
+                  mask, ef, low1, q, kv, p, p_sems, sems, rl, norms, rs1, at):
     join(ef, near, far)
     copies = [keep_copy(ef, ef_out, sems.at[0])]
     unpack(ids, SLOT_B, (wb0, wb1, wb2, wb3), (w, 0, 5, 16))
     set_mask(mask, segs, 2, 0, 3)
     gb = norm_rows((wb0, wb1, wb2, wb3))
     norms[...] = gb
+    copies.append(keep_copy(norms, norms_out, sems.at[6]))
     resid = xf[...].astype(F32) + dot(at1[...], w[0], TN)
     xhat, rstd, n1 = norm_forward(resid, gb[0:1], gb[3:4])
     xh1[...] = xhat
-    rs1[...] = rstd
+    rs1[...] = jnp.broadcast_to(rstd, rs1.shape)
+    copies.append(keep_copy(rs1, rs1_out, sems.at[7]))
     low1[...] = n1.astype(BF)
     copies.append(keep_copy(low1, low1_out, sems.at[1]))
     q[...] = (dot(low1[...], w[3]).astype(BF).astype(F32) * SCALE).astype(BF)
@@ -252,16 +257,25 @@
     kv[:, D:] = dot(ef[...], w[2]).astype(BF)
     copies += [keep_copy(q, q_out, sems.at[2]), keep_copy(kv, kv_out, sems.at[3])]
     attend(q, kv, mask, p, rl, at, p_out, p_sems)
+    copies += [keep_copy(rl, rl_out, sems.at[8]), keep_copy(at, at_out, sems.at[9])]
     for copy in copies:
         copy.wait()
 
 
-def ffn_both(ids, xh1, at2, teach, valid, wb, norms, wf0, wf1, wf2, wf3,
-             out, small, d_r2, d_mix, keep, send, act, hid, low2, wup, wdn):
+def ffn_both(ids, xh1, at2_in, teacher, message, dec_valid, wb, norms_in, wf0, wf1, wf2, wf3,
+             out, small, d_r2, d_mix, keep, send, act, hid, low2, wup, wdn, at2, norms, sems):
+    brought = [keep_copy(at2_in, at2, sems.at[0]), keep_copy(norms_in, norms, sems.at[1])]
+    unpack(ids, SLOT_F, (wf0, wf1, wf2, wf3), (wup, 0, 4, 16), (wdn, 4, 4, 64))
+    tok = teacher.shape[1]
+    marks = jnp.where(ids[MINE] == 0, dec_valid[0:1], dec_valid[1:2]).astype(F32)
+    marks = jnp.concatenate([marks, message[2 * tok : 2 * tok + 1, :tok].astype(F32)], 1)
+    valid = jnp.transpose(jnp.broadcast_to(marks, (8, 2 * tok)))[:, 0:1]
+    teach = jnp.concatenate([teacher[ids[MINE]], message[tok : 2 * tok]], 0)
+    for copy in brought:
+        copy.wait()
     gb = norms[...]
     n1 = xh1[...] * gb[0:1] + gb[3:4]
     wco = wb[4]
-    unpack(ids, SLOT_F, (wf0, wf1, wf2, wf3), (wup, 0, 4, 16), (wdn, 4, 4, 64))
     xh2, rs2, n2 = norm_forward(n1 + dot(at2[...], wco, TN), gb[1:2], gb[4:5])
     low2[...] = n2.astype(BF)
     for j in range(4):
@@ -271,11 +285,11 @@
     r3 = n2 + dot(act[...], wdn[...])
     xh3, rs3, final = norm_forward(r3, gb[2:3], gb[5:6])
     out[...] = final.astype(BF)
-    err = (final - teach[...].astype(F32)) * valid[...]
+    err = (final - teach.astype(F32)) * valid
     small[...] = jnp.zeros_like(small)
     small[6:7] = jnp.sum(err * err, axis=0, keepdims=True)
     lane = lax.broadcasted_iota(jnp.int32, (1, D), 1)
-    small[7:8] = jnp.where(lane == ids[DEVICE], jnp.sum(valid[...]), 0.0)
+    small[7:8] = jnp.where(lane == ids[DEVICE], jnp.sum(valid), 0.0)
     d_r3, dg, db = norm_back(err, xh3, rs3, gb[2:3])
     small[2:3] = dg
     small[5:6] = db
@@ -323,7 +337,7 @@
     dq = jnp.concatenate([dq_a[...], jnp.transpose(dqt[...]).astype(BF)], 1)
     gb = norms[...]
     dn1 = d_r2[...] + dot(dq, wb[3], NT)
-    dr1, dg, db = norm_back(dn1, xh1[...], rs1[...], gb[0:1])
+    dr1, dg, db = norm_back(dn1, xh1[...], rs1[:, 0:1], gb[0:1])
     row = lax.broadcasted_iota(jnp.int32, (16, D), 0)
     sums = jnp.where(row == 0, dg, jnp.where(row == 3, db, small[...]))
     send[1024:1040] = sums.astype(BF)
@@ -409,10 +423,10 @@
     outputs[mine] = out[...]
     outputs[1 - mine] = home[:tok]
     g_e[mine] = e_keep[...]
-    g_e[1 - mine] = home[tok : 2 * tok].astype(F32)
+    g_e[1 - mine] = home[tok:].astype(F32)
     g_x[mine] = x_keep[...]
-    g_x[1 - mine] = home_x[...].astype(F32)
-    t1 = tree_sum([r[...].astype(F32) for r in one] + [home[2 * tok :].astype(F32)])
+    g_x[1 - mine] = home_x[:tok].astype(F32)
+    t1 = tree_sum([r[...].astype(F32) for r in one] + [home_x[tok:].astype(F32)])
     for j in range(4):
         g_up[:, j * D : (j + 1) * D] = t1[16 * j : 16 * j + 16]
     g_down[...] = t1[64:128]
@@ -498,6 +512,31 @@
         enc_k = of(enc_seg, mine).reshape(ns, tok)[pieces(row_bits)].reshape(-1)
         segs = jnp.stack([dec_k, pos, enc_k] + [jnp.zeros_like(pos)] * 5).astype(F32)
 
+        def spread(v, bits):
+            return sum((((v & b) != 0).astype(jnp.int32) << i) for i, b in enumerate(bits))
+
+        if fast:
+            i16 = jnp.arange(16, dtype=jnp.int32)
+            g32 = jnp.arange(32, dtype=jnp.int32)
+            dev16 = (dp_at >> 1) * 8 + seq_at
+
+            def came_from(bits):
+                return dev ^ sum((((g32 >> i) & 1) * b for i, b in enumerate(bits)))
+
+            ids = jnp.concatenate(
+                [
+                    jnp.stack([dp_at & 1, dev, mine]).astype(jnp.int32),
+                    spread(i16 ^ dev16, (4, 2, 1, 8)),
+                    spread(i16 ^ dev16, (4, 2, 1, 8)),
+                    came_from((4, 2, 1, 16, 8)),
+                    came_from((4, 16, 1, 2, 8)),
+                    came_from((4, 2, 1, 16, 8)),
+                ]
+            )
+        else:
+            i16, g32 = jnp.arange(16, dtype=jnp.int32), jnp.arange(32, dtype=jnp.int32)
+            ids = jnp.concatenate([jnp.stack([0 * dev, dev, mine]).astype(jnp.int32), i16, i16, g32, g32, g32])
+
         if fast:
             mats = [self_in, self_out, cross_in, cross_query, cross_out, ffn_up, ffn_down, norm_gain, norm_bias]
             wa, wb, wf = run(
@@ -509,7 +548,7 @@
             )
             wa, wb, wf = wa[None], wb[None], wf[None]
             got_x, got_a = flip(zh, [other(inputs), wa])
-            got_x, got_a, wb, wf, segs = tie(got_x, got_a, wb, wf, segs)
+            got_x, got_a, wb, wf, segs, ids = tie(got_x, got_a, wb, wf, segs, ids)
             got_b, got_f = flip(zh, [wb, wf])
             xf, wa = jnp.stack([of(inputs, mine), got_x])[None], append(wa, got_a)
             got_x, got_a = flip(zl, [xf, wa])
@@ -517,7 +556,8 @@
             xf, wa = append(xf, got_x), append(wa, got_a)
             wb, wf = append(wb, got_b), append(wf, got_f)
             got_x, got_a = flip(x, [xf, wa])
-            got_e, got_t, got_v = flip(zh, [away_e, other(teacher), valid_away])
+            message = swap(zh, jnp.concatenate([away_e, other(teacher), valid_away], 0))
+            got_e = message[:tok]
             got_b, got_f = swap(y, wb), swap(zl, wf)
             ef = jnp.stack([of(encoder, mine), got_e])[None]
             got_x, got_a, got_b, got_f, ef = tie(got_x, got_a, got_b, got_f, ef)
@@ -533,9 +573,9 @@
             got_f = swap(y, wf)
             wb_far, wf_far = swap(core, wb), swap(core, wf)
         else:
-            got_x, got_e, got_t, got_v = flip(
-                ("seq", half), [other(inputs), other(encoder), other(teacher), valid_away]
-            )
+            got_x = swap(("seq", half), other(inputs))
+            message = swap(("seq", half), jnp.concatenate([other(encoder), other(teacher), valid_away], 0))
+            got_e = message[:tok]
             xf, ef = jnp.stack([of(inputs, mine), got_x])[None], jnp.stack([of(encoder, mine), got_e])[None]
             for bit in row_bits:
                 got_x, got_e = flip(("seq", bit), [xf, ef])
@@ -560,33 +600,6 @@
             wf = jnp.concatenate([grouped(gathered(ffn_up)), down], 1)
             wa, wb, wf = [[w[8 * i : 8 * i + 8] for i in range(4)] for w in (wa, wb, wf)]
         x_near, x_far = xf.reshape(-1, D), got_x.reshape(-1, D)
-        teach = jnp.concatenate([of(teacher, mine), got_t], 0)
-        valid = jnp.concatenate([of(dec_valid, mine).astype(F32), got_v[0, :tok].astype(F32)])[:, None]
-
-        def spread(v, bits):
-            return sum((((v & b) != 0).astype(jnp.int32) << i) for i, b in enumerate(bits))
-
-        if fast:
-            i16 = jnp.arange(16, dtype=jnp.int32)
-            g32 = jnp.arange(32, dtype=jnp.int32)
-            dev16 = (dp_at >> 1) * 8 + seq_at
-
-            def came_from(bits):
-                return dev ^ sum((((g32 >> i) & 1) * b for i, b in enumerate(bits)))
-
-            ids = jnp.concatenate(
-                [
-                    jnp.stack([dp_at & 1, dev]).astype(jnp.int32),
-                    spread(i16 ^ dev16, (4, 2, 1, 8)),
-                    spread(i16 ^ dev16, (4, 2, 1, 8)),
-                    came_from((4, 2, 1, 16, 8)),
-                    came_from((4, 16, 1, 2, 8)),
-                    came_from((4, 2, 1, 16, 8)),
-                ]
-            )
-        else:
-            i16, g32 = jnp.arange(16, dtype=jnp.int32), jnp.arange(32, dtype=jnp.int32)
-            ids = jnp.concatenate([jnp.stack([0 * dev, dev]).astype(jnp.int32), i16, i16, g32, g32, g32])
 
         sm = (ids, SMEM)
         p_shape = (HEADS, length, rows)
@@ -594,7 +607,8 @@
             return (
                 [pltpu.VMEM((length, rows), F32)]
                 + [pltpu.VMEM(v, BF) for v in shapes]
-                + [pltpu.VMEM((2, 2, length, rows), BF), pltpu.SemaphoreType.DMA((2,)), pltpu.SemaphoreType.DMA((4,))]
+                + [pltpu.VMEM((2, 2, length, rows), BF), pltpu.SemaphoreType.DMA((2,)), pltpu.SemaphoreType.DMA((10,))]
+                + [pltpu.VMEM((HEADS, rows), F32)]
             )
 
         all_rows, own_rows, both_kv = (length, D), (rows, D), (length, 2 * D)
@@ -603,7 +617,7 @@
             functools.partial(self_forward, rows),
             [sm, (x_near, None), (x_far, None)] + [(v, None) for v in wa] + [(segs, None)],
             [(all_rows, BF, True), ((3, D, D), BF, True), (own_rows, BF, True), (both_kv, BF, True),
-             (p_shape, BF, True), ((HEADS, 1, rows), F32), ((D, rows), BF)],
+             (p_shape, BF, True), ((HEADS, rows), F32, True), ((D, rows), BF)],
             scratch=held(all_rows, (3, D, D), own_rows, both_kv),
             name="self_forward",
         )
@@ -614,10 +628,11 @@
         ef, wb, norms, xh1, rs1, low1, q2, kv2, p2, rl2, at2 = run(
             functools.partial(cross_forward, rows),
             [sm, (own_x, None), (e_near, None), (e_far, None), (at1, None)] + [(v, None) for v in wb] + [(segs, None)],
-            [(all_rows, BF, True), ((5, D, D), BF), ((16, D), F32), (own_rows, F32), ((rows, 1), F32),
+            [(all_rows, BF, True), ((5, D, D), BF), ((16, D), F32, True), (own_rows, F32), ((rows, 128), F32, True),
              (own_rows, BF, True), (own_rows, BF, True), (both_kv, BF, True), (p_shape, BF, True),
-             ((HEADS, 1, rows), F32), ((D, rows), BF)],
-            scratch=held(all_rows, own_rows, own_rows, both_kv),
+             ((HEADS, rows), F32, True), ((D, rows), BF, True)],
+            scratch=held(all_rows, own_rows, own_rows, both_kv)
+            + [pltpu.VMEM((16, D), F32), pltpu.VMEM((rows, 128), F32), pltpu.VMEM((D, rows), BF)],
             name="cross_forward",
         )
         if fast:
@@ -625,11 +640,12 @@
             wf = [wf, got_f, wf_far, swap(core, got_f)]
         out, small, d_r2, d_mix2, keep1, send1 = run(
             ffn_both,
-            [sm, (xh1, None), (at2, None), (teach, None), (valid, None), (wb, None), (norms, None)]
+            [sm, (xh1, None), (at2, HBM), (teacher, None), (message, None), (dec_valid, None), (wb, None), (norms, HBM)]
             + [(v, None) for v in wf],
             [((rows, D), BF), ((16, D), F32), ((rows, D), F32), ((rows, D), BF)] + [((2304, D), BF)] * 2,
             scratch=[pltpu.VMEM((rows, FF), BF), pltpu.VMEM((4, rows, D), F32), pltpu.VMEM((rows, D), BF),
-                     pltpu.VMEM((4, D, D), BF), pltpu.VMEM((FF, D), BF)],
+                     pltpu.VMEM((4, D, D), BF), pltpu.VMEM((FF, D), BF), pltpu.VMEM((D, rows), BF),
+                     pltpu.VMEM((16, D), F32), pltpu.SemaphoreType.DMA((2,))],
             name="ffn_both",
         )
 
@@ -672,16 +688,7 @@
             name="self_back_a",
         )
         if fast:
-            got2, got_y1, d_mix1, dkv1, *e_got = tie(got2, got_y1, d_mix1, dkv1, *e_got)
-            one = lambda start, count: [(v, start, count) for v in (keep1, got1, got_y1)]
-            away, *quads1 = mix(
-                "sum_y2",
-                (BF, [[(keep2, 512, 512), (got2, 512, 512)], [(send2, 1024, 16), (got2, 1024, 16)]]),
-                *[(BF, [one(288 * i, 288)]) for i in (1, 2, 3)],
-            )
-            got_y2 = swap(y, away)
-            small_y2 = (away, 512, 16)
-            q1_got = [swap(("seq", m), part) for m, part in zip(partners, quads1)]
+            got2, d_mix1, dkv1 = tie(got2, d_mix1, dkv1)
         x_own, *rest = run(
             functools.partial(self_back_b, half - 1, rows),
             [sm, (xf, None), (q1, None), (kv1, None), (p1, None), (rl1, None), (d_mix1, None),
@@ -692,23 +699,39 @@
         )
         x_parts, (keep3, send3) = rest[: half - 1], rest[half - 1 :]
 
-        def summed_rows(name, own, got, *more):
-            terms = [own] + got
-            return mix(name, (F32, [[(t, 0, tok) for t in terms]]),
-                       (BF, [*more[:1], [(t, tok, tok) for t in terms], *more[1:]]))
-
-        if fast:
-            q1_got[0], q1_got[1], q1_got[2], got_y2, send3, *x_parts = tie(*q1_got, got_y2, send3, *x_parts)
-        x_got = [swap(("seq", m), part) for m, part in zip(partners, x_parts)]
+        if fast:
+            n = half - 1
+            got_y1, send3, *both_parts = tie(got_y1, send3, *x_parts, *e_got)
+            x_parts, e_got = both_parts[:n], both_parts[n:]
+            (away,) = mix(
+                "sum_y2",
+                (BF, [[(keep2, 512, 512), (got2, 512, 512)], [(send2, 1024, 16), (got2, 1024, 16)]]),
+            )
+            got_y2 = swap(y, away)
+            small_y2 = (away, 512, 16)
+            one = lambda start, count: [(v, start, count) for v in (keep1, got1, got_y1)]
+            quads1 = mix(
+                "sum_quads1", *[(BF, [one(288 * i, 288), [(x_parts[i - 1], 0, rows)]]) for i in (1, 2, 3)]
+            )
+            q1_got = [swap(("seq", m), part) for m, part in zip(partners, quads1)]
+        else:
+            x_got = [swap(("seq", m), part) for m, part in zip(partners, x_parts)]
         if fast:
             got3 = swap(core, send3)
-        more = [one(144, 144) + [(v, 144, 144) for v in q1_got]] if fast else []
-        e_keep, away = summed_rows("sum_e", e_own, e_got, [(out, tok, tok)], *more)
+        e_terms = lambda start: [(v, start, tok) for v in (e_own, *e_got)]
+        e_keep, away = mix("sum_e", (F32, [e_terms(0)]), (BF, [[(out, tok, tok)], e_terms(tok)]))
         home = swap(("seq", half), away)
         if fast:
             (away,) = mix("sum_y3", (BF, [[(keep3, 384, 384), (got3, 384, 384)]]))
             got_y3 = swap(y, away)
-        x_keep, away = summed_rows("sum_x", x_own, x_got)
+            got_y3, home = tie(got_y3, home)
+        if fast:
+            x_terms = lambda start: [(x_own, start, tok)] + [(v, 288 + start, tok) for v in q1_got]
+            more = [one(144, 144) + [(v, 144, 144) for v in q1_got]]
+        else:
+            x_terms = lambda start: [(v, start, tok) for v in (x_own, *x_got)]
+            more = []
+        x_keep, away = mix("sum_x", (F32, [x_terms(0)]), (BF, [x_terms(tok), *more]))
         home_x = swap(("seq", half), away)
 
         if fast:

time: 221 us -> 207 us (0.937)
  local copies, waits for them, and re-layouts: 18.6 us -> 5.25 us
    unnamed x68 -> x48, local copies, waits for them, and re-layouts: 12.1 us -> 1.86 us
    pallas_call x15 -> x16, Pallas kernels: 57.1 us -> 56 us  [call(): pl.pallas_call(body, grid=(1,), in_specs=[whole(a.shape) if s is None els...]
    ppermute x41 -> x38, waiting for transfers between devices: 81.5 us -> 82.6 us  [flip(): lax.ppermute(flat[0] if len(flat) == 1 else jnp.concatenate(flat, 0), axi...]
    ppermute x41 -> x38, starting transfers between devices: 57.6 us -> 58.3 us  [flip(): lax.ppermute(flat[0] if len(flat) == 1 else jnp.concatenate(flat, 0), axi...]
  transfers between devices with their start and end apart: 41 -> 38, of which waited for: 20 -> 21; matrix products, arithmetic and copies ran while one was open for 5% -> 1% of each run, Pallas kernels for 20% -> 22%
where the time goes in v6:
time: 207 us; the launch traced here: 206 us
  waiting for transfers between devices  82.6 us (40%)
  starting transfers between devices  58.3 us (28%)
  Pallas kernels  56 us (27%)
  local copies, waits for them, and re-layouts  5.25 us (3%)
  other arithmetic  2.86 us (1%)
    ppermute x38, waiting for transfers between devices, flip(): lax.ppermute(flat[0] if len(flat) == 1 else jnp.concatenate(flat, 0), axi...  82.6 us
    ppermute x38, starting transfers between devices, flip(): lax.ppermute(flat[0] if len(flat) == 1 else jnp.concatenate(flat, 0), axi...  58.3 us
    pallas_call x16, Pallas kernels, call(): pl.pallas_call(body, grid=(1,), in_specs=[whole(a.shape) if s is None els...  56 us
  transfers between devices with their start and end apart: 38, of which 21 were waited for; matrix products, arithmetic and copies ran while one was open for 1% of the time, Pallas kernels for 22%

profile of v6, /device:TPU:0, one launch (start us, length us, event | category | flops | bytes accessed | tf_op | source)
XLA Modules:
  0.0 206.4 jit_solution(6263904278362627820)
XLA Ops:
  4.4 4.1 %collective-permute-start = (bf16[176,512]{1,0:T(8,128)(2,1)S(1)}, bf16[176,512]{1,0:T(8,128)(2,1)S(1)}, u32[]{:S(2)}, u32[]{:S(2)}) collective-permute-start(bf16[176,512]{1,0:T(8,128)(2,1)S(1)} %pad_maximum_fusion.12), channel_id=1, source_target_pairs={{0,4},{1,5},{2,6},{3,7},{4,0},{5,1},{6,2},{7,3},{8,12},{9,13},{10,... | collective-permute-start | bytes 540680 | tf_op jit(solution)/shard_map/ppermute | solution.py:479
  10.9 6.0 %collective-permute-done = bf16[176,512]{1,0:T(8,128)(2,1)S(1)} collective-permute-done((bf16[176,512]{1,0:T(8,128)(2,1)S(1)}, bf16[176,512]{1,0:T(8,128)(2,1)S(1)}, u32[]{:S(2)}, u32[]{:S(2)}) %collective-permute-start) | collective-permute-done | bytes 180256 | tf_op jit(solution)/shard_map/ppermute | solution.py:479
  18.8 3.4 %collective-permute-start.2 = (bf16[224,512]{1,0:T(8,128)(2,1)S(1)}, bf16[224,512]{1,0:T(8,128)(2,1)S(1)}, u32[]{:S(2)}, u32[]{:S(2)}) collective-permute-start(bf16[224,512]{1,0:T(8,128)(2,1)S(1)} %pad_maximum_fusion.9), channel_id=1, source_target_pairs={{0,4},{1,5},{2,6},{3,7},{4,0},{5,1},{6,2},{7,3},{8,12},{9,13},{10,... | collective-permute-start | bytes 688136 | tf_op jit(solution)/shard_map/ppermute | solution.py:479
  22.3 9.2 %collective-permute-done.2 = bf16[224,512]{1,0:T(8,128)(2,1)S(1)} collective-permute-done((bf16[224,512]{1,0:T(8,128)(2,1)S(1)}, bf16[224,512]{1,0:T(8,128)(2,1)S(1)}, u32[]{:S(2)}, u32[]{:S(2)}) %collective-permute-start.2) | collective-permute-done | bytes 229408 | tf_op jit(solution)/shard_map/ppermute | solution.py:479
  40.9 7.5 %collective-permute-done.6.message = bf16[272,512]{1,0:T(8,128)(2,1)S(1)} collective-permute-done((bf16[272,512]{1,0:T(8,128)(2,1)S(1)}, bf16[272,512]{1,0:T(8,128)(2,1)S(1)}, u32[]{:S(2)}, u32[]{:S(2)}) %collective-permute-start.6) | collective-permute-done | bytes 278560 | tf_op jit(solution)/shard_map/ppermute | solution.py:479
  52.4 4.5 %collective-permute-start.9 = (bf16[256,512]{1,0:T(8,128)(2,1)S(1)}, bf16[256,512]{1,0:T(8,128)(2,1)S(1)}, u32[]{:S(2)}, u32[]{:S(2)}) collective-permute-start(bf16[256,512]{1,0:T(8,128)(2,1)S(1)} %bitcast.107), channel_id=1, source_target_pairs={{0,2},{1,3},{2,0},{3,1},{4,6},{5,7},{6,4},{7,5},{8,10},{9,11},{10,... | collective-permute-start | bytes 786440 | tf_op jit(solution)/shard_map/ppermute | solution.py:479
  57.6 5.7 %collective-permute-done.9 = bf16[256,512]{1,0:T(8,128)(2,1)S(1)} collective-permute-done((bf16[256,512]{1,0:T(8,128)(2,1)S(1)}, bf16[256,512]{1,0:T(8,128)(2,1)S(1)}, u32[]{:S(2)}, u32[]{:S(2)}) %collective-permute-start.9) | collective-permute-done | bytes 262176 | tf_op jit(solution)/shard_map/ppermute | solution.py:479
  63.4 4.1 %collective-permute-start.11 = (bf16[768,512]{1,0:T(8,128)(2,1)S(1)}, bf16[768,512]{1,0:T(8,128)(2,1)S(1)}, u32[]{:S(2)}, u32[]{:S(2)}) collective-permute-start(bf16[768,512]{1,0:T(8,128)(2,1)S(1)} %bitcast.84), channel_id=1, source_target_pairs={{0,2},{1,3},{2,0},{3,1},{4,6},{5,7},{6,4},{7,5},{8,10},{9,11},{10,... | collective-permute-start | bytes 2359304 | tf_op jit(solution)/shard_map/ppermute | solution.py:479
  69.3 4.8 %collective-permute-done.14 = bf16[512,512]{1,0:T(8,128)(2,1)S(1)} collective-permute-done((bf16[512,512]{1,0:T(8,128)(2,1)S(1)}, bf16[512,512]{1,0:T(8,128)(2,1)S(1)}, u32[]{:S(2)}, u32[]{:S(2)}) %collective-permute-start.14) | collective-permute-done | bytes 524320 | tf_op jit(solution)/shard_map/ppermute | solution.py:479
  74.9 10.4 %self_forward.1 = (bf16[1024,512]{1,0:T(8,128)(2,1)}, bf16[3,512,512]{2,1,0:T(8,128)(2,1)}, bf16[256,512]{1,0:T(8,128)(2,1)}, bf16[1024,1024]{1,0:T(8,128)(2,1)}...) custom-call(s32[131]{0:T(256)S(1)} %concatenate.58.ids, ...), custom_call_target="tpu_custom_call" | custom-call | flops 1000 | bytes 1000 | tf_op jit(solution)/shard_map/self_forward/pallas_call | solution.py:43
  87.9 11.0 %cross_forward.1 = (bf16[1024,512]{1,0:T(8,128)(2,1)}, bf16[5,512,512]{2,1,0:T(8,128)(2,1)S(1)}, f32[16,512]{1,0:T(8,128)}, f32[256,512]{1,0:T(8,128)S(1)}, f32[...) custom-call(s32[131]{0:T(256)S(1)} %concatenate.58.ids, ...), custom_call_target="tpu_custom_call" | custom-call | flops 1000 | bytes 1000 | tf_op jit(solution)/shard_map/cross_forward/pallas_call | solution.py:43
  104.2 6.9 %ffn_both.1 = (bf16[256,512]{1,0:T(8,128)(2,1)S(1)}, f32[16,512]{1,0:T(8,128)S(1)}, f32[256,512]{1,0:T(8,128)S(1)}, bf16[256,512]{1,0:T(8,128)(2,1)S(1)}, bf16[2...) custom-call(s32[131]{0:T(256)S(1)} %concatenate.58.ids, f32[256,512]{1,0:T(8,128)S(1)} %get-tuple-element.155.xh1, ...), custom_call_target="tpu_custom_call" | custom-call | flops 1000 | bytes 1000 | tf_op jit(solution)/shard_map/ffn_both/pallas_call | solution.py:43
  111.3 4.2 %cross_back_a.1 = (bf16[1024,512]{1,0:T(8,128)(2,1)S(1)}, bf16[256,256]{1,0:T(8,128)(2,1)S(1)}) custom-call(bf16[256,512]{1,0:T(8,128)(2,1)S(1)} %copy-done.8, bf16[1024,1024]{1,0:T(8,128)(2,1)S(1)} %copy-done.3, bf16[8,1024,256]{2,1,0:T(8,128)(2,1)S(1)} %copy-done, f32[8,256]{1,0:T(8,128)S(1)} %copy-done.15, bf16[256,512]{1,0:T(8,128)(2,1)S(1)} %get-tuple-element.178.d_mix), custom_call_target="tpu_custom_call" | custom-call | flops 1000 | bytes 1000 | tf_op jit(solution)/shard_map/cross_back_a/pallas_call | solution.py:43
  116.8 7.4 %cross_back_b.1 = (f32[256,512]{1,0:T(8,128)S(1)}, bf16[256,512]{1,0:T(8,128)(2,1)S(1)}, bf16[256,512]{1,0:T(8,128)(2,1)S(1)}, bf16[256,512]{1,0:T(8,128)(2,1)S(...) custom-call(s32[131]{0:T(256)S(1)} %concatenate.58.ids, ...), custom_call_target="tpu_custom_call" | custom-call | flops 1000 | bytes 1000 | tf_op jit(solution)/shard_map/cross_back_b/pallas_call | solution.py:43
  124.6 4.5 %collective-permute-start.23 = (bf16[256,512]{1,0:T(8,128)(2,1)S(1)}, bf16[256,512]{1,0:T(8,128)(2,1)S(1)}, u32[]{:S(2)}, u32[]{:S(2)}) collective-permute-start(bf16[256,512]{1,0:T(8,128)(2,1)S(1)} %get-tuple-element.197), channel_id=1, source_target_pairs={{0,2},{1,3},{2,0},{3,1},{4,6},{5,7},{6,4},{7,5},{8,10},{9,11},{10,... | collective-permute-start | bytes 786440 | tf_op jit(solution)/shard_map/ppermute | solution.py:479
  130.6 3.9 %self_back_a.1 = (bf16[1024,512]{1,0:T(8,128)(2,1)S(1)}, bf16[256,256]{1,0:T(8,128)(2,1)S(1)}) custom-call(bf16[256,512]{1,0:T(8,128)(2,1)S(1)} %copy-done.7, bf16[1024,1024]{1,0:T(8,128)(2,1)S(1)} %copy-done.2, bf16[8,1024,256]{2,1,0:T(8,128)(2,1)S(1)} %copy-done.1, f32[8,256]{1,0:T(8,128)S(1)} %copy-done.14, bf16[256,512]{1,0:T(8,128)(2,1)S(1)} %get-tuple-element.188.d_mix), custom_call_target="tpu_custom_call" | custom-call | flops 1000 | bytes 1000 | tf_op jit(solution)/shard_map/self_back_a/pallas_call | solution.py:43
  134.6 7.2 %self_back_b.1 = (f32[256,512]{1,0:T(8,128)S(1)}, bf16[256,512]{1,0:T(8,128)(2,1)S(1)}, bf16[256,512]{1,0:T(8,128)(2,1)S(1)}, bf16[256,512]{1,0:T(8,128)(2,1)S(1...) custom-call(s32[131]{0:T(256)S(1)} %concatenate.58.ids, bf16[1024,512]{1,0:T(8,128)(2,1)S(1)} %copy-done.5, ...), custom_call_target="tpu_custom_call" | custom-call | flops 1000 | bytes 1000 | tf_op jit(solution)/shard_map/self_back_b/pallas_call | solution.py:43
  144.3 3.5 %collective-permute-start.31 = (bf16[256,512]{1,0:T(8,128)(2,1)S(1)}, bf16[256,512]{1,0:T(8,128)(2,1)S(1)}, u32[]{:S(2)}, u32[]{:S(2)}) collective-permute-start(bf16[256,512]{1,0:T(8,128)(2,1)S(1)} %get-tuple-element.214), channel_id=1, source_target_pairs={{0,4},{1,5},{2,6},{3,7},{4,0},{5,1},{6,2},{7,3},{8,12},{9,13},{10,... | collective-permute-start | bytes 786440 | tf_op jit(solution)/shard_map/ppermute | solution.py:479
  152.9 7.6 %collective-permute-done.31.refs_8_ = bf16[256,512]{1,0:T(8,128)(2,1)S(1)} collective-permute-done((bf16[256,512]{1,0:T(8,128)(2,1)S(1)}, bf16[256,512]{1,0:T(8,128)(2,1)S(1)}, u32[]{:S(2)}, u32[]{:S(2)}) %collective-permute-start.31) | collective-permute-done | bytes 262176 | tf_op jit(solution)/shard_map/ppermute | solution.py:479
  161.0 12.4 %collective-permute-done.30.refs_5_.refs_8_.refs_22_ = bf16[384,512]{1,0:T(8,128)(2,1)S(1)} collective-permute-done((bf16[384,512]{1,0:T(8,128)(2,1)S(1)}, bf16[384,512]{1,0:T(8,128)(2,1)S(1)}, u32[]{:S(2)}, u32[]{:S(2)}) %collective-permute-start.30) | collective-permute-done | bytes 393248 | tf_op jit(solution)/shard_map/ppermute | solution.py:479
  179.9 4.2 %collective-permute-start.32 = (bf16[272,512]{1,0:T(8,128)(2,1)S(1)}, bf16[272,512]{1,0:T(8,128)(2,1)S(1)}, u32[]{:S(2)}, u32[]{:S(2)}) collective-permute-start(bf16[272,512]{1,0:T(8,128)(2,1)S(1)} %get-tuple-element.219), channel_id=1, source_target_pairs={{0,4},{1,5},{2,6},{3,7},{4,0},{5,1},{6,2},{7,3},{8,12},{9,13},{10,... | collective-permute-start | bytes 835592 | tf_op jit(solution)/shard_map/ppermute | solution.py:479
  184.1 5.4 %collective-permute-done.35.refs_4_.refs_18_ = bf16[240,512]{1,0:T(8,128)(2,1)S(1)} collective-permute-done((bf16[240,512]{1,0:T(8,128)(2,1)S(1)}, bf16[240,512]{1,0:T(8,128)(2,1)S(1)}, u32[]{:S(2)}, u32[]{:S(2)}) %collective-permute-start.35) | collective-permute-done | bytes 245792 | tf_op jit(solution)/shard_map/ppermute | solution.py:479
  190.9 4.2 %collective-permute-done.34.refs_3_.refs_17_ = bf16[240,512]{1,0:T(8,128)(2,1)S(1)} collective-permute-done((bf16[240,512]{1,0:T(8,128)(2,1)S(1)}, bf16[240,512]{1,0:T(8,128)(2,1)S(1)}, u32[]{:S(2)}, u32[]{:S(2)}) %collective-permute-start.34) | collective-permute-done | bytes 245792 | tf_op jit(solution)/shard_map/ppermute | solution.py:479
  198.7 5.7 %collective-permute-done.37.refs_13_ = bf16[128,512]{1,0:T(8,128)(2,1)S(1)} collective-permute-done((bf16[128,512]{1,0:T(8,128)(2,1)S(1)}, bf16[128,512]{1,0:T(8,128)(2,1)S(1)}, u32[]{:S(2)}, u32[]{:S(2)}) %collective-permute-start.37) | collective-permute-done | bytes 131104 | tf_op jit(solution)/shard_map/ppermute | solution.py:479
  (167 shorter events, 57.1 us)
Async XLA Ops:
  17.9 14.6 %collective-permute-start.1 = (bf16[352,512]{1,0:T(8,128)(2,1)S(1)}, bf16[352,512]{1,0:T(8,128)(2,1)S(1)}, u32[]{:S(2)}, u32[]{:S(2)}) collective-permute-start(bf16[352,512]{1,0:T(8,128)(2,1)S(1)} %pad_maximum_fusion.6), channel_id=1, source_target_pairs={{0,2},{1,3},{2,0},{3,1},{4,6},{5,7},{6,4},{7,5},{8,10},{9,11},{10,... | collective-permute-start | bytes 1081352 | tf_op jit(solution)/shard_map/ppermute | solution.py:479
  32.7 16.5 %collective-permute-start.3 = (bf16[704,512]{1,0:T(8,128)(2,1)S(1)}, bf16[704,512]{1,0:T(8,128)(2,1)S(1)}, u32[]{:S(2)}, u32[]{:S(2)}) collective-permute-start(bf16[704,512]{1,0:T(8,128)(2,1)S(1)} %pad_maximum_fusion), channel_id=1, source_target_pairs={{0,1},{1,0},{2,3},{3,2},{4,5},{5,4},{6,7},{7,6},{8,9},{9,8},{10,11... | collective-permute-start | bytes 2162696 | tf_op jit(solution)/shard_map/ppermute | solution.py:479
  34.0 14.4 %collective-permute-start.6 = (bf16[272,512]{1,0:T(8,128)(2,1)S(1)}, bf16[272,512]{1,0:T(8,128)(2,1)S(1)}, u32[]{:S(2)}, u32[]{:S(2)}) collective-permute-start(bf16[272,512]{1,0:T(8,128)(2,1)S(1)} %fusion.1), channel_id=1, source_target_pairs={{0,4},{1,5},{2,6},{3,7},{4,0},{5,1},{6,2},{7,3},{8,12},{9,13},{10,... | collective-permute-start | bytes 835592 | tf_op jit(solution)/shard_map/ppermute | solution.py:479
  49.3 14.0 %collective-permute-start.10 = (bf16[384,512]{1,0:T(8,128)(2,1)S(1)}, bf16[384,512]{1,0:T(8,128)(2,1)S(1)}, u32[]{:S(2)}, u32[]{:S(2)}) collective-permute-start(bf16[384,512]{1,0:T(8,128)(2,1)S(1)} %bitcast.76), channel_id=1, source_target_pairs={{0,8},{8,0},{16,24},{24,16},{1,9},{9,1},{17,25},{25,17},{2,10},{10... | collective-permute-start | bytes 1179656 | tf_op jit(solution)/shard_map/ppermute | solution.py:479
  49.4 13.9 %collective-permute-start.7 = (bf16[384,512]{1,0:T(8,128)(2,1)S(1)}, bf16[384,512]{1,0:T(8,128)(2,1)S(1)}, u32[]{:S(2)}, u32[]{:S(2)}) collective-permute-start(bf16[384,512]{1,0:T(8,128)(2,1)S(1)} %bitcast.77), channel_id=1, source_target_pairs={{0,16},{8,24},{16,0},{24,8},{1,17},{9,25},{17,1},{25,9},{2,18},{10... | collective-permute-start | bytes 1179656 | tf_op jit(solution)/shard_map/ppermute | solution.py:479
  57.0 17.1 %collective-permute-start.14 = (bf16[512,512]{1,0:T(8,128)(2,1)S(1)}, bf16[512,512]{1,0:T(8,128)(2,1)S(1)}, u32[]{:S(2)}, u32[]{:S(2)}) collective-permute-start(bf16[512,512]{1,0:T(8,128)(2,1)S(1)} %bitcast.123), channel_id=1, source_target_pairs={{0,1},{1,0},{2,3},{3,2},{4,5},{5,4},{6,7},{7,6},{8,9},{9,8},{10,11... | collective-permute-start | bytes 1572872 | tf_op jit(solution)/shard_map/ppermute | solution.py:479
  63.3 22.1 %collective-permute-start.13 = (bf16[768,512]{1,0:T(8,128)(2,1)S(1)}, bf16[768,512]{1,0:T(8,128)(2,1)S(1)}, u32[]{:S(2)}, u32[]{:S(2)}) collective-permute-start(bf16[768,512]{1,0:T(8,128)(2,1)S(1)} %bitcast.83), channel_id=1, source_target_pairs={{0,8},{8,0},{16,24},{24,16},{1,9},{9,1},{17,25},{25,17},{2,10},{10... | collective-permute-start | bytes 2359304 | tf_op jit(solution)/shard_map/ppermute | solution.py:479
  63.4 22.2 %collective-permute-start.11 = (bf16[768,512]{1,0:T(8,128)(2,1)S(1)}, bf16[768,512]{1,0:T(8,128)(2,1)S(1)}, u32[]{:S(2)}, u32[]{:S(2)}) collective-permute-start(bf16[768,512]{1,0:T(8,128)(2,1)S(1)} %bitcast.84), channel_id=1, source_target_pairs={{0,2},{1,3},{2,0},{3,1},{4,6},{5,7},{6,4},{7,5},{8,10},{9,11},{10,... | collective-permute-start | bytes 2359304 | tf_op jit(solution)/shard_map/ppermute | solution.py:479
  67.7 17.7 %collective-permute-start.12 = (bf16[512,512]{1,0:T(8,128)(2,1)S(1)}, bf16[512,512]{1,0:T(8,128)(2,1)S(1)}, u32[]{:S(2)}, u32[]{:S(2)}) collective-permute-start(bf16[512,512]{1,0:T(8,128)(2,1)S(1)} %bitcast.74), channel_id=1, source_target_pairs={{0,1},{1,0},{2,3},{3,2},{4,5},{5,4},{6,7},{7,6},{8,9},{9,8},{10,11... | collective-permute-start | bytes 1572872 | tf_op jit(solution)/shard_map/ppermute | solution.py:479
  74.1 24.8 %collective-permute-start.18 = (bf16[1024,512]{1,0:T(8,128)(2,1)S(1)}, bf16[1024,512]{1,0:T(8,128)(2,1)S(1)}, u32[]{:S(2)}, u32[]{:S(2)}) collective-permute-start(bf16[1024,512]{1,0:T(8,128)(2,1)S(1)} %bitcast.78), channel_id=1, source_target_pairs={{0,8},{8,0},{16,24},{24,16},{1,9},{9,1},{17,25},{25,17},{2,10},{10... | collective-permute-start | bytes 3145736 | tf_op jit(solution)/shard_map/ppermute | solution.py:479
  74.2 25.6 %collective-permute-start.17 = (bf16[1024,512]{1,0:T(8,128)(2,1)S(1)}, bf16[1024,512]{1,0:T(8,128)(2,1)S(1)}, u32[]{:S(2)}, u32[]{:S(2)}) collective-permute-start(bf16[1024,512]{1,0:T(8,128)(2,1)S(1)} %bitcast.79), channel_id=1, source_target_pairs={{0,16},{8,24},{16,0},{24,8},{1,17},{9,25},{17,1},{25,9},{2,18},{10... | collective-permute-start | bytes 3145736 | tf_op jit(solution)/shard_map/ppermute | solution.py:479
  116.0 28.1 %collective-permute-start.21 = (bf16[1152,512]{1,0:T(8,128)(2,1)S(1)}, bf16[1152,512]{1,0:T(8,128)(2,1)S(1)}, u32[]{:S(2)}, u32[]{:S(2)}) collective-permute-start(bf16[1152,512]{1,0:T(8,128)(2,1)S(1)} %add_convert_fusion), channel_id=1, source_target_pairs={{0,16},{8,24},{16,0},{24,8},{1,17},{9,25},{17,1},{25,9},{2,18},{10... | collective-permute-start | bytes 3538952 | tf_op jit(solution)/shard_map/ppermute | solution.py:479
  124.6 17.2 %collective-permute-start.23 = (bf16[256,512]{1,0:T(8,128)(2,1)S(1)}, bf16[256,512]{1,0:T(8,128)(2,1)S(1)}, u32[]{:S(2)}, u32[]{:S(2)}) collective-permute-start(bf16[256,512]{1,0:T(8,128)(2,1)S(1)} %get-tuple-element.197), channel_id=1, source_target_pairs={{0,2},{1,3},{2,0},{3,1},{4,6},{5,7},{6,4},{7,5},{8,10},{9,11},{10,... | collective-permute-start | bytes 786440 | tf_op jit(solution)/shard_map/ppermute | solution.py:479
  129.1 13.7 %collective-permute-start.24 = (bf16[256,512]{1,0:T(8,128)(2,1)S(1)}, bf16[256,512]{1,0:T(8,128)(2,1)S(1)}, u32[]{:S(2)}, u32[]{:S(2)}) collective-permute-start(bf16[256,512]{1,0:T(8,128)(2,1)S(1)} %get-tuple-element.198), channel_id=1, source_target_pairs={{0,1},{1,0},{2,3},{3,2},{4,5},{5,4},{6,7},{7,6},{8,9},{9,8},{10,11... | collective-permute-start | bytes 786440 | tf_op jit(solution)/shard_map/ppermute | solution.py:479
  144.3 16.2 %collective-permute-start.31 = (bf16[256,512]{1,0:T(8,128)(2,1)S(1)}, bf16[256,512]{1,0:T(8,128)(2,1)S(1)}, u32[]{:S(2)}, u32[]{:S(2)}) collective-permute-start(bf16[256,512]{1,0:T(8,128)(2,1)S(1)} %get-tuple-element.214), channel_id=1, source_target_pairs={{0,4},{1,5},{2,6},{3,7},{4,0},{5,1},{6,2},{7,3},{8,12},{9,13},{10,... | collective-permute-start | bytes 786440 | tf_op jit(solution)/shard_map/ppermute | solution.py:479
  148.1 27.4 %collective-permute-start.26 = (bf16[544,512]{1,0:T(8,128)(2,1)S(1)}, bf16[544,512]{1,0:T(8,128)(2,1)S(1)}, u32[]{:S(2)}, u32[]{:S(2)}) collective-permute-start(bf16[544,512]{1,0:T(8,128)(2,1)S(1)} %get-tuple-element.204), channel_id=1, source_target_pairs={{0,2},{1,3},{2,0},{3,1},{4,6},{5,7},{6,4},{7,5},{8,10},{9,11},{10,... | collective-permute-start | bytes 1671176 | tf_op jit(solution)/shard_map/ppermute | solution.py:479
  150.7 22.6 %collective-permute-start.33 = (bf16[528,512]{1,0:T(8,128)(2,1)S(1)}, bf16[528,512]{1,0:T(8,128)(2,1)S(1)}, u32[]{:S(2)}, u32[]{:S(2)}) collective-permute-start(bf16[528,512]{1,0:T(8,128)(2,1)S(1)} %sum_y2.1.refs_6_), channel_id=1, source_target_pairs={{0,16},{8,24},{16,0},{24,8},{1,17},{9,25},{17,1},{25,9},{2,18},{10... | collective-permute-start | bytes 1622024 | tf_op jit(solution)/shard_map/ppermute | solution.py:479
  151.3 25.9 %collective-permute-start.27 = (bf16[544,512]{1,0:T(8,128)(2,1)S(1)}, bf16[544,512]{1,0:T(8,128)(2,1)S(1)}, u32[]{:S(2)}, u32[]{:S(2)}) collective-permute-start(bf16[544,512]{1,0:T(8,128)(2,1)S(1)} %get-tuple-element.205), channel_id=1, source_target_pairs={{0,1},{1,0},{2,3},{3,2},{4,5},{5,4},{6,7},{7,6},{8,9},{9,8},{10,11... | collective-permute-start | bytes 1671176 | tf_op jit(solution)/shard_map/ppermute | solution.py:479
  152.8 26.9 %collective-permute-start.28 = (bf16[544,512]{1,0:T(8,128)(2,1)S(1)}, bf16[544,512]{1,0:T(8,128)(2,1)S(1)}, u32[]{:S(2)}, u32[]{:S(2)}) collective-permute-start(bf16[544,512]{1,0:T(8,128)(2,1)S(1)} %get-tuple-element.206), channel_id=1, source_target_pairs={{0,3},{1,2},{2,1},{3,0},{4,7},{5,6},{6,5},{7,4},{8,11},{9,10},{10,... | collective-permute-start | bytes 1671176 | tf_op jit(solution)/shard_map/ppermute | solution.py:479
  160.4 12.9 %collective-permute-start.30 = (bf16[384,512]{1,0:T(8,128)(2,1)S(1)}, bf16[384,512]{1,0:T(8,128)(2,1)S(1)}, u32[]{:S(2)}, u32[]{:S(2)}) collective-permute-start(bf16[384,512]{1,0:T(8,128)(2,1)S(1)} %sum_y3.1), channel_id=1, source_target_pairs={{0,16},{8,24},{16,0},{24,8},{1,17},{9,25},{17,1},{25,9},{2,18},{10... | collective-permute-start | bytes 1179656 | tf_op jit(solution)/shard_map/ppermute | solution.py:479
  173.6 15.9 %collective-permute-start.35 = (bf16[240,512]{1,0:T(8,128)(2,1)S(1)}, bf16[240,512]{1,0:T(8,128)(2,1)S(1)}, u32[]{:S(2)}, u32[]{:S(2)}) collective-permute-start(bf16[240,512]{1,0:T(8,128)(2,1)S(1)} %get-tuple-element.224), channel_id=1, source_target_pairs={{0,1},{1,0},{2,3},{3,2},{4,5},{5,4},{6,7},{7,6},{8,9},{9,8},{10,11... | collective-permute-start | bytes 737288 | tf_op jit(solution)/shard_map/ppermute | solution.py:479
  175.2 15.8 %collective-permute-start.36 = (bf16[240,512]{1,0:T(8,128)(2,1)S(1)}, bf16[240,512]{1,0:T(8,128)(2,1)S(1)}, u32[]{:S(2)}, u32[]{:S(2)}) collective-permute-start(bf16[240,512]{1,0:T(8,128)(2,1)S(1)} %get-tuple-element.225), channel_id=1, source_target_pairs={{0,3},{1,2},{2,1},{3,0},{4,7},{5,6},{6,5},{7,4},{8,11},{9,10},{10,... | collective-permute-start | bytes 737288 | tf_op jit(solution)/shard_map/ppermute | solution.py:479
  175.4 19.7 %collective-permute-start.34 = (bf16[240,512]{1,0:T(8,128)(2,1)S(1)}, bf16[240,512]{1,0:T(8,128)(2,1)S(1)}, u32[]{:S(2)}, u32[]{:S(2)}) collective-permute-start(bf16[240,512]{1,0:T(8,128)(2,1)S(1)} %get-tuple-element.223.refs_9_), channel_id=1, source_target_pairs={{0,2},{1,3},{2,0},{3,1},{4,6},{5,7},{6,4},{7,5},{8,10},{9,11},{10,... | collective-permute-start | bytes 737288 | tf_op jit(solution)/shard_map/ppermute | solution.py:479
  179.9 18.8 %collective-permute-start.32 = (bf16[272,512]{1,0:T(8,128)(2,1)S(1)}, bf16[272,512]{1,0:T(8,128)(2,1)S(1)}, u32[]{:S(2)}, u32[]{:S(2)}) collective-permute-start(bf16[272,512]{1,0:T(8,128)(2,1)S(1)} %get-tuple-element.219), channel_id=1, source_target_pairs={{0,4},{1,5},{2,6},{3,7},{4,0},{5,1},{6,2},{7,3},{8,12},{9,13},{10,... | collective-permute-start | bytes 835592 | tf_op jit(solution)/shard_map/ppermute | solution.py:479
  (35 other events, 332.7 us)

commit v7 on v6

--- a/solution.py
+++ b/solution.py
@@ -107,7 +107,13 @@
     return jnp.where((lane < HEAD_DIM) == (e == 0), x, jnp.zeros_like(x))
 
 
+def two_heads(x):
+    return jnp.concatenate([head_half(x, 0), head_half(x, 1)], 0)
+
+
 def attend(q_ref, kv_ref, mask_ref, p_ref, rl_ref, at_ref, p_out, sems):
+    rows = mask_ref.shape[1]
+
     def leave(hp, slot):
         return pltpu.make_async_copy(p_ref.at[slot], p_out.at[pl.ds(2 * hp, 2)], sems.at[slot])
 
@@ -122,17 +128,20 @@
         k2 = kv_ref[:, pl.ds(c0, 128)]
         v2 = kv_ref[:, pl.ds(pl.multiple_of(D + c0, 128), 128)]
         q2 = q_ref[:, pl.ds(c0, 128)]
+        both = dot(k2, two_heads(q2), NT)
+        probs, scales = [], []
         for e in range(2):
-            s = dot(k2, head_half(q2, e), NT) + mask_ref[...]
+            s = both[:, e * rows : (e + 1) * rows] + mask_ref[...]
             p = jnp.exp(s - jnp.max(s, axis=0, keepdims=True))
             rl = 1.0 / jnp.sum(p, axis=0, keepdims=True)
-            pb = p.astype(BF)
-            p_ref[slot, e] = pb
+            probs.append(p.astype(BF))
+            p_ref[slot, e] = probs[e]
             rl_ref[pl.ds(2 * hp + e, 1), :] = rl
-            o = dot(v2, pb, TN) * rl
-            at_ref[pl.ds(pl.multiple_of((2 * hp + e) * HEAD_DIM, HEAD_DIM), HEAD_DIM), :] = o[
-                e * HEAD_DIM : (e + 1) * HEAD_DIM
-            ].astype(BF)
+            scales.append(rl)
+        o = dot(v2, jnp.concatenate(probs, 1), TN)
+        for e in range(2):
+            out = o[e * HEAD_DIM : (e + 1) * HEAD_DIM, e * rows : (e + 1) * rows] * scales[e]
+            at_ref[pl.ds(pl.multiple_of((2 * hp + e) * HEAD_DIM, HEAD_DIM), HEAD_DIM), :] = out.astype(BF)
         leave(hp, slot).start()
         return carry
 
@@ -149,6 +158,8 @@
 
 
 def attend_back(first, q_ref, kv_ref, p_ref, rl_ref, do_ref, dkv_ref, dqt_ref):
+    rows = q_ref.shape[0]
+
     def pair(i, carry):
         hp = first // 2 + i
         c0 = pl.multiple_of(hp * 128, 128)
@@ -157,26 +168,27 @@
         v2 = kv_ref[:, pl.ds(pl.multiple_of(D + c0, 128), 128)]
         q2 = q_ref[:, pl.ds(c0, 128)]
         do2 = do_ref[:, pl.ds(c0, 128)]
-        dk = dv = None
+        dobd = two_heads(do2)
+        both = dot(v2, dobd, NT)
+        probs, grads = [], []
         for e in range(2):
-            dom = head_half(do2, e)
-            dp = dot(v2, dom, NT)
             p = p_ref[2 * hp + e].astype(F32) * rl_ref[pl.ds(2 * hp + e, 1), :]
-            t = p * dp
-            ds = (t - p * jnp.sum(t, axis=0, keepdims=True)).astype(BF)
-            dk_e = dot(ds, head_half(q2, e))
-            dv_e = dot(p.astype(BF), dom)
-            dk = dk_e if dk is None else dk + dk_e
-            dv = dv_e if dv is None else dv + dv_e
-            dqt = dot(k2, ds, TN) * SCALE
+            t = p * both[:, e * rows : (e + 1) * rows]
+            grads.append((t - p * jnp.sum(t, axis=0, keepdims=True)).astype(BF))
+            probs.append(p.astype(BF))
+        ds = jnp.concatenate(grads, 1)
+        dk = dot(ds, two_heads(q2))
+        dv = dot(jnp.concatenate(probs, 1), dobd)
+        dqt = dot(k2, ds, TN) * SCALE
+        for e in range(2):
             dqt_ref[pl.ds(pl.multiple_of((2 * i + e) * HEAD_DIM, HEAD_DIM), HEAD_DIM), :] = dqt[
-                e * HEAD_DIM : (e + 1) * HEAD_DIM
+                e * HEAD_DIM : (e + 1) * HEAD_DIM, e * rows : (e + 1) * rows
             ]
         dkv_ref[:, pl.ds(o0, 128)] = dk.astype(BF)
         dkv_ref[:, pl.ds(pl.multiple_of(HALF + o0, 128), 128)] = dv.astype(BF)
         return carry
 
-    lax.fori_loop(0, HEADS // 4, pair, 0)
+    lax.fori_loop(0, HEADS // 4, pair, 0, unroll=True)
 
 
 def cols(ref, c, width):
@@ -415,7 +427,7 @@
     where, refs = refs[0], refs[1:]
     sources, results = refs[: len(counts)], refs[len(counts) :]
     refs = [ref.at[:count] for ref, count in zip(sources, counts)]
-    one, (out, home, e_keep, x_keep, home_x, z_own, z_got, *refs) = refs[:6], refs[6:]
+    one, (out, home, e_keep, x_keep, home_x, z_own, z_got, *refs) = refs[:5], refs[5:]
     two, three = refs[:6], refs[6:]
     outputs, loss, g_x, g_e, g_in, g_so, g_cq, g_cin, g_co, g_up, g_down, g_gain, g_bias = results
     mine = where[0]
@@ -700,9 +712,9 @@
         x_parts, (keep3, send3) = rest[: half - 1], rest[half - 1 :]
 
         if fast:
-            n = half - 1
-            got_y1, send3, *both_parts = tie(got_y1, send3, *x_parts, *e_got)
-            x_parts, e_got = both_parts[:n], both_parts[n:]
+            (away,) = mix("away_x", (BF, [[(x_parts[0], 0, rows)], [(x_parts[2], 0, rows)]]))
+            got_xa = swap(zl, away)
+            got_y1, send3, *e_got = tie(got_y1, send3, *e_got)
             (away,) = mix(
                 "sum_y2",
                 (BF, [[(keep2, 512, 512), (got2, 512, 512)], [(send2, 1024, 16), (got2, 1024, 16)]]),
@@ -710,10 +722,8 @@
             got_y2 = swap(y, away)
             small_y2 = (away, 512, 16)
             one = lambda start, count: [(v, start, count) for v in (keep1, got1, got_y1)]
-            quads1 = mix(
-                "sum_quads1", *[(BF, [one(288 * i, 288), [(x_parts[i - 1], 0, rows)]]) for i in (1, 2, 3)]
-            )
-            q1_got = [swap(("seq", m), part) for m, part in zip(partners, quads1)]
+            (away,) = mix("sum_1x", (BF, [one(576, 576)]))
+            got_1a = swap(x, away)
         else:
             x_got = [swap(("seq", m), part) for m, part in zip(partners, x_parts)]
         if fast:
@@ -726,8 +736,12 @@
             got_y3 = swap(y, away)
             got_y3, home = tie(got_y3, home)
         if fast:
-            x_terms = lambda start: [(x_own, start, tok)] + [(v, 288 + start, tok) for v in q1_got]
-            more = [one(144, 144) + [(v, 144, 144) for v in q1_got]]
+            (away,) = mix("sum_xx", (BF, [[(x_parts[1], 0, rows), (got_xa, rows, rows)]]))
+            got_xb = swap(x, away)
+            (away,) = mix("sum_1z", (BF, [one(288, 288) + [(got_1a, 288, 288)]]))
+            got_1b = swap(zl, away)
+            x_terms = lambda start: [(v, start, tok) for v in (x_own, got_xa, got_xb)]
+            more = [one(144, 144) + [(got_1a, 144, 144), (got_1b, 144, 144)]]
         else:
             x_terms = lambda start: [(v, start, tok) for v in (x_own, *x_got)]
             more = []
@@ -754,7 +768,7 @@
             got_z = swap(zh, away)
             where = jnp.stack([mine, dev]).astype(jnp.int32)
 
-            last = [(v, 144) for v in (keep1, got1, got_y1, *q1_got)] + [(out, tok)]
+            last = [(v, 144) for v in (keep1, got1, got_y1, got_1a, got_1b)] + [(out, tok)]
             last += [(v, v.shape[0]) for v in (home, e_keep, x_keep, home_x, away, got_z)]
             last += [(v, 64) for v in (keep2, got2, got_y2)] + [(v, v.shape[0]) for v in q_got]
             last += [(v, 48) for v in (keep3, got3, got_y3)]

time: 207 us -> 202 us (0.976)
  Pallas kernels: 56 us -> 47.6 us
  waiting for transfers between devices: 82.6 us -> 87.9 us
    pallas_call x16 -> x19, Pallas kernels: 56 us -> 47.6 us  [call(): pl.pallas_call(body, grid=(1,), in_specs=[whole(a.shape) if s is None els...]
    ppermute x38 -> x39, waiting for transfers between devices: 82.6 us -> 87.9 us  [flip(): lax.ppermute(flat[0] if len(flat) == 1 else jnp.concatenate(flat, 0), axi...]
    ppermute x38 -> x39, starting transfers between devices: 58.3 us -> 56.7 us  [flip(): lax.ppermute(flat[0] if len(flat) == 1 else jnp.concatenate(flat, 0), axi...]
  transfers between devices with their start and end apart: 38 -> 39, of which waited for: 21 -> 24; matrix products, arithmetic and copies ran while one was open for 1% -> 1% of each run, Pallas kernels for 22% -> 18%
where the time goes in v7:
time: 202 us
  waiting for transfers between devices  87.9 us (44%)
  starting transfers between devices  56.7 us (28%)
  Pallas kernels  47.6 us (24%)
  local copies, waits for them, and re-layouts  5.26 us (3%)
  other arithmetic  2.86 us (1%)
    ppermute x39, waiting for transfers between devices, flip(): lax.ppermute(flat[0] if len(flat) == 1 else jnp.concatenate(flat, 0), axi...  87.9 us
    ppermute x39, starting transfers between devices, flip(): lax.ppermute(flat[0] if len(flat) == 1 else jnp.concatenate(flat, 0), axi...  56.7 us
    pallas_call x19, Pallas kernels, call(): pl.pallas_call(body, grid=(1,), in_specs=[whole(a.shape) if s is None els...  47.6 us
  transfers between devices with their start and end apart: 39, of which 24 were waited for; matrix products, arithmetic and copies ran while one was open for 1% of the time, Pallas kernels for 18%

profile of v7, /device:TPU:0, one launch (start us, length us, event | category | flops | bytes accessed | tf_op | source)
XLA Modules:
  0.0 201.7 jit_solution(5522045100618625845)
XLA Ops:
  4.4 4.1 %collective-permute-start = (bf16[176,512]{1,0:T(8,128)(2,1)S(1)}, bf16[176,512]{1,0:T(8,128)(2,1)S(1)}, u32[]{:S(2)}, u32[]{:S(2)}) collective-permute-start(bf16[176,512]{1,0:T(8,128)(2,1)S(1)} %pad_maximum_fusion.12), channel_id=1, source_target_pairs={{0,4},{1,5},{2,6},{3,7},{4,0},{5,1},{6,2},{7,3},{8,12},{9,13},{10,... | collective-permute-start | bytes 540680 | tf_op jit(solution)/shard_map/ppermute | solution.py:491
  10.9 6.0 %collective-permute-done = bf16[176,512]{1,0:T(8,128)(2,1)S(1)} collective-permute-done((bf16[176,512]{1,0:T(8,128)(2,1)S(1)}, bf16[176,512]{1,0:T(8,128)(2,1)S(1)}, u32[]{:S(2)}, u32[]{:S(2)}) %collective-permute-start) | collective-permute-done | bytes 180256 | tf_op jit(solution)/shard_map/ppermute | solution.py:491
  18.8 3.4 %collective-permute-start.2 = (bf16[224,512]{1,0:T(8,128)(2,1)S(1)}, bf16[224,512]{1,0:T(8,128)(2,1)S(1)}, u32[]{:S(2)}, u32[]{:S(2)}) collective-permute-start(bf16[224,512]{1,0:T(8,128)(2,1)S(1)} %pad_maximum_fusion.9), channel_id=1, source_target_pairs={{0,4},{1,5},{2,6},{3,7},{4,0},{5,1},{6,2},{7,3},{8,12},{9,13},{10,... | collective-permute-start | bytes 688136 | tf_op jit(solution)/shard_map/ppermute | solution.py:491
  22.3 9.2 %collective-permute-done.2 = bf16[224,512]{1,0:T(8,128)(2,1)S(1)} collective-permute-done((bf16[224,512]{1,0:T(8,128)(2,1)S(1)}, bf16[224,512]{1,0:T(8,128)(2,1)S(1)}, u32[]{:S(2)}, u32[]{:S(2)}) %collective-permute-start.2) | collective-permute-done | bytes 229408 | tf_op jit(solution)/shard_map/ppermute | solution.py:491
  40.9 7.5 %collective-permute-done.6.message = bf16[272,512]{1,0:T(8,128)(2,1)S(1)} collective-permute-done((bf16[272,512]{1,0:T(8,128)(2,1)S(1)}, bf16[272,512]{1,0:T(8,128)(2,1)S(1)}, u32[]{:S(2)}, u32[]{:S(2)}) %collective-permute-start.6) | collective-permute-done | bytes 278560 | tf_op jit(solution)/shard_map/ppermute | solution.py:491
  52.4 4.5 %collective-permute-start.9 = (bf16[256,512]{1,0:T(8,128)(2,1)S(1)}, bf16[256,512]{1,0:T(8,128)(2,1)S(1)}, u32[]{:S(2)}, u32[]{:S(2)}) collective-permute-start(bf16[256,512]{1,0:T(8,128)(2,1)S(1)} %bitcast.107), channel_id=1, source_target_pairs={{0,2},{1,3},{2,0},{3,1},{4,6},{5,7},{6,4},{7,5},{8,10},{9,11},{10,... | collective-permute-start | bytes 786440 | tf_op jit(solution)/shard_map/ppermute | solution.py:491
  57.6 5.7 %collective-permute-done.9 = bf16[256,512]{1,0:T(8,128)(2,1)S(1)} collective-permute-done((bf16[256,512]{1,0:T(8,128)(2,1)S(1)}, bf16[256,512]{1,0:T(8,128)(2,1)S(1)}, u32[]{:S(2)}, u32[]{:S(2)}) %collective-permute-start.9) | collective-permute-done | bytes 262176 | tf_op jit(solution)/shard_map/ppermute | solution.py:491
  63.4 4.1 %collective-permute-start.11 = (bf16[768,512]{1,0:T(8,128)(2,1)S(1)}, bf16[768,512]{1,0:T(8,128)(2,1)S(1)}, u32[]{:S(2)}, u32[]{:S(2)}) collective-permute-start(bf16[768,512]{1,0:T(8,128)(2,1)S(1)} %bitcast.84), channel_id=1, source_target_pairs={{0,2},{1,3},{2,0},{3,1},{4,6},{5,7},{6,4},{7,5},{8,10},{9,11},{10,... | collective-permute-start | bytes 2359304 | tf_op jit(solution)/shard_map/ppermute | solution.py:491
  69.3 4.8 %collective-permute-done.14 = bf16[512,512]{1,0:T(8,128)(2,1)S(1)} collective-permute-done((bf16[512,512]{1,0:T(8,128)(2,1)S(1)}, bf16[512,512]{1,0:T(8,128)(2,1)S(1)}, u32[]{:S(2)}, u32[]{:S(2)}) %collective-permute-start.14) | collective-permute-done | bytes 524320 | tf_op jit(solution)/shard_map/ppermute | solution.py:491
  74.9 8.4 %self_forward.1 = (bf16[1024,512]{1,0:T(8,128)(2,1)}, bf16[3,512,512]{2,1,0:T(8,128)(2,1)}, bf16[256,512]{1,0:T(8,128)(2,1)}, bf16[1024,1024]{1,0:T(8,128)(2,1)}...) custom-call(s32[131]{0:T(256)S(1)} %concatenate.58.ids, ...), custom_call_target="tpu_custom_call" | custom-call | flops 1000 | bytes 1000 | tf_op jit(solution)/shard_map/self_forward/pallas_call | solution.py:43
  87.9 9.1 %cross_forward.1 = (bf16[1024,512]{1,0:T(8,128)(2,1)}, bf16[5,512,512]{2,1,0:T(8,128)(2,1)S(1)}, f32[16,512]{1,0:T(8,128)}, f32[256,512]{1,0:T(8,128)S(1)}, f32[...) custom-call(s32[131]{0:T(256)S(1)} %concatenate.58.ids, ...), custom_call_target="tpu_custom_call" | custom-call | flops 1000 | bytes 1000 | tf_op jit(solution)/shard_map/cross_forward/pallas_call | solution.py:43
  104.2 7.1 %ffn_both.1 = (bf16[256,512]{1,0:T(8,128)(2,1)S(1)}, f32[16,512]{1,0:T(8,128)S(1)}, f32[256,512]{1,0:T(8,128)S(1)}, bf16[256,512]{1,0:T(8,128)(2,1)S(1)}, bf16[2...) custom-call(s32[131]{0:T(256)S(1)} %concatenate.58.ids, f32[256,512]{1,0:T(8,128)S(1)} %get-tuple-element.149.xh1, ...), custom_call_target="tpu_custom_call" | custom-call | flops 1000 | bytes 1000 | tf_op jit(solution)/shard_map/ffn_both/pallas_call | solution.py:43
  117.0 6.5 %cross_back_b.1 = (f32[256,512]{1,0:T(8,128)S(1)}, bf16[256,512]{1,0:T(8,128)(2,1)S(1)}, bf16[256,512]{1,0:T(8,128)(2,1)S(1)}, bf16[256,512]{1,0:T(8,128)(2,1)S(...) custom-call(s32[131]{0:T(256)S(1)} %concatenate.58.ids, ...), custom_call_target="tpu_custom_call" | custom-call | flops 1000 | bytes 1000 | tf_op jit(solution)/shard_map/cross_back_b/pallas_call | solution.py:43
  123.6 4.3 %collective-permute-start.23 = (bf16[256,512]{1,0:T(8,128)(2,1)S(1)}, bf16[256,512]{1,0:T(8,128)(2,1)S(1)}, u32[]{:S(2)}, u32[]{:S(2)}) collective-permute-start(bf16[256,512]{1,0:T(8,128)(2,1)S(1)} %get-tuple-element.188), channel_id=1, source_target_pairs={{0,2},{1,3},{2,0},{3,1},{4,6},{5,7},{6,4},{7,5},{8,10},{9,11},{10,... | collective-permute-start | bytes 786440 | tf_op jit(solution)/shard_map/ppermute | solution.py:491
  132.4 5.9 %self_back_b.1 = (f32[256,512]{1,0:T(8,128)S(1)}, bf16[256,512]{1,0:T(8,128)(2,1)S(1)}, bf16[256,512]{1,0:T(8,128)(2,1)S(1)}, bf16[256,512]{1,0:T(8,128)(2,1)S(1...) custom-call(s32[131]{0:T(256)S(1)} %concatenate.58.ids, bf16[1024,512]{1,0:T(8,128)(2,1)S(1)} %copy-done.5, ...), custom_call_target="tpu_custom_call" | custom-call | flops 1000 | bytes 1000 | tf_op jit(solution)/shard_map/self_back_b/pallas_call | solution.py:43
  138.3 3.6 %collective-permute-done.24.refs_2_ = bf16[256,512]{1,0:T(8,128)(2,1)S(1)} collective-permute-done((bf16[256,512]{1,0:T(8,128)(2,1)S(1)}, bf16[256,512]{1,0:T(8,128)(2,1)S(1)}, u32[]{:S(2)}, u32[]{:S(2)}) %collective-permute-start.24) | collective-permute-done | bytes 262176 | tf_op jit(solution)/shard_map/ppermute | solution.py:491
  146.1 4.5 %collective-permute-start.31 = (bf16[512,512]{1,0:T(8,128)(2,1)S(1)}, bf16[512,512]{1,0:T(8,128)(2,1)S(1)}, u32[]{:S(2)}, u32[]{:S(2)}) collective-permute-start(bf16[512,512]{1,0:T(8,128)(2,1)S(1)} %away_x.1), channel_id=1, source_target_pairs={{0,2},{1,3},{2,0},{3,1},{4,6},{5,7},{6,4},{7,5},{8,10},{9,11},{10,... | collective-permute-start | bytes 1572872 | tf_op jit(solution)/shard_map/ppermute | solution.py:491
  154.6 5.7 %collective-permute-done.26.refs_3_.refs_6_.refs_4_ = bf16[576,512]{1,0:T(8,128)(2,1)S(1)} collective-permute-done((bf16[576,512]{1,0:T(8,128)(2,1)S(1)}, bf16[576,512]{1,0:T(8,128)(2,1)S(1)}, u32[]{:S(2)}, u32[]{:S(2)}) %collective-permute-start.26) | collective-permute-done | bytes 589856 | tf_op jit(solution)/shard_map/ppermute | solution.py:491
  160.5 4.5 %collective-permute-start.27 = (bf16[288,512]{1,0:T(8,128)(2,1)S(1)}, bf16[288,512]{1,0:T(8,128)(2,1)S(1)}, u32[]{:S(2)}, u32[]{:S(2)}) collective-permute-start(bf16[288,512]{1,0:T(8,128)(2,1)S(1)} %sum_1z.1), channel_id=1, source_target_pairs={{0,2},{1,3},{2,0},{3,1},{4,6},{5,7},{6,4},{7,5},{8,10},{9,11},{10,... | collective-permute-start | bytes 884744 | tf_op jit(solution)/shard_map/ppermute | solution.py:491
  165.0 4.0 %collective-permute-done.31.refs_1_ = bf16[512,512]{1,0:T(8,128)(2,1)S(1)} collective-permute-done((bf16[512,512]{1,0:T(8,128)(2,1)S(1)}, bf16[512,512]{1,0:T(8,128)(2,1)S(1)}, u32[]{:S(2)}, u32[]{:S(2)}) %collective-permute-start.31) | collective-permute-done | bytes 524320 | tf_op jit(solution)/shard_map/ppermute | solution.py:491
  169.6 3.8 %collective-permute-done.29.refs_5_.refs_8_.refs_21_ = bf16[384,512]{1,0:T(8,128)(2,1)S(1)} collective-permute-done((bf16[384,512]{1,0:T(8,128)(2,1)S(1)}, bf16[384,512]{1,0:T(8,128)(2,1)S(1)}, u32[]{:S(2)}, u32[]{:S(2)}) %collective-permute-start.29) | collective-permute-done | bytes 393248 | tf_op jit(solution)/shard_map/ppermute | solution.py:491
  180.7 5.7 %collective-permute-done.36.refs_4_.refs_17_ = bf16[240,512]{1,0:T(8,128)(2,1)S(1)} collective-permute-done((bf16[240,512]{1,0:T(8,128)(2,1)S(1)}, bf16[240,512]{1,0:T(8,128)(2,1)S(1)}, u32[]{:S(2)}, u32[]{:S(2)}) %collective-permute-start.36) | collective-permute-done | bytes 245792 | tf_op jit(solution)/shard_map/ppermute | solution.py:491
  189.5 3.5 %collective-permute-done.35.refs_3_.refs_16_ = bf16[240,512]{1,0:T(8,128)(2,1)S(1)} collective-permute-done((bf16[240,512]{1,0:T(8,128)(2,1)S(1)}, bf16[240,512]{1,0:T(8,128)(2,1)S(1)}, u32[]{:S(2)}, u32[]{:S(2)}) %collective-permute-start.35) | collective-permute-done | bytes 245792 | tf_op jit(solution)/shard_map/ppermute | solution.py:491
  195.5 4.2 %collective-permute-done.38.refs_12_ = bf16[128,512]{1,0:T(8,128)(2,1)S(1)} collective-permute-done((bf16[128,512]{1,0:T(8,128)(2,1)S(1)}, bf16[128,512]{1,0:T(8,128)(2,1)S(1)}, u32[]{:S(2)}, u32[]{:S(2)}) %collective-permute-start.38) | collective-permute-done | bytes 131104 | tf_op jit(solution)/shard_map/ppermute | solution.py:491
  (174 shorter events, 70.2 us)
Async XLA Ops:
  17.9 14.6 %collective-permute-start.1 = (bf16[352,512]{1,0:T(8,128)(2,1)S(1)}, bf16[352,512]{1,0:T(8,128)(2,1)S(1)}, u32[]{:S(2)}, u32[]{:S(2)}) collective-permute-start(bf16[352,512]{1,0:T(8,128)(2,1)S(1)} %pad_maximum_fusion.6), channel_id=1, source_target_pairs={{0,2},{1,3},{2,0},{3,1},{4,6},{5,7},{6,4},{7,5},{8,10},{9,11},{10,... | collective-permute-start | bytes 1081352 | tf_op jit(solution)/shard_map/ppermute | solution.py:491
  32.7 16.5 %collective-permute-start.3 = (bf16[704,512]{1,0:T(8,128)(2,1)S(1)}, bf16[704,512]{1,0:T(8,128)(2,1)S(1)}, u32[]{:S(2)}, u32[]{:S(2)}) collective-permute-start(bf16[704,512]{1,0:T(8,128)(2,1)S(1)} %pad_maximum_fusion), channel_id=1, source_target_pairs={{0,1},{1,0},{2,3},{3,2},{4,5},{5,4},{6,7},{7,6},{8,9},{9,8},{10,11... | collective-permute-start | bytes 2162696 | tf_op jit(solution)/shard_map/ppermute | solution.py:491
  34.0 14.4 %collective-permute-start.6 = (bf16[272,512]{1,0:T(8,128)(2,1)S(1)}, bf16[272,512]{1,0:T(8,128)(2,1)S(1)}, u32[]{:S(2)}, u32[]{:S(2)}) collective-permute-start(bf16[272,512]{1,0:T(8,128)(2,1)S(1)} %fusion.1), channel_id=1, source_target_pairs={{0,4},{1,5},{2,6},{3,7},{4,0},{5,1},{6,2},{7,3},{8,12},{9,13},{10,... | collective-permute-start | bytes 835592 | tf_op jit(solution)/shard_map/ppermute | solution.py:491
  49.3 14.0 %collective-permute-start.10 = (bf16[384,512]{1,0:T(8,128)(2,1)S(1)}, bf16[384,512]{1,0:T(8,128)(2,1)S(1)}, u32[]{:S(2)}, u32[]{:S(2)}) collective-permute-start(bf16[384,512]{1,0:T(8,128)(2,1)S(1)} %bitcast.76), channel_id=1, source_target_pairs={{0,8},{8,0},{16,24},{24,16},{1,9},{9,1},{17,25},{25,17},{2,10},{10... | collective-permute-start | bytes 1179656 | tf_op jit(solution)/shard_map/ppermute | solution.py:491
  49.4 13.9 %collective-permute-start.7 = (bf16[384,512]{1,0:T(8,128)(2,1)S(1)}, bf16[384,512]{1,0:T(8,128)(2,1)S(1)}, u32[]{:S(2)}, u32[]{:S(2)}) collective-permute-start(bf16[384,512]{1,0:T(8,128)(2,1)S(1)} %bitcast.77), channel_id=1, source_target_pairs={{0,16},{8,24},{16,0},{24,8},{1,17},{9,25},{17,1},{25,9},{2,18},{10... | collective-permute-start | bytes 1179656 | tf_op jit(solution)/shard_map/ppermute | solution.py:491
  57.0 17.1 %collective-permute-start.14 = (bf16[512,512]{1,0:T(8,128)(2,1)S(1)}, bf16[512,512]{1,0:T(8,128)(2,1)S(1)}, u32[]{:S(2)}, u32[]{:S(2)}) collective-permute-start(bf16[512,512]{1,0:T(8,128)(2,1)S(1)} %bitcast.123), channel_id=1, source_target_pairs={{0,1},{1,0},{2,3},{3,2},{4,5},{5,4},{6,7},{7,6},{8,9},{9,8},{10,11... | collective-permute-start | bytes 1572872 | tf_op jit(solution)/shard_map/ppermute | solution.py:491
  63.3 21.2 %collective-permute-start.13 = (bf16[768,512]{1,0:T(8,128)(2,1)S(1)}, bf16[768,512]{1,0:T(8,128)(2,1)S(1)}, u32[]{:S(2)}, u32[]{:S(2)}) collective-permute-start(bf16[768,512]{1,0:T(8,128)(2,1)S(1)} %bitcast.83), channel_id=1, source_target_pairs={{0,8},{8,0},{16,24},{24,16},{1,9},{9,1},{17,25},{25,17},{2,10},{10... | collective-permute-start | bytes 2359304 | tf_op jit(solution)/shard_map/ppermute | solution.py:491
  63.4 22.2 %collective-permute-start.11 = (bf16[768,512]{1,0:T(8,128)(2,1)S(1)}, bf16[768,512]{1,0:T(8,128)(2,1)S(1)}, u32[]{:S(2)}, u32[]{:S(2)}) collective-permute-start(bf16[768,512]{1,0:T(8,128)(2,1)S(1)} %bitcast.84), channel_id=1, source_target_pairs={{0,2},{1,3},{2,0},{3,1},{4,6},{5,7},{6,4},{7,5},{8,10},{9,11},{10,... | collective-permute-start | bytes 2359304 | tf_op jit(solution)/shard_map/ppermute | solution.py:491
  67.7 16.8 %collective-permute-start.12 = (bf16[512,512]{1,0:T(8,128)(2,1)S(1)}, bf16[512,512]{1,0:T(8,128)(2,1)S(1)}, u32[]{:S(2)}, u32[]{:S(2)}) collective-permute-start(bf16[512,512]{1,0:T(8,128)(2,1)S(1)} %bitcast.74), channel_id=1, source_target_pairs={{0,1},{1,0},{2,3},{3,2},{4,5},{5,4},{6,7},{7,6},{8,9},{9,8},{10,11... | collective-permute-start | bytes 1572872 | tf_op jit(solution)/shard_map/ppermute | solution.py:491
  74.1 22.9 %collective-permute-start.18 = (bf16[1024,512]{1,0:T(8,128)(2,1)S(1)}, bf16[1024,512]{1,0:T(8,128)(2,1)S(1)}, u32[]{:S(2)}, u32[]{:S(2)}) collective-permute-start(bf16[1024,512]{1,0:T(8,128)(2,1)S(1)} %bitcast.78), channel_id=1, source_target_pairs={{0,8},{8,0},{16,24},{24,16},{1,9},{9,1},{17,25},{25,17},{2,10},{10... | collective-permute-start | bytes 3145736 | tf_op jit(solution)/shard_map/ppermute | solution.py:491
  74.2 25.6 %collective-permute-start.17 = (bf16[1024,512]{1,0:T(8,128)(2,1)S(1)}, bf16[1024,512]{1,0:T(8,128)(2,1)S(1)}, u32[]{:S(2)}, u32[]{:S(2)}) collective-permute-start(bf16[1024,512]{1,0:T(8,128)(2,1)S(1)} %bitcast.79), channel_id=1, source_target_pairs={{0,16},{8,24},{16,0},{24,8},{1,17},{9,25},{17,1},{25,9},{2,18},{10... | collective-permute-start | bytes 3145736 | tf_op jit(solution)/shard_map/ppermute | solution.py:491
  116.2 28.1 %collective-permute-start.21 = (bf16[1152,512]{1,0:T(8,128)(2,1)S(1)}, bf16[1152,512]{1,0:T(8,128)(2,1)S(1)}, u32[]{:S(2)}, u32[]{:S(2)}) collective-permute-start(bf16[1152,512]{1,0:T(8,128)(2,1)S(1)} %add_convert_fusion), channel_id=1, source_target_pairs={{0,16},{8,24},{16,0},{24,8},{1,17},{9,25},{17,1},{25,9},{2,18},{10... | collective-permute-start | bytes 3538952 | tf_op jit(solution)/shard_map/ppermute | solution.py:491
  123.6 14.7 %collective-permute-start.23 = (bf16[256,512]{1,0:T(8,128)(2,1)S(1)}, bf16[256,512]{1,0:T(8,128)(2,1)S(1)}, u32[]{:S(2)}, u32[]{:S(2)}) collective-permute-start(bf16[256,512]{1,0:T(8,128)(2,1)S(1)} %get-tuple-element.188), channel_id=1, source_target_pairs={{0,2},{1,3},{2,0},{3,1},{4,6},{5,7},{6,4},{7,5},{8,10},{9,11},{10,... | collective-permute-start | bytes 786440 | tf_op jit(solution)/shard_map/ppermute | solution.py:491
  127.9 14.0 %collective-permute-start.24 = (bf16[256,512]{1,0:T(8,128)(2,1)S(1)}, bf16[256,512]{1,0:T(8,128)(2,1)S(1)}, u32[]{:S(2)}, u32[]{:S(2)}) collective-permute-start(bf16[256,512]{1,0:T(8,128)(2,1)S(1)} %get-tuple-element.189), channel_id=1, source_target_pairs={{0,1},{1,0},{2,3},{3,2},{4,5},{5,4},{6,7},{7,6},{8,9},{9,8},{10,11... | collective-permute-start | bytes 786440 | tf_op jit(solution)/shard_map/ppermute | solution.py:491
  144.5 15.8 %collective-permute-start.26 = (bf16[576,512]{1,0:T(8,128)(2,1)S(1)}, bf16[576,512]{1,0:T(8,128)(2,1)S(1)}, u32[]{:S(2)}, u32[]{:S(2)}) collective-permute-start(bf16[576,512]{1,0:T(8,128)(2,1)S(1)} %sum_1x.1), channel_id=1, source_target_pairs={{0,1},{1,0},{2,3},{3,2},{4,5},{5,4},{6,7},{7,6},{8,9},{9,8},{10,11... | collective-permute-start | bytes 1769480 | tf_op jit(solution)/shard_map/ppermute | solution.py:491
  146.1 22.8 %collective-permute-start.31 = (bf16[512,512]{1,0:T(8,128)(2,1)S(1)}, bf16[512,512]{1,0:T(8,128)(2,1)S(1)}, u32[]{:S(2)}, u32[]{:S(2)}) collective-permute-start(bf16[512,512]{1,0:T(8,128)(2,1)S(1)} %away_x.1), channel_id=1, source_target_pairs={{0,2},{1,3},{2,0},{3,1},{4,6},{5,7},{6,4},{7,5},{8,10},{9,11},{10,... | collective-permute-start | bytes 1572872 | tf_op jit(solution)/shard_map/ppermute | solution.py:491
  150.7 22.6 %collective-permute-start.34 = (bf16[528,512]{1,0:T(8,128)(2,1)S(1)}, bf16[528,512]{1,0:T(8,128)(2,1)S(1)}, u32[]{:S(2)}, u32[]{:S(2)}) collective-permute-start(bf16[528,512]{1,0:T(8,128)(2,1)S(1)} %sum_y2.1.refs_6_), channel_id=1, source_target_pairs={{0,16},{8,24},{16,0},{24,8},{1,17},{9,25},{17,1},{25,9},{2,18},{10... | collective-permute-start | bytes 1622024 | tf_op jit(solution)/shard_map/ppermute | solution.py:491
  151.4 21.9 %collective-permute-start.29 = (bf16[384,512]{1,0:T(8,128)(2,1)S(1)}, bf16[384,512]{1,0:T(8,128)(2,1)S(1)}, u32[]{:S(2)}, u32[]{:S(2)}) collective-permute-start(bf16[384,512]{1,0:T(8,128)(2,1)S(1)} %sum_y3.1), channel_id=1, source_target_pairs={{0,16},{8,24},{16,0},{24,8},{1,17},{9,25},{17,1},{25,9},{2,18},{10... | collective-permute-start | bytes 1179656 | tf_op jit(solution)/shard_map/ppermute | solution.py:491
  153.1 16.5 %collective-permute-start.30 = (bf16[256,512]{1,0:T(8,128)(2,1)S(1)}, bf16[256,512]{1,0:T(8,128)(2,1)S(1)}, u32[]{:S(2)}, u32[]{:S(2)}) collective-permute-start(bf16[256,512]{1,0:T(8,128)(2,1)S(1)} %get-tuple-element.199), channel_id=1, source_target_pairs={{0,4},{1,5},{2,6},{3,7},{4,0},{5,1},{6,2},{7,3},{8,12},{9,13},{10,... | collective-permute-start | bytes 786440 | tf_op jit(solution)/shard_map/ppermute | solution.py:491
  160.5 20.0 %collective-permute-start.27 = (bf16[288,512]{1,0:T(8,128)(2,1)S(1)}, bf16[288,512]{1,0:T(8,128)(2,1)S(1)}, u32[]{:S(2)}, u32[]{:S(2)}) collective-permute-start(bf16[288,512]{1,0:T(8,128)(2,1)S(1)} %sum_1z.1), channel_id=1, source_target_pairs={{0,2},{1,3},{2,0},{3,1},{4,6},{5,7},{6,4},{7,5},{8,10},{9,11},{10,... | collective-permute-start | bytes 884744 | tf_op jit(solution)/shard_map/ppermute | solution.py:491
  173.6 12.7 %collective-permute-start.36 = (bf16[240,512]{1,0:T(8,128)(2,1)S(1)}, bf16[240,512]{1,0:T(8,128)(2,1)S(1)}, u32[]{:S(2)}, u32[]{:S(2)}) collective-permute-start(bf16[240,512]{1,0:T(8,128)(2,1)S(1)} %get-tuple-element.212), channel_id=1, source_target_pairs={{0,1},{1,0},{2,3},{3,2},{4,5},{5,4},{6,7},{7,6},{8,9},{9,8},{10,11... | collective-permute-start | bytes 737288 | tf_op jit(solution)/shard_map/ppermute | solution.py:491
  174.2 15.3 %collective-permute-start.37 = (bf16[240,512]{1,0:T(8,128)(2,1)S(1)}, bf16[240,512]{1,0:T(8,128)(2,1)S(1)}, u32[]{:S(2)}, u32[]{:S(2)}) collective-permute-start(bf16[240,512]{1,0:T(8,128)(2,1)S(1)} %get-tuple-element.213), channel_id=1, source_target_pairs={{0,3},{1,2},{2,1},{3,0},{4,7},{5,6},{6,5},{7,4},{8,11},{9,10},{10,... | collective-permute-start | bytes 737288 | tf_op jit(solution)/shard_map/ppermute | solution.py:491
  175.5 17.6 %collective-permute-start.35 = (bf16[240,512]{1,0:T(8,128)(2,1)S(1)}, bf16[240,512]{1,0:T(8,128)(2,1)S(1)}, u32[]{:S(2)}, u32[]{:S(2)}) collective-permute-start(bf16[240,512]{1,0:T(8,128)(2,1)S(1)} %get-tuple-element.211.refs_9_), channel_id=1, source_target_pairs={{0,2},{1,3},{2,0},{3,1},{4,6},{5,7},{6,4},{7,5},{8,10},{9,11},{10,... | collective-permute-start | bytes 737288 | tf_op jit(solution)/shard_map/ppermute | solution.py:491
  180.6 14.9 %collective-permute-start.33 = (bf16[272,512]{1,0:T(8,128)(2,1)S(1)}, bf16[272,512]{1,0:T(8,128)(2,1)S(1)}, u32[]{:S(2)}, u32[]{:S(2)}) collective-permute-start(bf16[272,512]{1,0:T(8,128)(2,1)S(1)} %get-tuple-element.207), channel_id=1, source_target_pairs={{0,4},{1,5},{2,6},{3,7},{4,0},{5,1},{6,2},{7,3},{8,12},{9,13},{10,... | collective-permute-start | bytes 835592 | tf_op jit(solution)/shard_map/ppermute | solution.py:491
  (37 other events, 338.7 us)

commit v8 on v7

--- a/solution.py
+++ b/solution.py
@@ -29,6 +29,10 @@
 
 def dot(a, b, dims=NN):
     return lax.dot_general(a, b, dims, preferred_element_type=F32)
+
+
+def in_hbm(v):
+    return pltpu.with_memory_space_constraint(v, pltpu.HBM)
 
 
 def whole(shape):
@@ -205,22 +209,30 @@
     return ((send, 1 - ids[0]), (keep, ids[0]))
 
 
-def pack(s_in, s_out, c_in, c_q, c_out, up, down, gain, bias, at, pa, pb, pf):
+def pack(s_in, s_out, c_in, c_q, c_out, up, down, gain, bias, inputs, encoder, teacher, valid, at,
+         first, second, third, own_x, own_e):
+    tok = own_x.shape[0]
+    mine = at[1]
+    first[:tok] = inputs[1 - mine]
+    own_x[...] = inputs[mine]
+    own_e[...] = encoder[mine]
     for j in range(3):
-        pa[j] = s_in[:, j * D : (j + 1) * D]
-    pb[0] = s_out[...]
-    for j in range(2):
-        pb[1 + j] = c_in[:, j * D : (j + 1) * D]
-    pb[3] = c_q[...]
-    pb[4] = c_out[...]
-    for j in range(4):
-        pf[j] = up[:, j * D : (j + 1) * D]
-        pf[4 + j] = down[16 * j : 16 * j + 16, :]
+        first[tok + 16 * j : tok + 16 * j + 16] = s_in[:, j * D : (j + 1) * D]
+    parts = [s_out] + [c_in.at[:, j * D : (j + 1) * D] for j in range(2)] + [c_q, c_out, None]
+    parts += [up.at[:, j * D : (j + 1) * D] for j in range(4)] + [down.at[16 * j : 16 * j + 16] for j in range(4)]
+    for j, part in enumerate(parts):
+        if part is not None:
+            second[16 * j : 16 * j + 16] = part[...]
     rows = jnp.concatenate([gain[...], bias[...], jnp.zeros((10, 16), BF)], 0)
     column = lax.broadcasted_iota(jnp.int32, (16, D), 1)
     row = lax.broadcasted_iota(jnp.int32, (16, D), 0)
     pick = (column == at[0] * 16 + row).astype(BF)
-    pb[5] = dot(rows, pick).astype(BF)
+    second[80:96] = dot(rows, pick).astype(BF)
+    third[:tok] = encoder[1 - mine]
+    third[tok : 2 * tok] = teacher[1 - mine]
+    marks = jnp.where(mine == 0, valid[1:2], valid[0:1]).astype(F32)
+    marks = jnp.concatenate([marks, jnp.zeros((1, D - tok), F32)], 1)
+    third[2 * tok :] = jnp.where(row == 0, marks, 0.0).astype(BF)
 
 
 def join(full, near, far):
@@ -510,7 +522,6 @@
         def append(v, got):
             return jnp.concatenate([v, got], 0)
 
-        valid_away = jnp.pad(other(dec_valid).astype(BF)[None], ((0, 15), (0, D - tok)))
 
         row_bits = (2, 1) if fast else tuple(1 << b for b in range(half.bit_length() - 1))
         slots = jnp.arange(half, dtype=jnp.int32)
@@ -551,27 +562,33 @@
 
         if fast:
             mats = [self_in, self_out, cross_in, cross_query, cross_out, ffn_up, ffn_down, norm_gain, norm_bias]
-            wa, wb, wf = run(
+            first, second, third, own_x, own_e = run(
                 pack,
-                [(w, None) for w in mats] + [(dev.astype(jnp.int32)[None], SMEM)],
-                [((3, 16, D), BF), ((6, 16, D), BF), ((8, 16, D), BF)],
+                [(w, None) for w in mats + [inputs, encoder, teacher, dec_valid]]
+                + [(jnp.stack([dev, mine]).astype(jnp.int32), SMEM)],
+                [((tok + 48, D), BF), ((224, D), BF), ((2 * tok + 16, D), BF), ((tok, D), BF), ((tok, D), BF)],
                 name="pack",
                 vmem=56,
             )
-            wa, wb, wf = wa[None], wb[None], wf[None]
-            got_x, got_a = flip(zh, [other(inputs), wa])
-            got_x, got_a, wb, wf, segs, ids = tie(got_x, got_a, wb, wf, segs, ids)
-            got_b, got_f = flip(zh, [wb, wf])
-            xf, wa = jnp.stack([of(inputs, mine), got_x])[None], append(wa, got_a)
+
+            def split(v, *counts):
+                ends = [sum(counts[: i + 1]) for i in range(len(counts))]
+                return [v[e - c : e].reshape(1, c // 16, 16, D) for c, e in zip(counts, ends)]
+
+            got = swap(zh, first)
+            got, second, segs, ids = tie(got, second, segs, ids)
+            xf = jnp.stack([own_x, got[:tok]])[None]
+            wa = append(*(v[tok:].reshape(1, 3, 16, D) for v in (first, got)))
+            got_bf = swap(zh, second)
             got_x, got_a = flip(zl, [xf, wa])
-            got_x, got_a, got_b, got_f, away_e = tie(got_x, got_a, got_b, got_f, other(encoder))
+            got_x, got_a, got_bf, third = tie(got_x, got_a, got_bf, third)
             xf, wa = append(xf, got_x), append(wa, got_a)
-            wb, wf = append(wb, got_b), append(wf, got_f)
+            wb, wf = (append(*both) for both in zip(split(second, 96, 128), split(got_bf, 96, 128)))
             got_x, got_a = flip(x, [xf, wa])
-            message = swap(zh, jnp.concatenate([away_e, other(teacher), valid_away], 0))
+            message = swap(zh, third)
             got_e = message[:tok]
             got_b, got_f = swap(y, wb), swap(zl, wf)
-            ef = jnp.stack([of(encoder, mine), got_e])[None]
+            ef = jnp.stack([own_e, got_e])[None]
             got_x, got_a, got_b, got_f, ef = tie(got_x, got_a, got_b, got_f, ef)
             wa, wb, wf = append(wa, got_a), append(wb, got_b), append(wf, got_f)
             got_a, got_b, got_e, got_f = swap(y, wa), swap(x, wb), swap(zl, ef), swap(x, wf)
@@ -585,6 +602,7 @@
             got_f = swap(y, wf)
             wb_far, wf_far = swap(core, wb), swap(core, wf)
         else:
+            valid_away = jnp.pad(other(dec_valid).astype(BF)[None], ((0, 15), (0, D - tok)))
             got_x = swap(("seq", half), other(inputs))
             message = swap(("seq", half), jnp.concatenate([other(encoder), other(teacher), valid_away], 0))
             got_e = message[:tok]
@@ -652,7 +670,7 @@
             wf = [wf, got_f, wf_far, swap(core, got_f)]
         out, small, d_r2, d_mix2, keep1, send1 = run(
             ffn_both,
-            [sm, (xh1, None), (at2, HBM), (teacher, None), (message, None), (dec_valid, None), (wb, None), (norms, HBM)]
+            [sm, (xh1, None), (in_hbm(at2), HBM), (teacher, None), (message, None), (dec_valid, None), (wb, None), (in_hbm(norms), HBM)]
             + [(v, None) for v in wf],
             [((rows, D), BF), ((16, D), F32), ((rows, D), F32), ((rows, D), BF)] + [((2304, D), BF)] * 2,
             scratch=[pltpu.VMEM((rows, FF), BF), pltpu.VMEM((4, rows, D), F32), pltpu.VMEM((rows, D), BF),

time: 202 us -> 199 us (0.985)
  waiting for transfers between devices: 87.9 us -> 83.4 us
  starting transfers between devices: 56.7 us -> 59.1 us
  local copies, waits for them, and re-layouts: 5.26 us -> 3.19 us
    ppermute x39, waiting for transfers between devices: 87.9 us -> 83.4 us  [flip(): lax.ppermute(flat[0] if len(flat) == 1 else jnp.concatenate(flat, 0), axi...]
    ppermute x39, starting transfers between devices: 56.7 us -> 59.1 us  [flip(): lax.ppermute(flat[0] if len(flat) == 1 else jnp.concatenate(flat, 0), axi...]
  transfers between devices with their start and end apart: 39 -> 39, of which waited for: 24 -> 22; matrix products, arithmetic and copies ran while one was open for 1% -> 2% of each run, Pallas kernels for 18% -> 19%
where the time goes in v8:
time: 199 us
  waiting for transfers between devices  83.4 us (42%)
  starting transfers between devices  59.1 us (30%)
  Pallas kernels  48.7 us (24%)
  local copies, waits for them, and re-layouts  3.19 us (2%)
  other arithmetic  2.78 us (1%)
    ppermute x39, waiting for transfers between devices, flip(): lax.ppermute(flat[0] if len(flat) == 1 else jnp.concatenate(flat, 0), axi...  83.4 us
    ppermute x39, starting transfers between devices, flip(): lax.ppermute(flat[0] if len(flat) == 1 else jnp.concatenate(flat, 0), axi...  59.1 us
    pallas_call x19, Pallas kernels, call(): pl.pallas_call(body, grid=(1,), in_specs=[whole(a.shape) if s is None els...  48.7 us
  transfers between devices with their start and end apart: 39, of which 22 were waited for; matrix products, arithmetic and copies ran while one was open for 2% of the time, Pallas kernels for 19%

profile of v8, /device:TPU:0, one launch (start us, length us, event | category | flops | bytes accessed | tf_op | source)
XLA Modules:
  0.0 198.5 jit_solution(16711201221534694677)
XLA Ops:
  3.5 4.1 %collective-permute-start = (bf16[176,512]{1,0:T(8,128)(2,1)}, bf16[176,512]{1,0:T(8,128)(2,1)S(1)}, u32[]{:S(2)}, u32[]{:S(2)}) collective-permute-start(bf16[176,512]{1,0:T(8,128)(2,1)} %get-tuple-element.119), channel_id=1, source_target_pairs={{0,4},{1,5},{2,6},{3,7},{4,0},{5,1},{6,2},{7,3},{8,12},{9,13},{10,... | collective-permute-start | bytes 540680 | tf_op jit(solution)/shard_map/ppermute | solution.py:503
  10.8 5.4 %collective-permute-done = bf16[176,512]{1,0:T(8,128)(2,1)S(1)} collective-permute-done((bf16[176,512]{1,0:T(8,128)(2,1)}, bf16[176,512]{1,0:T(8,128)(2,1)S(1)}, u32[]{:S(2)}, u32[]{:S(2)}) %collective-permute-start) | collective-permute-done | bytes 180256 | tf_op jit(solution)/shard_map/ppermute | solution.py:503
  18.1 3.3 %collective-permute-start.2 = (bf16[224,512]{1,0:T(8,128)(2,1)S(1)}, bf16[224,512]{1,0:T(8,128)(2,1)S(1)}, u32[]{:S(2)}, u32[]{:S(2)}) collective-permute-start(bf16[224,512]{1,0:T(8,128)(2,1)S(1)} %copy-done.16), channel_id=1, source_target_pairs={{0,4},{1,5},{2,6},{3,7},{4,0},{5,1},{6,2},{7,3},{8,12},{9,13},{10,... | collective-permute-start | bytes 688136 | tf_op jit(solution)/shard_map/ppermute | solution.py:503
  21.4 10.4 %collective-permute-done.1 = bf16[352,512]{1,0:T(8,128)(2,1)S(1)} collective-permute-done((bf16[352,512]{1,0:T(8,128)(2,1)S(1)}, bf16[352,512]{1,0:T(8,128)(2,1)S(1)}, u32[]{:S(2)}, u32[]{:S(2)}) %collective-permute-start.1) | collective-permute-done | bytes 360480 | tf_op jit(solution)/shard_map/ppermute | solution.py:503
  40.2 7.6 %collective-permute-done.6.message = bf16[272,512]{1,0:T(8,128)(2,1)S(1)} collective-permute-done((bf16[272,512]{1,0:T(8,128)(2,1)S(1)}, bf16[272,512]{1,0:T(8,128)(2,1)S(1)}, u32[]{:S(2)}, u32[]{:S(2)}) %collective-permute-start.6) | collective-permute-done | bytes 278560 | tf_op jit(solution)/shard_map/ppermute | solution.py:503
  51.6 4.3 %collective-permute-start.9 = (bf16[256,512]{1,0:T(8,128)(2,1)S(1)}, bf16[256,512]{1,0:T(8,128)(2,1)S(1)}, u32[]{:S(2)}, u32[]{:S(2)}) collective-permute-start(bf16[256,512]{1,0:T(8,128)(2,1)S(1)} %bitcast.97), channel_id=1, source_target_pairs={{0,2},{1,3},{2,0},{3,1},{4,6},{5,7},{6,4},{7,5},{8,10},{9,11},{10,... | collective-permute-start | bytes 786440 | tf_op jit(solution)/shard_map/ppermute | solution.py:503
  56.6 6.0 %collective-permute-done.9 = bf16[256,512]{1,0:T(8,128)(2,1)S(1)} collective-permute-done((bf16[256,512]{1,0:T(8,128)(2,1)S(1)}, bf16[256,512]{1,0:T(8,128)(2,1)S(1)}, u32[]{:S(2)}, u32[]{:S(2)}) %collective-permute-start.9) | collective-permute-done | bytes 262176 | tf_op jit(solution)/shard_map/ppermute | solution.py:503
  70.8 8.4 %self_forward.1 = (bf16[1024,512]{1,0:T(8,128)(2,1)}, bf16[3,512,512]{2,1,0:T(8,128)(2,1)}, bf16[256,512]{1,0:T(8,128)(2,1)}, bf16[1024,1024]{1,0:T(8,128)(2,1)}...) custom-call(s32[131]{0:T(256)S(1)} %concatenate.48.ids, ...), custom_call_target="tpu_custom_call" | custom-call | flops 1000 | bytes 1000 | tf_op jit(solution)/shard_map/self_forward/pallas_call | solution.py:47
  81.1 3.3 %collective-permute-done.11 = bf16[768,512]{1,0:T(8,128)(2,1)S(1)} collective-permute-done((bf16[768,512]{1,0:T(8,128)(2,1)S(1)}, bf16[768,512]{1,0:T(8,128)(2,1)S(1)}, u32[]{:S(2)}, u32[]{:S(2)}) %collective-permute-start.11) | collective-permute-done | bytes 786464 | tf_op jit(solution)/shard_map/ppermute | solution.py:503
  86.7 9.0 %cross_forward.1 = (bf16[1024,512]{1,0:T(8,128)(2,1)}, bf16[5,512,512]{2,1,0:T(8,128)(2,1)S(1)}, f32[16,512]{1,0:T(8,128)}, f32[256,512]{1,0:T(8,128)S(1)}, f32[...) custom-call(s32[131]{0:T(256)S(1)} %concatenate.48.ids, ...), custom_call_target="tpu_custom_call" | custom-call | flops 1000 | bytes 1000 | tf_op jit(solution)/shard_map/cross_forward/pallas_call | solution.py:47
  99.0 7.8 %ffn_both.1 = (bf16[256,512]{1,0:T(8,128)(2,1)S(1)}, f32[16,512]{1,0:T(8,128)S(1)}, f32[256,512]{1,0:T(8,128)S(1)}, bf16[256,512]{1,0:T(8,128)(2,1)S(1)}, bf16[2...) custom-call(s32[131]{0:T(256)S(1)} %concatenate.48.ids, f32[256,512]{1,0:T(8,128)S(1)} %get-tuple-element.147.xh1, ...), custom_call_target="tpu_custom_call" | custom-call | flops 1000 | bytes 1000 | tf_op jit(solution)/shard_map/ffn_both/pallas_call | solution.py:47
  112.9 6.5 %cross_back_b.1 = (f32[256,512]{1,0:T(8,128)S(1)}, bf16[256,512]{1,0:T(8,128)(2,1)S(1)}, bf16[256,512]{1,0:T(8,128)(2,1)S(1)}, bf16[256,512]{1,0:T(8,128)(2,1)S(...) custom-call(s32[131]{0:T(256)S(1)} %concatenate.48.ids, ...), custom_call_target="tpu_custom_call" | custom-call | flops 1000 | bytes 1000 | tf_op jit(solution)/shard_map/cross_back_b/pallas_call | solution.py:47
  119.5 6.2 %collective-permute-start.23 = (bf16[256,512]{1,0:T(8,128)(2,1)S(1)}, bf16[256,512]{1,0:T(8,128)(2,1)S(1)}, u32[]{:S(2)}, u32[]{:S(2)}) collective-permute-start(bf16[256,512]{1,0:T(8,128)(2,1)S(1)} %get-tuple-element.186), channel_id=1, source_target_pairs={{0,2},{1,3},{2,0},{3,1},{4,6},{5,7},{6,4},{7,5},{8,10},{9,11},{10,... | collective-permute-start | bytes 786440 | tf_op jit(solution)/shard_map/ppermute | solution.py:503
  130.2 5.9 %self_back_b.1 = (f32[256,512]{1,0:T(8,128)S(1)}, bf16[256,512]{1,0:T(8,128)(2,1)S(1)}, bf16[256,512]{1,0:T(8,128)(2,1)S(1)}, bf16[256,512]{1,0:T(8,128)(2,1)S(1...) custom-call(s32[131]{0:T(256)S(1)} %concatenate.48.ids, bf16[1024,512]{1,0:T(8,128)(2,1)S(1)} %copy-done.5, ...), custom_call_target="tpu_custom_call" | custom-call | flops 1000 | bytes 1000 | tf_op jit(solution)/shard_map/self_back_b/pallas_call | solution.py:47
  136.1 3.7 %collective-permute-done.24.refs_2_ = bf16[256,512]{1,0:T(8,128)(2,1)S(1)} collective-permute-done((bf16[256,512]{1,0:T(8,128)(2,1)S(1)}, bf16[256,512]{1,0:T(8,128)(2,1)S(1)}, u32[]{:S(2)}, u32[]{:S(2)}) %collective-permute-start.24) | collective-permute-done | bytes 262176 | tf_op jit(solution)/shard_map/ppermute | solution.py:503
  141.6 5.9 %collective-permute-start.31 = (bf16[512,512]{1,0:T(8,128)(2,1)S(1)}, bf16[512,512]{1,0:T(8,128)(2,1)S(1)}, u32[]{:S(2)}, u32[]{:S(2)}) collective-permute-start(bf16[512,512]{1,0:T(8,128)(2,1)S(1)} %away_x.1), channel_id=1, source_target_pairs={{0,2},{1,3},{2,0},{3,1},{4,6},{5,7},{6,4},{7,5},{8,10},{9,11},{10,... | collective-permute-start | bytes 1572872 | tf_op jit(solution)/shard_map/ppermute | solution.py:503
  151.5 4.4 %collective-permute-done.26.refs_3_.refs_6_.refs_4_ = bf16[576,512]{1,0:T(8,128)(2,1)S(1)} collective-permute-done((bf16[576,512]{1,0:T(8,128)(2,1)S(1)}, bf16[576,512]{1,0:T(8,128)(2,1)S(1)}, u32[]{:S(2)}, u32[]{:S(2)}) %collective-permute-start.26) | collective-permute-done | bytes 589856 | tf_op jit(solution)/shard_map/ppermute | solution.py:503
  156.0 5.8 %collective-permute-start.27 = (bf16[288,512]{1,0:T(8,128)(2,1)S(1)}, bf16[288,512]{1,0:T(8,128)(2,1)S(1)}, u32[]{:S(2)}, u32[]{:S(2)}) collective-permute-start(bf16[288,512]{1,0:T(8,128)(2,1)S(1)} %sum_1z.1), channel_id=1, source_target_pairs={{0,2},{1,3},{2,0},{3,1},{4,6},{5,7},{6,4},{7,5},{8,10},{9,11},{10,... | collective-permute-start | bytes 884744 | tf_op jit(solution)/shard_map/ppermute | solution.py:503
  161.8 4.0 %collective-permute-done.31.refs_1_ = bf16[512,512]{1,0:T(8,128)(2,1)S(1)} collective-permute-done((bf16[512,512]{1,0:T(8,128)(2,1)S(1)}, bf16[512,512]{1,0:T(8,128)(2,1)S(1)}, u32[]{:S(2)}, u32[]{:S(2)}) %collective-permute-start.31) | collective-permute-done | bytes 524320 | tf_op jit(solution)/shard_map/ppermute | solution.py:503
  166.4 3.8 %collective-permute-done.29.refs_5_.refs_8_.refs_21_ = bf16[384,512]{1,0:T(8,128)(2,1)S(1)} collective-permute-done((bf16[384,512]{1,0:T(8,128)(2,1)S(1)}, bf16[384,512]{1,0:T(8,128)(2,1)S(1)}, u32[]{:S(2)}, u32[]{:S(2)}) %collective-permute-start.29) | collective-permute-done | bytes 393248 | tf_op jit(solution)/shard_map/ppermute | solution.py:503
  177.5 5.6 %collective-permute-done.36.refs_4_.refs_17_ = bf16[240,512]{1,0:T(8,128)(2,1)S(1)} collective-permute-done((bf16[240,512]{1,0:T(8,128)(2,1)S(1)}, bf16[240,512]{1,0:T(8,128)(2,1)S(1)}, u32[]{:S(2)}, u32[]{:S(2)}) %collective-permute-start.36) | collective-permute-done | bytes 245792 | tf_op jit(solution)/shard_map/ppermute | solution.py:503
  183.2 3.3 %collective-permute-done.37.refs_5_.refs_18_ = bf16[240,512]{1,0:T(8,128)(2,1)S(1)} collective-permute-done((bf16[240,512]{1,0:T(8,128)(2,1)S(1)}, bf16[240,512]{1,0:T(8,128)(2,1)S(1)}, u32[]{:S(2)}, u32[]{:S(2)}) %collective-permute-start.37) | collective-permute-done | bytes 245792 | tf_op jit(solution)/shard_map/ppermute | solution.py:503
  186.4 3.5 %collective-permute-done.35.refs_3_.refs_16_ = bf16[240,512]{1,0:T(8,128)(2,1)S(1)} collective-permute-done((bf16[240,512]{1,0:T(8,128)(2,1)S(1)}, bf16[240,512]{1,0:T(8,128)(2,1)S(1)}, u32[]{:S(2)}, u32[]{:S(2)}) %collective-permute-start.35) | collective-permute-done | bytes 245792 | tf_op jit(solution)/shard_map/ppermute | solution.py:503
  190.2 6.4 %collective-permute-done.38.refs_12_ = bf16[128,512]{1,0:T(8,128)(2,1)S(1)} collective-permute-done((bf16[128,512]{1,0:T(8,128)(2,1)S(1)}, bf16[128,512]{1,0:T(8,128)(2,1)S(1)}, u32[]{:S(2)}, u32[]{:S(2)}) %collective-permute-start.38) | collective-permute-done | bytes 131104 | tf_op jit(solution)/shard_map/ppermute | solution.py:503
  (159 shorter events, 62.7 us)
Async XLA Ops:
  3.5 12.7 %collective-permute-start = (bf16[176,512]{1,0:T(8,128)(2,1)}, bf16[176,512]{1,0:T(8,128)(2,1)S(1)}, u32[]{:S(2)}, u32[]{:S(2)}) collective-permute-start(bf16[176,512]{1,0:T(8,128)(2,1)} %get-tuple-element.119), channel_id=1, source_target_pairs={{0,4},{1,5},{2,6},{3,7},{4,0},{5,1},{6,2},{7,3},{8,12},{9,13},{10,... | collective-permute-start | bytes 540680 | tf_op jit(solution)/shard_map/ppermute | solution.py:503
  17.2 14.6 %collective-permute-start.1 = (bf16[352,512]{1,0:T(8,128)(2,1)S(1)}, bf16[352,512]{1,0:T(8,128)(2,1)S(1)}, u32[]{:S(2)}, u32[]{:S(2)}) collective-permute-start(bf16[352,512]{1,0:T(8,128)(2,1)S(1)} %pad_maximum_fusion.8), channel_id=1, source_target_pairs={{0,2},{1,3},{2,0},{3,1},{4,6},{5,7},{6,4},{7,5},{8,10},{9,11},{10,... | collective-permute-start | bytes 1081352 | tf_op jit(solution)/shard_map/ppermute | solution.py:503
  18.1 13.7 %collective-permute-start.2 = (bf16[224,512]{1,0:T(8,128)(2,1)S(1)}, bf16[224,512]{1,0:T(8,128)(2,1)S(1)}, u32[]{:S(2)}, u32[]{:S(2)}) collective-permute-start(bf16[224,512]{1,0:T(8,128)(2,1)S(1)} %copy-done.16), channel_id=1, source_target_pairs={{0,4},{1,5},{2,6},{3,7},{4,0},{5,1},{6,2},{7,3},{8,12},{9,13},{10,... | collective-permute-start | bytes 688136 | tf_op jit(solution)/shard_map/ppermute | solution.py:503
  32.0 16.5 %collective-permute-start.3 = (bf16[704,512]{1,0:T(8,128)(2,1)S(1)}, bf16[704,512]{1,0:T(8,128)(2,1)S(1)}, u32[]{:S(2)}, u32[]{:S(2)}) collective-permute-start(bf16[704,512]{1,0:T(8,128)(2,1)S(1)} %pad_maximum_fusion.2), channel_id=1, source_target_pairs={{0,1},{1,0},{2,3},{3,2},{4,5},{5,4},{6,7},{7,6},{8,9},{9,8},{10,11... | collective-permute-start | bytes 2162696 | tf_op jit(solution)/shard_map/ppermute | solution.py:503
  33.4 14.4 %collective-permute-start.6 = (bf16[272,512]{1,0:T(8,128)(2,1)S(1)}, bf16[272,512]{1,0:T(8,128)(2,1)S(1)}, u32[]{:S(2)}, u32[]{:S(2)}) collective-permute-start(bf16[272,512]{1,0:T(8,128)(2,1)S(1)} %copy-done.18), channel_id=1, source_target_pairs={{0,4},{1,5},{2,6},{3,7},{4,0},{5,1},{6,2},{7,3},{8,12},{9,13},{10,... | collective-permute-start | bytes 835592 | tf_op jit(solution)/shard_map/ppermute | solution.py:503
  48.7 14.0 %collective-permute-start.8 = (bf16[384,512]{1,0:T(8,128)(2,1)S(1)}, bf16[384,512]{1,0:T(8,128)(2,1)S(1)}, u32[]{:S(2)}, u32[]{:S(2)}) collective-permute-start(bf16[384,512]{1,0:T(8,128)(2,1)S(1)} %bitcast.115), channel_id=1, source_target_pairs={{0,1},{1,0},{2,3},{3,2},{4,5},{5,4},{6,7},{7,6},{8,9},{9,8},{10,11... | collective-permute-start | bytes 1179656 | tf_op jit(solution)/shard_map/ppermute | solution.py:503
  56.0 14.5 %collective-permute-start.14 = (bf16[512,512]{1,0:T(8,128)(2,1)S(1)}, bf16[512,512]{1,0:T(8,128)(2,1)S(1)}, u32[]{:S(2)}, u32[]{:S(2)}) collective-permute-start(bf16[512,512]{1,0:T(8,128)(2,1)S(1)} %bitcast.113), channel_id=1, source_target_pairs={{0,1},{1,0},{2,3},{3,2},{4,5},{5,4},{6,7},{7,6},{8,9},{9,8},{10,11... | collective-permute-start | bytes 1572872 | tf_op jit(solution)/shard_map/ppermute | solution.py:503
  62.8 18.3 %collective-permute-start.13 = (bf16[768,512]{1,0:T(8,128)(2,1)S(1)}, bf16[768,512]{1,0:T(8,128)(2,1)S(1)}, u32[]{:S(2)}, u32[]{:S(2)}) collective-permute-start(bf16[768,512]{1,0:T(8,128)(2,1)S(1)} %bitcast.68), channel_id=1, source_target_pairs={{0,8},{8,0},{16,24},{24,16},{1,9},{9,1},{17,25},{25,17},{2,10},{10... | collective-permute-start | bytes 2359304 | tf_op jit(solution)/shard_map/ppermute | solution.py:503
  63.4 21.0 %collective-permute-start.11 = (bf16[768,512]{1,0:T(8,128)(2,1)S(1)}, bf16[768,512]{1,0:T(8,128)(2,1)S(1)}, u32[]{:S(2)}, u32[]{:S(2)}) collective-permute-start(bf16[768,512]{1,0:T(8,128)(2,1)S(1)} %bitcast.69), channel_id=1, source_target_pairs={{0,2},{1,3},{2,0},{3,1},{4,6},{5,7},{6,4},{7,5},{8,10},{9,11},{10,... | collective-permute-start | bytes 2359304 | tf_op jit(solution)/shard_map/ppermute | solution.py:503
  66.7 14.4 %collective-permute-start.12 = (bf16[512,512]{1,0:T(8,128)(2,1)S(1)}, bf16[512,512]{1,0:T(8,128)(2,1)S(1)}, u32[]{:S(2)}, u32[]{:S(2)}) collective-permute-start(bf16[512,512]{1,0:T(8,128)(2,1)S(1)} %bitcast.72), channel_id=1, source_target_pairs={{0,1},{1,0},{2,3},{3,2},{4,5},{5,4},{6,7},{7,6},{8,9},{9,8},{10,11... | collective-permute-start | bytes 1572872 | tf_op jit(solution)/shard_map/ppermute | solution.py:503
  70.6 25.1 %collective-permute-start.18 = (bf16[1024,512]{1,0:T(8,128)(2,1)S(1)}, bf16[1024,512]{1,0:T(8,128)(2,1)S(1)}, u32[]{:S(2)}, u32[]{:S(2)}) collective-permute-start(bf16[1024,512]{1,0:T(8,128)(2,1)S(1)} %bitcast.66), channel_id=1, source_target_pairs={{0,8},{8,0},{16,24},{24,16},{1,9},{9,1},{17,25},{25,17},{2,10},{10... | collective-permute-start | bytes 3145736 | tf_op jit(solution)/shard_map/ppermute | solution.py:503
  70.7 25.6 %collective-permute-start.17 = (bf16[1024,512]{1,0:T(8,128)(2,1)S(1)}, bf16[1024,512]{1,0:T(8,128)(2,1)S(1)}, u32[]{:S(2)}, u32[]{:S(2)}) collective-permute-start(bf16[1024,512]{1,0:T(8,128)(2,1)S(1)} %bitcast.67), channel_id=1, source_target_pairs={{0,16},{8,24},{16,0},{24,8},{1,17},{9,25},{17,1},{25,9},{2,18},{10... | collective-permute-start | bytes 3145736 | tf_op jit(solution)/shard_map/ppermute | solution.py:503
  111.8 28.1 %collective-permute-start.21 = (bf16[1152,512]{1,0:T(8,128)(2,1)S(1)}, bf16[1152,512]{1,0:T(8,128)(2,1)S(1)}, u32[]{:S(2)}, u32[]{:S(2)}) collective-permute-start(bf16[1152,512]{1,0:T(8,128)(2,1)S(1)} %add_convert_fusion), channel_id=1, source_target_pairs={{0,16},{8,24},{16,0},{24,8},{1,17},{9,25},{17,1},{25,9},{2,18},{10... | collective-permute-start | bytes 3538952 | tf_op jit(solution)/shard_map/ppermute | solution.py:503
  119.5 16.6 %collective-permute-start.23 = (bf16[256,512]{1,0:T(8,128)(2,1)S(1)}, bf16[256,512]{1,0:T(8,128)(2,1)S(1)}, u32[]{:S(2)}, u32[]{:S(2)}) collective-permute-start(bf16[256,512]{1,0:T(8,128)(2,1)S(1)} %get-tuple-element.186), channel_id=1, source_target_pairs={{0,2},{1,3},{2,0},{3,1},{4,6},{5,7},{6,4},{7,5},{8,10},{9,11},{10,... | collective-permute-start | bytes 786440 | tf_op jit(solution)/shard_map/ppermute | solution.py:503
  125.8 14.0 %collective-permute-start.24 = (bf16[256,512]{1,0:T(8,128)(2,1)S(1)}, bf16[256,512]{1,0:T(8,128)(2,1)S(1)}, u32[]{:S(2)}, u32[]{:S(2)}) collective-permute-start(bf16[256,512]{1,0:T(8,128)(2,1)S(1)} %get-tuple-element.187), channel_id=1, source_target_pairs={{0,1},{1,0},{2,3},{3,2},{4,5},{5,4},{6,7},{7,6},{8,9},{9,8},{10,11... | collective-permute-start | bytes 786440 | tf_op jit(solution)/shard_map/ppermute | solution.py:503
  140.0 15.8 %collective-permute-start.26 = (bf16[576,512]{1,0:T(8,128)(2,1)S(1)}, bf16[576,512]{1,0:T(8,128)(2,1)S(1)}, u32[]{:S(2)}, u32[]{:S(2)}) collective-permute-start(bf16[576,512]{1,0:T(8,128)(2,1)S(1)} %sum_1x.1), channel_id=1, source_target_pairs={{0,1},{1,0},{2,3},{3,2},{4,5},{5,4},{6,7},{7,6},{8,9},{9,8},{10,11... | collective-permute-start | bytes 1769480 | tf_op jit(solution)/shard_map/ppermute | solution.py:503
  141.6 24.2 %collective-permute-start.31 = (bf16[512,512]{1,0:T(8,128)(2,1)S(1)}, bf16[512,512]{1,0:T(8,128)(2,1)S(1)}, u32[]{:S(2)}, u32[]{:S(2)}) collective-permute-start(bf16[512,512]{1,0:T(8,128)(2,1)S(1)} %away_x.1), channel_id=1, source_target_pairs={{0,2},{1,3},{2,0},{3,1},{4,6},{5,7},{6,4},{7,5},{8,10},{9,11},{10,... | collective-permute-start | bytes 1572872 | tf_op jit(solution)/shard_map/ppermute | solution.py:503
  147.6 22.6 %collective-permute-start.34 = (bf16[528,512]{1,0:T(8,128)(2,1)S(1)}, bf16[528,512]{1,0:T(8,128)(2,1)S(1)}, u32[]{:S(2)}, u32[]{:S(2)}) collective-permute-start(bf16[528,512]{1,0:T(8,128)(2,1)S(1)} %sum_y2.1.refs_6_), channel_id=1, source_target_pairs={{0,16},{8,24},{16,0},{24,8},{1,17},{9,25},{17,1},{25,9},{2,18},{10... | collective-permute-start | bytes 1622024 | tf_op jit(solution)/shard_map/ppermute | solution.py:503
  149.2 20.9 %collective-permute-start.29 = (bf16[384,512]{1,0:T(8,128)(2,1)S(1)}, bf16[384,512]{1,0:T(8,128)(2,1)S(1)}, u32[]{:S(2)}, u32[]{:S(2)}) collective-permute-start(bf16[384,512]{1,0:T(8,128)(2,1)S(1)} %sum_y3.1), channel_id=1, source_target_pairs={{0,16},{8,24},{16,0},{24,8},{1,17},{9,25},{17,1},{25,9},{2,18},{10... | collective-permute-start | bytes 1179656 | tf_op jit(solution)/shard_map/ppermute | solution.py:503
  150.0 16.5 %collective-permute-start.30 = (bf16[256,512]{1,0:T(8,128)(2,1)S(1)}, bf16[256,512]{1,0:T(8,128)(2,1)S(1)}, u32[]{:S(2)}, u32[]{:S(2)}) collective-permute-start(bf16[256,512]{1,0:T(8,128)(2,1)S(1)} %get-tuple-element.197), channel_id=1, source_target_pairs={{0,4},{1,5},{2,6},{3,7},{4,0},{5,1},{6,2},{7,3},{8,12},{9,13},{10,... | collective-permute-start | bytes 786440 | tf_op jit(solution)/shard_map/ppermute | solution.py:503
  156.0 21.3 %collective-permute-start.27 = (bf16[288,512]{1,0:T(8,128)(2,1)S(1)}, bf16[288,512]{1,0:T(8,128)(2,1)S(1)}, u32[]{:S(2)}, u32[]{:S(2)}) collective-permute-start(bf16[288,512]{1,0:T(8,128)(2,1)S(1)} %sum_1z.1), channel_id=1, source_target_pairs={{0,2},{1,3},{2,0},{3,1},{4,6},{5,7},{6,4},{7,5},{8,10},{9,11},{10,... | collective-permute-start | bytes 884744 | tf_op jit(solution)/shard_map/ppermute | solution.py:503
  171.1 15.4 %collective-permute-start.37 = (bf16[240,512]{1,0:T(8,128)(2,1)S(1)}, bf16[240,512]{1,0:T(8,128)(2,1)S(1)}, u32[]{:S(2)}, u32[]{:S(2)}) collective-permute-start(bf16[240,512]{1,0:T(8,128)(2,1)S(1)} %get-tuple-element.211), channel_id=1, source_target_pairs={{0,3},{1,2},{2,1},{3,0},{4,7},{5,6},{6,5},{7,4},{8,11},{9,10},{10,... | collective-permute-start | bytes 737288 | tf_op jit(solution)/shard_map/ppermute | solution.py:503
  172.3 17.7 %collective-permute-start.35 = (bf16[240,512]{1,0:T(8,128)(2,1)S(1)}, bf16[240,512]{1,0:T(8,128)(2,1)S(1)}, u32[]{:S(2)}, u32[]{:S(2)}) collective-permute-start(bf16[240,512]{1,0:T(8,128)(2,1)S(1)} %get-tuple-element.209.refs_9_), channel_id=1, source_target_pairs={{0,2},{1,3},{2,0},{3,1},{4,6},{5,7},{6,4},{7,5},{8,10},{9,11},{10,... | collective-permute-start | bytes 737288 | tf_op jit(solution)/shard_map/ppermute | solution.py:503
  177.5 12.7 %collective-permute-start.33 = (bf16[272,512]{1,0:T(8,128)(2,1)S(1)}, bf16[272,512]{1,0:T(8,128)(2,1)S(1)}, u32[]{:S(2)}, u32[]{:S(2)}) collective-permute-start(bf16[272,512]{1,0:T(8,128)(2,1)S(1)} %get-tuple-element.205), channel_id=1, source_target_pairs={{0,4},{1,5},{2,6},{3,7},{4,0},{5,1},{6,2},{7,3},{8,12},{9,13},{10,... | collective-permute-start | bytes 835592 | tf_op jit(solution)/shard_map/ppermute | solution.py:503
  (34 other events, 319.1 us)
